TPU v7x, 32 devices: a whole 2x2x4 slice. The times are simulated.
32 devices in a mesh: energy: 4 (over z), slab: 8 (over y, x, core).
Axes of the slice: x: 2, y: 2, z: 4, core: 2. Of those that a mesh axis runs over, the one named last changes fastest.
Arguments:
- pivots: bfloat16 [4, 8, 2, 1024, 1024], P('energy', 'slab')
- injection: bfloat16 [4, 8, 1024, 128], P('energy', 'slab'), may hold values from -3 to 3
- previous: bfloat16 [4, 8, 1024, 128], P('energy', 'slab'), may hold values from -6 to 6
- coupling: bfloat16 [8, 256, 256], P('slab'), may hold values from -0.375 to 0.375
- strength: float32 [4, 4], replicated, may hold values from 0.1 to 1
- block_start: int32 [4, 4], replicated, may hold values from 0 to 12, as said below
- block_count: int32 [4, 4], replicated, may hold values from 0 to 4, as said below
Outputs:
- panel_out: bfloat16 [4, 8, 1024, 128], P('energy', 'slab')
Inputs may be any that keep to these rules, and one draw needn't show every extreme that they name: block_count[e, s] orbital blocks of partner s's panel feed energy e; in every draw some energy takes 4 blocks from every partner, and which one is drawn. block_start[e, s] + block_count[e, s] <= 16.
All inputs are finite; a program needn't handle non-finite values.
Results may differ from a plain program's by a relative error of at most 0.0057.
Values may be sent and summed in bfloat16 or wider, within the bound.
No kernel may reach another device: no remote copies, remote signals or barrier semaphores. Data moves between devices by JAX's collectives and lax.ppermute only.
A program may use at most 128 MiB of HBM per device.

v0:
```python
import jax
import jax.numpy as jnp
from jax import lax
from jax.sharding import PartitionSpec as P

NBLK = 16
CAP = 4


highest = lax.Precision.HIGHEST


def passed_along(block, axis, distance):
    devices = range(lax.axis_size(axis))
    route = [(i - distance, i) for i in devices if i - distance in devices]
    return lax.ppermute(block, axis, route)


def prefix(part, axis, combine, identity, reverse):
    count = lax.axis_size(axis)
    place = lax.axis_index(axis)
    ahead = count - 1 - place if reverse else place
    gathered = jax.tree.map(lambda a: lax.all_gather(a, axis), part)
    state = jax.tree.map(lambda a, e: jnp.zeros_like(a) + jnp.asarray(e, a.dtype), part, identity)

    def one(step, state):
        source = count - 1 - step if reverse else step
        return combine(
            state, jax.tree.map(lambda a: lax.dynamic_index_in_dim(a, source, 0, False), gathered)
        )

    return lax.fori_loop(0, ahead, one, state)


def panel_product(matrix, panel_in):
    half_cols = panel_in.shape[1] // 2
    real_part = jnp.dot(matrix[0], panel_in, preferred_element_type=jnp.float32)
    imag_part = jnp.dot(matrix[1], panel_in, preferred_element_type=jnp.float32)
    return jnp.concatenate(
        [
            real_part[:, :half_cols] - imag_part[:, half_cols:],
            real_part[:, half_cols:] + imag_part[:, :half_cols],
        ],
        axis=1,
    )


def map_apply(mapping, vector):
    half_cols = vector.shape[1] // 2
    real_part = jnp.dot(mapping[0], vector, precision=highest)
    imag_part = jnp.dot(mapping[1], vector, precision=highest)
    return jnp.concatenate(
        [
            real_part[:, :half_cols] - imag_part[:, half_cols:],
            real_part[:, half_cols:] + imag_part[:, :half_cols],
        ],
        axis=1,
    )


def map_compose(later_map, earlier_map):
    real_part = jnp.dot(later_map[0], earlier_map[0], precision=highest) - jnp.dot(
        later_map[1], earlier_map[1], precision=highest
    )
    imag_part = jnp.dot(later_map[0], earlier_map[1], precision=highest) + jnp.dot(
        later_map[1], earlier_map[0], precision=highest
    )
    return jnp.stack([real_part, imag_part])


def combine_maps(earlier, later):
    return (map_compose(later[0], earlier[0]), map_apply(later[0], earlier[1]) + later[1])


def body(pivots, injection, previous, coupling, strength, block_start, block_count):
    green = pivots[0, 0]
    norb = green.shape[1]
    layer = coupling.shape[1]
    width_cols = injection.shape[3]
    block_rows = norb // NBLK
    coupling_block = coupling[0]
    coupling_f = coupling_block.astype(jnp.float32)
    my_energy = lax.axis_index("energy")
    prev_blocks = previous[0, 0].reshape(NBLK, block_rows, width_cols)
    recv_start = lax.dynamic_index_in_dim(block_start, my_energy, 0, keepdims=False)
    recv_count = lax.dynamic_index_in_dim(block_count, my_energy, 0, keepdims=False)
    recv_strength = lax.dynamic_index_in_dim(strength, my_energy, 0, keepdims=False)
    block_ids = jnp.arange(NBLK, dtype=jnp.int32)
    slot_ids = jnp.arange(CAP, dtype=jnp.int32)
    send_start = lax.dynamic_index_in_dim(block_start, my_energy, 1, keepdims=False)
    send_count = lax.dynamic_index_in_dim(block_count, my_energy, 1, keepdims=False)
    block_index = jnp.minimum(send_start[:, None] + slot_ids[None, :], NBLK - 1)
    picked = jnp.take(prev_blocks, block_index, axis=0)
    live_slots = slot_ids[None, :] < send_count[:, None]
    picked = jnp.where(live_slots[:, :, None, None], picked, jnp.zeros_like(picked))
    received = lax.all_to_all(picked, "energy", split_axis=0, concat_axis=0, tiled=True)
    target_block = recv_start[:, None] + slot_ids[None, :]
    used_slots = slot_ids[None, :] < recv_count[:, None]
    placed = (block_ids[:, None, None] == target_block[None]) & used_slots[None]
    weight_table = jnp.where(placed, recv_strength[None, :, None], 0.0)
    scattered = jnp.einsum(
        "kec,ecrq->krq", weight_table, received.astype(jnp.float32), precision=highest
    )
    right_side = (injection[0, 0].astype(jnp.float32) + scattered.reshape(norb, width_cols)).astype(
        jnp.bfloat16
    )
    direct = panel_product(green, right_side)
    corner_block = green[:, norb - layer :, :layer]
    identity_map = jnp.stack(
        [jnp.eye(layer, dtype=jnp.float32), jnp.zeros((layer, layer), jnp.float32)]
    )
    zero_vec = jnp.zeros((layer, width_cols), jnp.float32)
    coupling_prior = passed_along(coupling, "slab", 1)[0]
    link_map = jnp.einsum(
        "kwu,vu->kwv", corner_block, coupling_prior, preferred_element_type=jnp.float32
    )
    seed_vec = direct[norb - layer :]
    prefix_maps, prefix_vec = prefix(
        (link_map, seed_vec), "slab", combine_maps, (identity_map, zero_vec), False
    )
    carried_vec = jnp.dot(coupling_prior.astype(jnp.float32).T, prefix_vec, precision=highest)
    forward = direct + panel_product(green[:, :, :layer], carried_vec.astype(jnp.bfloat16))
    back_map = jnp.einsum(
        "kwv,vu->kwu",
        green[:, :layer, norb - layer :],
        coupling_block,
        preferred_element_type=jnp.float32,
    )
    suffix_maps, suffix_vec = prefix(
        (back_map, forward[:layer]), "slab", combine_maps, (identity_map, zero_vec), True
    )
    outgoing = jnp.dot(coupling_f, suffix_vec, precision=highest).astype(jnp.bfloat16)
    panel_slab = (forward + panel_product(green[:, :, norb - layer :], outgoing)).astype(
        jnp.bfloat16
    )
    return panel_slab[None, None]


def solution(mesh):
    in_specs = (
        P("energy", "slab", None, None, None),
        P("energy", "slab", None, None),
        P("energy", "slab", None, None),
        P("slab", None, None),
        P(),
        P(),
        P(),
    )
    out_specs = P("energy", "slab", None, None)
    return jax.shard_map(body, mesh=mesh, in_specs=in_specs, out_specs=out_specs, check_vma=False)
```

profile of v0, /device:TPU:0, one launch (start us, length us, event | category | flops | bytes accessed | tf_op | source)
XLA Modules:
  0.0 208.2 jit_solution(3827761457979151533)
XLA Ops:
  9.4 6.3 %all-to-all-start = ((bf16[4,4,64,128]{3,1,2,0:T(4,128)(2,1)}), bf16[4,4,64,128]{3,1,2,0:T(4,128)(2,1)S(1)}, u32[]{:S(2)}, u32[]{:S(2)}) async-start(bf16[4,4,64,128]{3,1,2,0:T(4,128)(2,1)} %copy.17), calls=%async_computation | async-start | bytes 524288 | tf_op jit(solution)/shard_map/all_to_all | solution.py:96
  18.2 6.5 %all-to-all-done = bf16[4,4,64,128]{3,1,2,0:T(4,128)(2,1)S(1)} async-done(((bf16[4,4,64,128]{3,1,2,0:T(4,128)(2,1)}), bf16[4,4,64,128]{3,1,2,0:T(4,128)(2,1)S(1)}, u32[]{:S(2)}, u32[]{:S(2)}) %all-to-all-start) | async-done | bytes 262176 | tf_op jit(solution)/shard_map/all_to_all | solution.py:96
  25.7 2.7 %fusion.14 = f32[1024,128]{0,1:T(8,128)S(1)} fusion(bf16[1024,128]{1,0:T(8,128)(2,1)S(1)} %bitcast.159, bf16[1,1,2,1024,1024]{4,3,2,1,0:T(8,128)(2,1)} %param.11), kind=kOutput, calls=%fused_computation.29 | convolution fusion | flops 268435456 | bytes 2883584 | tf_op jit(solution)/shard_map/dot_general | solution.py:37
  32.4 2.0 fusion.28
  34.5 18.3 %all-gather.11.cloned.1.call-done = f32[2048,128]{0,1:T(8,128)} async-done(((f32[256,128]{0,1:T(8,128)}), f32[2048,128]{0,1:T(8,128)}) %all-gather.11.cloned.1.call-update) | async-done | bytes 1048592 | tf_op jit(solution)/shard_map/all_gather | solution.py:23
  52.7 1.6 copy.27
  54.3 36.9 %all-gather.9.cloned.1.call-done = f32[16,256,256]{2,1,0:T(8,128)} async-done(((f32[2,256,256]{2,1,0:T(8,128)}), f32[16,256,256]{2,1,0:T(8,128)}) %all-gather.9.cloned.1.call-update) | async-done | bytes 4194320 | tf_op jit(solution)/shard_map/all_gather | solution.py:23
  95.0 2.0 fusion.26
  97.0 41.8 %all-gather.15.cloned.1.call-done = f32[2048,128]{0,1:T(8,128)} async-done(((f32[256,128]{0,1:T(8,128)}), f32[2048,128]{0,1:T(8,128)}) %all-gather.15.cloned.1.call-update) | async-done | bytes 1048592 | tf_op jit(solution)/shard_map/all_gather | solution.py:23
  138.9 1.6 copy.28
  140.4 36.8 %all-gather.13.cloned.1.call-done = f32[16,256,256]{2,1,0:T(8,128)} async-done(((f32[2,256,256]{2,1,0:T(8,128)}), f32[16,256,256]{2,1,0:T(8,128)}) %all-gather.13.cloned.1.call-update) | async-done | bytes 4194320 | tf_op jit(solution)/shard_map/all_gather | solution.py:23
  177.2 20.4 %while.27 = (s32[]{:T(128)}, f32[256,128]{0,1:T(8,128)S(1)}, s32[]{:T(128)}, f32[8,2,256,256]{3,2,1,0:T(8,128)}, f32[8,256,128]{1,0,2:T(8,128)S(1)}, /*index=5*/s32[]{:T(128)}, s32[]{:T(128)}, s32[]{:T(128)}, s32[]{:T(128)}, s32[]{}) while((s32[]{:T(128)}, f32[256,128]{0,1:T(8,128)S(1)}, s32[]{:T(128)}, f32[8,2,256,256]{3,2,1,0:T(8,128)}, ...), condition=%wide.region_3.4_spmd, body=%wide.region_2.3_spmd.sunk | while | flops 201424896 | bytes 2097327 | solution.py:32
  177.3 1.4 fusion.75
  178.6 1.4 fusion.76
  180.2 1.4 fusion.75
  181.6 1.4 fusion.76
  183.1 1.4 fusion.75
  184.5 1.4 fusion.76
  186.0 1.4 fusion.75
  187.4 1.4 fusion.76
  188.9 1.4 fusion.75
  190.3 1.4 fusion.76
  191.8 1.4 fusion.75
  194.8 1.4 fusion.75
  (72 shorter events, 21.6 us)
Async XLA Ops:
  6.5 1.3 copy-start
  9.4 15.3 %all-to-all-start = ((bf16[4,4,64,128]{3,1,2,0:T(4,128)(2,1)}), bf16[4,4,64,128]{3,1,2,0:T(4,128)(2,1)S(1)}, u32[]{:S(2)}, u32[]{:S(2)}) async-start(bf16[4,4,64,128]{3,1,2,0:T(4,128)(2,1)} %copy.17), calls=%async_computation | async-start | bytes 524288 | tf_op jit(solution)/shard_map/all_to_all | solution.py:96
  15.8 36.9 %all-gather.11.cloned.1.call-start = ((), (), s32[]{:S(2)}) async-start(), calls=%async_computation.2 | async-start | bytes 1179648 | tf_op jit(solution)/shard_map/all_gather | solution.py:23
  24.7 3.7 %copy-start.1 = (bf16[1,1,2,1024,1024]{4,3,2,1,0:T(8,128)(2,1)S(1)}, bf16[1,1,2,1024,1024]{4,3,2,1,0:T(8,128)(2,1)}, u32[]{:S(2)}) copy-start(bf16[1,1,2,1024,1024]{4,3,2,1,0:T(8,128)(2,1)} %param.11) | copy-start | bytes 12582916
  25.7 4.4 %copy-start.2 = (bf16[1,256,256]{2,1,0:T(8,128)(2,1)S(1)}, bf16[1,256,256]{2,1,0:T(8,128)(2,1)}, u32[]{:S(2)}) copy-start(bf16[1,256,256]{2,1,0:T(8,128)(2,1)} %param.14) | copy-start | bytes 393220
  30.0 61.2 %all-gather.9.cloned.1.call-start = ((), (), s32[]{:S(2)}) async-start(), calls=%async_computation.1 | async-start | bytes 4718592 | tf_op jit(solution)/shard_map/all_gather | solution.py:23
  30.1 2.3 %collective-permute-start = (bf16[1,256,256]{2,1,0:T(8,128)(2,1)S(1)}, bf16[1,256,256]{2,1,0:T(8,128)(2,1)S(1)}, u32[]{:S(2)}, u32[]{:S(2)}) collective-permute-start(bf16[1,256,256]{2,1,0:T(8,128)(2,1)S(1)} %copy-done.2), channel_id=1, source_target_pairs={{0,1},{1,2},{2,3},{3,4},{4,5},{5,6},{6,7},{8,9},{9,10},{10,11},{11... | collective-permute-start | bytes 393224 | tf_op jit(solution)/shard_map/ppermute | solution.py:16
  34.4 104.5 %all-gather.15.cloned.1.call-start = ((), (), s32[]{:S(2)}) async-start(), calls=%async_computation.4 | async-start | bytes 1179648 | tf_op jit(solution)/shard_map/all_gather | solution.py:23
  95.0 82.3 %all-gather.13.cloned.1.call-start = ((), (), s32[]{:S(2)}) async-start(), calls=%async_computation.3 | async-start | bytes 4718592 | tf_op jit(solution)/shard_map/all_gather | solution.py:23
Sparse Core Ops, SparseCore 0:
  30.2 22.5 all-gather.10
  54.6 36.5 all-gather.8
  95.1 43.7 all-gather.14
  140.6 36.5 all-gather.12
where the time goes:
time: 209 us; the launch traced here: 208 us
  waiting for transfers between devices  141 us (67%)
  matrix products  33.4 us (16%)
  between operations  13.3 us (6%)
  local copies, waits for them, and re-layouts  8.69 us (4%)
  starting transfers between devices  7.77 us (4%)
  other arithmetic  3.23 us (2%)
    all_gather x4, waiting for transfers between devices, prefix(): gathered = jax.tree.map(lambda a: lax.all_gather(a, axis), part)  134 us
    dot_general x7, matrix products, map_apply(): imag_part = jnp.dot(mapping[1], vector, precision=highest)  9.52 us
    dot_general x7, matrix products, map_apply(): real_part = jnp.dot(mapping[0], vector, precision=highest)  9.49 us
    all_to_all x1, waiting for transfers between devices, body(): lax.all_to_all(picked, 'energy', split_axis=0, concat_axis=0, tiled=True)  6.49 us
    all_to_all x1, starting transfers between devices, body(): lax.all_to_all(picked, 'energy', split_axis=0, concat_axis=0, tiled=True)  6.35 us
    dot_general x3, matrix products, panel_product(): real_part = jnp.dot(matrix[0], panel_in, preferred_element_type=jnp.float32)  5.39 us
  transfers between devices with their start and end apart: 6, of which 6 were waited for; matrix products, arithmetic and copies ran while one was open for 5% of the time, Pallas kernels for 0%

commit v1 on v0

v1 whole, which is shorter than its diff:
```python
import jax
import jax.numpy as jnp
from jax import lax
from jax.sharding import PartitionSpec as P

NBLK = 16
CAP = 4
bf16 = jnp.bfloat16
f32 = jnp.float32


def swapped(block, axis, mask):
    count = lax.axis_size(axis)
    return lax.ppermute(block, axis, [(i, i ^ mask) for i in range(count)])


def turned(v):
    half = v.shape[1] // 2
    return jnp.concatenate([-v[:, half:], v[:, :half]], axis=1)


def doubled(v):
    return jnp.concatenate([v, turned(v)], axis=0)


def applied(wide, v):
    return jnp.dot(wide, doubled(v), preferred_element_type=f32)


def panel_product(real, imag, v):
    return jnp.dot(real, v, preferred_element_type=f32) + jnp.dot(
        imag, turned(v), preferred_element_type=f32
    )


def body(pivots, injection, previous, coupling, strength, block_start, block_count):
    green = pivots[0, 0]
    norb = green.shape[1]
    layer = coupling.shape[1]
    width = injection.shape[3]
    rows = norb // NBLK
    span = rows * CAP
    coup = coupling[0]
    energies = lax.axis_size("energy")
    slabs = lax.axis_size("slab")
    levels = slabs.bit_length() - 1
    me = lax.axis_index("energy")
    at = lax.axis_index("slab")
    bits = [((at >> k) & 1) == 1 for k in range(levels)]
    low = slice(norb - layer, norb)

    panel = previous[0, 0]
    received = [None] * energies
    for mask in range(energies - 1, 0, -1):
        first = block_start[me ^ mask, me] * rows
        piece = lax.dynamic_slice(panel, (first, 0), (span, width))
        received[mask] = swapped(piece, "energy", mask)
    first = block_start[me, me] * rows
    received[0] = lax.dynamic_slice(panel, (first, 0), (span, width))

    forward_map = jnp.concatenate(
        [
            jnp.dot(coup.T, green[k, low, :layer], preferred_element_type=f32).astype(bf16)
            for k in range(2)
        ],
        axis=1,
    )
    backward_map = jnp.concatenate(
        [
            jnp.dot(green[k, :layer, low], coup, preferred_element_type=f32).astype(bf16)
            for k in range(2)
        ],
        axis=1,
    )

    groups = []
    own = (forward_map, backward_map)
    prefix = [None, None]
    for level in range(levels):
        last = level == levels - 1
        theirs = (None, None)
        if level == 0:
            both = swapped(jnp.concatenate(own, axis=0), "slab", 1)
            theirs = (both[:layer], both[layer:])
        elif not last:
            mine = jnp.where(bits[0], own[1], own[0])
            near = swapped(mine, "slab", 1 << level)
            far = swapped(near, "slab", 1)
            theirs = (jnp.where(bits[0], far, near), jnp.where(bits[0], near, far))
        plan, grown = [], []
        for way in range(2):
            after = bits[level] if way == 0 else ~bits[level]
            later = None if last else jnp.where(after, own[way], theirs[way])
            plan.append((after, prefix[way], later))
            if last:
                continue
            earlier = jnp.where(after, theirs[way], own[way])
            grown.append(applied(later, earlier).astype(bf16) if level + 2 < levels else None)
            if level == 0:
                unit = jnp.concatenate(
                    [jnp.eye(layer, dtype=bf16), jnp.zeros((layer, layer), bf16)], axis=1
                )
                prefix[way] = jnp.where(after, theirs[way], unit)
            else:
                prefix[way] = jnp.where(
                    after, applied(prefix[way], theirs[way]).astype(bf16), prefix[way]
                )
        own = tuple(grown)
        groups.append(plan)

    def scan(vector, way):
        total = vector.astype(bf16)
        reach = None
        for level in range(levels):
            after, before, later = groups[level][way]
            last = level == levels - 1
            if last:
                half = slabs // 2
                if way == 0:
                    route = [(i, i + half) for i in range(half)]
                else:
                    route = [(i + half, i) for i in range(half)]
                other = lax.ppermute(total, "slab", route)
            else:
                other = swapped(total, "slab", 1 << level)
            if level == 0:
                reach = jnp.where(after, other, jnp.zeros_like(other)).astype(f32)
            else:
                reach = reach + jnp.where(after, applied(before, other), 0.0)
            if not last:
                earlier = jnp.where(after, other, total)
                latest = jnp.where(after, total, other)
                total = (applied(later, earlier) + latest.astype(f32)).astype(bf16)
        return reach

    scattered = injection[0, 0].astype(f32)
    slot = lax.broadcasted_iota(jnp.int32, (span, 1), 0) // rows
    for mask in range(energies):
        s = me ^ mask
        weight = jnp.where(slot < block_count[me, s], strength[me, s], 0.0)
        first = block_start[me, s] * rows
        held = lax.dynamic_slice(scattered, (first, 0), (span, width))
        scattered = lax.dynamic_update_slice(
            scattered, held + weight * received[mask].astype(f32), (first, 0)
        )
    source = scattered.astype(bf16)

    direct_low = panel_product(green[0, low], green[1, low], source)
    sent = jnp.dot(coup.T, direct_low.astype(bf16), preferred_element_type=f32)
    incoming = scan(sent, 0).astype(bf16)

    direct_top = panel_product(green[0, :layer], green[1, :layer], source)
    forward_top = direct_top + panel_product(green[0, :layer, :layer], green[1, :layer, :layer], incoming)
    coming_back = scan(forward_top, 1)

    direct_rest = panel_product(green[0, layer:], green[1, layer:], source)
    forward_rest = direct_rest + panel_product(green[0, layer:, :layer], green[1, layer:, :layer], incoming)
    outgoing = jnp.dot(coup, coming_back.astype(bf16), preferred_element_type=f32).astype(bf16)
    out = jnp.concatenate([forward_top, forward_rest], axis=0) + panel_product(
        green[0, :, low], green[1, :, low], outgoing
    )
    return out.astype(bf16)[None, None]


def solution(mesh):
    in_specs = (
        P("energy", "slab", None, None, None),
        P("energy", "slab", None, None),
        P("energy", "slab", None, None),
        P("slab", None, None),
        P(),
        P(),
        P(),
    )
    out_specs = P("energy", "slab", None, None)
    return jax.shard_map(body, mesh=mesh, in_specs=in_specs, out_specs=out_specs, check_vma=False)
```

time: 209 us -> 78.7 us (0.38)
  waiting for transfers between devices: 141 us -> 17.4 us
  between operations: 13.3 us -> 4.89 us
  starting transfers between devices: 7.77 us -> 13.9 us
  matrix products: 33.4 us -> 27.4 us
  other arithmetic: 3.23 us -> 7.77 us
  local copies, waits for them, and re-layouts: 8.69 us -> 6.33 us
    all_gather x4 -> x0, waiting for transfers between devices: 134 us -> none  [prefix(): gathered = jax.tree.map(lambda a: lax.all_gather(a, axis), part)]
    ppermute x1 -> x12, waiting for transfers between devices: 0.96 us -> 17.4 us  [the longest x10 10.9 us: swapped(): return lax.ppermute(block, axis, [(i, i ^ mask) for i in range(count)])]
    ppermute x1 -> x12, starting transfers between devices: 1.3 us -> 13.9 us  [the longest x10 9.15 us: swapped(): return lax.ppermute(block, axis, [(i, i ^ mask) for i in range(count)])]
    all_to_all x1 -> x0, waiting for transfers between devices: 6.49 us -> none  [body(): lax.all_to_all(picked, 'energy', split_axis=0, concat_axis=0, tiled=True)]
    all_to_all x1 -> x0, starting transfers between devices: 6.35 us -> none  [body(): lax.all_to_all(picked, 'energy', split_axis=0, concat_axis=0, tiled=True)]
    dot_general x25 -> x27, matrix products: 33.4 us -> 27.4 us  [the longest x6 8.53 us: panel_product(): jnp.dot(real, v, preferred_element_type=f32)]
    select_n x2 -> x9, other arithmetic: 0.18 us -> 5.13 us  [the longest x3 4.93 us: body(): weight = jnp.where(slot < block_count[me, s], strength[me, s], 0.0)]
    dynamic_slice x8 -> x4, local copies, waits for them, and re-layouts: 1.64 us -> 5.48 us  [the longest x2 2.95 us: body(): weight = jnp.where(slot < block_count[me, s], strength[me, s], 0.0)]
  transfers between devices with their start and end apart: 6 -> 12, of which waited for: 6 -> 6; matrix products, arithmetic and copies ran while one was open for 5% -> 37% of each run, Pallas kernels for 0% -> 0%
where the time goes in v1:
time: 78.7 us; the launch traced here: 77.7 us
  matrix products  27.4 us (35%)
  waiting for transfers between devices  17.4 us (22%)
  starting transfers between devices  13.9 us (18%)
  other arithmetic  7.77 us (10%)
  local copies, waits for them, and re-layouts  6.33 us (8%)
  between operations  4.89 us (6%)
    ppermute x10, waiting for transfers between devices, swapped(): return lax.ppermute(block, axis, [(i, i ^ mask) for i in range(count)])  10.9 us
    ppermute x10, starting transfers between devices, swapped(): return lax.ppermute(block, axis, [(i, i ^ mask) for i in range(count)])  9.15 us
    dot_general x6, matrix products, panel_product(): jnp.dot(real, v, preferred_element_type=f32)  8.53 us
    dot_general x5, matrix products, panel_product(): jnp.dot(imag, turned(v), preferred_element_type=f32)  7.41 us
    ppermute x2, waiting for transfers between devices, scan(): other = lax.ppermute(total, 'slab', route)  6.49 us
    dot_general x10, matrix products, applied(): return jnp.dot(wide, doubled(v), preferred_element_type=f32)  5.14 us
    select_n x3, other arithmetic, body(): weight = jnp.where(slot < block_count[me, s], strength[me, s], 0.0)  4.93 us
    ppermute x2, starting transfers between devices, scan(): other = lax.ppermute(total, 'slab', route)  4.72 us
  transfers between devices with their start and end apart: 12, of which 6 were waited for; matrix products, arithmetic and copies ran while one was open for 37% of the time, Pallas kernels for 0%

profile of v1, /device:TPU:0, one launch (start us, length us, event | category | flops | bytes accessed | tf_op | source)
XLA Modules:
  0.0 77.7 jit_solution(16636531317136755998)
XLA Ops:
  0.0 1.6 %fusion.159 = (s32[1,1]{1,0:T(1,128)}, s32[1,1]{1,0:T(1,128)}, s32[1,1]{1,0:T(1,128)}, s32[1,1]{1,0:T(1,128)}, s32[1,1]{1,0:T(1,128)}, /*index=5*/s32[1,1]{1,0:T(1,128)}, s32[1,1]{1,0:T(1,128)}) fusion(s32[4,4]{1,0:T(4,128)} %param.12, s32[]{:T(128)S(6)} %select_n.270, s32[]{:T(128)S(6)} %select_n.258, s32[]{:T(128)S(6)} %select_n.266, s32[]{:T(128)S(6)} %select_n.262), kind=kLoop, calls=%fused_computation.217 | loop fusion | bytes 72 | tf_op jit(solution)/shard_map/dynamic_slice | solution.py:55
  4.4 3.1 %collective-permute-start = (bf16[256,128]{1,0:T(8,128)(2,1)S(1)}, bf16[256,128]{1,0:T(8,128)(2,1)S(1)}, u32[]{:S(2)}, u32[]{:S(2)}) collective-permute-start(bf16[256,128]{1,0:T(8,128)(2,1)S(1)} %get-tuple-element.12), channel_id=1, source_target_pairs={{0,8},{8,0},{16,24},{24,16},{1,9},{9,1},{17,25},{25,17},{2,10},{10... | collective-permute-start | bytes 196616 | tf_op jit(solution)/shard_map/ppermute | solution.py:14
  7.5 2.6 %collective-permute-start.1 = (bf16[256,128]{1,0:T(8,128)(2,1)S(1)}, bf16[256,128]{1,0:T(8,128)(2,1)S(1)}, u32[]{:S(2)}, u32[]{:S(2)}) collective-permute-start(bf16[256,128]{1,0:T(8,128)(2,1)S(1)} %get-tuple-element.13), channel_id=1, source_target_pairs={{0,16},{8,24},{16,0},{24,8},{1,17},{9,25},{17,1},{25,9},{2,18},{10... | collective-permute-start | bytes 196616 | tf_op jit(solution)/shard_map/ppermute | solution.py:14
  17.4 1.5 %fusion.157 = (s32[1,1]{1,0:T(1,128)}, s32[1,1]{1,0:T(1,128)}, s32[1,1]{1,0:T(1,128)}, s32[1,1]{1,0:T(1,128)}) fusion(s32[4,4]{1,0:T(4,128)} %param.13, s32[]{:T(128)S(6)} %select_n.258, s32[]{:T(128)S(6)} %select_n.270, s32[]{:T(128)S(6)} %select_n.262, s32[]{:T(128)S(6)} %select_n.266), kind=kLoop, calls=%fused_computation.215 | loop fusion | bytes 48 | tf_op jit(solution)/shard_map/dynamic_slice | solution.py:140
  18.8 1.5 %fusion.158 = (f32[1,1]{1,0:T(1,128)}, f32[1,1]{1,0:T(1,128)}, f32[1,1]{1,0:T(1,128)}, f32[1,1]{1,0:T(1,128)}) fusion(f32[4,4]{1,0:T(4,128)} %param.11, s32[]{:T(128)S(6)} %select_n.258, s32[]{:T(128)S(6)} %select_n.270, s32[]{:T(128)S(6)} %select_n.262, s32[]{:T(128)S(6)} %select_n.266), kind=kLoop, calls=%fused_computation.216 | loop fusion | bytes 48 | tf_op jit(solution)/shard_map/dynamic_slice | solution.py:140
  23.5 2.5 %compare_select_fusion = (f32[256]{0:T(256)S(1)}, f32[256]{0:T(256)S(1)}) fusion(f32[]{:T(128)} %bitcast.18, s32[]{:T(128)} %bitcast.17, f32[]{:T(128)} %bitcast.13, s32[]{:T(128)} %bitcast.12), kind=kLoop, calls=%fused_computation.192 | loop fusion | flops 3072 | bytes 2064 | tf_op jit(solution)/shard_map/jit(_where)/select_n | solution.py:140
  27.8 1.4 %fusion.24 = f32[128,256]{1,0:T(8,128)S(1)} fusion(bf16[1024,128]{1,0:T(8,128)(2,1)S(1)} %convert_element_type.115, bf16[2,1024,1024]{2,1,0:T(8,128)(2,1)} %bitcast.123), kind=kOutput, calls=%fused_computation.51 | convolution fusion | flops 67108864 | bytes 917504 | tf_op jit(solution)/shard_map/dot_general | solution.py:31
  29.2 2.2 %fusion = f32[128,768]{1,0:T(8,128)S(1)} fusion(bf16[2,1024,1024]{2,1,0:T(8,128)(2,1)} %bitcast.124, bf16[1024,64]{1,0:T(8,128)(2,1)S(1)} %get-tuple-element.10, bf16[1024,64]{1,0:T(8,128)(2,1)S(1)} %get-tuple-element.9), kind=kOutput, calls=%fused_computation.1 | convolution fusion | flops 201850880 | bytes 2228224 | tf_op jit(solution)/shard_map/dot_general | solution.py:31
  31.4 2.1 %fusion.9 = f32[128,768]{1,0:T(8,128)S(1)} fusion(f32[128,768]{1,0:T(8,128)S(1)} %fusion, bf16[1024,128]{1,0:T(8,128)(2,1)S(1)} %convert_element_type.115, bf16[2,1024,1024]{2,1,0:T(8,128)(2,1)} %bitcast.125), kind=kOutput, calls=%fused_computation.17 | convolution fusion | flops 201424896 | bytes 2621440 | tf_op jit(solution)/shard_map/dot_general | solution.py:31
  33.5 1.6 %fusion.22 = bf16[256,128]{0,1:T(8,128)(2,1)S(1)} fusion(f32[128,256]{1,0:T(8,128)S(1)} %fusion.24, bf16[2,1024,1024]{2,1,0:T(8,128)(2,1)} %bitcast.126, bf16[1,256,256]{2,1,0:T(8,128)(2,1)S(1)} %copy-done, bf16[1024,64]{1,0:T(8,128)(2,1)S(1)} %get-tuple-element.10, bf16[1024,64]{1,0:T(8,128)(2,1)S(1)} %get-tuple-element.9), kind=kOutput, calls=%fused_computation.45 | convolution fusion | flops 84508672 | bytes 1114112 | tf_op jit(solution)/shard_map/dot_general | solution.py:149
  35.6 1.4 %fusion.25 = f32[128,256]{1,0:T(8,128)S(1)} fusion(bf16[1024,128]{1,0:T(8,128)(2,1)S(1)} %convert_element_type.115, bf16[2,1024,1024]{2,1,0:T(8,128)(2,1)} %bitcast.127), kind=kOutput, calls=%fused_computation.54 | convolution fusion | flops 67108864 | bytes 917504 | tf_op jit(solution)/shard_map/dot_general | solution.py:31
  37.3 1.7 %collective-permute-start.5 = (bf16[256,128]{0,1:T(8,128)(2,1)S(1)}, bf16[256,128]{0,1:T(8,128)(2,1)S(1)}, u32[]{:S(2)}, u32[]{:S(2)}) collective-permute-start(bf16[256,128]{0,1:T(8,128)(2,1)S(1)} %fusion.18), channel_id=1, source_target_pairs={{0,2},{1,3},{2,0},{3,1},{4,6},{5,7},{6,4},{7,5},{8,10},{9,11},{10,... | collective-permute-start | bytes 196616 | tf_op jit(solution)/shard_map/ppermute | solution.py:14
  41.7 6.9 %collective-permute-done.6 = bf16[256,512]{0,1:T(8,128)(2,1)S(1)} collective-permute-done((bf16[256,512]{0,1:T(8,128)(2,1)S(1)}, bf16[256,512]{0,1:T(8,128)(2,1)S(1)}, u32[]{:S(2)}, u32[]{:S(2)}) %collective-permute-start.6) | collective-permute-done | bytes 262176 | tf_op jit(solution)/shard_map/ppermute | solution.py:14
  50.3 3.4 %collective-permute-start.8 = (bf16[256,128]{0,1:T(8,128)(2,1)S(1)}, bf16[256,128]{0,1:T(8,128)(2,1)S(1)}, u32[]{:S(2)}, u32[]{:S(2)}) collective-permute-start(bf16[256,128]{0,1:T(8,128)(2,1)S(1)} %fusion.19), channel_id=1, source_target_pairs={{0,4},{1,5},{2,6},{3,7},{8,12},{9,13},{10,14},{11,15},{16,20},{17,... | collective-permute-start | bytes 196616 | tf_op jit(solution)/shard_map/ppermute | solution.py:123
  53.8 1.9 %collective-permute-done.8 = bf16[256,128]{0,1:T(8,128)(2,1)S(1)} collective-permute-done((bf16[256,128]{0,1:T(8,128)(2,1)S(1)}, bf16[256,128]{0,1:T(8,128)(2,1)S(1)}, u32[]{:S(2)}, u32[]{:S(2)}) %collective-permute-start.8) | collective-permute-done | bytes 65568 | tf_op jit(solution)/shard_map/ppermute | solution.py:123
  55.7 1.4 %fusion.41 = bf16[256,128]{0,1:T(8,128)(2,1)S(1)} fusion(bf16[256,256]{0,1:T(8,128)(2,1)S(1)} %get-tuple-element.17, bf16[256,256]{0,1:T(8,128)(2,1)S(1)} %get-tuple-element.16, bf16[256,512]{0,1:T(8,128)(2,1)S(1)} %get-tuple-element.5, pred[]{:T(512)S(6)} %eq.14, pred[256,256]{0,1:T(32,128)(4,1)S(1)} %iota_compare_fusion, pred[]{:T(512)S(6)} %eq.13, ...), kind=kOutput, calls=%fused_computation.68 | convolution fusion | flops 170721280 | bytes 1575424 | tf_op jit(solution)/shard_map/dot_general | solution.py:27
  59.3 1.5 %fusion.160 = (bf16[256,128]{0,1:T(8,128)(2,1)S(1)}, f32[256,128]{0,1:T(8,128)S(1)}) fusion(f32[128,256]{1,0:T(8,128)S(1)} %convolution_add_fusion.8, f32[128,256]{1,0:T(8,128)S(1)} %fusion.25, bf16[2,1024,1024]{2,1,0:T(8,128)(2,1)} %bitcast.130, bf16[1024,64]{1,0:T(8,128)(2,1)S(1)} %get-tuple-element.10, bf16[1024,64]{1,0:T(8,128)(2,1)S(1)} %get-tuple-element.9), kind=kOutput, calls=%fused_computation.218 | convolution fusion | flops 67731456 | bytes 1245184 | tf_op jit(solution)/shard_map/dot_general | solution.py:31
  60.9 1.3 %fusion.68 = f32[128,768]{1,0:T(8,128)S(1)} fusion(bf16[256,128]{0,1:T(8,128)(2,1)S(1)} %fusion.41, bf16[2,1024,1024]{2,1,0:T(8,128)(2,1)} %bitcast.131), kind=kOutput, calls=%fused_computation.83 | convolution fusion | flops 50331648 | bytes 851968 | tf_op jit(solution)/shard_map/dot_general | solution.py:31
  63.0 1.3 %fusion.8 = f32[768,128]{0,1:T(8,128)S(1)} fusion(f32[128,768]{1,0:T(8,128)S(1)} %fusion.9, f32[128,768]{1,0:T(8,128)S(1)} %fusion.68, bf16[2,1024,1024]{2,1,0:T(8,128)(2,1)} %bitcast.132, bf16[256,64]{0,1:T(8,128)(2,1)S(1)} %get-tuple-element.35, bf16[256,64]{0,1:T(8,128)(2,1)S(1)} %get-tuple-element.34), kind=kOutput, calls=%fused_computation.16 | convolution fusion | flops 50659328 | bytes 1638400 | tf_op jit(solution)/shard_map/dot_general | solution.py:31
  64.3 2.7 %collective-permute-done.10 = bf16[256,128]{0,1:T(8,128)(2,1)S(1)} collective-permute-done((bf16[256,128]{0,1:T(8,128)(2,1)S(1)}, bf16[256,128]{0,1:T(8,128)(2,1)S(1)}, u32[]{:S(2)}, u32[]{:S(2)}) %collective-permute-start.10) | collective-permute-done | bytes 65568 | tf_op jit(solution)/shard_map/ppermute | solution.py:14
  67.2 1.3 %collective-permute-start.11 = (bf16[256,128]{0,1:T(8,128)(2,1)S(1)}, bf16[256,128]{0,1:T(8,128)(2,1)S(1)}, u32[]{:S(2)}, u32[]{:S(2)}) collective-permute-start(bf16[256,128]{0,1:T(8,128)(2,1)S(1)} %fusion.21), channel_id=1, source_target_pairs={{4,0},{5,1},{6,2},{7,3},{12,8},{13,9},{14,10},{15,11},{20,16},{21,... | collective-permute-start | bytes 196616 | tf_op jit(solution)/shard_map/ppermute | solution.py:123
  68.8 4.6 %collective-permute-done.11 = bf16[256,128]{0,1:T(8,128)(2,1)S(1)} collective-permute-done((bf16[256,128]{0,1:T(8,128)(2,1)S(1)}, bf16[256,128]{0,1:T(8,128)(2,1)S(1)}, u32[]{:S(2)}, u32[]{:S(2)}) %collective-permute-start.11) | collective-permute-done | bytes 65568 | tf_op jit(solution)/shard_map/ppermute | solution.py:123
  74.1 1.4 %fusion.23 = f32[128,1024]{1,0:T(8,128)S(1)} fusion(bf16[128,256]{1,0:T(8,128)(2,1)S(1)} %convolution_convert_fusion.8, bf16[2,1024,1024]{2,1,0:T(8,128)(2,1)} %bitcast.133), kind=kOutput, calls=%fused_computation.48 | convolution fusion | flops 67108864 | bytes 1114112 | tf_op jit(solution)/shard_map/dot_general | solution.py:31
  75.5 1.4 %fusion.12 = bf16[1,1,1024,128]{2,3,1,0:T(8,128)(2,1)S(1)} fusion(f32[128,1024]{1,0:T(8,128)S(1)} %fusion.23, bf16[2,1024,1024]{2,1,0:T(8,128)(2,1)} %bitcast.134, f32[768,128]{0,1:T(8,128)S(1)} %fusion.8, f32[256,128]{0,1:T(8,128)S(1)} %get-tuple-element.62, bf16[256,64]{0,1:T(8,128)(2,1)S(1)} %get-tuple-element.25, bf16[256,64]{0,1:T(8,128)(2,1)S(1)} %get-tuple-element.24), kind=kOutput, calls=%fused_computation.20 | convolution fusion | flops 67764224 | bytes 1900544 | tf_op jit(solution)/shard_map/dot_general | solution.py:31
  (67 shorter events, 20.8 us)
Async XLA Ops:
  0.0 10.2 %copy-start = (bf16[1,256,256]{2,1,0:T(8,128)(2,1)S(1)}, bf16[1,256,256]{2,1,0:T(8,128)(2,1)}, u32[]{:S(2)}) copy-start(bf16[1,256,256]{2,1,0:T(8,128)(2,1)} %param.10) | copy-start | bytes 393220
  4.4 22.9 %collective-permute-start = (bf16[256,128]{1,0:T(8,128)(2,1)S(1)}, bf16[256,128]{1,0:T(8,128)(2,1)S(1)}, u32[]{:S(2)}, u32[]{:S(2)}) collective-permute-start(bf16[256,128]{1,0:T(8,128)(2,1)S(1)} %get-tuple-element.12), channel_id=1, source_target_pairs={{0,8},{8,0},{16,24},{24,16},{1,9},{9,1},{17,25},{25,17},{2,10},{10... | collective-permute-start | bytes 196616 | tf_op jit(solution)/shard_map/ppermute | solution.py:14
  7.5 19.9 %collective-permute-start.1 = (bf16[256,128]{1,0:T(8,128)(2,1)S(1)}, bf16[256,128]{1,0:T(8,128)(2,1)S(1)}, u32[]{:S(2)}, u32[]{:S(2)}) collective-permute-start(bf16[256,128]{1,0:T(8,128)(2,1)S(1)} %get-tuple-element.13), channel_id=1, source_target_pairs={{0,16},{8,24},{16,0},{24,8},{1,17},{9,25},{17,1},{25,9},{2,18},{10... | collective-permute-start | bytes 196616 | tf_op jit(solution)/shard_map/ppermute | solution.py:14
  10.2 17.4 %collective-permute-start.2 = (bf16[256,128]{1,0:T(8,128)(2,1)S(1)}, bf16[256,128]{1,0:T(8,128)(2,1)S(1)}, u32[]{:S(2)}, u32[]{:S(2)}) collective-permute-start(bf16[256,128]{1,0:T(8,128)(2,1)S(1)} %get-tuple-element.11), channel_id=1, source_target_pairs={{0,24},{8,16},{16,8},{24,0},{1,25},{9,17},{17,9},{25,1},{2,26},{10... | collective-permute-start | bytes 196616 | tf_op jit(solution)/shard_map/ppermute | solution.py:14
  14.8 22.3 %collective-permute-start.4 = (bf16[512,512]{0,1:T(8,128)(2,1)S(1)}, bf16[512,512]{0,1:T(8,128)(2,1)S(1)}, u32[]{:S(2)}, u32[]{:S(2)}) collective-permute-start(bf16[512,512]{0,1:T(8,128)(2,1)S(1)} %maximum_maximum_fusion), channel_id=1, source_target_pairs={{0,1},{1,0},{2,3},{3,2},{4,5},{5,4},{6,7},{7,6},{8,9},{9,8},{10,11... | collective-permute-start | bytes 1572872 | tf_op jit(solution)/shard_map/ppermute | solution.py:14
  35.1 1.9 %collective-permute-start.3 = (bf16[256,128]{0,1:T(8,128)(2,1)S(1)}, bf16[256,128]{0,1:T(8,128)(2,1)S(1)}, u32[]{:S(2)}, u32[]{:S(2)}) collective-permute-start(bf16[256,128]{0,1:T(8,128)(2,1)S(1)} %fusion.22), channel_id=1, source_target_pairs={{0,1},{1,0},{2,3},{3,2},{4,5},{5,4},{6,7},{7,6},{8,9},{9,8},{10,11... | collective-permute-start | bytes 196616 | tf_op jit(solution)/shard_map/ppermute | solution.py:14
  37.3 4.3 %collective-permute-start.5 = (bf16[256,128]{0,1:T(8,128)(2,1)S(1)}, bf16[256,128]{0,1:T(8,128)(2,1)S(1)}, u32[]{:S(2)}, u32[]{:S(2)}) collective-permute-start(bf16[256,128]{0,1:T(8,128)(2,1)S(1)} %fusion.18), channel_id=1, source_target_pairs={{0,2},{1,3},{2,0},{3,1},{4,6},{5,7},{6,4},{7,5},{8,10},{9,11},{10,... | collective-permute-start | bytes 196616 | tf_op jit(solution)/shard_map/ppermute | solution.py:14
  40.6 7.9 %collective-permute-start.6 = (bf16[256,512]{0,1:T(8,128)(2,1)S(1)}, bf16[256,512]{0,1:T(8,128)(2,1)S(1)}, u32[]{:S(2)}, u32[]{:S(2)}) collective-permute-start(bf16[256,512]{0,1:T(8,128)(2,1)S(1)} %get-tuple-element.59), channel_id=1, source_target_pairs={{0,2},{1,3},{2,0},{3,1},{4,6},{5,7},{6,4},{7,5},{8,10},{9,11},{10,... | collective-permute-start | bytes 786440 | tf_op jit(solution)/shard_map/ppermute | solution.py:14
  48.5 1.5 %collective-permute-start.7 = (bf16[256,512]{0,1:T(8,128)(2,1)S(1)}, bf16[256,512]{0,1:T(8,128)(2,1)S(1)}, u32[]{:S(2)}, u32[]{:S(2)}) collective-permute-start(bf16[256,512]{0,1:T(8,128)(2,1)S(1)} %collective-permute-done.6), channel_id=1, source_target_pairs={{0,1},{1,0},{2,3},{3,2},{4,5},{5,4},{6,7},{7,6},{8,9},{9,8},{10,11... | collective-permute-start | bytes 786440 | tf_op jit(solution)/shard_map/ppermute | solution.py:14
  50.3 5.3 %collective-permute-start.8 = (bf16[256,128]{0,1:T(8,128)(2,1)S(1)}, bf16[256,128]{0,1:T(8,128)(2,1)S(1)}, u32[]{:S(2)}, u32[]{:S(2)}) collective-permute-start(bf16[256,128]{0,1:T(8,128)(2,1)S(1)} %fusion.19), channel_id=1, source_target_pairs={{0,4},{1,5},{2,6},{3,7},{8,12},{9,13},{10,14},{11,15},{16,20},{17,... | collective-permute-start | bytes 196616 | tf_op jit(solution)/shard_map/ppermute | solution.py:123
  57.1 10.0 %copy-start.1 = (bf16[256,512]{0,1:T(8,128)(2,1)S(1)}, bf16[256,512]{0,1:T(8,128)(2,1)}, u32[]{:S(2)}) copy-start(bf16[256,512]{0,1:T(8,128)(2,1)} %get-tuple-element.60) | copy-start | bytes 786436
  60.8 1.4 %collective-permute-start.9 = (bf16[256,128]{0,1:T(8,128)(2,1)S(1)}, bf16[256,128]{0,1:T(8,128)(2,1)S(1)}, u32[]{:S(2)}, u32[]{:S(2)}) collective-permute-start(bf16[256,128]{0,1:T(8,128)(2,1)S(1)} %get-tuple-element.61), channel_id=1, source_target_pairs={{0,1},{1,0},{2,3},{3,2},{4,5},{5,4},{6,7},{7,6},{8,9},{9,8},{10,11... | collective-permute-start | bytes 196616 | tf_op jit(solution)/shard_map/ppermute | solution.py:14
  62.4 4.6 %collective-permute-start.10 = (bf16[256,128]{0,1:T(8,128)(2,1)S(1)}, bf16[256,128]{0,1:T(8,128)(2,1)S(1)}, u32[]{:S(2)}, u32[]{:S(2)}) collective-permute-start(bf16[256,128]{0,1:T(8,128)(2,1)S(1)} %fusion.20), channel_id=1, source_target_pairs={{0,2},{1,3},{2,0},{3,1},{4,6},{5,7},{6,4},{7,5},{8,10},{9,11},{10,... | collective-permute-start | bytes 196616 | tf_op jit(solution)/shard_map/ppermute | solution.py:14
  67.2 6.2 %collective-permute-start.11 = (bf16[256,128]{0,1:T(8,128)(2,1)S(1)}, bf16[256,128]{0,1:T(8,128)(2,1)S(1)}, u32[]{:S(2)}, u32[]{:S(2)}) collective-permute-start(bf16[256,128]{0,1:T(8,128)(2,1)S(1)} %fusion.21), channel_id=1, source_target_pairs={{4,0},{5,1},{6,2},{7,3},{12,8},{13,9},{14,10},{15,11},{20,16},{21,... | collective-permute-start | bytes 196616 | tf_op jit(solution)/shard_map/ppermute | solution.py:123

commit v2 on v0

v2 whole, which is shorter than its diff:
```python
import math

import jax
import jax.numpy as jnp
from jax import lax
from jax.experimental import pallas as pl
from jax.experimental.pallas import tpu as pltpu
from jax.sharding import PartitionSpec as P


NBLK = 16
CAP = 4
bf16 = jnp.bfloat16
f32 = jnp.float32
VMEM = pltpu.VMEM


def swapped(block, axis, mask):
    count = lax.axis_size(axis)
    return lax.ppermute(block, axis, [(i, i ^ mask) for i in range(count)])


def dot(a, b):
    return jnp.dot(a, b, preferred_element_type=f32)


def turned(v):
    half = v.shape[1] // 2
    if half % 128 == 0:
        return jnp.concatenate([-v[:, half:], v[:, :half]], axis=1)
    lane = lax.broadcasted_iota(jnp.int32, v.shape, 1)
    moved = pltpu.roll(v, half, 1)
    return jnp.where(lane < half, -moved, moved)


def applied(real, imag, v):
    v = v.astype(f32)
    return dot(real, v.astype(bf16)) + dot(imag, turned(v).astype(bf16))


def mapped(wide, v):
    side = wide.shape[1] // 2
    return applied(wide[:, :side], wide[:, side:], v)


def fine(real, v):
    high = v.astype(bf16)
    return dot(real, high) + dot(real, (v - high.astype(f32)).astype(bf16))


def place(k):
    return ((lax.axis_index("slab") >> k) & 1) == 1


def call(kernel, outs, args, flops, spaces=None, scratch=()):
    spaces = spaces or {}
    specs = [pl.BlockSpec(memory_space=spaces.get(i, VMEM)) for i in range(len(args))]
    moved = sum(a.size * a.dtype.itemsize for a in args)
    kept = sum(math.prod(s) * jnp.dtype(t).itemsize for s, t in outs)
    kept += sum(a.size * a.dtype.itemsize for i, a in enumerate(args) if i not in spaces)
    shapes = [jax.ShapeDtypeStruct(s, t) for s, t in outs]
    return pl.pallas_call(
        kernel,
        out_shape=shapes,
        in_specs=specs,
        out_specs=[pl.BlockSpec(memory_space=VMEM)] * len(shapes),
        scratch_shapes=list(scratch),
        compiler_params=pltpu.CompilerParams(vmem_limit_bytes=kept + (4 << 20)),
        cost_estimate=pl.CostEstimate(
            flops=flops, bytes_accessed=moved, transcendentals=0
        ),
    )(*args)


def body(pivots, injection, previous, coupling, strength, block_start, block_count):
    green = pivots[0, 0]
    norb = green.shape[1]
    layer = coupling.shape[1]
    width = injection.shape[3]
    rows = norb // NBLK
    span = rows * CAP
    coup = coupling[0]
    panel = previous[0, 0]
    energies = lax.axis_size("energy")
    slabs = lax.axis_size("slab")
    levels = slabs.bit_length() - 1
    low = norb - layer
    SMEM = pltpu.SMEM

    def pick(start_ref, panel_ref, *outs):
        me = lax.axis_index("energy")
        for k in range(energies - 1):
            first = pl.multiple_of(start_ref[me ^ (k + 1), me] * rows, rows)
            outs[k][...] = panel_ref[pl.ds(first, span)]

    pieces = call(
        pick, [((span, width), bf16)] * (energies - 1), (block_start, panel), 0, {0: SMEM}
    )
    received = [None] * (energies - 1)
    for mask in range(energies - 1, 0, -1):
        received[mask - 1] = swapped(pieces[mask - 1], "energy", mask)

    def own_maps(green_ref, coup_ref, maps_ref, turn_ref):
        c = coup_ref[...]
        ct = c.astype(f32).T.astype(bf16)
        turn_ref[...] = ct
        for k in range(2):
            part = slice(k * layer, (k + 1) * layer)
            maps_ref[:layer, part] = dot(ct, green_ref[k, low:, :layer]).astype(bf16)
            maps_ref[layer:, part] = dot(green_ref[k, :layer, low:], c).astype(bf16)

    maps, coup_t = call(
        own_maps,
        [((2 * layer, 2 * layer), bf16), ((layer, layer), bf16)],
        (green, coup),
        8 * layer**3,
    )
    held = green

    ways = (slice(0, layer), slice(layer, 2 * layer))
    wide = (2 * layer, 2 * layer)
    laters, befores = [], [None]
    own = maps
    for level in range(levels - 1):
        grow = level + 2 < levels

        def group(*refs, level=level, grow=grow):
            refs = list(refs)
            mine = refs.pop(0)
            if level == 0:
                near = refs.pop(0)
                theirs = [near[w] for w in ways]
            else:
                near, far, old = refs.pop(0), refs.pop(0), refs.pop(0)
                first = place(0)
                a, b = near[...], far[...]
                theirs = [jnp.where(first, b, a), jnp.where(first, a, b)]
            later_ref, before_ref = refs.pop(0), refs.pop(0)
            if grow:
                total_ref, send_ref = refs
            grown = []
            for way in range(2):
                after = place(level) if way == 0 else ~place(level)
                other, self = theirs[way], mine[ways[way]]
                later = jnp.where(after, self, other)
                later_ref[ways[way]] = later
                if level == 0:
                    row = lax.broadcasted_iota(jnp.int32, (layer, 2 * layer), 0)
                    col = lax.broadcasted_iota(jnp.int32, (layer, 2 * layer), 1)
                    before = (row == col).astype(f32).astype(bf16)
                    before_ref[ways[way]] = jnp.where(after, other, before)
                else:
                    before = old[ways[way]]
                    before_ref[ways[way]] = jnp.where(
                        after, mapped(before, other).astype(bf16), before
                    )
                if grow:
                    earlier = jnp.where(after, other, self)
                    grown.append(mapped(later, earlier).astype(bf16))
                    total_ref[ways[way]] = grown[way]
            if grow:
                send_ref[...] = jnp.where(place(0), grown[1], grown[0])

        if level == 0:
            args = (own, swapped(own, "slab", 1))
        else:
            near = swapped(send, "slab", 1 << level)
            args = (own, near, swapped(near, "slab", 1), befores[-1])
        outs = [(wide, bf16), (wide, bf16)]
        if grow:
            outs += [(wide, bf16), ((layer, 2 * layer), bf16)]
        res = call(group, outs, args, 32 * layer**3)
        laters.append(res[0])
        befores.append(res[1])
        if grow:
            own, send = res[2], res[3]

    def reach_step(level, way, reach_ref, before_ref, other):
        after = place(level) if way == 0 else ~place(level)
        if level == 0:
            return jnp.where(after, other, jnp.zeros_like(other))
        more = mapped(before_ref[ways[way]], other)
        return reach_ref[...] + jnp.where(after, more, jnp.zeros_like(more))

    def scan(vector, way):
        total, reach, sent = vector, None, vector
        for level in range(levels - 1):
            other = swapped(sent, "slab", 1 << level)

            def step(*refs, level=level):
                refs = list(refs)
                mine, other_ref, later = refs[:3]
                total_ref, sent_ref, reached = refs[-3:]
                after = place(level) if way == 0 else ~place(level)
                theirs = other_ref[...].astype(f32)
                self = mine[...]
                earlier = jnp.where(after, theirs, self)
                latest = jnp.where(after, self, theirs)
                new = mapped(later[ways[way]], earlier) + latest
                total_ref[...] = new
                sent_ref[...] = new.astype(bf16)
                before = refs[3] if level else None
                so_far = refs[4] if level else None
                reached[...] = reach_step(level, way, so_far, before, theirs)

            args = (total, other, laters[level])
            if level:
                args += (befores[level], reach)
            size = (layer, width)
            total, sent, reach = call(
                step, [(size, f32), (size, bf16), (size, f32)], args, 16 * layer * layer * width
            )
        half = slabs // 2
        if way == 0:
            route = [(i, i + half) for i in range(half)]
        else:
            route = [(i + half, i) for i in range(half)]
        return lax.ppermute(sent, "slab", route), reach

    def load(inj_ref, panel_ref, start_ref, count_ref, strength_ref, held_ref, turn_ref, *refs):
        got, (source_ref, spun_ref, low_ref, sent_ref, acc) = refs[:-5], refs[-5:]
        me = lax.axis_index("energy")
        acc[...] = inj_ref[...].astype(f32)
        row = lax.broadcasted_iota(jnp.int32, (span, width), 0)
        for k in range(energies):
            s = me ^ k
            first = pl.multiple_of(start_ref[me, s] * rows, rows)
            taken = panel_ref[pl.ds(first, span)] if k == 0 else got[k - 1][...]
            term = jnp.where(
                row < count_ref[me, s] * rows, taken.astype(f32) * strength_ref[me, s], 0.0
            )
            acc[pl.ds(first, span)] = acc[pl.ds(first, span)] + term
        source = acc[...].astype(bf16)
        spun = turned(source.astype(f32)).astype(bf16)
        source_ref[...] = source
        spun_ref[...] = spun
        direct = dot(held_ref[0, low:], source) + dot(held_ref[1, low:], spun)
        low_ref[...] = direct
        sent_ref[...] = fine(turn_ref[...], direct)

    source, spun, direct_low, sent = call(
        load,
        [((norb, width), bf16)] * 2 + [((layer, width), f32)] * 2,
        (injection[0, 0], panel, block_start, block_count, strength, held, coup_t, *received),
        4 * layer * norb * width,
        {2: SMEM, 3: SMEM, 4: SMEM},
        [pltpu.VMEM((norb, width), f32)],
    )
    arrived, reach = scan(sent, 0)

    def direct_step(held_ref, source_ref, spun_ref, out_ref):
        out_ref[...] = dot(held_ref[0, :low], source_ref[...]) + dot(
            held_ref[1, :low], spun_ref[...]
        )

    (direct,) = call(
        direct_step, [((low, width), f32)], (held, source, spun), 4 * low * norb * width
    )

    def turn_round(other_ref, reach_ref, before_ref, held_ref, direct_ref, inc_ref, top_ref):
        incoming = reach_step(levels - 1, 0, reach_ref, before_ref, other_ref[...]).astype(bf16)
        inc_ref[...] = incoming
        top_ref[...] = direct_ref[:layer] + applied(
            held_ref[0, :layer, :layer], held_ref[1, :layer, :layer], incoming
        )

    incoming, forward_top = call(
        turn_round,
        [((layer, width), bf16), ((layer, width), f32)],
        (arrived, reach, befores[levels - 1], held, direct),
        16 * layer * layer * width,
    )
    arrived, reach = scan(forward_top, 1)

    def forward_step(held_ref, inc_ref, direct_ref, low_ref, out_ref):
        incoming = inc_ref[...]
        spun = turned(incoming.astype(f32)).astype(bf16)
        more = dot(held_ref[0, :, :layer], incoming) + dot(held_ref[1, :, :layer], spun)
        out_ref[:low] = direct_ref[...] + more[:low]
        out_ref[low:] = low_ref[...] + more[low:]

    (forward,) = call(
        forward_step,
        [((norb, width), f32)],
        (held, incoming, direct, direct_low),
        8 * norb * layer * width,
    )

    def finish(other_ref, reach_ref, before_ref, held_ref, coup_ref, forward_ref, out_ref):
        back = reach_step(levels - 1, 1, reach_ref, before_ref, other_ref[...])
        outgoing = fine(coup_ref[...], back).astype(bf16)
        spun = turned(outgoing.astype(f32)).astype(bf16)
        out_ref[...] = (
            forward_ref[...]
            + dot(held_ref[0, :, low:], outgoing)
            + dot(held_ref[1, :, low:], spun)
        ).astype(bf16)

    (out,) = call(
        finish,
        [((norb, width), bf16)],
        (arrived, reach, befores[levels - 1], held, coup, forward),
        8 * norb * layer * width,
    )
    return out[None, None]


def solution(mesh):
    in_specs = (
        P("energy", "slab", None, None, None),
        P("energy", "slab", None, None),
        P("energy", "slab", None, None),
        P("slab", None, None),
        P(),
        P(),
        P(),
    )
    out_specs = P("energy", "slab", None, None)
    return jax.shard_map(body, mesh=mesh, in_specs=in_specs, out_specs=out_specs, check_vma=False)
```

time: 209 us -> 56.1 us (0.27)
  waiting for transfers between devices: 141 us -> 27.2 us
  matrix products: 33.4 us -> 0 us
  between operations: 13.3 us -> 0.14 us
  Pallas kernels: 0 us -> 9.56 us
  starting transfers between devices: 7.77 us -> 15.9 us
  local copies, waits for them, and re-layouts: 8.69 us -> 3.13 us
  other arithmetic: 3.23 us -> 0 us
    all_gather x4 -> x0, waiting for transfers between devices: 134 us -> none  [prefix(): gathered = jax.tree.map(lambda a: lax.all_gather(a, axis), part)]
    dot_general x25 -> x0, matrix products: 33.4 us -> none  [the longest x7 9.52 us: map_apply(): imag_part = jnp.dot(mapping[1], vector, precision=highest)]
    ppermute x1 -> x12, waiting for transfers between devices: 0.96 us -> 27.2 us  [the longest x10 21.9 us: swapped(): return lax.ppermute(block, axis, [(i, i ^ mask) for i in range(count)])]
    ppermute x1 -> x12, starting transfers between devices: 1.3 us -> 15.9 us  [the longest x10 11.2 us: swapped(): return lax.ppermute(block, axis, [(i, i ^ mask) for i in range(count)])]
    pallas_call x0 -> x13, Pallas kernels: none -> 9.56 us  [call(): pl.pallas_call(kernel, out_shape=shapes, in_specs=specs, out_specs=[pl.Bl...]
    all_to_all x1 -> x0, waiting for transfers between devices: 6.49 us -> none  [body(): lax.all_to_all(picked, 'energy', split_axis=0, concat_axis=0, tiled=True)]
    all_to_all x1 -> x0, starting transfers between devices: 6.35 us -> none  [body(): lax.all_to_all(picked, 'energy', split_axis=0, concat_axis=0, tiled=True)]
  transfers between devices with their start and end apart: 6 -> 12, of which waited for: 6 -> 11; matrix products, arithmetic and copies ran while one was open for 5% -> 0% of each run, Pallas kernels for 0% -> 8%
where the time goes in v2:
time: 56.1 us; the launch traced here: 55.9 us
  waiting for transfers between devices  27.2 us (48%)
  starting transfers between devices  15.9 us (28%)
  Pallas kernels  9.56 us (17%)
  local copies, waits for them, and re-layouts  3.13 us (6%)
    ppermute x10, waiting for transfers between devices, swapped(): return lax.ppermute(block, axis, [(i, i ^ mask) for i in range(count)])  21.9 us
    ppermute x10, starting transfers between devices, swapped(): return lax.ppermute(block, axis, [(i, i ^ mask) for i in range(count)])  11.2 us
    pallas_call x13, Pallas kernels, call(): pl.pallas_call(kernel, out_shape=shapes, in_specs=specs, out_specs=[pl.Bl...  9.56 us
    ppermute x2, waiting for transfers between devices, scan(): return (lax.ppermute(sent, 'slab', route), reach)  5.25 us
    ppermute x2, starting transfers between devices, scan(): return (lax.ppermute(sent, 'slab', route), reach)  4.69 us
    unnamed x16, local copies, waits for them, and re-layouts  3.13 us
  transfers between devices with their start and end apart: 12, of which 11 were waited for; matrix products, arithmetic and copies ran while one was open for 0% of the time, Pallas kernels for 8%

profile of v2, /device:TPU:0, one launch (start us, length us, event | category | flops | bytes accessed | tf_op | source)
XLA Modules:
  0.0 55.9 jit_solution(13962902561909455516)
XLA Ops:
  0.0 2.2 %copy-done = bf16[1,1,2,1024,1024]{4,3,2,1,0:T(8,128)(2,1)S(1)} copy-done((bf16[1,1,2,1024,1024]{4,3,2,1,0:T(8,128)(2,1)S(1)}, bf16[1,1,2,1024,1024]{4,3,2,1,0:T(8,128)(2,1)}, u32[]{:S(2)}) %copy-start) | copy-done | bytes 4194328
  2.2 0.9 %copy-done.3 = bf16[1,256,256]{2,1,0:T(8,128)(2,1)S(1)} copy-done((bf16[1,256,256]{2,1,0:T(8,128)(2,1)S(1)}, bf16[1,256,256]{2,1,0:T(8,128)(2,1)}, u32[]{:S(2)}) %copy-start.3) | copy-done | bytes 131096
  4.0 1.5 %collective-permute-done.4.refs_1_ = bf16[512,512]{1,0:T(8,128)(2,1)S(1)} collective-permute-done((bf16[512,512]{1,0:T(8,128)(2,1)S(1)}, bf16[512,512]{1,0:T(8,128)(2,1)S(1)}, u32[]{:S(2)}, u32[]{:S(2)}) %collective-permute-start.4) | collective-permute-done | bytes 524320 | tf_op jit(solution)/shard_map/ppermute | solution.py:20
  6.1 2.9 %collective-permute-start.6 = (bf16[256,512]{1,0:T(8,128)(2,1)S(1)}, bf16[256,512]{1,0:T(8,128)(2,1)S(1)}, u32[]{:S(2)}, u32[]{:S(2)}) collective-permute-start(bf16[256,512]{1,0:T(8,128)(2,1)S(1)} %get-tuple-element.42), channel_id=1, source_target_pairs={{0,2},{1,3},{2,0},{3,1},{4,6},{5,7},{6,4},{7,5},{8,10},{9,11},{10,... | collective-permute-start | bytes 786440 | tf_op jit(solution)/shard_map/ppermute | solution.py:20
  9.0 6.6 %collective-permute-done.6.refs_1_ = bf16[256,512]{1,0:T(8,128)(2,1)S(1)} collective-permute-done((bf16[256,512]{1,0:T(8,128)(2,1)S(1)}, bf16[256,512]{1,0:T(8,128)(2,1)S(1)}, u32[]{:S(2)}, u32[]{:S(2)}) %collective-permute-start.6) | collective-permute-done | bytes 262176 | tf_op jit(solution)/shard_map/ppermute | solution.py:20
  16.2 1.9 %collective-permute-start = (bf16[256,128]{1,0:T(8,128)(2,1)S(1)}, bf16[256,128]{1,0:T(8,128)(2,1)S(1)}, u32[]{:S(2)}, u32[]{:S(2)}) collective-permute-start(bf16[256,128]{1,0:T(8,128)(2,1)S(1)} %get-tuple-element.33), channel_id=1, source_target_pairs={{0,8},{8,0},{16,24},{24,16},{1,9},{9,1},{17,25},{25,17},{2,10},{10... | collective-permute-start | bytes 196616 | tf_op jit(solution)/shard_map/ppermute | solution.py:20
  18.1 2.6 %collective-permute-start.1 = (bf16[256,128]{1,0:T(8,128)(2,1)S(1)}, bf16[256,128]{1,0:T(8,128)(2,1)S(1)}, u32[]{:S(2)}, u32[]{:S(2)}) collective-permute-start(bf16[256,128]{1,0:T(8,128)(2,1)S(1)} %get-tuple-element.34), channel_id=1, source_target_pairs={{0,16},{8,24},{16,0},{24,8},{1,17},{9,25},{17,1},{25,9},{2,18},{10... | collective-permute-start | bytes 196616 | tf_op jit(solution)/shard_map/ppermute | solution.py:20
  20.9 4.2 %collective-permute-done.1.refs_1_ = bf16[256,128]{1,0:T(8,128)(2,1)S(1)} collective-permute-done((bf16[256,128]{1,0:T(8,128)(2,1)S(1)}, bf16[256,128]{1,0:T(8,128)(2,1)S(1)}, u32[]{:S(2)}, u32[]{:S(2)}) %collective-permute-start.1) | collective-permute-done | bytes 65568 | tf_op jit(solution)/shard_map/ppermute | solution.py:20
  25.1 1.7 %collective-permute-done.2.refs_2_ = bf16[256,128]{1,0:T(8,128)(2,1)S(1)} collective-permute-done((bf16[256,128]{1,0:T(8,128)(2,1)S(1)}, bf16[256,128]{1,0:T(8,128)(2,1)S(1)}, u32[]{:S(2)}, u32[]{:S(2)}) %collective-permute-start.2) | collective-permute-done | bytes 65568 | tf_op jit(solution)/shard_map/ppermute | solution.py:20
  26.8 1.5 %shard_map.75 = (bf16[1024,128]{1,0:T(8,128)(2,1)S(1)}, bf16[1024,128]{1,0:T(8,128)(2,1)S(1)}, f32[256,128]{1,0:T(8,128)S(1)}, f32[256,128]{1,0:T(8,128)S(1)}) custom-call(bf16[1024,128]{1,0:T(8,128)(2,1)S(1)} %bitcast.15, bf16[1024,128]{1,0:T(8,128)(2,1)S(1)} %bitcast.12, s32[4,4]{1,0:T(4,128)S(1)} %copy-done.5, s32[4,4]{1,0:T(4,128)S(1)} %copy-done.6, ...), custom_call_target="tpu_custom_call" | custom-call | flops 134217728 | bytes 5046464 | tf_op jit(solution)/shard_map/pallas_call | solution.py:62
  28.4 1.3 %collective-permute-done.3.refs_1_ = f32[256,128]{1,0:T(8,128)S(1)} collective-permute-done((f32[256,128]{1,0:T(8,128)S(1)}, f32[256,128]{1,0:T(8,128)S(1)}, u32[]{:S(2)}, u32[]{:S(2)}) %collective-permute-start.3) | collective-permute-done | bytes 131104 | tf_op jit(solution)/shard_map/ppermute | solution.py:20
  30.0 1.6 %collective-permute-start.5 = (bf16[256,128]{1,0:T(8,128)(2,1)S(1)}, bf16[256,128]{1,0:T(8,128)(2,1)S(1)}, u32[]{:S(2)}, u32[]{:S(2)}) collective-permute-start(bf16[256,128]{1,0:T(8,128)(2,1)S(1)} %get-tuple-element.40), channel_id=1, source_target_pairs={{0,2},{1,3},{2,0},{3,1},{4,6},{5,7},{6,4},{7,5},{8,10},{9,11},{10,... | collective-permute-start | bytes 196616 | tf_op jit(solution)/shard_map/ppermute | solution.py:20
  32.0 2.3 %collective-permute-done.5.refs_1_ = bf16[256,128]{1,0:T(8,128)(2,1)S(1)} collective-permute-done((bf16[256,128]{1,0:T(8,128)(2,1)S(1)}, bf16[256,128]{1,0:T(8,128)(2,1)S(1)}, u32[]{:S(2)}, u32[]{:S(2)}) %collective-permute-start.5) | collective-permute-done | bytes 65568 | tf_op jit(solution)/shard_map/ppermute | solution.py:20
  34.3 1.0 %shard_map.79 = (f32[256,128]{1,0:T(8,128)}, bf16[256,128]{1,0:T(8,128)(2,1)S(1)}, f32[256,128]{1,0:T(8,128)S(1)}) custom-call(f32[256,128]{1,0:T(8,128)S(1)} %get-tuple-element.39.refs_0_, bf16[256,128]{1,0:T(8,128)(2,1)S(1)} %collective-permute-done.5.refs_1_, bf16[512,512]{1,0:T(8,128)(2,1)S(1)} %get-tuple-element.44.refs_2_, ...), custom_call_target="tpu_custom_call" | custom-call | flops 134217728 | bytes 1376256 | tf_op jit(solution)/shard_map/pallas_call | solution.py:62
  35.3 3.4 %collective-permute-start.8 = (bf16[256,128]{1,0:T(8,128)(2,1)S(1)}, bf16[256,128]{1,0:T(8,128)(2,1)S(1)}, u32[]{:S(2)}, u32[]{:S(2)}) collective-permute-start(bf16[256,128]{1,0:T(8,128)(2,1)S(1)} %get-tuple-element.46), channel_id=1, source_target_pairs={{0,4},{1,5},{2,6},{3,7},{8,12},{9,13},{10,14},{11,15},{16,20},{17,... | collective-permute-start | bytes 196616 | tf_op jit(solution)/shard_map/ppermute | solution.py:218
  38.7 1.0 %shard_map.80.direct_ref = f32[768,128]{1,0:T(8,128)S(1)} custom-call(bf16[2,1024,1024]{2,1,0:T(8,128)(2,1)S(1)} %bitcast.7, bf16[1024,128]{1,0:T(8,128)(2,1)S(1)} %get-tuple-element.49.source_ref, bf16[1024,128]{1,0:T(8,128)(2,1)S(1)} %get-tuple-element.50.spun_ref), custom_call_target="tpu_custom_call" | custom-call | flops 402653184 | bytes 4718592 | tf_op jit(solution)/shard_map/pallas_call | solution.py:62
  39.7 0.9 %collective-permute-done.8.other_ref = bf16[256,128]{1,0:T(8,128)(2,1)S(1)} collective-permute-done((bf16[256,128]{1,0:T(8,128)(2,1)S(1)}, bf16[256,128]{1,0:T(8,128)(2,1)S(1)}, u32[]{:S(2)}, u32[]{:S(2)}) %collective-permute-start.8) | collective-permute-done | bytes 65568 | tf_op jit(solution)/shard_map/ppermute | solution.py:218
  41.2 1.3 %collective-permute-done.9.refs_1_ = f32[256,128]{1,0:T(8,128)S(1)} collective-permute-done((f32[256,128]{1,0:T(8,128)S(1)}, f32[256,128]{1,0:T(8,128)S(1)}, u32[]{:S(2)}, u32[]{:S(2)}) %collective-permute-start.9) | collective-permute-done | bytes 131104 | tf_op jit(solution)/shard_map/ppermute | solution.py:20
  42.8 1.6 %collective-permute-start.10 = (bf16[256,128]{1,0:T(8,128)(2,1)S(1)}, bf16[256,128]{1,0:T(8,128)(2,1)S(1)}, u32[]{:S(2)}, u32[]{:S(2)}) collective-permute-start(bf16[256,128]{1,0:T(8,128)(2,1)S(1)} %get-tuple-element.53), channel_id=1, source_target_pairs={{0,2},{1,3},{2,0},{3,1},{4,6},{5,7},{6,4},{7,5},{8,10},{9,11},{10,... | collective-permute-start | bytes 196616 | tf_op jit(solution)/shard_map/ppermute | solution.py:20
  44.4 2.8 %collective-permute-done.10.refs_1_ = bf16[256,128]{1,0:T(8,128)(2,1)S(1)} collective-permute-done((bf16[256,128]{1,0:T(8,128)(2,1)S(1)}, bf16[256,128]{1,0:T(8,128)(2,1)S(1)}, u32[]{:S(2)}, u32[]{:S(2)}) %collective-permute-start.10) | collective-permute-done | bytes 65568 | tf_op jit(solution)/shard_map/ppermute | solution.py:20
  47.2 1.0 %shard_map.83 = (f32[256,128]{1,0:T(8,128)}, bf16[256,128]{1,0:T(8,128)(2,1)S(1)}, f32[256,128]{1,0:T(8,128)S(1)}) custom-call(f32[256,128]{1,0:T(8,128)S(1)} %get-tuple-element.52.refs_0_, bf16[256,128]{1,0:T(8,128)(2,1)S(1)} %collective-permute-done.10.refs_1_, bf16[512,512]{1,0:T(8,128)(2,1)S(1)} %get-tuple-element.44.refs_2_, ...), custom_call_target="tpu_custom_call" | custom-call | flops 134217728 | bytes 1376256 | tf_op jit(solution)/shard_map/pallas_call | solution.py:62
  48.1 1.3 %collective-permute-start.11 = (bf16[256,128]{1,0:T(8,128)(2,1)S(1)}, bf16[256,128]{1,0:T(8,128)(2,1)S(1)}, u32[]{:S(2)}, u32[]{:S(2)}) collective-permute-start(bf16[256,128]{1,0:T(8,128)(2,1)S(1)} %get-tuple-element.55), channel_id=1, source_target_pairs={{4,0},{5,1},{6,2},{7,3},{12,8},{13,9},{14,10},{15,11},{20,16},{21,... | collective-permute-start | bytes 196616 | tf_op jit(solution)/shard_map/ppermute | solution.py:218
  49.9 4.4 %collective-permute-done.11.other_ref = bf16[256,128]{1,0:T(8,128)(2,1)S(1)} collective-permute-done((bf16[256,128]{1,0:T(8,128)(2,1)S(1)}, bf16[256,128]{1,0:T(8,128)(2,1)S(1)}, u32[]{:S(2)}, u32[]{:S(2)}) %collective-permute-start.11) | collective-permute-done | bytes 65568 | tf_op jit(solution)/shard_map/ppermute | solution.py:218
  54.3 1.6 %shard_map.85 = bf16[1024,128]{1,0:T(8,128)(2,1)} custom-call(bf16[256,128]{1,0:T(8,128)(2,1)S(1)} %collective-permute-done.11.other_ref, f32[256,128]{1,0:T(8,128)S(1)} %get-tuple-element.56.reach_ref, bf16[512,512]{1,0:T(8,128)(2,1)S(1)} %get-tuple-element.48.before_ref, bf16[2,1024,1024]{2,1,0:T(8,128)(2,1)S(1)} %bitcast.10, ...), custom_call_target="tpu_custom_call" | custom-call | flops 268435456 | bytes 5570560 | tf_op jit(solution)/shard_map/pallas_call | solution.py:62
  (29 shorter events, 4.4 us)
Async XLA Ops:
  0.0 15.6 %copy-start.5 = (s32[4,4]{1,0:T(4,128)S(1)}, s32[4,4]{1,0:T(4,128)}, u32[]{:S(2)}) copy-start(s32[4,4]{1,0:T(4,128)} %start_ref.3) | copy-start | bytes 196
  0.0 2.2 %copy-start = (bf16[1,1,2,1024,1024]{4,3,2,1,0:T(8,128)(2,1)S(1)}, bf16[1,1,2,1024,1024]{4,3,2,1,0:T(8,128)(2,1)}, u32[]{:S(2)}) copy-start(bf16[1,1,2,1024,1024]{4,3,2,1,0:T(8,128)(2,1)} %param.7) | copy-start | bytes 12582916
  2.2 0.9 %copy-start.3 = (bf16[1,256,256]{2,1,0:T(8,128)(2,1)S(1)}, bf16[1,256,256]{2,1,0:T(8,128)(2,1)}, u32[]{:S(2)}) copy-start(bf16[1,256,256]{2,1,0:T(8,128)(2,1)} %param.10) | copy-start | bytes 393220
  3.1 12.5 %copy-start.2 = (bf16[1,1,1024,128]{3,2,1,0:T(8,128)(2,1)S(1)}, bf16[1,1,1024,128]{3,2,1,0:T(8,128)(2,1)}, u32[]{:S(2)}) copy-start(bf16[1,1,1024,128]{3,2,1,0:T(8,128)(2,1)} %param.9) | copy-start | bytes 786436
  3.1 23.6 %copy-start.1 = (bf16[1,1,2,1024,1024]{4,3,2,1,0:T(8,128)(2,1)S(1)}, bf16[1,1,2,1024,1024]{4,3,2,1,0:T(8,128)(2,1)}, u32[]{:S(2)}) copy-start(bf16[1,1,2,1024,1024]{4,3,2,1,0:T(8,128)(2,1)} %param.7) | copy-start | bytes 12582916
  3.1 23.6 %copy-start.4 = (bf16[1,1,1024,128]{3,2,1,0:T(8,128)(2,1)S(1)}, bf16[1,1,1024,128]{3,2,1,0:T(8,128)(2,1)}, u32[]{:S(2)}) copy-start(bf16[1,1,1024,128]{3,2,1,0:T(8,128)(2,1)} %param.8) | copy-start | bytes 786436
  3.1 23.6 %copy-start.6 = (s32[4,4]{1,0:T(4,128)S(1)}, s32[4,4]{1,0:T(4,128)}, u32[]{:S(2)}) copy-start(s32[4,4]{1,0:T(4,128)} %count_ref.1) | copy-start | bytes 196
  3.1 23.6 %copy-start.7 = (f32[4,4]{1,0:T(4,128)S(1)}, f32[4,4]{1,0:T(4,128)}, u32[]{:S(2)}) copy-start(f32[4,4]{1,0:T(4,128)} %strength_ref.1) | copy-start | bytes 196
  3.5 2.1 %collective-permute-start.4 = (bf16[512,512]{1,0:T(8,128)(2,1)S(1)}, bf16[512,512]{1,0:T(8,128)(2,1)S(1)}, u32[]{:S(2)}, u32[]{:S(2)}) collective-permute-start(bf16[512,512]{1,0:T(8,128)(2,1)S(1)} %get-tuple-element.37.refs_0_), channel_id=1, source_target_pairs={{0,1},{1,0},{2,3},{3,2},{4,5},{5,4},{6,7},{7,6},{8,9},{9,8},{10,11... | collective-permute-start | bytes 1572872 | tf_op jit(solution)/shard_map/ppermute | solution.py:20
  6.1 9.5 %collective-permute-start.6 = (bf16[256,512]{1,0:T(8,128)(2,1)S(1)}, bf16[256,512]{1,0:T(8,128)(2,1)S(1)}, u32[]{:S(2)}, u32[]{:S(2)}) collective-permute-start(bf16[256,512]{1,0:T(8,128)(2,1)S(1)} %get-tuple-element.42), channel_id=1, source_target_pairs={{0,2},{1,3},{2,0},{3,1},{4,6},{5,7},{6,4},{7,5},{8,10},{9,11},{10,... | collective-permute-start | bytes 786440 | tf_op jit(solution)/shard_map/ppermute | solution.py:20
  15.6 16.0 %collective-permute-start.7 = (bf16[256,512]{1,0:T(8,128)(2,1)S(1)}, bf16[256,512]{1,0:T(8,128)(2,1)S(1)}, u32[]{:S(2)}, u32[]{:S(2)}) collective-permute-start(bf16[256,512]{1,0:T(8,128)(2,1)S(1)} %collective-permute-done.6.refs_1_), channel_id=1, source_target_pairs={{0,1},{1,0},{2,3},{3,2},{4,5},{5,4},{6,7},{7,6},{8,9},{9,8},{10,11... | collective-permute-start | bytes 786440 | tf_op jit(solution)/shard_map/ppermute | solution.py:20
  16.2 4.7 %collective-permute-start = (bf16[256,128]{1,0:T(8,128)(2,1)S(1)}, bf16[256,128]{1,0:T(8,128)(2,1)S(1)}, u32[]{:S(2)}, u32[]{:S(2)}) collective-permute-start(bf16[256,128]{1,0:T(8,128)(2,1)S(1)} %get-tuple-element.33), channel_id=1, source_target_pairs={{0,8},{8,0},{16,24},{24,16},{1,9},{9,1},{17,25},{25,17},{2,10},{10... | collective-permute-start | bytes 196616 | tf_op jit(solution)/shard_map/ppermute | solution.py:20
  18.1 7.0 %collective-permute-start.1 = (bf16[256,128]{1,0:T(8,128)(2,1)S(1)}, bf16[256,128]{1,0:T(8,128)(2,1)S(1)}, u32[]{:S(2)}, u32[]{:S(2)}) collective-permute-start(bf16[256,128]{1,0:T(8,128)(2,1)S(1)} %get-tuple-element.34), channel_id=1, source_target_pairs={{0,16},{8,24},{16,0},{24,8},{1,17},{9,25},{17,1},{25,9},{2,18},{10... | collective-permute-start | bytes 196616 | tf_op jit(solution)/shard_map/ppermute | solution.py:20
  20.7 6.1 %collective-permute-start.2 = (bf16[256,128]{1,0:T(8,128)(2,1)S(1)}, bf16[256,128]{1,0:T(8,128)(2,1)S(1)}, u32[]{:S(2)}, u32[]{:S(2)}) collective-permute-start(bf16[256,128]{1,0:T(8,128)(2,1)S(1)} %get-tuple-element.35), channel_id=1, source_target_pairs={{0,24},{8,16},{16,8},{24,0},{1,25},{9,17},{17,9},{25,1},{2,26},{10... | collective-permute-start | bytes 196616 | tf_op jit(solution)/shard_map/ppermute | solution.py:20
  28.3 1.4 %collective-permute-start.3 = (f32[256,128]{1,0:T(8,128)S(1)}, f32[256,128]{1,0:T(8,128)S(1)}, u32[]{:S(2)}, u32[]{:S(2)}) collective-permute-start(f32[256,128]{1,0:T(8,128)S(1)} %get-tuple-element.36.refs_0_), channel_id=1, source_target_pairs={{0,1},{1,0},{2,3},{3,2},{4,5},{5,4},{6,7},{7,6},{8,9},{9,8},{10,11... | collective-permute-start | bytes 393224 | tf_op jit(solution)/shard_map/ppermute | solution.py:20
  30.0 4.3 %collective-permute-start.5 = (bf16[256,128]{1,0:T(8,128)(2,1)S(1)}, bf16[256,128]{1,0:T(8,128)(2,1)S(1)}, u32[]{:S(2)}, u32[]{:S(2)}) collective-permute-start(bf16[256,128]{1,0:T(8,128)(2,1)S(1)} %get-tuple-element.40), channel_id=1, source_target_pairs={{0,2},{1,3},{2,0},{3,1},{4,6},{5,7},{6,4},{7,5},{8,10},{9,11},{10,... | collective-permute-start | bytes 196616 | tf_op jit(solution)/shard_map/ppermute | solution.py:20
  35.3 5.3 %collective-permute-start.8 = (bf16[256,128]{1,0:T(8,128)(2,1)S(1)}, bf16[256,128]{1,0:T(8,128)(2,1)S(1)}, u32[]{:S(2)}, u32[]{:S(2)}) collective-permute-start(bf16[256,128]{1,0:T(8,128)(2,1)S(1)} %get-tuple-element.46), channel_id=1, source_target_pairs={{0,4},{1,5},{2,6},{3,7},{8,12},{9,13},{10,14},{11,15},{16,20},{17,... | collective-permute-start | bytes 196616 | tf_op jit(solution)/shard_map/ppermute | solution.py:218
  41.1 1.4 %collective-permute-start.9 = (f32[256,128]{1,0:T(8,128)S(1)}, f32[256,128]{1,0:T(8,128)S(1)}, u32[]{:S(2)}, u32[]{:S(2)}) collective-permute-start(f32[256,128]{1,0:T(8,128)S(1)} %get-tuple-element.51.refs_0_), channel_id=1, source_target_pairs={{0,1},{1,0},{2,3},{3,2},{4,5},{5,4},{6,7},{7,6},{8,9},{9,8},{10,11... | collective-permute-start | bytes 393224 | tf_op jit(solution)/shard_map/ppermute | solution.py:20
  42.8 4.3 %collective-permute-start.10 = (bf16[256,128]{1,0:T(8,128)(2,1)S(1)}, bf16[256,128]{1,0:T(8,128)(2,1)S(1)}, u32[]{:S(2)}, u32[]{:S(2)}) collective-permute-start(bf16[256,128]{1,0:T(8,128)(2,1)S(1)} %get-tuple-element.53), channel_id=1, source_target_pairs={{0,2},{1,3},{2,0},{3,1},{4,6},{5,7},{6,4},{7,5},{8,10},{9,11},{10,... | collective-permute-start | bytes 196616 | tf_op jit(solution)/shard_map/ppermute | solution.py:20
  48.1 6.1 %collective-permute-start.11 = (bf16[256,128]{1,0:T(8,128)(2,1)S(1)}, bf16[256,128]{1,0:T(8,128)(2,1)S(1)}, u32[]{:S(2)}, u32[]{:S(2)}) collective-permute-start(bf16[256,128]{1,0:T(8,128)(2,1)S(1)} %get-tuple-element.55), channel_id=1, source_target_pairs={{4,0},{5,1},{6,2},{7,3},{12,8},{13,9},{14,10},{15,11},{20,16},{21,... | collective-permute-start | bytes 196616 | tf_op jit(solution)/shard_map/ppermute | solution.py:218

commit v3 on v2

--- a/solution.py
+++ b/solution.py
@@ -10,6 +10,7 @@
 
 NBLK = 16
 CAP = 4
+VMEM_BYTES = 67043328
 bf16 = jnp.bfloat16
 f32 = jnp.float32
 VMEM = pltpu.VMEM
@@ -52,20 +53,21 @@
     return ((lax.axis_index("slab") >> k) & 1) == 1
 
 
-def call(kernel, outs, args, flops, spaces=None, scratch=()):
+def call(kernel, outs, args, flops, spaces=None, scratch=(), out_space=VMEM, spare=None):
     spaces = spaces or {}
     specs = [pl.BlockSpec(memory_space=spaces.get(i, VMEM)) for i in range(len(args))]
     moved = sum(a.size * a.dtype.itemsize for a in args)
     kept = sum(math.prod(s) * jnp.dtype(t).itemsize for s, t in outs)
     kept += sum(a.size * a.dtype.itemsize for i, a in enumerate(args) if i not in spaces)
+    limit = kept + (4 << 20) if spare is None else VMEM_BYTES - spare
     shapes = [jax.ShapeDtypeStruct(s, t) for s, t in outs]
     return pl.pallas_call(
         kernel,
         out_shape=shapes,
         in_specs=specs,
-        out_specs=[pl.BlockSpec(memory_space=VMEM)] * len(shapes),
+        out_specs=[pl.BlockSpec(memory_space=out_space)] * len(shapes),
         scratch_shapes=list(scratch),
-        compiler_params=pltpu.CompilerParams(vmem_limit_bytes=kept + (4 << 20)),
+        compiler_params=pltpu.CompilerParams(vmem_limit_bytes=limit),
         cost_estimate=pl.CostEstimate(
             flops=flops, bytes_accessed=moved, transcendentals=0
         ),
@@ -79,7 +81,9 @@
     width = injection.shape[3]
     rows = norb // NBLK
     span = rows * CAP
+    far_green = pltpu.with_memory_space_constraint(green, pltpu.HBM)
     coup = coupling[0]
+    far_coup = pltpu.with_memory_space_constraint(coup, pltpu.HBM)
     panel = previous[0, 0]
     energies = lax.axis_size("energy")
     slabs = lax.axis_size("slab")
@@ -87,6 +91,42 @@
     low = norb - layer
     SMEM = pltpu.SMEM
 
+    def own_maps(green_ref, coup_ref, maps_ref, turn_ref, corner, near, sem, sem_c):
+        spots = ((pl.ds(low, layer), pl.ds(0, layer)), (pl.ds(0, layer), pl.ds(low, layer)))
+        copies = [
+            [pltpu.make_async_copy(green_ref.at[k, r, c], corner.at[i, k], sem.at[i, k]) for k in range(2)]
+            for i, (r, c) in enumerate(spots)
+        ]
+        first = pltpu.make_async_copy(coup_ref, near, sem_c)
+        first.start()
+        for pair in copies:
+            for copy in pair:
+                copy.start()
+        first.wait()
+        c = near[...]
+        ct = c.astype(f32).T.astype(bf16)
+        turn_ref[...] = ct
+        for k in range(2):
+            copies[0][k].wait()
+            maps_ref[:layer, k * layer : (k + 1) * layer] = dot(ct, corner[0, k]).astype(bf16)
+        for k in range(2):
+            copies[1][k].wait()
+            maps_ref[layer:, k * layer : (k + 1) * layer] = dot(corner[1, k], c).astype(bf16)
+
+    maps, coup_t = call(
+        own_maps,
+        [((2 * layer, 2 * layer), bf16), ((layer, layer), bf16)],
+        (far_green, far_coup),
+        8 * layer**3,
+        {0: pltpu.HBM, 1: pltpu.HBM},
+        [
+            pltpu.VMEM((2, 2, layer, layer), bf16),
+            pltpu.VMEM((layer, layer), bf16),
+            pltpu.SemaphoreType.DMA((2, 2)),
+            pltpu.SemaphoreType.DMA,
+        ],
+    )
+
     def pick(start_ref, panel_ref, *outs):
         me = lax.axis_index("energy")
         for k in range(energies - 1):
@@ -100,22 +140,27 @@
     for mask in range(energies - 1, 0, -1):
         received[mask - 1] = swapped(pieces[mask - 1], "energy", mask)
 
-    def own_maps(green_ref, coup_ref, maps_ref, turn_ref):
-        c = coup_ref[...]
-        ct = c.astype(f32).T.astype(bf16)
-        turn_ref[...] = ct
-        for k in range(2):
-            part = slice(k * layer, (k + 1) * layer)
-            maps_ref[:layer, part] = dot(ct, green_ref[k, low:, :layer]).astype(bf16)
-            maps_ref[layer:, part] = dot(green_ref[k, :layer, low:], c).astype(bf16)
-
-    maps, coup_t = call(
-        own_maps,
-        [((2 * layer, 2 * layer), bf16), ((layer, layer), bf16)],
-        (green, coup),
-        8 * layer**3,
-    )
     held = green
+
+    def fetch(green_ref, hint_ref, held_ref, sem):
+        parts = [(k, pl.ds(i * layer, layer)) for k in range(2) for i in range(norb // layer)]
+        copies = [
+            pltpu.make_async_copy(green_ref.at[k, r], held_ref.at[k, r], sem.at[i])
+            for i, (k, r) in enumerate(parts)
+        ]
+        for copy in copies:
+            copy.start()
+        for copy in copies:
+            copy.wait()
+
+    (held,) = call(
+        fetch,
+        [(green.shape, bf16)],
+        (far_green, coup_t),
+        0,
+        {0: pltpu.HBM, 1: pl.ANY},
+        [pltpu.SemaphoreType.DMA((2 * norb // layer,))],
+    )
 
     ways = (slice(0, layer), slice(layer, 2 * layer))
     wide = (2 * layer, 2 * layer)
@@ -187,18 +232,21 @@
         for level in range(levels - 1):
             other = swapped(sent, "slab", 1 << level)
 
-            def step(*refs, level=level):
+            final = level == levels - 2
+
+            def step(*refs, level=level, final=final):
                 refs = list(refs)
                 mine, other_ref, later = refs[:3]
-                total_ref, sent_ref, reached = refs[-3:]
+                sent_ref, reached = refs[-2:]
                 after = place(level) if way == 0 else ~place(level)
                 theirs = other_ref[...].astype(f32)
                 self = mine[...]
                 earlier = jnp.where(after, theirs, self)
                 latest = jnp.where(after, self, theirs)
                 new = mapped(later[ways[way]], earlier) + latest
-                total_ref[...] = new
                 sent_ref[...] = new.astype(bf16)
+                if not final:
+                    refs[-3][...] = new
                 before = refs[3] if level else None
                 so_far = refs[4] if level else None
                 reached[...] = reach_step(level, way, so_far, before, theirs)
@@ -207,30 +255,31 @@
             if level:
                 args += (befores[level], reach)
             size = (layer, width)
-            total, sent, reach = call(
-                step, [(size, f32), (size, bf16), (size, f32)], args, 16 * layer * layer * width
+            res = call(
+                step,
+                [(size, f32)] * (not final) + [(size, bf16), (size, f32)],
+                args,
+                16 * layer * layer * width,
             )
-        half = slabs // 2
-        if way == 0:
-            route = [(i, i + half) for i in range(half)]
-        else:
-            route = [(i + half, i) for i in range(half)]
-        return lax.ppermute(sent, "slab", route), reach
-
-    def load(inj_ref, panel_ref, start_ref, count_ref, strength_ref, held_ref, turn_ref, *refs):
-        got, (source_ref, spun_ref, low_ref, sent_ref, acc) = refs[:-5], refs[-5:]
-        me = lax.axis_index("energy")
-        acc[...] = inj_ref[...].astype(f32)
-        row = lax.broadcasted_iota(jnp.int32, (span, width), 0)
-        for k in range(energies):
-            s = me ^ k
-            first = pl.multiple_of(start_ref[me, s] * rows, rows)
-            taken = panel_ref[pl.ds(first, span)] if k == 0 else got[k - 1][...]
-            term = jnp.where(
-                row < count_ref[me, s] * rows, taken.astype(f32) * strength_ref[me, s], 0.0
-            )
-            acc[pl.ds(first, span)] = acc[pl.ds(first, span)] + term
-        source = acc[...].astype(bf16)
+            total, sent, reach = res if not final else [None] + list(res)
+        return swapped(sent, "slab", slabs // 2), reach
+
+    me = lax.axis_index("energy")
+    row = lax.broadcasted_iota(jnp.int32, (span, width), 0)
+    scattered = injection[0, 0].astype(f32)
+    own_piece = lax.dynamic_slice(panel, (block_start[me, me] * rows, 0), (span, width))
+    for k, piece in enumerate([own_piece] + received):
+        s = me ^ k
+        first = block_start[me, s] * rows
+        term = jnp.where(
+            row < block_count[me, s] * rows, piece.astype(f32) * strength[me, s], 0.0
+        )
+        so_far = lax.dynamic_slice(scattered, (first, 0), (span, width))
+        scattered = lax.dynamic_update_slice(scattered, so_far + term, (first, 0))
+
+    def load(sum_ref, held_ref, turn_ref, source_ref, spun_ref, low_ref, sent_ref):
+        total = sum_ref[...]
+        source = total.astype(bf16)
         spun = turned(source.astype(f32)).astype(bf16)
         source_ref[...] = source
         spun_ref[...] = spun
@@ -241,10 +290,8 @@
     source, spun, direct_low, sent = call(
         load,
         [((norb, width), bf16)] * 2 + [((layer, width), f32)] * 2,
-        (injection[0, 0], panel, block_start, block_count, strength, held, coup_t, *received),
+        (scattered, held, coup_t),
         4 * layer * norb * width,
-        {2: SMEM, 3: SMEM, 4: SMEM},
-        [pltpu.VMEM((norb, width), f32)],
     )
     arrived, reach = scan(sent, 0)
 
@@ -286,21 +333,33 @@
         8 * norb * layer * width,
     )
 
-    def finish(other_ref, reach_ref, before_ref, held_ref, coup_ref, forward_ref, out_ref):
+    def finish(
+        other_ref, reach_ref, before_ref, held_ref, coup_ref, forward_ref, out_ref, kept, sem
+    ):
         back = reach_step(levels - 1, 1, reach_ref, before_ref, other_ref[...])
         outgoing = fine(coup_ref[...], back).astype(bf16)
         spun = turned(outgoing.astype(f32)).astype(bf16)
-        out_ref[...] = (
-            forward_ref[...]
-            + dot(held_ref[0, :, low:], outgoing)
-            + dot(held_ref[1, :, low:], spun)
-        ).astype(bf16)
+        copies = []
+        for i in range(norb // layer):
+            part = pl.ds(i * layer, layer)
+            kept[part] = (
+                forward_ref[part]
+                + dot(held_ref[0, part, low:], outgoing)
+                + dot(held_ref[1, part, low:], spun)
+            ).astype(bf16)
+            copy = pltpu.make_async_copy(kept.at[part], out_ref.at[part], sem.at[i])
+            copy.start()
+            copies.append(copy)
+        for copy in copies:
+            copy.wait()
 
     (out,) = call(
         finish,
         [((norb, width), bf16)],
         (arrived, reach, befores[levels - 1], held, coup, forward),
         8 * norb * layer * width,
+        scratch=[pltpu.VMEM((norb, width), bf16), pltpu.SemaphoreType.DMA((norb // layer,))],
+        out_space=pltpu.HBM,
     )
     return out[None, None]
 

time: 56.1 us -> 60.2 us (1.073)
  waiting for transfers between devices: 27.2 us -> 16.1 us
  between operations: 0.14 us -> 5.29 us
  local copies, waits for them, and re-layouts: 3.13 us -> 7.76 us
  other arithmetic: 0 us -> 3.8 us
  Pallas kernels: 9.56 us -> 11.5 us
    ppermute x10 -> x12, waiting for transfers between devices: 21.9 us -> 16.1 us  [swapped(): return lax.ppermute(block, axis, [(i, i ^ mask) for i in range(count)])]
    ppermute x2 -> x0, waiting for transfers between devices: 5.25 us -> none  [scan(): return (lax.ppermute(sent, 'slab', route), reach)]
    ppermute x2 -> x0, starting transfers between devices: 4.69 us -> none  [scan(): return (lax.ppermute(sent, 'slab', route), reach)]
    ppermute x10 -> x12, starting transfers between devices: 11.2 us -> 15.3 us  [swapped(): return lax.ppermute(block, axis, [(i, i ^ mask) for i in range(count)])]
    dynamic_update_slice x0 -> x4, other arithmetic: none -> 3.69 us  [body(): scattered = lax.dynamic_update_slice(scattered, so_far + term, (first, 0))]
    unnamed x16 -> x20, local copies, waits for them, and re-layouts: 3.13 us -> 5.8 us
    dynamic_slice x0 -> x3, local copies, waits for them, and re-layouts: none -> 1.97 us  [the longest x1 0.67 us: body(): first = block_start[me, s] * rows]
    pallas_call x13 -> x14, Pallas kernels: 9.56 us -> 11.5 us  [call(): pl.pallas_call(kernel, out_shape=shapes, in_specs=specs, out_specs=[pl.Bl...]
  transfers between devices with their start and end apart: 12 -> 12, of which waited for: 11 -> 7; matrix products, arithmetic and copies ran while one was open for 0% -> 10% of each run, Pallas kernels for 8% -> 13%
where the time goes in v3:
time: 60.2 us; the launch traced here: 59.8 us
  waiting for transfers between devices  16.1 us (27%)
  starting transfers between devices  15.3 us (25%)
  Pallas kernels  11.5 us (19%)
  local copies, waits for them, and re-layouts  7.76 us (13%)
  between operations  5.29 us (9%)
  other arithmetic  3.8 us (6%)
    ppermute x12, waiting for transfers between devices, swapped(): return lax.ppermute(block, axis, [(i, i ^ mask) for i in range(count)])  16.1 us
    ppermute x12, starting transfers between devices, swapped(): return lax.ppermute(block, axis, [(i, i ^ mask) for i in range(count)])  15.3 us
    pallas_call x14, Pallas kernels, call(): pl.pallas_call(kernel, out_shape=shapes, in_specs=specs, out_specs=[pl.Bl...  11.5 us
    unnamed x20, local copies, waits for them, and re-layouts  5.8 us
    dynamic_update_slice x4, other arithmetic, body(): scattered = lax.dynamic_update_slice(scattered, so_far + term, (first, 0))  3.69 us
  transfers between devices with their start and end apart: 12, of which 7 were waited for; matrix products, arithmetic and copies ran while one was open for 10% of the time, Pallas kernels for 13%

profile of v3, /device:TPU:0, one launch (start us, length us, event | category | flops | bytes accessed | tf_op | source)
XLA Modules:
  0.0 59.8 jit_solution(5008353381701899412)
XLA Ops:
  0.0 0.9 %copy-done.4 = bf16[1,1,1024,128]{3,2,1,0:T(8,128)(2,1)S(1)} copy-done((bf16[1,1,1024,128]{3,2,1,0:T(8,128)(2,1)S(1)}, bf16[1,1,1024,128]{3,2,1,0:T(8,128)(2,1)}, u32[]{:S(2)}) %copy-start.4) | copy-done | bytes 262168
  2.2 3.1 %collective-permute-start = (bf16[256,128]{1,0:T(8,128)(2,1)S(1)}, bf16[256,128]{1,0:T(8,128)(2,1)S(1)}, u32[]{:S(2)}, u32[]{:S(2)}) collective-permute-start(bf16[256,128]{1,0:T(8,128)(2,1)S(1)} %get-tuple-element.32), channel_id=1, source_target_pairs={{0,8},{8,0},{16,24},{24,16},{1,9},{9,1},{17,25},{25,17},{2,10},{10... | collective-permute-start | bytes 196616 | tf_op jit(solution)/shard_map/ppermute | solution.py:21
  5.4 2.6 %collective-permute-start.1 = (bf16[256,128]{1,0:T(8,128)(2,1)S(1)}, bf16[256,128]{1,0:T(8,128)(2,1)S(1)}, u32[]{:S(2)}, u32[]{:S(2)}) collective-permute-start(bf16[256,128]{1,0:T(8,128)(2,1)S(1)} %get-tuple-element.33), channel_id=1, source_target_pairs={{0,16},{8,24},{16,0},{24,8},{1,17},{9,25},{17,1},{25,9},{2,18},{10... | collective-permute-start | bytes 196616 | tf_op jit(solution)/shard_map/ppermute | solution.py:21
  8.0 2.1 %shard_map.74 = (bf16[512,512]{1,0:T(8,128)(2,1)S(1)}, bf16[256,256]{1,0:T(8,128)(2,1)S(1)}) custom-call(bf16[2,1024,1024]{2,1,0:T(8,128)(2,1)} %bitcast.29, bf16[256,256]{1,0:T(8,128)(2,1)} %bitcast.26), custom_call_target="tpu_custom_call" | custom-call | flops 134217728 | bytes 4325376 | tf_op jit(solution)/shard_map/pallas_call | solution.py:64
  15.4 1.5 %fusion.1 = f32[1024,128]{1,0:T(8,128)S(1)} fusion(f32[1024,128]{1,0:T(8,128)S(1)} %get-tuple-element.60, s32[]{:T(128)S(6)} %select_n.30, f32[1,1,1024,128]{3,2,1,0:T(8,128)S(1)} %get-tuple-element.59, f32[]{:T(128)} %bitcast.4, bf16[1,1,1024,128]{3,2,1,0:T(8,128)(2,1)} %param.9, pred[256]{0:T(512)(128)(4,1)S(1)} %iota_compare_fusion.3), kind=kLoop, calls=%fused_computation.2 | loop fusion | flops 131072 | bytes 328200 | tf_op jit(solution)/shard_map/dynamic_update_slice | solution.py:278
  18.9 2.2 %shard_map.75.held_ref = bf16[2,1024,1024]{2,1,0:T(8,128)(2,1)S(1)} custom-call(bf16[2,1024,1024]{2,1,0:T(8,128)(2,1)} %bitcast.30, bf16[256,256]{1,0:T(8,128)(2,1)S(1)} %get-tuple-element.35.hint_ref.turn_ref), custom_call_target="tpu_custom_call" | custom-call | bytes 4325376 | tf_op jit(solution)/shard_map/pallas_call | solution.py:64
  21.1 2.0 %copy-done = bf16[2,1024,1024]{2,1,0:T(8,128)(2,1)} copy-done((bf16[2,1024,1024]{2,1,0:T(8,128)(2,1)}, bf16[2,1024,1024]{2,1,0:T(8,128)(2,1)S(1)}, u32[]{:S(2)}) %copy-start) | copy-done | bytes 4194328
  23.6 1.8 %collective-permute-start.6 = (bf16[256,512]{1,0:T(8,128)(2,1)S(1)}, bf16[256,512]{1,0:T(8,128)(2,1)S(1)}, u32[]{:S(2)}, u32[]{:S(2)}) collective-permute-start(bf16[256,512]{1,0:T(8,128)(2,1)S(1)} %get-tuple-element.42), channel_id=1, source_target_pairs={{0,2},{1,3},{2,0},{3,1},{4,6},{5,7},{6,4},{7,5},{8,10},{9,11},{10,... | collective-permute-start | bytes 786440 | tf_op jit(solution)/shard_map/ppermute | solution.py:21
  26.1 0.7 %add_dynamic-update-slice_fusion.1 = f32[1024,128]{1,0:T(8,128)S(1)} fusion(f32[1024,128]{1,0:T(8,128)S(1)} %add_dynamic-update-slice_fusion.2, s32[]{:T(128)S(6)} %select_n.36, bf16[256,128]{1,0:T(8,128)(2,1)S(1)} %collective-permute-done.1, f32[]{:T(128)} %bitcast.12, pred[256]{0:T(512)(128)(4,1)S(1)} %iota_compare_fusion.1), kind=kLoop, calls=%fused_computation.4 | loop fusion | flops 131072 | bytes 328200 | tf_op jit(solution)/shard_map/dynamic_update_slice | solution.py:278
  26.8 5.5 %collective-permute-done.6.refs_1_ = bf16[256,512]{1,0:T(8,128)(2,1)S(1)} collective-permute-done((bf16[256,512]{1,0:T(8,128)(2,1)S(1)}, bf16[256,512]{1,0:T(8,128)(2,1)S(1)}, u32[]{:S(2)}, u32[]{:S(2)}) %collective-permute-start.6) | collective-permute-done | bytes 262176 | tf_op jit(solution)/shard_map/ppermute | solution.py:21
  32.3 0.7 %add_dynamic-update-slice_fusion.sum_ref = f32[1024,128]{1,0:T(8,128)S(1)} fusion(f32[1024,128]{1,0:T(8,128)S(1)} %add_dynamic-update-slice_fusion.1, s32[]{:T(128)S(6)} %select_n.74, bf16[256,128]{1,0:T(8,128)(2,1)S(1)} %collective-permute-done.2, f32[]{:T(128)} %bitcast.15, pred[256]{0:T(512)(128)(4,1)S(1)} %iota_compare_fusion), kind=kLoop, calls=%fused_computation.3 | loop fusion | flops 131072 | bytes 328200 | tf_op jit(solution)/shard_map/dynamic_update_slice | solution.py:278
  33.0 2.2 %copy-done.1 = bf16[2,1024,1024]{2,1,0:T(8,128)(2,1)S(1)} copy-done((bf16[2,1024,1024]{2,1,0:T(8,128)(2,1)S(1)}, bf16[2,1024,1024]{2,1,0:T(8,128)(2,1)}, u32[]{:S(2)}) %copy-start.1) | copy-done | bytes 4194328
  36.5 1.0 %collective-permute-done.3.refs_1_ = f32[256,128]{1,0:T(8,128)S(1)} collective-permute-done((f32[256,128]{1,0:T(8,128)S(1)}, f32[256,128]{1,0:T(8,128)S(1)}, u32[]{:S(2)}, u32[]{:S(2)}) %collective-permute-start.3) | collective-permute-done | bytes 131104 | tf_op jit(solution)/shard_map/ppermute | solution.py:21
  37.8 1.8 %collective-permute-start.5 = (bf16[256,128]{1,0:T(8,128)(2,1)S(1)}, bf16[256,128]{1,0:T(8,128)(2,1)S(1)}, u32[]{:S(2)}, u32[]{:S(2)}) collective-permute-start(bf16[256,128]{1,0:T(8,128)(2,1)S(1)} %get-tuple-element.40), channel_id=1, source_target_pairs={{0,2},{1,3},{2,0},{3,1},{4,6},{5,7},{6,4},{7,5},{8,10},{9,11},{10,... | collective-permute-start | bytes 196616 | tf_op jit(solution)/shard_map/ppermute | solution.py:21
  40.1 2.2 %collective-permute-done.5.refs_1_ = bf16[256,128]{1,0:T(8,128)(2,1)S(1)} collective-permute-done((bf16[256,128]{1,0:T(8,128)(2,1)S(1)}, bf16[256,128]{1,0:T(8,128)(2,1)S(1)}, u32[]{:S(2)}, u32[]{:S(2)}) %collective-permute-start.5) | collective-permute-done | bytes 65568 | tf_op jit(solution)/shard_map/ppermute | solution.py:21
  42.6 1.8 %collective-permute-start.8 = (bf16[256,128]{1,0:T(8,128)(2,1)S(1)}, bf16[256,128]{1,0:T(8,128)(2,1)S(1)}, u32[]{:S(2)}, u32[]{:S(2)}) collective-permute-start(bf16[256,128]{1,0:T(8,128)(2,1)S(1)} %get-tuple-element.46), channel_id=1, source_target_pairs={{0,4},{1,5},{2,6},{3,7},{4,0},{5,1},{6,2},{7,3},{8,12},{9,13},{10,... | collective-permute-start | bytes 196616 | tf_op jit(solution)/shard_map/ppermute | solution.py:21
  44.4 1.0 %shard_map.81.direct_ref = f32[768,128]{1,0:T(8,128)S(1)} custom-call(bf16[2,1024,1024]{2,1,0:T(8,128)(2,1)S(1)} %copy-done.2, bf16[1024,128]{1,0:T(8,128)(2,1)S(1)} %get-tuple-element.49.source_ref, bf16[1024,128]{1,0:T(8,128)(2,1)S(1)} %get-tuple-element.50.spun_ref), custom_call_target="tpu_custom_call" | custom-call | flops 402653184 | bytes 4718592 | tf_op jit(solution)/shard_map/pallas_call | solution.py:64
  45.4 1.5 %collective-permute-done.8.other_ref = bf16[256,128]{1,0:T(8,128)(2,1)S(1)} collective-permute-done((bf16[256,128]{1,0:T(8,128)(2,1)S(1)}, bf16[256,128]{1,0:T(8,128)(2,1)S(1)}, u32[]{:S(2)}, u32[]{:S(2)}) %collective-permute-start.8) | collective-permute-done | bytes 65568 | tf_op jit(solution)/shard_map/ppermute | solution.py:21
  47.6 1.3 %collective-permute-done.9.refs_1_ = f32[256,128]{1,0:T(8,128)S(1)} collective-permute-done((f32[256,128]{1,0:T(8,128)S(1)}, f32[256,128]{1,0:T(8,128)S(1)}, u32[]{:S(2)}, u32[]{:S(2)}) %collective-permute-start.9) | collective-permute-done | bytes 131104 | tf_op jit(solution)/shard_map/ppermute | solution.py:21
  49.2 1.8 %collective-permute-start.10 = (bf16[256,128]{1,0:T(8,128)(2,1)S(1)}, bf16[256,128]{1,0:T(8,128)(2,1)S(1)}, u32[]{:S(2)}, u32[]{:S(2)}) collective-permute-start(bf16[256,128]{1,0:T(8,128)(2,1)S(1)} %get-tuple-element.53), channel_id=1, source_target_pairs={{0,2},{1,3},{2,0},{3,1},{4,6},{5,7},{6,4},{7,5},{8,10},{9,11},{10,... | collective-permute-start | bytes 196616 | tf_op jit(solution)/shard_map/ppermute | solution.py:21
  51.0 2.6 %collective-permute-done.10.refs_1_ = bf16[256,128]{1,0:T(8,128)(2,1)S(1)} collective-permute-done((bf16[256,128]{1,0:T(8,128)(2,1)S(1)}, bf16[256,128]{1,0:T(8,128)(2,1)S(1)}, u32[]{:S(2)}, u32[]{:S(2)}) %collective-permute-start.10) | collective-permute-done | bytes 65568 | tf_op jit(solution)/shard_map/ppermute | solution.py:21
  53.9 1.8 %collective-permute-start.11 = (bf16[256,128]{1,0:T(8,128)(2,1)S(1)}, bf16[256,128]{1,0:T(8,128)(2,1)S(1)}, u32[]{:S(2)}, u32[]{:S(2)}) collective-permute-start(bf16[256,128]{1,0:T(8,128)(2,1)S(1)} %get-tuple-element.55), channel_id=1, source_target_pairs={{0,4},{1,5},{2,6},{3,7},{4,0},{5,1},{6,2},{7,3},{8,12},{9,13},{10,... | collective-permute-start | bytes 196616 | tf_op jit(solution)/shard_map/ppermute | solution.py:21
  56.2 2.0 %collective-permute-done.11.other_ref = bf16[256,128]{1,0:T(8,128)(2,1)S(1)} collective-permute-done((bf16[256,128]{1,0:T(8,128)(2,1)S(1)}, bf16[256,128]{1,0:T(8,128)(2,1)S(1)}, u32[]{:S(2)}, u32[]{:S(2)}) %collective-permute-start.11) | collective-permute-done | bytes 65568 | tf_op jit(solution)/shard_map/ppermute | solution.py:21
  58.2 1.6 %shard_map.86 = bf16[1024,128]{1,0:T(8,128)(2,1)} custom-call(bf16[256,128]{1,0:T(8,128)(2,1)S(1)} %collective-permute-done.11.other_ref, f32[256,128]{1,0:T(8,128)S(1)} %get-tuple-element.56.reach_ref, bf16[512,512]{1,0:T(8,128)(2,1)S(1)} %get-tuple-element.48.before_ref, bf16[2,1024,1024]{2,1,0:T(8,128)(2,1)S(1)} %copy-done.2, ...), custom_call_target="tpu_custom_call" | custom-call | flops 268435456 | bytes 5570560 | tf_op jit(solution)/shard_map/pallas_call | solution.py:64
  (46 shorter events, 8.8 us)
Async XLA Ops:
  0.0 0.9 %copy-start.4 = (bf16[1,1,1024,128]{3,2,1,0:T(8,128)(2,1)S(1)}, bf16[1,1,1024,128]{3,2,1,0:T(8,128)(2,1)}, u32[]{:S(2)}) copy-start(bf16[1,1,1024,128]{3,2,1,0:T(8,128)(2,1)} %param.9) | copy-start | bytes 786436
  1.0 0.7 %copy-start.5 = (s32[4,4]{1,0:T(4,128)S(1)}, s32[4,4]{1,0:T(4,128)}, u32[]{:S(2)}) copy-start(s32[4,4]{1,0:T(4,128)} %start_ref.1) | copy-start | bytes 196
  1.6 8.5 %copy-start.6 = (s32[4,4]{1,0:T(4,128)S(1)}, s32[4,4]{1,0:T(4,128)}, u32[]{:S(2)}) copy-start(s32[4,4]{1,0:T(4,128)} %start_ref.1) | copy-start | bytes 196
  1.6 9.2 %copy-start.8 = (f32[4,4]{1,0:T(4,128)S(1)}, f32[4,4]{1,0:T(4,128)}, u32[]{:S(2)}) copy-start(f32[4,4]{1,0:T(4,128)} %param.11) | copy-start | bytes 196
  1.6 9.9 %copy-start.9 = (s32[4,4]{1,0:T(4,128)S(1)}, s32[4,4]{1,0:T(4,128)}, u32[]{:S(2)}) copy-start(s32[4,4]{1,0:T(4,128)} %param.13) | copy-start | bytes 196
  1.6 13.7 %copy-start.7 = (bf16[1,1,1024,128]{3,2,1,0:T(8,128)(2,1)S(1)}, bf16[1,1,1024,128]{3,2,1,0:T(8,128)(2,1)}, u32[]{:S(2)}) copy-start(bf16[1,1,1024,128]{3,2,1,0:T(8,128)(2,1)} %param.8) | copy-start | bytes 786436
  2.2 23.1 %collective-permute-start = (bf16[256,128]{1,0:T(8,128)(2,1)S(1)}, bf16[256,128]{1,0:T(8,128)(2,1)S(1)}, u32[]{:S(2)}, u32[]{:S(2)}) collective-permute-start(bf16[256,128]{1,0:T(8,128)(2,1)S(1)} %get-tuple-element.32), channel_id=1, source_target_pairs={{0,8},{8,0},{16,24},{24,16},{1,9},{9,1},{17,25},{25,17},{2,10},{10... | collective-permute-start | bytes 196616 | tf_op jit(solution)/shard_map/ppermute | solution.py:21
  5.4 20.7 %collective-permute-start.1 = (bf16[256,128]{1,0:T(8,128)(2,1)S(1)}, bf16[256,128]{1,0:T(8,128)(2,1)S(1)}, u32[]{:S(2)}, u32[]{:S(2)}) collective-permute-start(bf16[256,128]{1,0:T(8,128)(2,1)S(1)} %get-tuple-element.33), channel_id=1, source_target_pairs={{0,16},{8,24},{16,0},{24,8},{1,17},{9,25},{17,1},{25,9},{2,18},{10... | collective-permute-start | bytes 196616 | tf_op jit(solution)/shard_map/ppermute | solution.py:21
  8.0 24.3 %collective-permute-start.2 = (bf16[256,128]{1,0:T(8,128)(2,1)S(1)}, bf16[256,128]{1,0:T(8,128)(2,1)S(1)}, u32[]{:S(2)}, u32[]{:S(2)}) collective-permute-start(bf16[256,128]{1,0:T(8,128)(2,1)S(1)} %get-tuple-element.34), channel_id=1, source_target_pairs={{0,24},{8,16},{16,8},{24,0},{1,25},{9,17},{17,9},{25,1},{2,26},{10... | collective-permute-start | bytes 196616 | tf_op jit(solution)/shard_map/ppermute | solution.py:21
  10.1 13.0 %collective-permute-start.4 = (bf16[512,512]{1,0:T(8,128)(2,1)S(1)}, bf16[512,512]{1,0:T(8,128)(2,1)S(1)}, u32[]{:S(2)}, u32[]{:S(2)}) collective-permute-start(bf16[512,512]{1,0:T(8,128)(2,1)S(1)} %get-tuple-element.37.refs_0_), channel_id=1, source_target_pairs={{0,1},{1,0},{2,3},{3,2},{4,5},{5,4},{6,7},{7,6},{8,9},{9,8},{10,11... | collective-permute-start | bytes 1572872 | tf_op jit(solution)/shard_map/ppermute | solution.py:21
  21.1 2.0 %copy-start = (bf16[2,1024,1024]{2,1,0:T(8,128)(2,1)}, bf16[2,1024,1024]{2,1,0:T(8,128)(2,1)S(1)}, u32[]{:S(2)}) copy-start(bf16[2,1024,1024]{2,1,0:T(8,128)(2,1)S(1)} %shard_map.75.held_ref) | copy-start | bytes 12582916
  23.6 8.7 %collective-permute-start.6 = (bf16[256,512]{1,0:T(8,128)(2,1)S(1)}, bf16[256,512]{1,0:T(8,128)(2,1)S(1)}, u32[]{:S(2)}, u32[]{:S(2)}) collective-permute-start(bf16[256,512]{1,0:T(8,128)(2,1)S(1)} %get-tuple-element.42), channel_id=1, source_target_pairs={{0,2},{1,3},{2,0},{3,1},{4,6},{5,7},{6,4},{7,5},{8,10},{9,11},{10,... | collective-permute-start | bytes 786440 | tf_op jit(solution)/shard_map/ppermute | solution.py:21
  32.3 7.3 %collective-permute-start.7 = (bf16[256,512]{1,0:T(8,128)(2,1)S(1)}, bf16[256,512]{1,0:T(8,128)(2,1)S(1)}, u32[]{:S(2)}, u32[]{:S(2)}) collective-permute-start(bf16[256,512]{1,0:T(8,128)(2,1)S(1)} %collective-permute-done.6.refs_1_), channel_id=1, source_target_pairs={{0,1},{1,0},{2,3},{3,2},{4,5},{5,4},{6,7},{7,6},{8,9},{9,8},{10,11... | collective-permute-start | bytes 786440 | tf_op jit(solution)/shard_map/ppermute | solution.py:21
  33.0 2.2 %copy-start.1 = (bf16[2,1024,1024]{2,1,0:T(8,128)(2,1)S(1)}, bf16[2,1024,1024]{2,1,0:T(8,128)(2,1)}, u32[]{:S(2)}) copy-start(bf16[2,1024,1024]{2,1,0:T(8,128)(2,1)} %copy-done) | copy-start | bytes 12582916
  35.2 9.2 %copy-start.2 = (bf16[2,1024,1024]{2,1,0:T(8,128)(2,1)S(1)}, bf16[2,1024,1024]{2,1,0:T(8,128)(2,1)}, u32[]{:S(2)}) copy-start(bf16[2,1024,1024]{2,1,0:T(8,128)(2,1)} %copy-done) | copy-start | bytes 12582916
  36.0 1.6 %collective-permute-start.3 = (f32[256,128]{1,0:T(8,128)S(1)}, f32[256,128]{1,0:T(8,128)S(1)}, u32[]{:S(2)}, u32[]{:S(2)}) collective-permute-start(f32[256,128]{1,0:T(8,128)S(1)} %get-tuple-element.36.refs_0_), channel_id=1, source_target_pairs={{0,1},{1,0},{2,3},{3,2},{4,5},{5,4},{6,7},{7,6},{8,9},{9,8},{10,11... | collective-permute-start | bytes 393224 | tf_op jit(solution)/shard_map/ppermute | solution.py:21
  37.8 4.4 %collective-permute-start.5 = (bf16[256,128]{1,0:T(8,128)(2,1)S(1)}, bf16[256,128]{1,0:T(8,128)(2,1)S(1)}, u32[]{:S(2)}, u32[]{:S(2)}) collective-permute-start(bf16[256,128]{1,0:T(8,128)(2,1)S(1)} %get-tuple-element.40), channel_id=1, source_target_pairs={{0,2},{1,3},{2,0},{3,1},{4,6},{5,7},{6,4},{7,5},{8,10},{9,11},{10,... | collective-permute-start | bytes 196616 | tf_op jit(solution)/shard_map/ppermute | solution.py:21
  42.6 4.3 %collective-permute-start.8 = (bf16[256,128]{1,0:T(8,128)(2,1)S(1)}, bf16[256,128]{1,0:T(8,128)(2,1)S(1)}, u32[]{:S(2)}, u32[]{:S(2)}) collective-permute-start(bf16[256,128]{1,0:T(8,128)(2,1)S(1)} %get-tuple-element.46), channel_id=1, source_target_pairs={{0,4},{1,5},{2,6},{3,7},{4,0},{5,1},{6,2},{7,3},{8,12},{9,13},{10,... | collective-permute-start | bytes 196616 | tf_op jit(solution)/shard_map/ppermute | solution.py:21
  47.5 10.8 %copy-start.3 = (bf16[1,256,256]{2,1,0:T(8,128)(2,1)S(1)}, bf16[1,256,256]{2,1,0:T(8,128)(2,1)}, u32[]{:S(2)}) copy-start(bf16[1,256,256]{2,1,0:T(8,128)(2,1)} %param.10) | copy-start | bytes 393220
  47.5 1.4 %collective-permute-start.9 = (f32[256,128]{1,0:T(8,128)S(1)}, f32[256,128]{1,0:T(8,128)S(1)}, u32[]{:S(2)}, u32[]{:S(2)}) collective-permute-start(f32[256,128]{1,0:T(8,128)S(1)} %get-tuple-element.51.refs_0_), channel_id=1, source_target_pairs={{0,1},{1,0},{2,3},{3,2},{4,5},{5,4},{6,7},{7,6},{8,9},{9,8},{10,11... | collective-permute-start | bytes 393224 | tf_op jit(solution)/shard_map/ppermute | solution.py:21
  49.2 4.3 %collective-permute-start.10 = (bf16[256,128]{1,0:T(8,128)(2,1)S(1)}, bf16[256,128]{1,0:T(8,128)(2,1)S(1)}, u32[]{:S(2)}, u32[]{:S(2)}) collective-permute-start(bf16[256,128]{1,0:T(8,128)(2,1)S(1)} %get-tuple-element.53), channel_id=1, source_target_pairs={{0,2},{1,3},{2,0},{3,1},{4,6},{5,7},{6,4},{7,5},{8,10},{9,11},{10,... | collective-permute-start | bytes 196616 | tf_op jit(solution)/shard_map/ppermute | solution.py:21
  53.9 4.3 %collective-permute-start.11 = (bf16[256,128]{1,0:T(8,128)(2,1)S(1)}, bf16[256,128]{1,0:T(8,128)(2,1)S(1)}, u32[]{:S(2)}, u32[]{:S(2)}) collective-permute-start(bf16[256,128]{1,0:T(8,128)(2,1)S(1)} %get-tuple-element.55), channel_id=1, source_target_pairs={{0,4},{1,5},{2,6},{3,7},{4,0},{5,1},{6,2},{7,3},{8,12},{9,13},{10,... | collective-permute-start | bytes 196616 | tf_op jit(solution)/shard_map/ppermute | solution.py:21

commit v4 on v3

--- a/solution.py
+++ b/solution.py
@@ -264,22 +264,37 @@
             total, sent, reach = res if not final else [None] + list(res)
         return swapped(sent, "slab", slabs // 2), reach
 
-    me = lax.axis_index("energy")
-    row = lax.broadcasted_iota(jnp.int32, (span, width), 0)
-    scattered = injection[0, 0].astype(f32)
-    own_piece = lax.dynamic_slice(panel, (block_start[me, me] * rows, 0), (span, width))
-    for k, piece in enumerate([own_piece] + received):
-        s = me ^ k
-        first = block_start[me, s] * rows
-        term = jnp.where(
-            row < block_count[me, s] * rows, piece.astype(f32) * strength[me, s], 0.0
-        )
-        so_far = lax.dynamic_slice(scattered, (first, 0), (span, width))
-        scattered = lax.dynamic_update_slice(scattered, so_far + term, (first, 0))
-
-    def load(sum_ref, held_ref, turn_ref, source_ref, spun_ref, low_ref, sent_ref):
-        total = sum_ref[...]
-        source = total.astype(bf16)
+    def prepare(inj_ref, panel_ref, start_ref, count_ref, strength_ref, acc_ref, weight_ref):
+        me = lax.axis_index("energy")
+        row = lax.broadcasted_iota(jnp.int32, (span, width), 0)
+        acc_ref[...] = inj_ref[...].astype(f32)
+        for k in range(energies):
+            s = me ^ k
+            weight = jnp.where(row < count_ref[me, s] * rows, strength_ref[me, s], 0.0)
+            if k:
+                weight_ref[k - 1] = weight
+            else:
+                first = pl.multiple_of(start_ref[me, me] * rows, rows)
+                part = pl.ds(first, span)
+                acc_ref[part] = acc_ref[part] + panel_ref[part].astype(f32) * weight
+
+    acc, weights = call(
+        prepare,
+        [((norb, width), f32), ((energies - 1, span, width), f32)],
+        (injection[0, 0], panel, block_start, block_count, strength),
+        0,
+        {2: SMEM, 3: SMEM, 4: SMEM},
+    )
+
+    def load(start_ref, acc_ref, weight_ref, held_ref, turn_ref, *refs):
+        got, (source_ref, spun_ref, low_ref, sent_ref, sum_ref) = refs[:-5], refs[-5:]
+        me = lax.axis_index("energy")
+        sum_ref[...] = acc_ref[...]
+        for k in range(1, energies):
+            first = pl.multiple_of(start_ref[me, me ^ k] * rows, rows)
+            part = pl.ds(first, span)
+            sum_ref[part] = sum_ref[part] + got[k - 1][...].astype(f32) * weight_ref[k - 1]
+        source = sum_ref[...].astype(bf16)
         spun = turned(source.astype(f32)).astype(bf16)
         source_ref[...] = source
         spun_ref[...] = spun
@@ -290,8 +305,10 @@
     source, spun, direct_low, sent = call(
         load,
         [((norb, width), bf16)] * 2 + [((layer, width), f32)] * 2,
-        (scattered, held, coup_t),
+        (block_start, acc, weights, held, coup_t, *received),
         4 * layer * norb * width,
+        {0: SMEM},
+        [pltpu.VMEM((norb, width), f32)],
     )
     arrived, reach = scan(sent, 0)
 

time: 60.2 us -> 50.6 us (0.84)
  local copies, waits for them, and re-layouts: 7.76 us -> 0.02 us
  waiting for transfers between devices: 16.1 us -> 22.9 us
  between operations: 5.29 us -> 0.17 us
  other arithmetic: 3.8 us -> 0 us
  Pallas kernels: 11.5 us -> 13 us
  starting transfers between devices: 15.3 us -> 14.4 us
    ppermute x12, waiting for transfers between devices: 16.1 us -> 22.9 us  [swapped(): return lax.ppermute(block, axis, [(i, i ^ mask) for i in range(count)])]
    unnamed x20 -> x12, local copies, waits for them, and re-layouts: 5.8 us -> 0.02 us
    dynamic_update_slice x4 -> x0, other arithmetic: 3.69 us -> none  [body(): scattered = lax.dynamic_update_slice(scattered, so_far + term, (first, 0))]
    dynamic_slice x3 -> x0, local copies, waits for them, and re-layouts: 1.97 us -> none  [the longest x1 0.67 us: body(): first = block_start[me, s] * rows]
    pallas_call x14 -> x15, Pallas kernels: 11.5 us -> 13 us  [call(): pl.pallas_call(kernel, out_shape=shapes, in_specs=specs, out_specs=[pl.Bl...]
    ppermute x12, starting transfers between devices: 15.3 us -> 14.4 us  [swapped(): return lax.ppermute(block, axis, [(i, i ^ mask) for i in range(count)])]
  transfers between devices with their start and end apart: 12 -> 12, of which waited for: 7 -> 10; matrix products, arithmetic and copies ran while one was open for 10% -> 0% of each run, Pallas kernels for 13% -> 14%
where the time goes in v4:
time: 50.6 us; the launch traced here: 50.5 us
  waiting for transfers between devices  22.9 us (45%)
  starting transfers between devices  14.4 us (28%)
  Pallas kernels  13 us (26%)
    ppermute x12, waiting for transfers between devices, swapped(): return lax.ppermute(block, axis, [(i, i ^ mask) for i in range(count)])  22.9 us
    ppermute x12, starting transfers between devices, swapped(): return lax.ppermute(block, axis, [(i, i ^ mask) for i in range(count)])  14.4 us
    pallas_call x15, Pallas kernels, call(): pl.pallas_call(kernel, out_shape=shapes, in_specs=specs, out_specs=[pl.Bl...  13 us
  transfers between devices with their start and end apart: 12, of which 10 were waited for; matrix products, arithmetic and copies ran while one was open for 0% of the time, Pallas kernels for 14%

profile of v4, /device:TPU:0, one launch (start us, length us, event | category | flops | bytes accessed | tf_op | source)
XLA Modules:
  0.0 50.5 jit_solution(8360396744704662652)
XLA Ops:
  0.0 2.2 %shard_map.74 = (bf16[512,512]{1,0:T(8,128)(2,1)S(1)}, bf16[256,256]{1,0:T(8,128)(2,1)S(1)}) custom-call(bf16[2,1024,1024]{2,1,0:T(8,128)(2,1)} %bitcast.10, bf16[256,256]{1,0:T(8,128)(2,1)} %bitcast.7), custom_call_target="tpu_custom_call" | custom-call | flops 134217728 | bytes 4325376 | tf_op jit(solution)/shard_map/pallas_call | solution.py:64
  2.7 1.5 %collective-permute-done.4.refs_1_ = bf16[512,512]{1,0:T(8,128)(2,1)S(1)} collective-permute-done((bf16[512,512]{1,0:T(8,128)(2,1)S(1)}, bf16[512,512]{1,0:T(8,128)(2,1)S(1)}, u32[]{:S(2)}, u32[]{:S(2)}) %collective-permute-start.4) | collective-permute-done | bytes 524320 | tf_op jit(solution)/shard_map/ppermute | solution.py:21
  4.8 2.9 %collective-permute-start.6 = (bf16[256,512]{1,0:T(8,128)(2,1)S(1)}, bf16[256,512]{1,0:T(8,128)(2,1)S(1)}, u32[]{:S(2)}, u32[]{:S(2)}) collective-permute-start(bf16[256,512]{1,0:T(8,128)(2,1)S(1)} %get-tuple-element.46), channel_id=1, source_target_pairs={{0,2},{1,3},{2,0},{3,1},{4,6},{5,7},{6,4},{7,5},{8,10},{9,11},{10,... | collective-permute-start | bytes 786440 | tf_op jit(solution)/shard_map/ppermute | solution.py:21
  7.7 6.6 %collective-permute-done.6.refs_1_ = bf16[256,512]{1,0:T(8,128)(2,1)S(1)} collective-permute-done((bf16[256,512]{1,0:T(8,128)(2,1)S(1)}, bf16[256,512]{1,0:T(8,128)(2,1)S(1)}, u32[]{:S(2)}, u32[]{:S(2)}) %collective-permute-start.6) | collective-permute-done | bytes 262176 | tf_op jit(solution)/shard_map/ppermute | solution.py:21
  14.3 0.6 %shard_map.76 = (bf16[256,128]{1,0:T(8,128)(2,1)S(1)}, bf16[256,128]{1,0:T(8,128)(2,1)S(1)}, bf16[256,128]{1,0:T(8,128)(2,1)S(1)}) custom-call(s32[4,4]{1,0:T(4,128)S(1)} %copy-done.3, bf16[1024,128]{1,0:T(8,128)(2,1)S(1)} %bitcast.5), custom_call_target="tpu_custom_call" | custom-call | bytes 262208 | tf_op jit(solution)/shard_map/pallas_call | solution.py:64
  14.9 1.9 %collective-permute-start = (bf16[256,128]{1,0:T(8,128)(2,1)S(1)}, bf16[256,128]{1,0:T(8,128)(2,1)S(1)}, u32[]{:S(2)}, u32[]{:S(2)}) collective-permute-start(bf16[256,128]{1,0:T(8,128)(2,1)S(1)} %get-tuple-element.37), channel_id=1, source_target_pairs={{0,8},{8,0},{16,24},{24,16},{1,9},{9,1},{17,25},{25,17},{2,10},{10... | collective-permute-start | bytes 196616 | tf_op jit(solution)/shard_map/ppermute | solution.py:21
  16.8 2.6 %collective-permute-start.1 = (bf16[256,128]{1,0:T(8,128)(2,1)S(1)}, bf16[256,128]{1,0:T(8,128)(2,1)S(1)}, u32[]{:S(2)}, u32[]{:S(2)}) collective-permute-start(bf16[256,128]{1,0:T(8,128)(2,1)S(1)} %get-tuple-element.38), channel_id=1, source_target_pairs={{0,16},{8,24},{16,0},{24,8},{1,17},{9,25},{17,1},{25,9},{2,18},{10... | collective-permute-start | bytes 196616 | tf_op jit(solution)/shard_map/ppermute | solution.py:21
  19.4 2.3 %shard_map.75.held_ref = bf16[2,1024,1024]{2,1,0:T(8,128)(2,1)S(1)} custom-call(bf16[2,1024,1024]{2,1,0:T(8,128)(2,1)} %bitcast.11, bf16[256,256]{1,0:T(8,128)(2,1)S(1)} %get-tuple-element.36.hint_ref.turn_ref), custom_call_target="tpu_custom_call" | custom-call | bytes 4325376 | tf_op jit(solution)/shard_map/pallas_call | solution.py:64
  21.7 0.7 %shard_map.73 = (f32[1024,128]{1,0:T(8,128)S(1)}, f32[3,256,128]{2,1,0:T(8,128)S(1)}) custom-call(bf16[1024,128]{1,0:T(8,128)(2,1)S(1)} %bitcast.9, bf16[1024,128]{1,0:T(8,128)(2,1)S(1)} %bitcast.6, s32[4,4]{1,0:T(4,128)S(1)} %copy-done.3, s32[4,4]{1,0:T(4,128)S(1)} %copy-done.4, f32[4,4]{1,0:T(4,128)S(1)} %copy-done.5), custom_call_target="tpu_custom_call" | custom-call | bytes 524480 | tf_op jit(solution)/shard_map/pallas_call | solution.py:64
  22.5 1.3 %collective-permute-done.1.refs_1_ = bf16[256,128]{1,0:T(8,128)(2,1)S(1)} collective-permute-done((bf16[256,128]{1,0:T(8,128)(2,1)S(1)}, bf16[256,128]{1,0:T(8,128)(2,1)S(1)}, u32[]{:S(2)}, u32[]{:S(2)}) %collective-permute-start.1) | collective-permute-done | bytes 65568 | tf_op jit(solution)/shard_map/ppermute | solution.py:21
  23.8 1.7 %collective-permute-done.2.refs_2_ = bf16[256,128]{1,0:T(8,128)(2,1)S(1)} collective-permute-done((bf16[256,128]{1,0:T(8,128)(2,1)S(1)}, bf16[256,128]{1,0:T(8,128)(2,1)S(1)}, u32[]{:S(2)}, u32[]{:S(2)}) %collective-permute-start.2) | collective-permute-done | bytes 65568 | tf_op jit(solution)/shard_map/ppermute | solution.py:21
  25.4 1.4 %shard_map.77 = (bf16[1024,128]{1,0:T(8,128)(2,1)S(1)}, bf16[1024,128]{1,0:T(8,128)(2,1)S(1)}, f32[256,128]{1,0:T(8,128)S(1)}, f32[256,128]{1,0:T(8,128)S(1)}) custom-call(s32[4,4]{1,0:T(4,128)S(1)} %copy-done.3, f32[1024,128]{1,0:T(8,128)S(1)} %get-tuple-element.34.acc_ref, f32[3,256,128]{2,1,0:T(8,128)S(1)} %get-tuple-element.35.weight_ref, ...), custom_call_target="tpu_custom_call" | custom-call | flops 134217728 | bytes 5439552 | tf_op jit(solution)/shard_map/pallas_call | solution.py:64
  26.9 1.3 %collective-permute-done.3.refs_1_ = f32[256,128]{1,0:T(8,128)S(1)} collective-permute-done((f32[256,128]{1,0:T(8,128)S(1)}, f32[256,128]{1,0:T(8,128)S(1)}, u32[]{:S(2)}, u32[]{:S(2)}) %collective-permute-start.3) | collective-permute-done | bytes 131104 | tf_op jit(solution)/shard_map/ppermute | solution.py:21
  28.5 1.6 %collective-permute-start.5 = (bf16[256,128]{1,0:T(8,128)(2,1)S(1)}, bf16[256,128]{1,0:T(8,128)(2,1)S(1)}, u32[]{:S(2)}, u32[]{:S(2)}) collective-permute-start(bf16[256,128]{1,0:T(8,128)(2,1)S(1)} %get-tuple-element.44), channel_id=1, source_target_pairs={{0,2},{1,3},{2,0},{3,1},{4,6},{5,7},{6,4},{7,5},{8,10},{9,11},{10,... | collective-permute-start | bytes 196616 | tf_op jit(solution)/shard_map/ppermute | solution.py:21
  30.6 2.3 %collective-permute-done.5.refs_1_ = bf16[256,128]{1,0:T(8,128)(2,1)S(1)} collective-permute-done((bf16[256,128]{1,0:T(8,128)(2,1)S(1)}, bf16[256,128]{1,0:T(8,128)(2,1)S(1)}, u32[]{:S(2)}, u32[]{:S(2)}) %collective-permute-start.5) | collective-permute-done | bytes 65568 | tf_op jit(solution)/shard_map/ppermute | solution.py:21
  33.2 1.6 %collective-permute-start.8 = (bf16[256,128]{1,0:T(8,128)(2,1)S(1)}, bf16[256,128]{1,0:T(8,128)(2,1)S(1)}, u32[]{:S(2)}, u32[]{:S(2)}) collective-permute-start(bf16[256,128]{1,0:T(8,128)(2,1)S(1)} %get-tuple-element.50), channel_id=1, source_target_pairs={{0,4},{1,5},{2,6},{3,7},{4,0},{5,1},{6,2},{7,3},{8,12},{9,13},{10,... | collective-permute-start | bytes 196616 | tf_op jit(solution)/shard_map/ppermute | solution.py:21
  34.8 1.0 %shard_map.82.direct_ref = f32[768,128]{1,0:T(8,128)S(1)} custom-call(bf16[2,1024,1024]{2,1,0:T(8,128)(2,1)S(1)} %shard_map.75.held_ref, bf16[1024,128]{1,0:T(8,128)(2,1)S(1)} %get-tuple-element.53.source_ref, bf16[1024,128]{1,0:T(8,128)(2,1)S(1)} %get-tuple-element.54.spun_ref), custom_call_target="tpu_custom_call" | custom-call | flops 402653184 | bytes 4718592 | tf_op jit(solution)/shard_map/pallas_call | solution.py:64
  35.8 1.8 %collective-permute-done.8.other_ref = bf16[256,128]{1,0:T(8,128)(2,1)S(1)} collective-permute-done((bf16[256,128]{1,0:T(8,128)(2,1)S(1)}, bf16[256,128]{1,0:T(8,128)(2,1)S(1)}, u32[]{:S(2)}, u32[]{:S(2)}) %collective-permute-start.8) | collective-permute-done | bytes 65568 | tf_op jit(solution)/shard_map/ppermute | solution.py:21
  38.2 1.3 %collective-permute-done.9.refs_1_ = f32[256,128]{1,0:T(8,128)S(1)} collective-permute-done((f32[256,128]{1,0:T(8,128)S(1)}, f32[256,128]{1,0:T(8,128)S(1)}, u32[]{:S(2)}, u32[]{:S(2)}) %collective-permute-start.9) | collective-permute-done | bytes 131104 | tf_op jit(solution)/shard_map/ppermute | solution.py:21
  39.8 1.6 %collective-permute-start.10 = (bf16[256,128]{1,0:T(8,128)(2,1)S(1)}, bf16[256,128]{1,0:T(8,128)(2,1)S(1)}, u32[]{:S(2)}, u32[]{:S(2)}) collective-permute-start(bf16[256,128]{1,0:T(8,128)(2,1)S(1)} %get-tuple-element.57), channel_id=1, source_target_pairs={{0,2},{1,3},{2,0},{3,1},{4,6},{5,7},{6,4},{7,5},{8,10},{9,11},{10,... | collective-permute-start | bytes 196616 | tf_op jit(solution)/shard_map/ppermute | solution.py:21
  41.4 2.8 %collective-permute-done.10.refs_1_ = bf16[256,128]{1,0:T(8,128)(2,1)S(1)} collective-permute-done((bf16[256,128]{1,0:T(8,128)(2,1)S(1)}, bf16[256,128]{1,0:T(8,128)(2,1)S(1)}, u32[]{:S(2)}, u32[]{:S(2)}) %collective-permute-start.10) | collective-permute-done | bytes 65568 | tf_op jit(solution)/shard_map/ppermute | solution.py:21
  44.5 1.6 %collective-permute-start.11 = (bf16[256,128]{1,0:T(8,128)(2,1)S(1)}, bf16[256,128]{1,0:T(8,128)(2,1)S(1)}, u32[]{:S(2)}, u32[]{:S(2)}) collective-permute-start(bf16[256,128]{1,0:T(8,128)(2,1)S(1)} %get-tuple-element.59), channel_id=1, source_target_pairs={{0,4},{1,5},{2,6},{3,7},{4,0},{5,1},{6,2},{7,3},{8,12},{9,13},{10,... | collective-permute-start | bytes 196616 | tf_op jit(solution)/shard_map/ppermute | solution.py:21
  46.6 2.2 %collective-permute-done.11.other_ref = bf16[256,128]{1,0:T(8,128)(2,1)S(1)} collective-permute-done((bf16[256,128]{1,0:T(8,128)(2,1)S(1)}, bf16[256,128]{1,0:T(8,128)(2,1)S(1)}, u32[]{:S(2)}, u32[]{:S(2)}) %collective-permute-start.11) | collective-permute-done | bytes 65568 | tf_op jit(solution)/shard_map/ppermute | solution.py:21
  48.9 1.6 %shard_map.87 = bf16[1024,128]{1,0:T(8,128)(2,1)} custom-call(bf16[256,128]{1,0:T(8,128)(2,1)S(1)} %collective-permute-done.11.other_ref, f32[256,128]{1,0:T(8,128)S(1)} %get-tuple-element.60.reach_ref, bf16[512,512]{1,0:T(8,128)(2,1)S(1)} %get-tuple-element.52.before_ref, bf16[2,1024,1024]{2,1,0:T(8,128)(2,1)S(1)} %shard_map.75.held_ref, ...), custom_call_target="tpu_custom_call" | custom-call | flops 268435456 | bytes 5570560 | tf_op jit(solution)/shard_map/pallas_call | solution.py:64
  (27 shorter events, 4.1 us)
Async XLA Ops:
  0.0 14.3 %copy-start.3 = (s32[4,4]{1,0:T(4,128)S(1)}, s32[4,4]{1,0:T(4,128)}, u32[]{:S(2)}) copy-start(s32[4,4]{1,0:T(4,128)} %start_ref.5) | copy-start | bytes 196
  0.0 14.3 %copy-start = (bf16[1,1,1024,128]{3,2,1,0:T(8,128)(2,1)S(1)}, bf16[1,1,1024,128]{3,2,1,0:T(8,128)(2,1)}, u32[]{:S(2)}) copy-start(bf16[1,1,1024,128]{3,2,1,0:T(8,128)(2,1)} %param.9) | copy-start | bytes 786436
  2.2 2.1 %collective-permute-start.4 = (bf16[512,512]{1,0:T(8,128)(2,1)S(1)}, bf16[512,512]{1,0:T(8,128)(2,1)S(1)}, u32[]{:S(2)}, u32[]{:S(2)}) collective-permute-start(bf16[512,512]{1,0:T(8,128)(2,1)S(1)} %get-tuple-element.41.refs_0_), channel_id=1, source_target_pairs={{0,1},{1,0},{2,3},{3,2},{4,5},{5,4},{6,7},{7,6},{8,9},{9,8},{10,11... | collective-permute-start | bytes 1572872 | tf_op jit(solution)/shard_map/ppermute | solution.py:21
  4.8 9.5 %collective-permute-start.6 = (bf16[256,512]{1,0:T(8,128)(2,1)S(1)}, bf16[256,512]{1,0:T(8,128)(2,1)S(1)}, u32[]{:S(2)}, u32[]{:S(2)}) collective-permute-start(bf16[256,512]{1,0:T(8,128)(2,1)S(1)} %get-tuple-element.46), channel_id=1, source_target_pairs={{0,2},{1,3},{2,0},{3,1},{4,6},{5,7},{6,4},{7,5},{8,10},{9,11},{10,... | collective-permute-start | bytes 786440 | tf_op jit(solution)/shard_map/ppermute | solution.py:21
  14.3 15.8 %collective-permute-start.7 = (bf16[256,512]{1,0:T(8,128)(2,1)S(1)}, bf16[256,512]{1,0:T(8,128)(2,1)S(1)}, u32[]{:S(2)}, u32[]{:S(2)}) collective-permute-start(bf16[256,512]{1,0:T(8,128)(2,1)S(1)} %collective-permute-done.6.refs_1_), channel_id=1, source_target_pairs={{0,1},{1,0},{2,3},{3,2},{4,5},{5,4},{6,7},{7,6},{8,9},{9,8},{10,11... | collective-permute-start | bytes 786440 | tf_op jit(solution)/shard_map/ppermute | solution.py:21
  14.9 7.6 %collective-permute-start = (bf16[256,128]{1,0:T(8,128)(2,1)S(1)}, bf16[256,128]{1,0:T(8,128)(2,1)S(1)}, u32[]{:S(2)}, u32[]{:S(2)}) collective-permute-start(bf16[256,128]{1,0:T(8,128)(2,1)S(1)} %get-tuple-element.37), channel_id=1, source_target_pairs={{0,8},{8,0},{16,24},{24,16},{1,9},{9,1},{17,25},{25,17},{2,10},{10... | collective-permute-start | bytes 196616 | tf_op jit(solution)/shard_map/ppermute | solution.py:21
  16.8 7.0 %collective-permute-start.1 = (bf16[256,128]{1,0:T(8,128)(2,1)S(1)}, bf16[256,128]{1,0:T(8,128)(2,1)S(1)}, u32[]{:S(2)}, u32[]{:S(2)}) collective-permute-start(bf16[256,128]{1,0:T(8,128)(2,1)S(1)} %get-tuple-element.38), channel_id=1, source_target_pairs={{0,16},{8,24},{16,0},{24,8},{1,17},{9,25},{17,1},{25,9},{2,18},{10... | collective-permute-start | bytes 196616 | tf_op jit(solution)/shard_map/ppermute | solution.py:21
  19.4 6.1 %collective-permute-start.2 = (bf16[256,128]{1,0:T(8,128)(2,1)S(1)}, bf16[256,128]{1,0:T(8,128)(2,1)S(1)}, u32[]{:S(2)}, u32[]{:S(2)}) collective-permute-start(bf16[256,128]{1,0:T(8,128)(2,1)S(1)} %get-tuple-element.39), channel_id=1, source_target_pairs={{0,24},{8,16},{16,8},{24,0},{1,25},{9,17},{17,9},{25,1},{2,26},{10... | collective-permute-start | bytes 196616 | tf_op jit(solution)/shard_map/ppermute | solution.py:21
  19.4 2.3 %copy-start.2 = (bf16[1,1,1024,128]{3,2,1,0:T(8,128)(2,1)S(1)}, bf16[1,1,1024,128]{3,2,1,0:T(8,128)(2,1)}, u32[]{:S(2)}) copy-start(bf16[1,1,1024,128]{3,2,1,0:T(8,128)(2,1)} %param.8) | copy-start | bytes 786436
  19.4 2.3 %copy-start.4 = (s32[4,4]{1,0:T(4,128)S(1)}, s32[4,4]{1,0:T(4,128)}, u32[]{:S(2)}) copy-start(s32[4,4]{1,0:T(4,128)} %count_ref.1) | copy-start | bytes 196
  19.4 2.3 %copy-start.5 = (f32[4,4]{1,0:T(4,128)S(1)}, f32[4,4]{1,0:T(4,128)}, u32[]{:S(2)}) copy-start(f32[4,4]{1,0:T(4,128)} %strength_ref.1) | copy-start | bytes 196
  26.8 1.4 %collective-permute-start.3 = (f32[256,128]{1,0:T(8,128)S(1)}, f32[256,128]{1,0:T(8,128)S(1)}, u32[]{:S(2)}, u32[]{:S(2)}) collective-permute-start(f32[256,128]{1,0:T(8,128)S(1)} %get-tuple-element.40.refs_0_), channel_id=1, source_target_pairs={{0,1},{1,0},{2,3},{3,2},{4,5},{5,4},{6,7},{7,6},{8,9},{9,8},{10,11... | collective-permute-start | bytes 393224 | tf_op jit(solution)/shard_map/ppermute | solution.py:21
  28.5 4.3 %collective-permute-start.5 = (bf16[256,128]{1,0:T(8,128)(2,1)S(1)}, bf16[256,128]{1,0:T(8,128)(2,1)S(1)}, u32[]{:S(2)}, u32[]{:S(2)}) collective-permute-start(bf16[256,128]{1,0:T(8,128)(2,1)S(1)} %get-tuple-element.44), channel_id=1, source_target_pairs={{0,2},{1,3},{2,0},{3,1},{4,6},{5,7},{6,4},{7,5},{8,10},{9,11},{10,... | collective-permute-start | bytes 196616 | tf_op jit(solution)/shard_map/ppermute | solution.py:21
  33.2 4.3 %collective-permute-start.8 = (bf16[256,128]{1,0:T(8,128)(2,1)S(1)}, bf16[256,128]{1,0:T(8,128)(2,1)S(1)}, u32[]{:S(2)}, u32[]{:S(2)}) collective-permute-start(bf16[256,128]{1,0:T(8,128)(2,1)S(1)} %get-tuple-element.50), channel_id=1, source_target_pairs={{0,4},{1,5},{2,6},{3,7},{4,0},{5,1},{6,2},{7,3},{8,12},{9,13},{10,... | collective-permute-start | bytes 196616 | tf_op jit(solution)/shard_map/ppermute | solution.py:21
  38.1 10.8 %copy-start.1 = (bf16[1,256,256]{2,1,0:T(8,128)(2,1)S(1)}, bf16[1,256,256]{2,1,0:T(8,128)(2,1)}, u32[]{:S(2)}) copy-start(bf16[1,256,256]{2,1,0:T(8,128)(2,1)} %param.10) | copy-start | bytes 393220
  38.1 1.4 %collective-permute-start.9 = (f32[256,128]{1,0:T(8,128)S(1)}, f32[256,128]{1,0:T(8,128)S(1)}, u32[]{:S(2)}, u32[]{:S(2)}) collective-permute-start(f32[256,128]{1,0:T(8,128)S(1)} %get-tuple-element.55.refs_0_), channel_id=1, source_target_pairs={{0,1},{1,0},{2,3},{3,2},{4,5},{5,4},{6,7},{7,6},{8,9},{9,8},{10,11... | collective-permute-start | bytes 393224 | tf_op jit(solution)/shard_map/ppermute | solution.py:21
  39.8 4.3 %collective-permute-start.10 = (bf16[256,128]{1,0:T(8,128)(2,1)S(1)}, bf16[256,128]{1,0:T(8,128)(2,1)S(1)}, u32[]{:S(2)}, u32[]{:S(2)}) collective-permute-start(bf16[256,128]{1,0:T(8,128)(2,1)S(1)} %get-tuple-element.57), channel_id=1, source_target_pairs={{0,2},{1,3},{2,0},{3,1},{4,6},{5,7},{6,4},{7,5},{8,10},{9,11},{10,... | collective-permute-start | bytes 196616 | tf_op jit(solution)/shard_map/ppermute | solution.py:21
  44.5 4.3 %collective-permute-start.11 = (bf16[256,128]{1,0:T(8,128)(2,1)S(1)}, bf16[256,128]{1,0:T(8,128)(2,1)S(1)}, u32[]{:S(2)}, u32[]{:S(2)}) collective-permute-start(bf16[256,128]{1,0:T(8,128)(2,1)S(1)} %get-tuple-element.59), channel_id=1, source_target_pairs={{0,4},{1,5},{2,6},{3,7},{4,0},{5,1},{6,2},{7,3},{8,12},{9,13},{10,... | collective-permute-start | bytes 196616 | tf_op jit(solution)/shard_map/ppermute | solution.py:21

commit v5 on v4

v5 whole, which is shorter than its diff:
```python
import math

import jax
import jax.numpy as jnp
from jax import lax
from jax.experimental import pallas as pl
from jax.experimental.pallas import tpu as pltpu
from jax.sharding import PartitionSpec as P


NBLK = 16
CAP = 4
VMEM_BYTES = 67043328
bf16 = jnp.bfloat16
f32 = jnp.float32
VMEM = pltpu.VMEM


def swapped(block, axis, mask):
    count = lax.axis_size(axis)
    return lax.ppermute(block, axis, [(i, i ^ mask) for i in range(count)])


def dot(a, b):
    return jnp.dot(a, b, preferred_element_type=f32)


def turned(v):
    half = v.shape[1] // 2
    if half % 128 == 0:
        return jnp.concatenate([-v[:, half:], v[:, :half]], axis=1)
    lane = lax.broadcasted_iota(jnp.int32, v.shape, 1)
    moved = pltpu.roll(v, half, 1)
    return jnp.where(lane < half, -moved, moved)


def applied(real, imag, v):
    v = v.astype(f32)
    return dot(real, v.astype(bf16)) + dot(imag, turned(v).astype(bf16))


def mapped(wide, v):
    side = wide.shape[1] // 2
    return applied(wide[:, :side], wide[:, side:], v)


def fine(real, v):
    high = v.astype(bf16)
    return dot(real, high) + dot(real, (v - high.astype(f32)).astype(bf16))


def place(k):
    return ((lax.axis_index("slab") >> k) & 1) == 1


def call(kernel, outs, args, flops, spaces=None, scratch=(), out_space=VMEM, spare=None):
    spaces = spaces or {}
    specs = [pl.BlockSpec(memory_space=spaces.get(i, VMEM)) for i in range(len(args))]
    moved = sum(a.size * a.dtype.itemsize for a in args)
    kept = sum(math.prod(s) * jnp.dtype(t).itemsize for s, t in outs)
    kept += sum(a.size * a.dtype.itemsize for i, a in enumerate(args) if i not in spaces)
    limit = kept + (4 << 20) if spare is None else VMEM_BYTES - spare
    shapes = [jax.ShapeDtypeStruct(s, t) for s, t in outs]
    return pl.pallas_call(
        kernel,
        out_shape=shapes,
        in_specs=specs,
        out_specs=[pl.BlockSpec(memory_space=out_space)] * len(shapes),
        scratch_shapes=list(scratch),
        compiler_params=pltpu.CompilerParams(vmem_limit_bytes=limit),
        cost_estimate=pl.CostEstimate(
            flops=flops, bytes_accessed=moved, transcendentals=0
        ),
    )(*args)


def body(pivots, injection, previous, coupling, strength, block_start, block_count):
    green = pivots[0, 0]
    norb = green.shape[1]
    layer = coupling.shape[1]
    width = injection.shape[3]
    rows = norb // NBLK
    span = rows * CAP
    far_green = pltpu.with_memory_space_constraint(green, pltpu.HBM)
    coup = coupling[0]
    far_coup = pltpu.with_memory_space_constraint(coup, pltpu.HBM)
    panel = previous[0, 0]
    energies = lax.axis_size("energy")
    slabs = lax.axis_size("slab")
    levels = slabs.bit_length() - 1
    low = norb - layer
    SMEM = pltpu.SMEM

    rows_of = [slice(k * layer, (k + 1) * layer) for k in range(6)]
    triple, one_map = (3 * layer, 2 * layer), (layer, 2 * layer)

    def own_maps(green_ref, coup_ref, maps_ref, turn_ref, corner, near, sem, sem_c):
        top, end = pl.ds(0, layer), pl.ds(low, layer)
        copies = [
            [
                pltpu.make_async_copy(green_ref.at[k, r, c], corner.at[i, k], sem.at[i, k])
                for k in range(2)
            ]
            for i, (r, c) in enumerate(((end, top), (top, end), (top, top)))
        ]
        first = pltpu.make_async_copy(coup_ref, near, sem_c)
        first.start()
        for pair in copies:
            for copy in pair:
                copy.start()
        first.wait()
        c = near[...]
        ct = c.astype(f32).T.astype(bf16)
        turn_ref[...] = ct
        for i in range(3):
            for k in range(2):
                copies[i][k].wait()
                held = corner[i, k]
                if i == 0:
                    held = dot(ct, held).astype(bf16)
                elif i == 1:
                    held = dot(held, c).astype(bf16)
                maps_ref[rows_of[i], rows_of[k]] = held

    maps, coup_t = call(
        own_maps,
        [(triple, bf16), ((layer, layer), bf16)],
        (far_green, far_coup),
        8 * layer**3,
        {0: pltpu.HBM, 1: pltpu.HBM},
        [
            pltpu.VMEM((3, 2, layer, layer), bf16),
            pltpu.VMEM((layer, layer), bf16),
            pltpu.SemaphoreType.DMA((3, 2)),
            pltpu.SemaphoreType.DMA,
        ],
    )

    def pick(start_ref, panel_ref, *outs):
        me = lax.axis_index("energy")
        for k in range(energies - 1):
            first = pl.multiple_of(start_ref[me ^ (k + 1), me] * rows, rows)
            outs[k][...] = panel_ref[pl.ds(first, span)]

    pieces = call(
        pick, [((span, width), bf16)] * (energies - 1), (block_start, panel), 0, {0: SMEM}
    )
    received = [None] * (energies - 1)
    for mask in range(energies - 1, 0, -1):
        received[mask - 1] = swapped(pieces[mask - 1], "energy", mask)

    held = green

    def fetch(green_ref, hint_ref, held_ref, sem):
        parts = [(k, pl.ds(i * layer, layer)) for k in range(2) for i in range(norb // layer)]
        copies = [
            pltpu.make_async_copy(green_ref.at[k, r], held_ref.at[k, r], sem.at[i])
            for i, (k, r) in enumerate(parts)
        ]
        for copy in copies:
            copy.start()
        for copy in copies:
            copy.wait()

    (held,) = call(
        fetch,
        [(green.shape, bf16)],
        (far_green, coup_t),
        0,
        {0: pltpu.HBM, 1: pl.ANY},
        [pltpu.SemaphoreType.DMA((2 * norb // layer,))],
    )

    half = 3 * layer // 2
    final = levels - 1
    plans, members, totals = [], None, maps
    for level in range(final):
        near = swapped(totals if level == 0 else send, "slab", 1 << level)
        far = None if level == 0 else swapped(near, "slab", 1)
        closing = level == final - 1

        def group(*refs, level=level, closing=closing):
            refs = list(refs)
            mine, near_ref = refs[:2]
            plan, member, send_ref = refs[-3:]
            total = None if closing else refs[-4]
            after = place(level)
            if level == 0:
                theirs = near_ref[...]
            else:
                first = place(0)
                a, b = near_ref[...], refs[2][...]
                theirs = jnp.concatenate(
                    [jnp.where(first, b, a), jnp.where(first, a, b)], axis=0
                )
                old = refs[3]
            own_a, own_b, own_e = (mine[rows_of[k]] for k in range(3))
            its_a, its_b, its_e = (theirs[rows_of[k]] for k in range(3))
            a_left = jnp.where(after, its_a, own_a)
            a_right = jnp.where(after, own_a, its_a)
            b_left = jnp.where(after, its_b, own_b)
            b_right = jnp.where(after, own_b, its_b)
            e_left = jnp.where(after, its_e, own_e)
            e_right = jnp.where(after, own_e, its_e)
            plan[rows_of[0]] = a_right
            plan[rows_of[1]] = e_right
            if level:
                plan[rows_of[2]] = old[rows_of[0]]
                plan[rows_of[3]] = b_left
                plan[rows_of[4]] = jnp.where(after, old[rows_of[2]], old[rows_of[1]])
            else:
                plan[rows_of[2]] = b_left

            def reflected():
                bounce = mapped(e_right, a_left).astype(bf16)
                return bounce, (e_left.astype(f32) + mapped(b_left, bounce)).astype(bf16)

            def before():
                p = old[rows_of[0]]
                return jnp.where(after, mapped(p, a_left).astype(bf16), p)

            def behind():
                q = old[rows_of[1]]
                return jnp.where(after, q, mapped(q, b_right).astype(bf16))

            def turned_round(bounce):
                q, r = old[rows_of[1]], old[rows_of[2]]
                more = mapped(jnp.where(after, r, q), jnp.where(after, a_left, bounce))
                return jnp.where(after, more, more + r.astype(f32)).astype(bf16)

            if level == 0:
                bounce, e_total = reflected()
                row = lax.broadcasted_iota(jnp.int32, one_map, 0)
                col = lax.broadcasted_iota(jnp.int32, one_map, 1)
                unit = (row == col).astype(f32).astype(bf16)
                ends = (
                    jnp.where(after, a_left, unit),
                    jnp.where(after, unit, b_right),
                    jnp.where(after, jnp.zeros_like(bounce), bounce),
                )
            elif not closing:
                bounce, e_total = reflected()
                ends = (before(), behind(), turned_round(bounce))
            if not closing:
                grown = (
                    mapped(a_right, a_left).astype(bf16),
                    mapped(b_left, b_right).astype(bf16),
                    e_total,
                )
                for k in range(3):
                    total[rows_of[k]] = grown[k]
                whole = jnp.concatenate(grown, axis=0)
                send_ref[...] = jnp.where(place(0), whole[half:], whole[:half])
                for k, end in enumerate(ends):
                    member[rows_of[k]] = end
                return

            @pl.when(place(final))
            def _():
                bounce, e_total = reflected()
                member[rows_of[0]] = before()
                member[rows_of[1]] = turned_round(bounce)
                cut = layer // 2
                send_ref[...] = jnp.where(place(0), e_total[cut:], e_total[:cut])

            @pl.when(~place(final))
            def _():
                member[rows_of[0]] = jnp.zeros(one_map, bf16)
                member[rows_of[1]] = behind()
                send_ref[...] = jnp.zeros((layer // 2, 2 * layer), bf16)

        plan_size = (5 * layer if level else 3 * layer, 2 * layer)
        args = (totals, near) if level == 0 else (totals, near, far, members)
        *grown, plan, members, send = call(
            group,
            [(triple, bf16)] * (not closing)
            + [
                (plan_size, bf16),
                ((2 * layer, 2 * layer) if closing else triple, bf16),
                ((layer // 2 if closing else half, 2 * layer), bf16),
            ],
            args,
            64 * layer**3,
        )
        totals = None if closing else grown[0]
        plans.append(plan)
    e_near = swapped(send, "slab", 1 << final)
    e_far = swapped(e_near, "slab", 1)

    ways = (slice(0, layer), slice(layer, 2 * layer))
    pair = (2 * layer, width)

    def scan(vector):
        total, sent, reach = vector, vector, None
        for level in range(final):
            other = swapped(sent, "slab", 1 << level)
            closing = level == final - 1

            def step(*refs, level=level, closing=closing):
                mine, other_ref, plan = refs[:3]
                total_ref, sent_ref, reach_ref = refs[-3:]
                after = place(level)
                own = [mine[w] for w in ways]
                its = [other_ref[w].astype(f32) for w in ways]
                c_left, c_right = jnp.where(after, its[0], own[0]), jnp.where(after, own[0], its[0])
                f_left, f_right = jnp.where(after, its[1], own[1]), jnp.where(after, own[1], its[1])
                spread = mapped(plan[: (3 if level else 2) * layer], c_left)
                back = f_right + spread[ways[1]]
                c_new = c_right + spread[ways[0]]
                f_new = f_left + mapped(plan[rows_of[3 if level else 2]], back)
                if level:
                    so_far = refs[3]
                    more = mapped(plan[rows_of[4]], jnp.where(after, c_left, back))
                    z = so_far[ways[0]] + jnp.where(after, spread[rows_of[2]], 0.0)
                    u = so_far[ways[1]] + more
                else:
                    z = jnp.where(after, c_left, jnp.zeros_like(c_left))
                    u = jnp.where(after, jnp.zeros_like(back), back)
                reach_ref[ways[0]] = z
                reach_ref[ways[1]] = u
                if closing:
                    total_ref[...] = c_new
                    sent_ref[...] = jnp.where(place(final), f_new, c_new).astype(bf16)
                else:
                    total_ref[ways[0]] = c_new
                    total_ref[ways[1]] = f_new
                    sent_ref[ways[0]] = c_new.astype(bf16)
                    sent_ref[ways[1]] = f_new.astype(bf16)

            size = (layer, width) if closing else pair
            args = (total, other, plans[level]) + ((reach,) if level else ())
            total, sent, reach = call(
                step, [(size, f32), (size, bf16), (pair, f32)], args, 40 * layer * layer * width
            )
        return total, swapped(sent, "slab", 1 << final), reach

    def prepare(inj_ref, panel_ref, start_ref, count_ref, strength_ref, acc_ref, weight_ref):
        me = lax.axis_index("energy")
        row = lax.broadcasted_iota(jnp.int32, (span, width), 0)
        acc_ref[...] = inj_ref[...].astype(f32)
        for k in range(energies):
            s = me ^ k
            weight = jnp.where(row < count_ref[me, s] * rows, strength_ref[me, s], 0.0)
            if k:
                weight_ref[k - 1] = weight
            else:
                first = pl.multiple_of(start_ref[me, me] * rows, rows)
                part = pl.ds(first, span)
                acc_ref[part] = acc_ref[part] + panel_ref[part].astype(f32) * weight

    acc, weights = call(
        prepare,
        [((norb, width), f32), ((energies - 1, span, width), f32)],
        (injection[0, 0], panel, block_start, block_count, strength),
        0,
        {2: SMEM, 3: SMEM, 4: SMEM},
    )

    def load(start_ref, acc_ref, weight_ref, held_ref, turn_ref, *refs):
        got, (source_ref, spun_ref, low_ref, sent_ref, sum_ref) = refs[:-5], refs[-5:]
        me = lax.axis_index("energy")
        sum_ref[...] = acc_ref[...]
        for k in range(1, energies):
            first = pl.multiple_of(start_ref[me, me ^ k] * rows, rows)
            part = pl.ds(first, span)
            sum_ref[part] = sum_ref[part] + got[k - 1][...].astype(f32) * weight_ref[k - 1]
        source = sum_ref[...].astype(bf16)
        spun = turned(source.astype(f32)).astype(bf16)
        source_ref[...] = source
        spun_ref[...] = spun
        direct = dot(held_ref[0, low:], source) + dot(held_ref[1, low:], spun)
        low_ref[...] = direct
        sent_ref[ways[0]] = fine(turn_ref[...], direct)
        sent_ref[ways[1]] = dot(held_ref[0, :layer], source) + dot(held_ref[1, :layer], spun)

    source, spun, direct_low, sent = call(
        load,
        [((norb, width), bf16)] * 2 + [((layer, width), f32), (pair, f32)],
        (block_start, acc, weights, held, coup_t, *received),
        8 * layer * norb * width,
        {0: SMEM},
        [pltpu.VMEM((norb, width), f32)],
    )
    c_total, arrived, reach = scan(sent)

    def direct_step(held_ref, source_ref, spun_ref, ends_ref, low_ref, out_ref):
        mid = slice(layer, low)
        out_ref[:layer] = ends_ref[ways[1]]
        out_ref[mid] = dot(held_ref[0, mid], source_ref[...]) + dot(
            held_ref[1, mid], spun_ref[...]
        )
        out_ref[low:] = low_ref[...]

    (direct,) = call(
        direct_step,
        [((norb, width), f32)],
        (held, source, spun, sent, direct_low),
        4 * (low - layer) * norb * width,
    )

    def finish(
        other_ref, c_ref, near_ref, far_ref, member, reach_ref, held_ref, coup_ref, direct_ref,
        out_ref, kept, sem,
    ):
        after, first = place(final), place(0)
        other = other_ref[...].astype(f32)
        c_left = c_ref[...]
        a, b = mapped(near_ref[...], c_left), mapped(far_ref[...], c_left)
        bounce = jnp.concatenate([jnp.where(first, b, a), jnp.where(first, a, b)], axis=0)
        back = other + jnp.where(after, jnp.zeros_like(bounce), bounce)
        more = mapped(member[ways[0]], other)
        z = reach_ref[ways[0]] + jnp.where(after, more, jnp.zeros_like(more))
        incoming = z.astype(bf16)
        spun_z = turned(incoming.astype(f32)).astype(bf16)
        u = reach_ref[ways[1]] + mapped(member[ways[1]], back)
        outgoing = fine(coup_ref[...], u).astype(bf16)
        spun_u = turned(outgoing.astype(f32)).astype(bf16)
        copies = []
        for i in range(norb // layer):
            part = pl.ds(i * layer, layer)
            kept[part] = (
                direct_ref[part]
                + dot(held_ref[0, part, :layer], incoming)
                + dot(held_ref[1, part, :layer], spun_z)
                + dot(held_ref[0, part, low:], outgoing)
                + dot(held_ref[1, part, low:], spun_u)
            ).astype(bf16)
            copy = pltpu.make_async_copy(kept.at[part], out_ref.at[part], sem.at[i])
            copy.start()
            copies.append(copy)
        for copy in copies:
            copy.wait()

    (out,) = call(
        finish,
        [((norb, width), bf16)],
        (arrived, c_total, e_near, e_far, members, reach, held, coup, direct),
        16 * norb * layer * width,
        scratch=[pltpu.VMEM((norb, width), bf16), pltpu.SemaphoreType.DMA((norb // layer,))],
        out_space=pltpu.HBM,
    )
    return out[None, None]


def solution(mesh):
    in_specs = (
        P("energy", "slab", None, None, None),
        P("energy", "slab", None, None),
        P("energy", "slab", None, None),
        P("slab", None, None),
        P(),
        P(),
        P(),
    )
    out_specs = P("energy", "slab", None, None)
    return jax.shard_map(body, mesh=mesh, in_specs=in_specs, out_specs=out_specs, check_vma=False)
```

time: 50.6 us -> 47.6 us (0.941)
  starting transfers between devices: 14.4 us -> 12.1 us
  waiting for transfers between devices: 22.9 us -> 21.7 us
    ppermute x12 -> x11, starting transfers between devices: 14.4 us -> 12.1 us  [swapped(): return lax.ppermute(block, axis, [(i, i ^ mask) for i in range(count)])]
    ppermute x12 -> x11, waiting for transfers between devices: 22.9 us -> 21.7 us  [swapped(): return lax.ppermute(block, axis, [(i, i ^ mask) for i in range(count)])]
    pallas_call x15 -> x11, Pallas kernels: 13 us -> 13.5 us  [call(): pl.pallas_call(kernel, out_shape=shapes, in_specs=specs, out_specs=[pl.Bl...]
  transfers between devices with their start and end apart: 12 -> 11, of which waited for: 10 -> 7; matrix products, arithmetic and copies ran while one was open for 0% -> 0% of each run, Pallas kernels for 14% -> 17%
where the time goes in v5:
time: 47.6 us; the launch traced here: 47.4 us
  waiting for transfers between devices  21.7 us (46%)
  Pallas kernels  13.5 us (28%)
  starting transfers between devices  12.1 us (25%)
    ppermute x11, waiting for transfers between devices, swapped(): return lax.ppermute(block, axis, [(i, i ^ mask) for i in range(count)])  21.7 us
    pallas_call x11, Pallas kernels, call(): pl.pallas_call(kernel, out_shape=shapes, in_specs=specs, out_specs=[pl.Bl...  13.5 us
    ppermute x11, starting transfers between devices, swapped(): return lax.ppermute(block, axis, [(i, i ^ mask) for i in range(count)])  12.1 us
  transfers between devices with their start and end apart: 11, of which 7 were waited for; matrix products, arithmetic and copies ran while one was open for 0% of the time, Pallas kernels for 17%

profile of v5, /device:TPU:0, one launch (start us, length us, event | category | flops | bytes accessed | tf_op | source)
XLA Modules:
  0.0 47.4 jit_solution(270394307065019747)
XLA Ops:
  0.0 2.3 %shard_map.74 = (bf16[768,512]{1,0:T(8,128)(2,1)S(1)}, bf16[256,256]{1,0:T(8,128)(2,1)S(1)}) custom-call(bf16[2,1024,1024]{2,1,0:T(8,128)(2,1)} %bitcast.10, bf16[256,256]{1,0:T(8,128)(2,1)} %bitcast.7), custom_call_target="tpu_custom_call" | custom-call | flops 134217728 | bytes 4325376 | tf_op jit(solution)/shard_map/pallas_call | solution.py:64
  2.3 0.6 %collective-permute-start.4 = (bf16[768,512]{1,0:T(8,128)(2,1)S(1)}, bf16[768,512]{1,0:T(8,128)(2,1)S(1)}, u32[]{:S(2)}, u32[]{:S(2)}) collective-permute-start(bf16[768,512]{1,0:T(8,128)(2,1)S(1)} %get-tuple-element.36.refs_0_), channel_id=1, source_target_pairs={{0,1},{1,0},{2,3},{3,2},{4,5},{5,4},{6,7},{7,6},{8,9},{9,8},{10,11... | collective-permute-start | bytes 2359304 | tf_op jit(solution)/shard_map/ppermute | solution.py:21
  2.9 1.9 %collective-permute-done.4.refs_1_ = bf16[768,512]{1,0:T(8,128)(2,1)S(1)} collective-permute-done((bf16[768,512]{1,0:T(8,128)(2,1)S(1)}, bf16[768,512]{1,0:T(8,128)(2,1)S(1)}, u32[]{:S(2)}, u32[]{:S(2)}) %collective-permute-start.4) | collective-permute-done | bytes 786464 | tf_op jit(solution)/shard_map/ppermute | solution.py:21
  4.8 0.9 %shard_map.78 = (bf16[768,512]{1,0:T(8,128)(2,1)S(1)}, bf16[768,512]{1,0:T(8,128)(2,1)S(1)}, bf16[768,512]{1,0:T(8,128)(2,1)S(1)}, bf16[384,512]{1,0:T(8,128)(2,1)S(1)}) custom-call(bf16[768,512]{1,0:T(8,128)(2,1)S(1)} %get-tuple-element.36.refs_0_, bf16[768,512]{1,0:T(8,128)(2,1)S(1)} %collective-permute-done.4.refs_1_), custom_call_target="tpu_custom_call" | custom-call | flops 1073741824 | bytes 1572864 | tf_op jit(solution)/shard_map/pallas_call | solution.py:64
  5.7 2.9 %collective-permute-start.6 = (bf16[384,512]{1,0:T(8,128)(2,1)S(1)}, bf16[384,512]{1,0:T(8,128)(2,1)S(1)}, u32[]{:S(2)}, u32[]{:S(2)}) collective-permute-start(bf16[384,512]{1,0:T(8,128)(2,1)S(1)} %get-tuple-element.41), channel_id=1, source_target_pairs={{0,2},{1,3},{2,0},{3,1},{4,6},{5,7},{6,4},{7,5},{8,10},{9,11},{10,... | collective-permute-start | bytes 1179656 | tf_op jit(solution)/shard_map/ppermute | solution.py:21
  8.6 9.4 %collective-permute-done.6.refs_1_ = bf16[384,512]{1,0:T(8,128)(2,1)S(1)} collective-permute-done((bf16[384,512]{1,0:T(8,128)(2,1)S(1)}, bf16[384,512]{1,0:T(8,128)(2,1)S(1)}, u32[]{:S(2)}, u32[]{:S(2)}) %collective-permute-start.6) | collective-permute-done | bytes 393248 | tf_op jit(solution)/shard_map/ppermute | solution.py:21
  18.1 0.6 %shard_map.76 = (bf16[256,128]{1,0:T(8,128)(2,1)S(1)}, bf16[256,128]{1,0:T(8,128)(2,1)S(1)}, bf16[256,128]{1,0:T(8,128)(2,1)S(1)}) custom-call(s32[4,4]{1,0:T(4,128)S(1)} %copy-done.3, bf16[1024,128]{1,0:T(8,128)(2,1)S(1)} %bitcast.5), custom_call_target="tpu_custom_call" | custom-call | bytes 262208 | tf_op jit(solution)/shard_map/pallas_call | solution.py:64
  18.7 1.9 %collective-permute-start = (bf16[256,128]{1,0:T(8,128)(2,1)S(1)}, bf16[256,128]{1,0:T(8,128)(2,1)S(1)}, u32[]{:S(2)}, u32[]{:S(2)}) collective-permute-start(bf16[256,128]{1,0:T(8,128)(2,1)S(1)} %get-tuple-element.32), channel_id=1, source_target_pairs={{0,8},{8,0},{16,24},{24,16},{1,9},{9,1},{17,25},{25,17},{2,10},{10... | collective-permute-start | bytes 196616 | tf_op jit(solution)/shard_map/ppermute | solution.py:21
  20.6 2.6 %collective-permute-start.1 = (bf16[256,128]{1,0:T(8,128)(2,1)S(1)}, bf16[256,128]{1,0:T(8,128)(2,1)S(1)}, u32[]{:S(2)}, u32[]{:S(2)}) collective-permute-start(bf16[256,128]{1,0:T(8,128)(2,1)S(1)} %get-tuple-element.33), channel_id=1, source_target_pairs={{0,16},{8,24},{16,0},{24,8},{1,17},{9,25},{17,1},{25,9},{2,18},{10... | collective-permute-start | bytes 196616 | tf_op jit(solution)/shard_map/ppermute | solution.py:21
  23.2 2.3 %shard_map.75.held_ref = bf16[2,1024,1024]{2,1,0:T(8,128)(2,1)S(1)} custom-call(bf16[2,1024,1024]{2,1,0:T(8,128)(2,1)} %bitcast.11, bf16[256,256]{1,0:T(8,128)(2,1)S(1)} %get-tuple-element.31.hint_ref.turn_ref), custom_call_target="tpu_custom_call" | custom-call | bytes 4325376 | tf_op jit(solution)/shard_map/pallas_call | solution.py:64
  25.5 0.7 %shard_map.73 = (f32[1024,128]{1,0:T(8,128)S(1)}, f32[3,256,128]{2,1,0:T(8,128)S(1)}) custom-call(bf16[1024,128]{1,0:T(8,128)(2,1)S(1)} %bitcast.9, bf16[1024,128]{1,0:T(8,128)(2,1)S(1)} %bitcast.6, s32[4,4]{1,0:T(4,128)S(1)} %copy-done.3, s32[4,4]{1,0:T(4,128)S(1)} %copy-done.4, f32[4,4]{1,0:T(4,128)S(1)} %copy-done.5), custom_call_target="tpu_custom_call" | custom-call | bytes 524480 | tf_op jit(solution)/shard_map/pallas_call | solution.py:64
  26.2 1.3 %collective-permute-done.1.refs_1_ = bf16[256,128]{1,0:T(8,128)(2,1)S(1)} collective-permute-done((bf16[256,128]{1,0:T(8,128)(2,1)S(1)}, bf16[256,128]{1,0:T(8,128)(2,1)S(1)}, u32[]{:S(2)}, u32[]{:S(2)}) %collective-permute-start.1) | collective-permute-done | bytes 65568 | tf_op jit(solution)/shard_map/ppermute | solution.py:21
  27.5 1.7 %collective-permute-done.2.refs_2_ = bf16[256,128]{1,0:T(8,128)(2,1)S(1)} collective-permute-done((bf16[256,128]{1,0:T(8,128)(2,1)S(1)}, bf16[256,128]{1,0:T(8,128)(2,1)S(1)}, u32[]{:S(2)}, u32[]{:S(2)}) %collective-permute-start.2) | collective-permute-done | bytes 65568 | tf_op jit(solution)/shard_map/ppermute | solution.py:21
  29.2 1.7 %shard_map.77 = (bf16[1024,128]{1,0:T(8,128)(2,1)S(1)}, bf16[1024,128]{1,0:T(8,128)(2,1)S(1)}, f32[256,128]{1,0:T(8,128)S(1)}, f32[512,128]{1,0:T(8,128)S(1)}) custom-call(s32[4,4]{1,0:T(4,128)S(1)} %copy-done.3, f32[1024,128]{1,0:T(8,128)S(1)} %get-tuple-element.29.acc_ref, f32[3,256,128]{2,1,0:T(8,128)S(1)} %get-tuple-element.30.weight_ref, ...), custom_call_target="tpu_custom_call" | custom-call | flops 268435456 | bytes 5439552 | tf_op jit(solution)/shard_map/pallas_call | solution.py:64
  31.0 0.6 %shard_map.80 = (bf16[1280,512]{1,0:T(8,128)(2,1)S(1)}, bf16[512,512]{1,0:T(8,128)(2,1)S(1)}, bf16[128,512]{1,0:T(8,128)(2,1)S(1)}) custom-call(bf16[768,512]{1,0:T(8,128)(2,1)S(1)} %get-tuple-element.40.refs_0_, bf16[384,512]{1,0:T(8,128)(2,1)S(1)} %collective-permute-done.6.refs_1_, bf16[384,512]{1,0:T(8,128)(2,1)S(1)} %collective-permute-done.7.refs_2_, ...), custom_call_target="tpu_custom_call" | custom-call | flops 1073741824 | bytes 2359296 | tf_op jit(solution)/shard_map/pallas_call | solution.py:64
  31.5 2.1 %collective-permute-start.9 = (bf16[128,512]{1,0:T(8,128)(2,1)S(1)}, bf16[128,512]{1,0:T(8,128)(2,1)S(1)}, u32[]{:S(2)}, u32[]{:S(2)}) collective-permute-start(bf16[128,512]{1,0:T(8,128)(2,1)S(1)} %get-tuple-element.47), channel_id=1, source_target_pairs={{0,4},{1,5},{2,6},{3,7},{4,0},{5,1},{6,2},{7,3},{8,12},{9,13},{10,... | collective-permute-start | bytes 393224 | tf_op jit(solution)/shard_map/ppermute | solution.py:21
  33.7 0.6 %shard_map.79 = (f32[512,128]{1,0:T(8,128)S(1)}, bf16[512,128]{1,0:T(8,128)(2,1)S(1)}, f32[512,128]{1,0:T(8,128)S(1)}) custom-call(f32[512,128]{1,0:T(8,128)S(1)} %get-tuple-element.35.refs_0_.ends_ref, f32[512,128]{1,0:T(8,128)S(1)} %collective-permute-done.3.refs_1_, bf16[768,512]{1,0:T(8,128)(2,1)S(1)} %get-tuple-element.37.refs_2_), custom_call_target="tpu_custom_call" | custom-call | flops 335544320 | bytes 1310720 | tf_op jit(solution)/shard_map/pallas_call | solution.py:64
  34.3 1.6 %collective-permute-start.5 = (bf16[512,128]{1,0:T(8,128)(2,1)S(1)}, bf16[512,128]{1,0:T(8,128)(2,1)S(1)}, u32[]{:S(2)}, u32[]{:S(2)}) collective-permute-start(bf16[512,128]{1,0:T(8,128)(2,1)S(1)} %get-tuple-element.39), channel_id=1, source_target_pairs={{0,2},{1,3},{2,0},{3,1},{4,6},{5,7},{6,4},{7,5},{8,10},{9,11},{10,... | collective-permute-start | bytes 393224 | tf_op jit(solution)/shard_map/ppermute | solution.py:21
  35.8 2.0 %collective-permute-done.9.near_ref = bf16[128,512]{1,0:T(8,128)(2,1)S(1)} collective-permute-done((bf16[128,512]{1,0:T(8,128)(2,1)S(1)}, bf16[128,512]{1,0:T(8,128)(2,1)S(1)}, u32[]{:S(2)}, u32[]{:S(2)}) %collective-permute-start.9) | collective-permute-done | bytes 131104 | tf_op jit(solution)/shard_map/ppermute | solution.py:21
  37.8 2.2 %collective-permute-done.5.refs_1_ = bf16[512,128]{1,0:T(8,128)(2,1)S(1)} collective-permute-done((bf16[512,128]{1,0:T(8,128)(2,1)S(1)}, bf16[512,128]{1,0:T(8,128)(2,1)S(1)}, u32[]{:S(2)}, u32[]{:S(2)}) %collective-permute-start.5) | collective-permute-done | bytes 131104 | tf_op jit(solution)/shard_map/ppermute | solution.py:21
  40.0 1.0 %shard_map.81 = (f32[256,128]{1,0:T(8,128)S(1)}, bf16[256,128]{1,0:T(8,128)(2,1)S(1)}, f32[512,128]{1,0:T(8,128)S(1)}) custom-call(f32[512,128]{1,0:T(8,128)S(1)} %get-tuple-element.38.refs_0_, bf16[512,128]{1,0:T(8,128)(2,1)S(1)} %collective-permute-done.5.refs_1_, bf16[1280,512]{1,0:T(8,128)(2,1)S(1)} %get-tuple-element.43.refs_2_, ...), custom_call_target="tpu_custom_call" | custom-call | flops 335544320 | bytes 1966080 | tf_op jit(solution)/shard_map/pallas_call | solution.py:64
  41.3 0.7 %shard_map.82.direct_ref = f32[1024,128]{1,0:T(8,128)S(1)} custom-call(bf16[2,1024,1024]{2,1,0:T(8,128)(2,1)S(1)} %shard_map.75.held_ref, bf16[1024,128]{1,0:T(8,128)(2,1)S(1)} %get-tuple-element.50.source_ref, bf16[1024,128]{1,0:T(8,128)(2,1)S(1)} %get-tuple-element.51.spun_ref, f32[512,128]{1,0:T(8,128)S(1)} %get-tuple-element.35.refs_0_.ends_ref, ...), custom_call_target="tpu_custom_call" | custom-call | flops 268435456 | bytes 5111808 | tf_op jit(solution)/shard_map/pallas_call | solution.py:64
  42.0 3.2 %collective-permute-done.8.other_ref = bf16[256,128]{1,0:T(8,128)(2,1)S(1)} collective-permute-done((bf16[256,128]{1,0:T(8,128)(2,1)S(1)}, bf16[256,128]{1,0:T(8,128)(2,1)S(1)}, u32[]{:S(2)}, u32[]{:S(2)}) %collective-permute-start.8) | collective-permute-done | bytes 65568 | tf_op jit(solution)/shard_map/ppermute | solution.py:21
  45.3 2.1 %shard_map.83 = bf16[1024,128]{1,0:T(8,128)(2,1)} custom-call(bf16[256,128]{1,0:T(8,128)(2,1)S(1)} %collective-permute-done.8.other_ref, f32[256,128]{1,0:T(8,128)S(1)} %get-tuple-element.46.c_ref, bf16[128,512]{1,0:T(8,128)(2,1)S(1)} %collective-permute-done.9.near_ref, bf16[128,512]{1,0:T(8,128)(2,1)S(1)} %collective-permute-done.10.far_ref, ...), custom_call_target="tpu_custom_call" | custom-call | flops 536870912 | bytes 6094848 | tf_op jit(solution)/shard_map/pallas_call | solution.py:64
  (21 shorter events, 0.5 us)
Async XLA Ops:
  0.0 18.1 %copy-start.3 = (s32[4,4]{1,0:T(4,128)S(1)}, s32[4,4]{1,0:T(4,128)}, u32[]{:S(2)}) copy-start(s32[4,4]{1,0:T(4,128)} %start_ref.5) | copy-start | bytes 196
  0.0 18.1 %copy-start = (bf16[1,1,1024,128]{3,2,1,0:T(8,128)(2,1)S(1)}, bf16[1,1,1024,128]{3,2,1,0:T(8,128)(2,1)}, u32[]{:S(2)}) copy-start(bf16[1,1,1024,128]{3,2,1,0:T(8,128)(2,1)} %param.9) | copy-start | bytes 786436
  2.3 2.5 %collective-permute-start.4 = (bf16[768,512]{1,0:T(8,128)(2,1)S(1)}, bf16[768,512]{1,0:T(8,128)(2,1)S(1)}, u32[]{:S(2)}, u32[]{:S(2)}) collective-permute-start(bf16[768,512]{1,0:T(8,128)(2,1)S(1)} %get-tuple-element.36.refs_0_), channel_id=1, source_target_pairs={{0,1},{1,0},{2,3},{3,2},{4,5},{5,4},{6,7},{7,6},{8,9},{9,8},{10,11... | collective-permute-start | bytes 2359304 | tf_op jit(solution)/shard_map/ppermute | solution.py:21
  5.7 12.3 %collective-permute-start.6 = (bf16[384,512]{1,0:T(8,128)(2,1)S(1)}, bf16[384,512]{1,0:T(8,128)(2,1)S(1)}, u32[]{:S(2)}, u32[]{:S(2)}) collective-permute-start(bf16[384,512]{1,0:T(8,128)(2,1)S(1)} %get-tuple-element.41), channel_id=1, source_target_pairs={{0,2},{1,3},{2,0},{3,1},{4,6},{5,7},{6,4},{7,5},{8,10},{9,11},{10,... | collective-permute-start | bytes 1179656 | tf_op jit(solution)/shard_map/ppermute | solution.py:21
  18.1 12.9 %collective-permute-start.7 = (bf16[384,512]{1,0:T(8,128)(2,1)S(1)}, bf16[384,512]{1,0:T(8,128)(2,1)S(1)}, u32[]{:S(2)}, u32[]{:S(2)}) collective-permute-start(bf16[384,512]{1,0:T(8,128)(2,1)S(1)} %collective-permute-done.6.refs_1_), channel_id=1, source_target_pairs={{0,1},{1,0},{2,3},{3,2},{4,5},{5,4},{6,7},{7,6},{8,9},{9,8},{10,11... | collective-permute-start | bytes 1179656 | tf_op jit(solution)/shard_map/ppermute | solution.py:21
  18.7 7.5 %collective-permute-start = (bf16[256,128]{1,0:T(8,128)(2,1)S(1)}, bf16[256,128]{1,0:T(8,128)(2,1)S(1)}, u32[]{:S(2)}, u32[]{:S(2)}) collective-permute-start(bf16[256,128]{1,0:T(8,128)(2,1)S(1)} %get-tuple-element.32), channel_id=1, source_target_pairs={{0,8},{8,0},{16,24},{24,16},{1,9},{9,1},{17,25},{25,17},{2,10},{10... | collective-permute-start | bytes 196616 | tf_op jit(solution)/shard_map/ppermute | solution.py:21
  20.6 7.0 %collective-permute-start.1 = (bf16[256,128]{1,0:T(8,128)(2,1)S(1)}, bf16[256,128]{1,0:T(8,128)(2,1)S(1)}, u32[]{:S(2)}, u32[]{:S(2)}) collective-permute-start(bf16[256,128]{1,0:T(8,128)(2,1)S(1)} %get-tuple-element.33), channel_id=1, source_target_pairs={{0,16},{8,24},{16,0},{24,8},{1,17},{9,25},{17,1},{25,9},{2,18},{10... | collective-permute-start | bytes 196616 | tf_op jit(solution)/shard_map/ppermute | solution.py:21
  23.1 6.1 %collective-permute-start.2 = (bf16[256,128]{1,0:T(8,128)(2,1)S(1)}, bf16[256,128]{1,0:T(8,128)(2,1)S(1)}, u32[]{:S(2)}, u32[]{:S(2)}) collective-permute-start(bf16[256,128]{1,0:T(8,128)(2,1)S(1)} %get-tuple-element.34), channel_id=1, source_target_pairs={{0,24},{8,16},{16,8},{24,0},{1,25},{9,17},{17,9},{25,1},{2,26},{10... | collective-permute-start | bytes 196616 | tf_op jit(solution)/shard_map/ppermute | solution.py:21
  23.1 2.3 %copy-start.2 = (bf16[1,1,1024,128]{3,2,1,0:T(8,128)(2,1)S(1)}, bf16[1,1,1024,128]{3,2,1,0:T(8,128)(2,1)}, u32[]{:S(2)}) copy-start(bf16[1,1,1024,128]{3,2,1,0:T(8,128)(2,1)} %param.8) | copy-start | bytes 786436
  23.1 2.3 %copy-start.4 = (s32[4,4]{1,0:T(4,128)S(1)}, s32[4,4]{1,0:T(4,128)}, u32[]{:S(2)}) copy-start(s32[4,4]{1,0:T(4,128)} %count_ref.1) | copy-start | bytes 196
  23.1 2.3 %copy-start.5 = (f32[4,4]{1,0:T(4,128)S(1)}, f32[4,4]{1,0:T(4,128)}, u32[]{:S(2)}) copy-start(f32[4,4]{1,0:T(4,128)} %strength_ref.1) | copy-start | bytes 196
  30.9 2.8 %collective-permute-start.3 = (f32[512,128]{1,0:T(8,128)S(1)}, f32[512,128]{1,0:T(8,128)S(1)}, u32[]{:S(2)}, u32[]{:S(2)}) collective-permute-start(f32[512,128]{1,0:T(8,128)S(1)} %get-tuple-element.35.refs_0_.ends_ref), channel_id=1, source_target_pairs={{0,1},{1,0},{2,3},{3,2},{4,5},{5,4},{6,7},{7,6},{8,9},{9,8},{10,11... | collective-permute-start | bytes 786440 | tf_op jit(solution)/shard_map/ppermute | solution.py:21
  31.5 6.3 %collective-permute-start.9 = (bf16[128,512]{1,0:T(8,128)(2,1)S(1)}, bf16[128,512]{1,0:T(8,128)(2,1)S(1)}, u32[]{:S(2)}, u32[]{:S(2)}) collective-permute-start(bf16[128,512]{1,0:T(8,128)(2,1)S(1)} %get-tuple-element.47), channel_id=1, source_target_pairs={{0,4},{1,5},{2,6},{3,7},{4,0},{5,1},{6,2},{7,3},{8,12},{9,13},{10,... | collective-permute-start | bytes 393224 | tf_op jit(solution)/shard_map/ppermute | solution.py:21
  33.7 11.6 %copy-start.1 = (bf16[1,256,256]{2,1,0:T(8,128)(2,1)S(1)}, bf16[1,256,256]{2,1,0:T(8,128)(2,1)}, u32[]{:S(2)}) copy-start(bf16[1,256,256]{2,1,0:T(8,128)(2,1)} %param.10) | copy-start | bytes 393220
  34.3 5.7 %collective-permute-start.5 = (bf16[512,128]{1,0:T(8,128)(2,1)S(1)}, bf16[512,128]{1,0:T(8,128)(2,1)S(1)}, u32[]{:S(2)}, u32[]{:S(2)}) collective-permute-start(bf16[512,128]{1,0:T(8,128)(2,1)S(1)} %get-tuple-element.39), channel_id=1, source_target_pairs={{0,2},{1,3},{2,0},{3,1},{4,6},{5,7},{6,4},{7,5},{8,10},{9,11},{10,... | collective-permute-start | bytes 393224 | tf_op jit(solution)/shard_map/ppermute | solution.py:21
  37.8 7.5 %collective-permute-start.10 = (bf16[128,512]{1,0:T(8,128)(2,1)S(1)}, bf16[128,512]{1,0:T(8,128)(2,1)S(1)}, u32[]{:S(2)}, u32[]{:S(2)}) collective-permute-start(bf16[128,512]{1,0:T(8,128)(2,1)S(1)} %collective-permute-done.9.near_ref), channel_id=1, source_target_pairs={{0,1},{1,0},{2,3},{3,2},{4,5},{5,4},{6,7},{7,6},{8,9},{9,8},{10,11... | collective-permute-start | bytes 393224 | tf_op jit(solution)/shard_map/ppermute | solution.py:21
  40.9 4.3 %collective-permute-start.8 = (bf16[256,128]{1,0:T(8,128)(2,1)S(1)}, bf16[256,128]{1,0:T(8,128)(2,1)S(1)}, u32[]{:S(2)}, u32[]{:S(2)}) collective-permute-start(bf16[256,128]{1,0:T(8,128)(2,1)S(1)} %get-tuple-element.45), channel_id=1, source_target_pairs={{0,4},{1,5},{2,6},{3,7},{4,0},{5,1},{6,2},{7,3},{8,12},{9,13},{10,... | collective-permute-start | bytes 196616 | tf_op jit(solution)/shard_map/ppermute | solution.py:21

commit v6 on v5

--- a/solution.py
+++ b/solution.py
@@ -74,6 +74,10 @@
     )(*args)
 
 
+def in_hbm(array):
+    return pltpu.with_memory_space_constraint(array, pltpu.HBM)
+
+
 def body(pivots, injection, previous, coupling, strength, block_start, block_count):
     green = pivots[0, 0]
     norb = green.shape[1]
@@ -81,9 +85,9 @@
     width = injection.shape[3]
     rows = norb // NBLK
     span = rows * CAP
-    far_green = pltpu.with_memory_space_constraint(green, pltpu.HBM)
+    far_green = in_hbm(green)
     coup = coupling[0]
-    far_coup = pltpu.with_memory_space_constraint(coup, pltpu.HBM)
+    far_coup = in_hbm(coup)
     panel = previous[0, 0]
     energies = lax.axis_size("energy")
     slabs = lax.axis_size("slab")
@@ -94,7 +98,12 @@
     rows_of = [slice(k * layer, (k + 1) * layer) for k in range(6)]
     triple, one_map = (3 * layer, 2 * layer), (layer, 2 * layer)
 
-    def own_maps(green_ref, coup_ref, maps_ref, turn_ref, corner, near, sem, sem_c):
+    def own_maps(green_ref, coup_ref, start_ref, panel_ref, *refs):
+        maps_ref, turn_ref = refs[:2]
+        pieces = refs[2 : energies + 1]
+        corner, near, table, sem, sem_c, sem_t, sem_p = refs[energies + 1 :]
+        ask = pltpu.make_async_copy(start_ref, table, sem_t)
+        ask.start()
         top, end = pl.ds(0, layer), pl.ds(low, layer)
         copies = [
             [
@@ -108,6 +117,15 @@
         for pair in copies:
             for copy in pair:
                 copy.start()
+        me = lax.axis_index("energy")
+        ask.wait()
+        picks = []
+        for k in range(energies - 1):
+            begin = pl.multiple_of(table[me ^ (k + 1), me] * rows, rows)
+            picks.append(
+                pltpu.make_async_copy(panel_ref.at[pl.ds(begin, span)], pieces[k], sem_p.at[k])
+            )
+            picks[k].start()
         first.wait()
         c = near[...]
         ct = c.astype(f32).T.astype(bf16)
@@ -121,55 +139,28 @@
                 elif i == 1:
                     held = dot(held, c).astype(bf16)
                 maps_ref[rows_of[i], rows_of[k]] = held
-
-    maps, coup_t = call(
+        for pick in picks:
+            pick.wait()
+
+    maps, coup_t, *pieces = call(
         own_maps,
-        [(triple, bf16), ((layer, layer), bf16)],
-        (far_green, far_coup),
+        [(triple, bf16), ((layer, layer), bf16)] + [((span, width), bf16)] * (energies - 1),
+        (far_green, far_coup, in_hbm(block_start), in_hbm(panel)),
         8 * layer**3,
-        {0: pltpu.HBM, 1: pltpu.HBM},
+        {k: pltpu.HBM for k in range(4)},
         [
             pltpu.VMEM((3, 2, layer, layer), bf16),
             pltpu.VMEM((layer, layer), bf16),
+            pltpu.SMEM(block_start.shape, block_start.dtype),
             pltpu.SemaphoreType.DMA((3, 2)),
             pltpu.SemaphoreType.DMA,
+            pltpu.SemaphoreType.DMA,
+            pltpu.SemaphoreType.DMA((energies - 1,)),
         ],
-    )
-
-    def pick(start_ref, panel_ref, *outs):
-        me = lax.axis_index("energy")
-        for k in range(energies - 1):
-            first = pl.multiple_of(start_ref[me ^ (k + 1), me] * rows, rows)
-            outs[k][...] = panel_ref[pl.ds(first, span)]
-
-    pieces = call(
-        pick, [((span, width), bf16)] * (energies - 1), (block_start, panel), 0, {0: SMEM}
     )
     received = [None] * (energies - 1)
     for mask in range(energies - 1, 0, -1):
         received[mask - 1] = swapped(pieces[mask - 1], "energy", mask)
-
-    held = green
-
-    def fetch(green_ref, hint_ref, held_ref, sem):
-        parts = [(k, pl.ds(i * layer, layer)) for k in range(2) for i in range(norb // layer)]
-        copies = [
-            pltpu.make_async_copy(green_ref.at[k, r], held_ref.at[k, r], sem.at[i])
-            for i, (k, r) in enumerate(parts)
-        ]
-        for copy in copies:
-            copy.start()
-        for copy in copies:
-            copy.wait()
-
-    (held,) = call(
-        fetch,
-        [(green.shape, bf16)],
-        (far_green, coup_t),
-        0,
-        {0: pltpu.HBM, 1: pl.ANY},
-        [pltpu.SemaphoreType.DMA((2 * norb // layer,))],
-    )
 
     half = 3 * layer // 2
     final = levels - 1
@@ -334,7 +325,21 @@
             )
         return total, swapped(sent, "slab", 1 << final), reach
 
-    def prepare(inj_ref, panel_ref, start_ref, count_ref, strength_ref, acc_ref, weight_ref):
+    def fetch(green_ref, held_ref, sem, spots):
+        copies = [
+            pltpu.make_async_copy(green_ref.at[k, r], held_ref.at[k, i], sem.at[i, k])
+            for i, r in enumerate(spots)
+            for k in range(2)
+        ]
+        for copy in copies:
+            copy.start()
+        return copies
+
+    def prepare(
+        green_ref, inj_ref, panel_ref, start_ref, count_ref, strength_ref,
+        ends_ref, acc_ref, weight_ref, sem,
+    ):
+        copies = fetch(green_ref, ends_ref, sem, (pl.ds(0, layer), pl.ds(low, layer)))
         me = lax.axis_index("energy")
         row = lax.broadcasted_iota(jnp.int32, (span, width), 0)
         acc_ref[...] = inj_ref[...].astype(f32)
@@ -347,16 +352,23 @@
                 first = pl.multiple_of(start_ref[me, me] * rows, rows)
                 part = pl.ds(first, span)
                 acc_ref[part] = acc_ref[part] + panel_ref[part].astype(f32) * weight
-
-    acc, weights = call(
+        for copy in copies:
+            copy.wait()
+
+    ends, acc, weights = call(
         prepare,
-        [((norb, width), f32), ((energies - 1, span, width), f32)],
-        (injection[0, 0], panel, block_start, block_count, strength),
+        [
+            ((2, 2, layer, norb), bf16),
+            ((norb, width), f32),
+            ((energies - 1, span, width), f32),
+        ],
+        (far_green, injection[0, 0], panel, block_start, block_count, strength),
         0,
-        {2: SMEM, 3: SMEM, 4: SMEM},
-    )
-
-    def load(start_ref, acc_ref, weight_ref, held_ref, turn_ref, *refs):
+        {0: pltpu.HBM, 3: SMEM, 4: SMEM, 5: SMEM},
+        [pltpu.SemaphoreType.DMA((2, 2))],
+    )
+
+    def load(start_ref, acc_ref, weight_ref, ends_ref, turn_ref, *refs):
         got, (source_ref, spun_ref, low_ref, sent_ref, sum_ref) = refs[:-5], refs[-5:]
         me = lax.axis_index("energy")
         sum_ref[...] = acc_ref[...]
@@ -368,39 +380,51 @@
         spun = turned(source.astype(f32)).astype(bf16)
         source_ref[...] = source
         spun_ref[...] = spun
-        direct = dot(held_ref[0, low:], source) + dot(held_ref[1, low:], spun)
+        direct = dot(ends_ref[0, 1], source) + dot(ends_ref[1, 1], spun)
         low_ref[...] = direct
         sent_ref[ways[0]] = fine(turn_ref[...], direct)
-        sent_ref[ways[1]] = dot(held_ref[0, :layer], source) + dot(held_ref[1, :layer], spun)
+        sent_ref[ways[1]] = dot(ends_ref[0, 0], source) + dot(ends_ref[1, 0], spun)
 
     source, spun, direct_low, sent = call(
         load,
         [((norb, width), bf16)] * 2 + [((layer, width), f32), (pair, f32)],
-        (block_start, acc, weights, held, coup_t, *received),
+        (block_start, acc, weights, ends, coup_t, *received),
         8 * layer * norb * width,
         {0: SMEM},
         [pltpu.VMEM((norb, width), f32)],
     )
     c_total, arrived, reach = scan(sent)
 
-    def direct_step(held_ref, source_ref, spun_ref, ends_ref, low_ref, out_ref):
-        mid = slice(layer, low)
-        out_ref[:layer] = ends_ref[ways[1]]
-        out_ref[mid] = dot(held_ref[0, mid], source_ref[...]) + dot(
-            held_ref[1, mid], spun_ref[...]
-        )
-        out_ref[low:] = low_ref[...]
-
-    (direct,) = call(
+    blocks = (low - layer) // layer
+
+    def fetch_mid(green_ref, hint_ref, mid_ref, sem):
+        spots = [pl.ds((i + 1) * layer, layer) for i in range(blocks)]
+        for copy in fetch(green_ref, mid_ref, sem, spots):
+            copy.wait()
+
+    (mid,) = call(
+        fetch_mid,
+        [((2, blocks, layer, norb), bf16)],
+        (far_green, direct_low),
+        0,
+        {0: pltpu.HBM, 1: pl.ANY},
+        [pltpu.SemaphoreType.DMA((blocks, 2))],
+    )
+
+    def direct_step(mid_ref, source_ref, spun_ref, out_ref):
+        for i in range(blocks):
+            out_ref[i] = dot(mid_ref[0, i], source_ref[...]) + dot(mid_ref[1, i], spun_ref[...])
+
+    (direct_mid,) = call(
         direct_step,
-        [((norb, width), f32)],
-        (held, source, spun, sent, direct_low),
+        [((blocks, layer, width), f32)],
+        (mid, source, spun),
         4 * (low - layer) * norb * width,
     )
 
     def finish(
-        other_ref, c_ref, near_ref, far_ref, member, reach_ref, held_ref, coup_ref, direct_ref,
-        out_ref, kept, sem,
+        other_ref, c_ref, near_ref, far_ref, member, reach_ref, ends_ref, mid_ref, coup_ref,
+        sent_ref, low_ref, direct_ref, out_ref, kept, sem,
     ):
         after, first = place(final), place(0)
         other = other_ref[...].astype(f32)
@@ -416,14 +440,21 @@
         outgoing = fine(coup_ref[...], u).astype(bf16)
         spun_u = turned(outgoing.astype(f32)).astype(bf16)
         copies = []
-        for i in range(norb // layer):
+        tail = slice(low, norb)
+        for i in range(blocks + 2):
+            if i == 0:
+                direct, held = sent_ref[ways[1]], [ends_ref.at[k, 0] for k in range(2)]
+            elif i > blocks:
+                direct, held = low_ref[...], [ends_ref.at[k, 1] for k in range(2)]
+            else:
+                direct, held = direct_ref[i - 1], [mid_ref.at[k, i - 1] for k in range(2)]
             part = pl.ds(i * layer, layer)
             kept[part] = (
-                direct_ref[part]
-                + dot(held_ref[0, part, :layer], incoming)
-                + dot(held_ref[1, part, :layer], spun_z)
-                + dot(held_ref[0, part, low:], outgoing)
-                + dot(held_ref[1, part, low:], spun_u)
+                direct
+                + dot(held[0][:, :layer], incoming)
+                + dot(held[1][:, :layer], spun_z)
+                + dot(held[0][:, tail], outgoing)
+                + dot(held[1][:, tail], spun_u)
             ).astype(bf16)
             copy = pltpu.make_async_copy(kept.at[part], out_ref.at[part], sem.at[i])
             copy.start()
@@ -434,7 +465,10 @@
     (out,) = call(
         finish,
         [((norb, width), bf16)],
-        (arrived, c_total, e_near, e_far, members, reach, held, coup, direct),
+        (
+            arrived, c_total, e_near, e_far, members, reach, ends, mid, coup,
+            sent, direct_low, direct_mid,
+        ),
         16 * norb * layer * width,
         scratch=[pltpu.VMEM((norb, width), bf16), pltpu.SemaphoreType.DMA((norb // layer,))],
         out_space=pltpu.HBM,

time: 47.6 us -> 46.9 us (0.985)
  waiting for transfers between devices: 21.7 us -> 21 us
    ppermute x11, waiting for transfers between devices: 21.7 us -> 21 us  [swapped(): return lax.ppermute(block, axis, [(i, i ^ mask) for i in range(count)])]
    pallas_call x11 -> x10, Pallas kernels: 13.5 us -> 13.6 us  [call(): pl.pallas_call(kernel, out_shape=shapes, in_specs=specs, out_specs=[pl.Bl...]
  transfers between devices with their start and end apart: 11 -> 11, of which waited for: 7 -> 7; matrix products, arithmetic and copies ran while one was open for 0% -> 0% of each run, Pallas kernels for 17% -> 18%
where the time goes in v6:
time: 46.9 us; the launch traced here: 46.7 us
  waiting for transfers between devices  21 us (45%)
  Pallas kernels  13.6 us (29%)
  starting transfers between devices  12 us (26%)
    ppermute x11, waiting for transfers between devices, swapped(): return lax.ppermute(block, axis, [(i, i ^ mask) for i in range(count)])  21 us
    pallas_call x10, Pallas kernels, call(): pl.pallas_call(kernel, out_shape=shapes, in_specs=specs, out_specs=[pl.Bl...  13.6 us
    ppermute x11, starting transfers between devices, swapped(): return lax.ppermute(block, axis, [(i, i ^ mask) for i in range(count)])  12 us
  transfers between devices with their start and end apart: 11, of which 7 were waited for; matrix products, arithmetic and copies ran while one was open for 0% of the time, Pallas kernels for 18%

profile of v6, /device:TPU:0, one launch (start us, length us, event | category | flops | bytes accessed | tf_op | source)
XLA Modules:
  0.0 46.7 jit_solution(15458124518122763270)
XLA Ops:
  0.0 2.3 %shard_map.74 = (bf16[768,512]{1,0:T(8,128)(2,1)S(1)}, bf16[256,256]{1,0:T(8,128)(2,1)S(1)}, bf16[256,128]{1,0:T(8,128)(2,1)S(1)}, bf16[256,128]{1,0:T(8,128)(2,1)S(1)}, bf16[256,128]{1,0:T(8,128)(2,1)S(1)}) custom-call(bf16[2,1024,1024]{2,1,0:T(8,128)(2,1)} %bitcast.10, bf16[256,256]{1,0:T(8,128)(2,1)} %bitcast.7, s32[4,4]{1,0:T(4,128)} %start_ref.5, ...), custom_call_target="tpu_custom_call" | custom-call | flops 134217728 | bytes 4587584 | tf_op jit(solution)/shard_map/pallas_call | solution.py:64
  2.4 0.6 %collective-permute-start.4 = (bf16[768,512]{1,0:T(8,128)(2,1)S(1)}, bf16[768,512]{1,0:T(8,128)(2,1)S(1)}, u32[]{:S(2)}, u32[]{:S(2)}) collective-permute-start(bf16[768,512]{1,0:T(8,128)(2,1)S(1)} %get-tuple-element.38.refs_0_), channel_id=1, source_target_pairs={{0,1},{1,0},{2,3},{3,2},{4,5},{5,4},{6,7},{7,6},{8,9},{9,8},{10,11... | collective-permute-start | bytes 2359304 | tf_op jit(solution)/shard_map/ppermute | solution.py:21
  2.9 1.9 %collective-permute-done.4.refs_1_ = bf16[768,512]{1,0:T(8,128)(2,1)S(1)} collective-permute-done((bf16[768,512]{1,0:T(8,128)(2,1)S(1)}, bf16[768,512]{1,0:T(8,128)(2,1)S(1)}, u32[]{:S(2)}, u32[]{:S(2)}) %collective-permute-start.4) | collective-permute-done | bytes 786464 | tf_op jit(solution)/shard_map/ppermute | solution.py:21
  4.8 0.9 %shard_map.76 = (bf16[768,512]{1,0:T(8,128)(2,1)S(1)}, bf16[768,512]{1,0:T(8,128)(2,1)S(1)}, bf16[768,512]{1,0:T(8,128)(2,1)S(1)}, bf16[384,512]{1,0:T(8,128)(2,1)S(1)}) custom-call(bf16[768,512]{1,0:T(8,128)(2,1)S(1)} %get-tuple-element.38.refs_0_, bf16[768,512]{1,0:T(8,128)(2,1)S(1)} %collective-permute-done.4.refs_1_), custom_call_target="tpu_custom_call" | custom-call | flops 1073741824 | bytes 1572864 | tf_op jit(solution)/shard_map/pallas_call | solution.py:64
  5.8 2.9 %collective-permute-start.6 = (bf16[384,512]{1,0:T(8,128)(2,1)S(1)}, bf16[384,512]{1,0:T(8,128)(2,1)S(1)}, u32[]{:S(2)}, u32[]{:S(2)}) collective-permute-start(bf16[384,512]{1,0:T(8,128)(2,1)S(1)} %get-tuple-element.43), channel_id=1, source_target_pairs={{0,2},{1,3},{2,0},{3,1},{4,6},{5,7},{6,4},{7,5},{8,10},{9,11},{10,... | collective-permute-start | bytes 1179656 | tf_op jit(solution)/shard_map/ppermute | solution.py:21
  8.7 9.4 %collective-permute-done.6.refs_1_ = bf16[384,512]{1,0:T(8,128)(2,1)S(1)} collective-permute-done((bf16[384,512]{1,0:T(8,128)(2,1)S(1)}, bf16[384,512]{1,0:T(8,128)(2,1)S(1)}, u32[]{:S(2)}, u32[]{:S(2)}) %collective-permute-start.6) | collective-permute-done | bytes 393248 | tf_op jit(solution)/shard_map/ppermute | solution.py:21
  18.1 1.8 %collective-permute-start = (bf16[256,128]{1,0:T(8,128)(2,1)S(1)}, bf16[256,128]{1,0:T(8,128)(2,1)S(1)}, u32[]{:S(2)}, u32[]{:S(2)}) collective-permute-start(bf16[256,128]{1,0:T(8,128)(2,1)S(1)} %get-tuple-element.34), channel_id=1, source_target_pairs={{0,8},{8,0},{16,24},{24,16},{1,9},{9,1},{17,25},{25,17},{2,10},{10... | collective-permute-start | bytes 196616 | tf_op jit(solution)/shard_map/ppermute | solution.py:21
  19.9 2.6 %collective-permute-start.1 = (bf16[256,128]{1,0:T(8,128)(2,1)S(1)}, bf16[256,128]{1,0:T(8,128)(2,1)S(1)}, u32[]{:S(2)}, u32[]{:S(2)}) collective-permute-start(bf16[256,128]{1,0:T(8,128)(2,1)S(1)} %get-tuple-element.35), channel_id=1, source_target_pairs={{0,16},{8,24},{16,0},{24,8},{1,17},{9,25},{17,1},{25,9},{2,18},{10... | collective-permute-start | bytes 196616 | tf_op jit(solution)/shard_map/ppermute | solution.py:21
  22.6 2.2 %shard_map.73 = (bf16[2,2,256,1024]{3,2,1,0:T(8,128)(2,1)S(1)}, f32[1024,128]{1,0:T(8,128)S(1)}, f32[3,256,128]{2,1,0:T(8,128)S(1)}) custom-call(bf16[2,1024,1024]{2,1,0:T(8,128)(2,1)} %bitcast.11, bf16[1024,128]{1,0:T(8,128)(2,1)S(1)} %bitcast.9, bf16[1024,128]{1,0:T(8,128)(2,1)S(1)} %bitcast.6, s32[4,4]{1,0:T(4,128)S(1)} %copy-done.3, ...), custom_call_target="tpu_custom_call" | custom-call | bytes 4718784 | tf_op jit(solution)/shard_map/pallas_call | solution.py:64
  24.8 2.2 %collective-permute-done.1.refs_1_ = bf16[256,128]{1,0:T(8,128)(2,1)S(1)} collective-permute-done((bf16[256,128]{1,0:T(8,128)(2,1)S(1)}, bf16[256,128]{1,0:T(8,128)(2,1)S(1)}, u32[]{:S(2)}, u32[]{:S(2)}) %collective-permute-start.1) | collective-permute-done | bytes 65568 | tf_op jit(solution)/shard_map/ppermute | solution.py:21
  26.9 1.7 %collective-permute-done.2.refs_2_ = bf16[256,128]{1,0:T(8,128)(2,1)S(1)} collective-permute-done((bf16[256,128]{1,0:T(8,128)(2,1)S(1)}, bf16[256,128]{1,0:T(8,128)(2,1)S(1)}, u32[]{:S(2)}, u32[]{:S(2)}) %collective-permute-start.2) | collective-permute-done | bytes 65568 | tf_op jit(solution)/shard_map/ppermute | solution.py:21
  28.6 1.7 %shard_map.75 = (bf16[1024,128]{1,0:T(8,128)(2,1)S(1)}, bf16[1024,128]{1,0:T(8,128)(2,1)S(1)}, f32[256,128]{1,0:T(8,128)S(1)}, f32[512,128]{1,0:T(8,128)S(1)}) custom-call(s32[4,4]{1,0:T(4,128)S(1)} %copy-done.3, f32[1024,128]{1,0:T(8,128)S(1)} %get-tuple-element.30.acc_ref, f32[3,256,128]{2,1,0:T(8,128)S(1)} %get-tuple-element.31.weight_ref, ...), custom_call_target="tpu_custom_call" | custom-call | flops 268435456 | bytes 3342400 | tf_op jit(solution)/shard_map/pallas_call | solution.py:64
  30.3 0.6 %shard_map.78 = (bf16[1280,512]{1,0:T(8,128)(2,1)S(1)}, bf16[512,512]{1,0:T(8,128)(2,1)S(1)}, bf16[128,512]{1,0:T(8,128)(2,1)S(1)}) custom-call(bf16[768,512]{1,0:T(8,128)(2,1)S(1)} %get-tuple-element.42.refs_0_, bf16[384,512]{1,0:T(8,128)(2,1)S(1)} %collective-permute-done.6.refs_1_, bf16[384,512]{1,0:T(8,128)(2,1)S(1)} %collective-permute-done.7.refs_2_, ...), custom_call_target="tpu_custom_call" | custom-call | flops 1073741824 | bytes 2359296 | tf_op jit(solution)/shard_map/pallas_call | solution.py:64
  30.9 2.1 %collective-permute-start.9 = (bf16[128,512]{1,0:T(8,128)(2,1)S(1)}, bf16[128,512]{1,0:T(8,128)(2,1)S(1)}, u32[]{:S(2)}, u32[]{:S(2)}) collective-permute-start(bf16[128,512]{1,0:T(8,128)(2,1)S(1)} %get-tuple-element.49), channel_id=1, source_target_pairs={{0,4},{1,5},{2,6},{3,7},{4,0},{5,1},{6,2},{7,3},{8,12},{9,13},{10,... | collective-permute-start | bytes 393224 | tf_op jit(solution)/shard_map/ppermute | solution.py:21
  33.0 0.6 %shard_map.77 = (f32[512,128]{1,0:T(8,128)S(1)}, bf16[512,128]{1,0:T(8,128)(2,1)S(1)}, f32[512,128]{1,0:T(8,128)S(1)}) custom-call(f32[512,128]{1,0:T(8,128)S(1)} %get-tuple-element.37.refs_0_.sent_ref, f32[512,128]{1,0:T(8,128)S(1)} %collective-permute-done.3.refs_1_, bf16[768,512]{1,0:T(8,128)(2,1)S(1)} %get-tuple-element.39.refs_2_), custom_call_target="tpu_custom_call" | custom-call | flops 335544320 | bytes 1310720 | tf_op jit(solution)/shard_map/pallas_call | solution.py:64
  33.6 1.6 %collective-permute-start.5 = (bf16[512,128]{1,0:T(8,128)(2,1)S(1)}, bf16[512,128]{1,0:T(8,128)(2,1)S(1)}, u32[]{:S(2)}, u32[]{:S(2)}) collective-permute-start(bf16[512,128]{1,0:T(8,128)(2,1)S(1)} %get-tuple-element.41), channel_id=1, source_target_pairs={{0,2},{1,3},{2,0},{3,1},{4,6},{5,7},{6,4},{7,5},{8,10},{9,11},{10,... | collective-permute-start | bytes 393224 | tf_op jit(solution)/shard_map/ppermute | solution.py:21
  35.2 2.0 %collective-permute-done.9.near_ref = bf16[128,512]{1,0:T(8,128)(2,1)S(1)} collective-permute-done((bf16[128,512]{1,0:T(8,128)(2,1)S(1)}, bf16[128,512]{1,0:T(8,128)(2,1)S(1)}, u32[]{:S(2)}, u32[]{:S(2)}) %collective-permute-start.9) | collective-permute-done | bytes 131104 | tf_op jit(solution)/shard_map/ppermute | solution.py:21
  37.2 2.1 %collective-permute-done.5.refs_1_ = bf16[512,128]{1,0:T(8,128)(2,1)S(1)} collective-permute-done((bf16[512,128]{1,0:T(8,128)(2,1)S(1)}, bf16[512,128]{1,0:T(8,128)(2,1)S(1)}, u32[]{:S(2)}, u32[]{:S(2)}) %collective-permute-start.5) | collective-permute-done | bytes 131104 | tf_op jit(solution)/shard_map/ppermute | solution.py:21
  39.3 1.0 %shard_map.79 = (f32[256,128]{1,0:T(8,128)S(1)}, bf16[256,128]{1,0:T(8,128)(2,1)S(1)}, f32[512,128]{1,0:T(8,128)S(1)}) custom-call(f32[512,128]{1,0:T(8,128)S(1)} %get-tuple-element.40.refs_0_, bf16[512,128]{1,0:T(8,128)(2,1)S(1)} %collective-permute-done.5.refs_1_, bf16[1280,512]{1,0:T(8,128)(2,1)S(1)} %get-tuple-element.45.refs_2_, ...), custom_call_target="tpu_custom_call" | custom-call | flops 335544320 | bytes 1966080 | tf_op jit(solution)/shard_map/pallas_call | solution.py:64
  40.3 0.4 collective-permute-start.8
  40.7 1.5 %shard_map.80.mid_ref = bf16[2,2,256,1024]{3,2,1,0:T(8,128)(2,1)S(1)} custom-call(bf16[2,1024,1024]{2,1,0:T(8,128)(2,1)} %bitcast.12, f32[256,128]{1,0:T(8,128)S(1)} %get-tuple-element.52.hint_ref.low_ref), custom_call_target="tpu_custom_call" | custom-call | bytes 4325376 | tf_op jit(solution)/shard_map/pallas_call | solution.py:64
  42.2 0.7 %shard_map.81.direct_ref = f32[2,256,128]{2,1,0:T(8,128)S(1)} custom-call(bf16[2,2,256,1024]{3,2,1,0:T(8,128)(2,1)S(1)} %shard_map.80.mid_ref, bf16[1024,128]{1,0:T(8,128)(2,1)S(1)} %get-tuple-element.53.source_ref, bf16[1024,128]{1,0:T(8,128)(2,1)S(1)} %get-tuple-element.54.spun_ref), custom_call_target="tpu_custom_call" | custom-call | flops 268435456 | bytes 2621440 | tf_op jit(solution)/shard_map/pallas_call | solution.py:64
  42.9 1.7 %collective-permute-done.8.other_ref = bf16[256,128]{1,0:T(8,128)(2,1)S(1)} collective-permute-done((bf16[256,128]{1,0:T(8,128)(2,1)S(1)}, bf16[256,128]{1,0:T(8,128)(2,1)S(1)}, u32[]{:S(2)}, u32[]{:S(2)}) %collective-permute-start.8) | collective-permute-done | bytes 65568 | tf_op jit(solution)/shard_map/ppermute | solution.py:21
  44.6 2.1 %shard_map.82 = bf16[1024,128]{1,0:T(8,128)(2,1)} custom-call(bf16[256,128]{1,0:T(8,128)(2,1)S(1)} %collective-permute-done.8.other_ref, f32[256,128]{1,0:T(8,128)S(1)} %get-tuple-element.48.c_ref, bf16[128,512]{1,0:T(8,128)(2,1)S(1)} %collective-permute-done.9.near_ref, bf16[128,512]{1,0:T(8,128)(2,1)S(1)} %collective-permute-done.10.far_ref, ...), custom_call_target="tpu_custom_call" | custom-call | flops 536870912 | bytes 6225920 | tf_op jit(solution)/shard_map/pallas_call | solution.py:64
  (20 shorter events, 0.1 us)
Async XLA Ops:
  2.3 20.2 %copy-start = (bf16[1,1,1024,128]{3,2,1,0:T(8,128)(2,1)S(1)}, bf16[1,1,1024,128]{3,2,1,0:T(8,128)(2,1)}, u32[]{:S(2)}) copy-start(bf16[1,1,1024,128]{3,2,1,0:T(8,128)(2,1)} %param.9) | copy-start | bytes 786436
  2.3 20.2 %copy-start.2 = (bf16[1,1,1024,128]{3,2,1,0:T(8,128)(2,1)S(1)}, bf16[1,1,1024,128]{3,2,1,0:T(8,128)(2,1)}, u32[]{:S(2)}) copy-start(bf16[1,1,1024,128]{3,2,1,0:T(8,128)(2,1)} %param.8) | copy-start | bytes 786436
  2.3 20.2 %copy-start.3 = (s32[4,4]{1,0:T(4,128)S(1)}, s32[4,4]{1,0:T(4,128)}, u32[]{:S(2)}) copy-start(s32[4,4]{1,0:T(4,128)} %start_ref.5) | copy-start | bytes 196
  2.3 20.2 %copy-start.4 = (s32[4,4]{1,0:T(4,128)S(1)}, s32[4,4]{1,0:T(4,128)}, u32[]{:S(2)}) copy-start(s32[4,4]{1,0:T(4,128)} %count_ref.1) | copy-start | bytes 196
  2.4 20.2 %copy-start.5 = (f32[4,4]{1,0:T(4,128)S(1)}, f32[4,4]{1,0:T(4,128)}, u32[]{:S(2)}) copy-start(f32[4,4]{1,0:T(4,128)} %strength_ref.1) | copy-start | bytes 196
  2.4 2.5 %collective-permute-start.4 = (bf16[768,512]{1,0:T(8,128)(2,1)S(1)}, bf16[768,512]{1,0:T(8,128)(2,1)S(1)}, u32[]{:S(2)}, u32[]{:S(2)}) collective-permute-start(bf16[768,512]{1,0:T(8,128)(2,1)S(1)} %get-tuple-element.38.refs_0_), channel_id=1, source_target_pairs={{0,1},{1,0},{2,3},{3,2},{4,5},{5,4},{6,7},{7,6},{8,9},{9,8},{10,11... | collective-permute-start | bytes 2359304 | tf_op jit(solution)/shard_map/ppermute | solution.py:21
  5.8 12.3 %collective-permute-start.6 = (bf16[384,512]{1,0:T(8,128)(2,1)S(1)}, bf16[384,512]{1,0:T(8,128)(2,1)S(1)}, u32[]{:S(2)}, u32[]{:S(2)}) collective-permute-start(bf16[384,512]{1,0:T(8,128)(2,1)S(1)} %get-tuple-element.43), channel_id=1, source_target_pairs={{0,2},{1,3},{2,0},{3,1},{4,6},{5,7},{6,4},{7,5},{8,10},{9,11},{10,... | collective-permute-start | bytes 1179656 | tf_op jit(solution)/shard_map/ppermute | solution.py:21
  18.1 12.2 %collective-permute-start.7 = (bf16[384,512]{1,0:T(8,128)(2,1)S(1)}, bf16[384,512]{1,0:T(8,128)(2,1)S(1)}, u32[]{:S(2)}, u32[]{:S(2)}) collective-permute-start(bf16[384,512]{1,0:T(8,128)(2,1)S(1)} %collective-permute-done.6.refs_1_), channel_id=1, source_target_pairs={{0,1},{1,0},{2,3},{3,2},{4,5},{5,4},{6,7},{7,6},{8,9},{9,8},{10,11... | collective-permute-start | bytes 1179656 | tf_op jit(solution)/shard_map/ppermute | solution.py:21
  18.1 6.6 %collective-permute-start = (bf16[256,128]{1,0:T(8,128)(2,1)S(1)}, bf16[256,128]{1,0:T(8,128)(2,1)S(1)}, u32[]{:S(2)}, u32[]{:S(2)}) collective-permute-start(bf16[256,128]{1,0:T(8,128)(2,1)S(1)} %get-tuple-element.34), channel_id=1, source_target_pairs={{0,8},{8,0},{16,24},{24,16},{1,9},{9,1},{17,25},{25,17},{2,10},{10... | collective-permute-start | bytes 196616 | tf_op jit(solution)/shard_map/ppermute | solution.py:21
  19.9 7.0 %collective-permute-start.1 = (bf16[256,128]{1,0:T(8,128)(2,1)S(1)}, bf16[256,128]{1,0:T(8,128)(2,1)S(1)}, u32[]{:S(2)}, u32[]{:S(2)}) collective-permute-start(bf16[256,128]{1,0:T(8,128)(2,1)S(1)} %get-tuple-element.35), channel_id=1, source_target_pairs={{0,16},{8,24},{16,0},{24,8},{1,17},{9,25},{17,1},{25,9},{2,18},{10... | collective-permute-start | bytes 196616 | tf_op jit(solution)/shard_map/ppermute | solution.py:21
  22.5 6.1 %collective-permute-start.2 = (bf16[256,128]{1,0:T(8,128)(2,1)S(1)}, bf16[256,128]{1,0:T(8,128)(2,1)S(1)}, u32[]{:S(2)}, u32[]{:S(2)}) collective-permute-start(bf16[256,128]{1,0:T(8,128)(2,1)S(1)} %get-tuple-element.36), channel_id=1, source_target_pairs={{0,24},{8,16},{16,8},{24,0},{1,25},{9,17},{17,9},{25,1},{2,26},{10... | collective-permute-start | bytes 196616 | tf_op jit(solution)/shard_map/ppermute | solution.py:21
  30.2 2.8 %collective-permute-start.3 = (f32[512,128]{1,0:T(8,128)S(1)}, f32[512,128]{1,0:T(8,128)S(1)}, u32[]{:S(2)}, u32[]{:S(2)}) collective-permute-start(f32[512,128]{1,0:T(8,128)S(1)} %get-tuple-element.37.refs_0_.sent_ref), channel_id=1, source_target_pairs={{0,1},{1,0},{2,3},{3,2},{4,5},{5,4},{6,7},{7,6},{8,9},{9,8},{10,11... | collective-permute-start | bytes 786440 | tf_op jit(solution)/shard_map/ppermute | solution.py:21
  30.9 6.3 %collective-permute-start.9 = (bf16[128,512]{1,0:T(8,128)(2,1)S(1)}, bf16[128,512]{1,0:T(8,128)(2,1)S(1)}, u32[]{:S(2)}, u32[]{:S(2)}) collective-permute-start(bf16[128,512]{1,0:T(8,128)(2,1)S(1)} %get-tuple-element.49), channel_id=1, source_target_pairs={{0,4},{1,5},{2,6},{3,7},{4,0},{5,1},{6,2},{7,3},{8,12},{9,13},{10,... | collective-permute-start | bytes 393224 | tf_op jit(solution)/shard_map/ppermute | solution.py:21
  33.6 5.7 %collective-permute-start.5 = (bf16[512,128]{1,0:T(8,128)(2,1)S(1)}, bf16[512,128]{1,0:T(8,128)(2,1)S(1)}, u32[]{:S(2)}, u32[]{:S(2)}) collective-permute-start(bf16[512,128]{1,0:T(8,128)(2,1)S(1)} %get-tuple-element.41), channel_id=1, source_target_pairs={{0,2},{1,3},{2,0},{3,1},{4,6},{5,7},{6,4},{7,5},{8,10},{9,11},{10,... | collective-permute-start | bytes 393224 | tf_op jit(solution)/shard_map/ppermute | solution.py:21
  37.2 7.5 %collective-permute-start.10 = (bf16[128,512]{1,0:T(8,128)(2,1)S(1)}, bf16[128,512]{1,0:T(8,128)(2,1)S(1)}, u32[]{:S(2)}, u32[]{:S(2)}) collective-permute-start(bf16[128,512]{1,0:T(8,128)(2,1)S(1)} %collective-permute-done.9.near_ref), channel_id=1, source_target_pairs={{0,1},{1,0},{2,3},{3,2},{4,5},{5,4},{6,7},{7,6},{8,9},{9,8},{10,11... | collective-permute-start | bytes 393224 | tf_op jit(solution)/shard_map/ppermute | solution.py:21
  40.3 4.3 %collective-permute-start.8 = (bf16[256,128]{1,0:T(8,128)(2,1)S(1)}, bf16[256,128]{1,0:T(8,128)(2,1)S(1)}, u32[]{:S(2)}, u32[]{:S(2)}) collective-permute-start(bf16[256,128]{1,0:T(8,128)(2,1)S(1)} %get-tuple-element.47), channel_id=1, source_target_pairs={{0,4},{1,5},{2,6},{3,7},{4,0},{5,1},{6,2},{7,3},{8,12},{9,13},{10,... | collective-permute-start | bytes 196616 | tf_op jit(solution)/shard_map/ppermute | solution.py:21
  42.2 2.4 %copy-start.1 = (bf16[1,256,256]{2,1,0:T(8,128)(2,1)S(1)}, bf16[1,256,256]{2,1,0:T(8,128)(2,1)}, u32[]{:S(2)}) copy-start(bf16[1,256,256]{2,1,0:T(8,128)(2,1)} %param.10) | copy-start | bytes 393220

commit v7 on v6

--- a/solution.py
+++ b/solution.py
@@ -47,6 +47,19 @@
 def fine(real, v):
     high = v.astype(bf16)
     return dot(real, high) + dot(real, (v - high.astype(f32)).astype(bf16))
+
+
+def member_before(after, p, a_left):
+    return jnp.where(after, mapped(p, a_left).astype(bf16), p)
+
+
+def member_behind(after, q, b_right):
+    return jnp.where(after, q, mapped(q, b_right).astype(bf16))
+
+
+def member_turned(after, q, r, a_left, bounce):
+    more = mapped(jnp.where(after, r, q), jnp.where(after, a_left, bounce))
+    return jnp.where(after, more, more + r.astype(f32)).astype(bf16)
 
 
 def place(k):
@@ -101,9 +114,10 @@
     def own_maps(green_ref, coup_ref, start_ref, panel_ref, *refs):
         maps_ref, turn_ref = refs[:2]
         pieces = refs[2 : energies + 1]
-        corner, near, table, sem, sem_c, sem_t, sem_p = refs[energies + 1 :]
+        corner, near, whole, table, sem, sem_c, sem_t, sem_p = refs[energies + 1 :]
         ask = pltpu.make_async_copy(start_ref, table, sem_t)
-        ask.start()
+        panel_copy = pltpu.make_async_copy(panel_ref, whole, sem_p)
+        first = pltpu.make_async_copy(coup_ref, near, sem_c)
         top, end = pl.ds(0, layer), pl.ds(low, layer)
         copies = [
             [
@@ -112,24 +126,22 @@
             ]
             for i, (r, c) in enumerate(((end, top), (top, end), (top, top)))
         ]
-        first = pltpu.make_async_copy(coup_ref, near, sem_c)
+        ask.start()
         first.start()
+        panel_copy.start()
         for pair in copies:
             for copy in pair:
                 copy.start()
         me = lax.axis_index("energy")
-        ask.wait()
-        picks = []
-        for k in range(energies - 1):
-            begin = pl.multiple_of(table[me ^ (k + 1), me] * rows, rows)
-            picks.append(
-                pltpu.make_async_copy(panel_ref.at[pl.ds(begin, span)], pieces[k], sem_p.at[k])
-            )
-            picks[k].start()
         first.wait()
         c = near[...]
         ct = c.astype(f32).T.astype(bf16)
         turn_ref[...] = ct
+        panel_copy.wait()
+        ask.wait()
+        for k in range(energies - 1):
+            begin = pl.multiple_of(table[me ^ (k + 1), me] * rows, rows)
+            pieces[k][...] = whole[pl.ds(begin, span)]
         for i in range(3):
             for k in range(2):
                 copies[i][k].wait()
@@ -139,8 +151,6 @@
                 elif i == 1:
                     held = dot(held, c).astype(bf16)
                 maps_ref[rows_of[i], rows_of[k]] = held
-        for pick in picks:
-            pick.wait()
 
     maps, coup_t, *pieces = call(
         own_maps,
@@ -151,11 +161,12 @@
         [
             pltpu.VMEM((3, 2, layer, layer), bf16),
             pltpu.VMEM((layer, layer), bf16),
+            pltpu.VMEM(panel.shape, bf16),
             pltpu.SMEM(block_start.shape, block_start.dtype),
             pltpu.SemaphoreType.DMA((3, 2)),
             pltpu.SemaphoreType.DMA,
             pltpu.SemaphoreType.DMA,
-            pltpu.SemaphoreType.DMA((energies - 1,)),
+            pltpu.SemaphoreType.DMA,
         ],
     )
     received = [None] * (energies - 1)
@@ -206,19 +217,6 @@
                 bounce = mapped(e_right, a_left).astype(bf16)
                 return bounce, (e_left.astype(f32) + mapped(b_left, bounce)).astype(bf16)
 
-            def before():
-                p = old[rows_of[0]]
-                return jnp.where(after, mapped(p, a_left).astype(bf16), p)
-
-            def behind():
-                q = old[rows_of[1]]
-                return jnp.where(after, q, mapped(q, b_right).astype(bf16))
-
-            def turned_round(bounce):
-                q, r = old[rows_of[1]], old[rows_of[2]]
-                more = mapped(jnp.where(after, r, q), jnp.where(after, a_left, bounce))
-                return jnp.where(after, more, more + r.astype(f32)).astype(bf16)
-
             if level == 0:
                 bounce, e_total = reflected()
                 row = lax.broadcasted_iota(jnp.int32, one_map, 0)
@@ -231,7 +229,12 @@
                 )
             elif not closing:
                 bounce, e_total = reflected()
-                ends = (before(), behind(), turned_round(bounce))
+                q, r = old[rows_of[1]], old[rows_of[2]]
+                ends = (
+                    member_before(after, old[rows_of[0]], a_left),
+                    member_behind(after, q, b_right),
+                    member_turned(after, q, r, a_left, bounce),
+                )
             if not closing:
                 grown = (
                     mapped(a_right, a_left).astype(bf16),
@@ -249,34 +252,62 @@
             @pl.when(place(final))
             def _():
                 bounce, e_total = reflected()
-                member[rows_of[0]] = before()
-                member[rows_of[1]] = turned_round(bounce)
+                member[...] = bounce
                 cut = layer // 2
                 send_ref[...] = jnp.where(place(0), e_total[cut:], e_total[:cut])
 
             @pl.when(~place(final))
             def _():
-                member[rows_of[0]] = jnp.zeros(one_map, bf16)
-                member[rows_of[1]] = behind()
+                member[...] = jnp.zeros(one_map, bf16)
                 send_ref[...] = jnp.zeros((layer // 2, 2 * layer), bf16)
 
         plan_size = (5 * layer if level else 3 * layer, 2 * layer)
         args = (totals, near) if level == 0 else (totals, near, far, members)
-        *grown, plan, members, send = call(
+        *grown, plan, member, send = call(
             group,
             [(triple, bf16)] * (not closing)
             + [
                 (plan_size, bf16),
-                ((2 * layer, 2 * layer) if closing else triple, bf16),
+                (one_map if closing else triple, bf16),
                 ((layer // 2 if closing else half, 2 * layer), bf16),
             ],
             args,
             64 * layer**3,
         )
-        totals = None if closing else grown[0]
         plans.append(plan)
+        if not closing:
+            totals, members = grown[0], member
+
+    def last_ends(mine, near_ref, far_ref, old, bounce_ref, hint_ref, out_ref):
+        after, first = place(final - 1), place(0)
+
+        @pl.when(place(final))
+        def _():
+            its_a = jnp.where(first, far_ref[:layer], near_ref[:layer])
+            a_left = jnp.where(after, its_a, mine[rows_of[0]])
+            out_ref[rows_of[0]] = member_before(after, old[rows_of[0]], a_left)
+            out_ref[rows_of[1]] = member_turned(
+                after, old[rows_of[1]], old[rows_of[2]], a_left, bounce_ref[...]
+            )
+
+        @pl.when(~place(final))
+        def _():
+            a, b = near_ref[...], far_ref[...]
+            theirs = jnp.concatenate([jnp.where(first, b, a), jnp.where(first, a, b)], axis=0)
+            b_right = jnp.where(after, mine[rows_of[1]], theirs[rows_of[1]])
+            out_ref[rows_of[0]] = jnp.zeros(one_map, bf16)
+            out_ref[rows_of[1]] = member_behind(after, old[rows_of[1]], b_right)
+
     e_near = swapped(send, "slab", 1 << final)
     e_far = swapped(e_near, "slab", 1)
+
+    (ends_last,) = call(
+        last_ends,
+        [((2 * layer, 2 * layer), bf16)],
+        (totals, near, far, members, member, send),
+        64 * layer**3,
+        {5: pl.ANY},
+    )
 
     ways = (slice(0, layer), slice(layer, 2 * layer))
     pair = (2 * layer, width)
@@ -466,7 +497,7 @@
         finish,
         [((norb, width), bf16)],
         (
-            arrived, c_total, e_near, e_far, members, reach, ends, mid, coup,
+            arrived, c_total, e_near, e_far, ends_last, reach, ends, mid, coup,
             sent, direct_low, direct_mid,
         ),
         16 * norb * layer * width,

time: 46.9 us -> 47.8 us (1.019)
  waiting for transfers between devices: 21 us -> 21.7 us
    ppermute x11, waiting for transfers between devices: 21 us -> 21.7 us  [swapped(): return lax.ppermute(block, axis, [(i, i ^ mask) for i in range(count)])]
    pallas_call x10 -> x11, Pallas kernels: 13.6 us -> 13.6 us  [call(): pl.pallas_call(kernel, out_shape=shapes, in_specs=specs, out_specs=[pl.Bl...]
  transfers between devices with their start and end apart: 11 -> 11, of which waited for: 7 -> 7; matrix products, arithmetic and copies ran while one was open for 0% -> 0% of each run, Pallas kernels for 18% -> 17%
where the time goes in v7:
time: 47.8 us; the launch traced here: 47.6 us
  waiting for transfers between devices  21.7 us (45%)
  Pallas kernels  13.6 us (28%)
  starting transfers between devices  12.1 us (25%)
    ppermute x11, waiting for transfers between devices, swapped(): return lax.ppermute(block, axis, [(i, i ^ mask) for i in range(count)])  21.7 us
    pallas_call x11, Pallas kernels, call(): pl.pallas_call(kernel, out_shape=shapes, in_specs=specs, out_specs=[pl.Bl...  13.6 us
    ppermute x11, starting transfers between devices, swapped(): return lax.ppermute(block, axis, [(i, i ^ mask) for i in range(count)])  12.1 us
  transfers between devices with their start and end apart: 11, of which 7 were waited for; matrix products, arithmetic and copies ran while one was open for 0% of the time, Pallas kernels for 17%

profile of v7, /device:TPU:0, one launch (start us, length us, event | category | flops | bytes accessed | tf_op | source)
XLA Modules:
  0.0 47.6 jit_solution(7413661379235866152)
XLA Ops:
  0.0 2.3 %shard_map.74 = (bf16[768,512]{1,0:T(8,128)(2,1)S(1)}, bf16[256,256]{1,0:T(8,128)(2,1)S(1)}, bf16[256,128]{1,0:T(8,128)(2,1)S(1)}, bf16[256,128]{1,0:T(8,128)(2,1)S(1)}, bf16[256,128]{1,0:T(8,128)(2,1)S(1)}) custom-call(bf16[2,1024,1024]{2,1,0:T(8,128)(2,1)} %bitcast.10, bf16[256,256]{1,0:T(8,128)(2,1)} %bitcast.7, s32[4,4]{1,0:T(4,128)} %start_ref.5, ...), custom_call_target="tpu_custom_call" | custom-call | flops 134217728 | bytes 4587584 | tf_op jit(solution)/shard_map/pallas_call | solution.py:77
  2.4 0.6 %collective-permute-start.4 = (bf16[768,512]{1,0:T(8,128)(2,1)S(1)}, bf16[768,512]{1,0:T(8,128)(2,1)S(1)}, u32[]{:S(2)}, u32[]{:S(2)}) collective-permute-start(bf16[768,512]{1,0:T(8,128)(2,1)S(1)} %get-tuple-element.38.refs_0_), channel_id=1, source_target_pairs={{0,1},{1,0},{2,3},{3,2},{4,5},{5,4},{6,7},{7,6},{8,9},{9,8},{10,11... | collective-permute-start | bytes 2359304 | tf_op jit(solution)/shard_map/ppermute | solution.py:21
  2.9 1.9 %collective-permute-done.4.refs_1_ = bf16[768,512]{1,0:T(8,128)(2,1)S(1)} collective-permute-done((bf16[768,512]{1,0:T(8,128)(2,1)S(1)}, bf16[768,512]{1,0:T(8,128)(2,1)S(1)}, u32[]{:S(2)}, u32[]{:S(2)}) %collective-permute-start.4) | collective-permute-done | bytes 786464 | tf_op jit(solution)/shard_map/ppermute | solution.py:21
  4.8 0.9 %shard_map.76 = (bf16[768,512]{1,0:T(8,128)(2,1)S(1)}, bf16[768,512]{1,0:T(8,128)(2,1)S(1)}, bf16[768,512]{1,0:T(8,128)(2,1)S(1)}, bf16[384,512]{1,0:T(8,128)(2,1)S(1)}) custom-call(bf16[768,512]{1,0:T(8,128)(2,1)S(1)} %get-tuple-element.38.refs_0_, bf16[768,512]{1,0:T(8,128)(2,1)S(1)} %collective-permute-done.4.refs_1_), custom_call_target="tpu_custom_call" | custom-call | flops 1073741824 | bytes 1572864 | tf_op jit(solution)/shard_map/pallas_call | solution.py:77
  5.8 2.9 %collective-permute-start.6 = (bf16[384,512]{1,0:T(8,128)(2,1)S(1)}, bf16[384,512]{1,0:T(8,128)(2,1)S(1)}, u32[]{:S(2)}, u32[]{:S(2)}) collective-permute-start(bf16[384,512]{1,0:T(8,128)(2,1)S(1)} %get-tuple-element.43), channel_id=1, source_target_pairs={{0,2},{1,3},{2,0},{3,1},{4,6},{5,7},{6,4},{7,5},{8,10},{9,11},{10,... | collective-permute-start | bytes 1179656 | tf_op jit(solution)/shard_map/ppermute | solution.py:21
  8.7 9.4 %collective-permute-done.6.refs_1_.near_ref = bf16[384,512]{1,0:T(8,128)(2,1)S(1)} collective-permute-done((bf16[384,512]{1,0:T(8,128)(2,1)S(1)}, bf16[384,512]{1,0:T(8,128)(2,1)S(1)}, u32[]{:S(2)}, u32[]{:S(2)}) %collective-permute-start.6) | collective-permute-done | bytes 393248 | tf_op jit(solution)/shard_map/ppermute | solution.py:21
  18.1 1.8 %collective-permute-start = (bf16[256,128]{1,0:T(8,128)(2,1)S(1)}, bf16[256,128]{1,0:T(8,128)(2,1)S(1)}, u32[]{:S(2)}, u32[]{:S(2)}) collective-permute-start(bf16[256,128]{1,0:T(8,128)(2,1)S(1)} %get-tuple-element.34), channel_id=1, source_target_pairs={{0,8},{8,0},{16,24},{24,16},{1,9},{9,1},{17,25},{25,17},{2,10},{10... | collective-permute-start | bytes 196616 | tf_op jit(solution)/shard_map/ppermute | solution.py:21
  20.0 2.6 %collective-permute-start.1 = (bf16[256,128]{1,0:T(8,128)(2,1)S(1)}, bf16[256,128]{1,0:T(8,128)(2,1)S(1)}, u32[]{:S(2)}, u32[]{:S(2)}) collective-permute-start(bf16[256,128]{1,0:T(8,128)(2,1)S(1)} %get-tuple-element.35), channel_id=1, source_target_pairs={{0,16},{8,24},{16,0},{24,8},{1,17},{9,25},{17,1},{25,9},{2,18},{10... | collective-permute-start | bytes 196616 | tf_op jit(solution)/shard_map/ppermute | solution.py:21
  22.6 2.2 %shard_map.73 = (bf16[2,2,256,1024]{3,2,1,0:T(8,128)(2,1)S(1)}, f32[1024,128]{1,0:T(8,128)S(1)}, f32[3,256,128]{2,1,0:T(8,128)S(1)}) custom-call(bf16[2,1024,1024]{2,1,0:T(8,128)(2,1)} %bitcast.11, bf16[1024,128]{1,0:T(8,128)(2,1)S(1)} %bitcast.9, bf16[1024,128]{1,0:T(8,128)(2,1)S(1)} %bitcast.6, s32[4,4]{1,0:T(4,128)S(1)} %copy-done.3, ...), custom_call_target="tpu_custom_call" | custom-call | bytes 4718784 | tf_op jit(solution)/shard_map/pallas_call | solution.py:77
  24.8 2.2 %collective-permute-done.1.refs_1_ = bf16[256,128]{1,0:T(8,128)(2,1)S(1)} collective-permute-done((bf16[256,128]{1,0:T(8,128)(2,1)S(1)}, bf16[256,128]{1,0:T(8,128)(2,1)S(1)}, u32[]{:S(2)}, u32[]{:S(2)}) %collective-permute-start.1) | collective-permute-done | bytes 65568 | tf_op jit(solution)/shard_map/ppermute | solution.py:21
  27.0 1.6 %collective-permute-done.2.refs_2_ = bf16[256,128]{1,0:T(8,128)(2,1)S(1)} collective-permute-done((bf16[256,128]{1,0:T(8,128)(2,1)S(1)}, bf16[256,128]{1,0:T(8,128)(2,1)S(1)}, u32[]{:S(2)}, u32[]{:S(2)}) %collective-permute-start.2) | collective-permute-done | bytes 65568 | tf_op jit(solution)/shard_map/ppermute | solution.py:21
  28.6 1.6 %shard_map.75 = (bf16[1024,128]{1,0:T(8,128)(2,1)S(1)}, bf16[1024,128]{1,0:T(8,128)(2,1)S(1)}, f32[256,128]{1,0:T(8,128)S(1)}, f32[512,128]{1,0:T(8,128)S(1)}) custom-call(s32[4,4]{1,0:T(4,128)S(1)} %copy-done.3, f32[1024,128]{1,0:T(8,128)S(1)} %get-tuple-element.30.acc_ref, f32[3,256,128]{2,1,0:T(8,128)S(1)} %get-tuple-element.31.weight_ref, ...), custom_call_target="tpu_custom_call" | custom-call | flops 268435456 | bytes 3342400 | tf_op jit(solution)/shard_map/pallas_call | solution.py:77
  30.3 1.5 %collective-permute-done.3.refs_1_ = f32[512,128]{1,0:T(8,128)S(1)} collective-permute-done((f32[512,128]{1,0:T(8,128)S(1)}, f32[512,128]{1,0:T(8,128)S(1)}, u32[]{:S(2)}, u32[]{:S(2)}) %collective-permute-start.3) | collective-permute-done | bytes 262176 | tf_op jit(solution)/shard_map/ppermute | solution.py:21
  31.9 0.6 %shard_map.77 = (f32[512,128]{1,0:T(8,128)S(1)}, bf16[512,128]{1,0:T(8,128)(2,1)S(1)}, f32[512,128]{1,0:T(8,128)S(1)}) custom-call(f32[512,128]{1,0:T(8,128)S(1)} %get-tuple-element.37.refs_0_.sent_ref, f32[512,128]{1,0:T(8,128)S(1)} %collective-permute-done.3.refs_1_, bf16[768,512]{1,0:T(8,128)(2,1)S(1)} %get-tuple-element.39.refs_2_), custom_call_target="tpu_custom_call" | custom-call | flops 335544320 | bytes 1310720 | tf_op jit(solution)/shard_map/pallas_call | solution.py:77
  32.7 2.1 %collective-permute-start.9 = (bf16[128,512]{1,0:T(8,128)(2,1)S(1)}, bf16[128,512]{1,0:T(8,128)(2,1)S(1)}, u32[]{:S(2)}, u32[]{:S(2)}) collective-permute-start(bf16[128,512]{1,0:T(8,128)(2,1)S(1)} %get-tuple-element.49.hint_ref), channel_id=1, source_target_pairs={{0,4},{1,5},{2,6},{3,7},{4,0},{5,1},{6,2},{7,3},{8,12},{9,13},{10,... | collective-permute-start | bytes 393224 | tf_op jit(solution)/shard_map/ppermute | solution.py:21
  34.9 1.5 %collective-permute-start.5 = (bf16[512,128]{1,0:T(8,128)(2,1)S(1)}, bf16[512,128]{1,0:T(8,128)(2,1)S(1)}, u32[]{:S(2)}, u32[]{:S(2)}) collective-permute-start(bf16[512,128]{1,0:T(8,128)(2,1)S(1)} %get-tuple-element.41), channel_id=1, source_target_pairs={{0,2},{1,3},{2,0},{3,1},{4,6},{5,7},{6,4},{7,5},{8,10},{9,11},{10,... | collective-permute-start | bytes 393224 | tf_op jit(solution)/shard_map/ppermute | solution.py:21
  36.4 1.5 %shard_map.81.mid_ref = bf16[2,2,256,1024]{3,2,1,0:T(8,128)(2,1)S(1)} custom-call(bf16[2,1024,1024]{2,1,0:T(8,128)(2,1)} %bitcast.12, f32[256,128]{1,0:T(8,128)S(1)} %get-tuple-element.52.hint_ref.low_ref), custom_call_target="tpu_custom_call" | custom-call | bytes 4325376 | tf_op jit(solution)/shard_map/pallas_call | solution.py:77
  37.9 0.7 %shard_map.82.direct_ref = f32[2,256,128]{2,1,0:T(8,128)S(1)} custom-call(bf16[2,2,256,1024]{3,2,1,0:T(8,128)(2,1)S(1)} %shard_map.81.mid_ref, bf16[1024,128]{1,0:T(8,128)(2,1)S(1)} %get-tuple-element.53.source_ref, bf16[1024,128]{1,0:T(8,128)(2,1)S(1)} %get-tuple-element.54.spun_ref), custom_call_target="tpu_custom_call" | custom-call | flops 268435456 | bytes 2621440 | tf_op jit(solution)/shard_map/pallas_call | solution.py:77
  38.7 1.4 %collective-permute-done.5.refs_1_ = bf16[512,128]{1,0:T(8,128)(2,1)S(1)} collective-permute-done((bf16[512,128]{1,0:T(8,128)(2,1)S(1)}, bf16[512,128]{1,0:T(8,128)(2,1)S(1)}, u32[]{:S(2)}, u32[]{:S(2)}) %collective-permute-start.5) | collective-permute-done | bytes 131104 | tf_op jit(solution)/shard_map/ppermute | solution.py:21
  40.1 1.0 %shard_map.79 = (f32[256,128]{1,0:T(8,128)S(1)}, bf16[256,128]{1,0:T(8,128)(2,1)S(1)}, f32[512,128]{1,0:T(8,128)S(1)}) custom-call(f32[512,128]{1,0:T(8,128)S(1)} %get-tuple-element.40.refs_0_, bf16[512,128]{1,0:T(8,128)(2,1)S(1)} %collective-permute-done.5.refs_1_, bf16[1280,512]{1,0:T(8,128)(2,1)S(1)} %get-tuple-element.45.refs_2_, ...), custom_call_target="tpu_custom_call" | custom-call | flops 335544320 | bytes 1966080 | tf_op jit(solution)/shard_map/pallas_call | solution.py:77
  41.1 0.4 collective-permute-start.8
  41.5 0.3 shard_map.80.member
  41.9 3.6 %collective-permute-done.8.other_ref = bf16[256,128]{1,0:T(8,128)(2,1)S(1)} collective-permute-done((bf16[256,128]{1,0:T(8,128)(2,1)S(1)}, bf16[256,128]{1,0:T(8,128)(2,1)S(1)}, u32[]{:S(2)}, u32[]{:S(2)}) %collective-permute-start.8) | collective-permute-done | bytes 65568 | tf_op jit(solution)/shard_map/ppermute | solution.py:21
  45.5 2.1 %shard_map.83 = bf16[1024,128]{1,0:T(8,128)(2,1)} custom-call(bf16[256,128]{1,0:T(8,128)(2,1)S(1)} %collective-permute-done.8.other_ref, f32[256,128]{1,0:T(8,128)S(1)} %get-tuple-element.48.c_ref, bf16[128,512]{1,0:T(8,128)(2,1)S(1)} %collective-permute-done.9.near_ref, bf16[128,512]{1,0:T(8,128)(2,1)S(1)} %collective-permute-done.10.far_ref, ...), custom_call_target="tpu_custom_call" | custom-call | flops 536870912 | bytes 6225920 | tf_op jit(solution)/shard_map/pallas_call | solution.py:77
  (21 shorter events, 0.4 us)
Async XLA Ops:
  2.3 20.2 %copy-start = (bf16[1,1,1024,128]{3,2,1,0:T(8,128)(2,1)S(1)}, bf16[1,1,1024,128]{3,2,1,0:T(8,128)(2,1)}, u32[]{:S(2)}) copy-start(bf16[1,1,1024,128]{3,2,1,0:T(8,128)(2,1)} %param.9) | copy-start | bytes 786436
  2.3 20.2 %copy-start.2 = (bf16[1,1,1024,128]{3,2,1,0:T(8,128)(2,1)S(1)}, bf16[1,1,1024,128]{3,2,1,0:T(8,128)(2,1)}, u32[]{:S(2)}) copy-start(bf16[1,1,1024,128]{3,2,1,0:T(8,128)(2,1)} %param.8) | copy-start | bytes 786436
  2.3 20.2 %copy-start.3 = (s32[4,4]{1,0:T(4,128)S(1)}, s32[4,4]{1,0:T(4,128)}, u32[]{:S(2)}) copy-start(s32[4,4]{1,0:T(4,128)} %start_ref.5) | copy-start | bytes 196
  2.4 20.2 %copy-start.4 = (s32[4,4]{1,0:T(4,128)S(1)}, s32[4,4]{1,0:T(4,128)}, u32[]{:S(2)}) copy-start(s32[4,4]{1,0:T(4,128)} %count_ref.1) | copy-start | bytes 196
  2.4 20.2 %copy-start.5 = (f32[4,4]{1,0:T(4,128)S(1)}, f32[4,4]{1,0:T(4,128)}, u32[]{:S(2)}) copy-start(f32[4,4]{1,0:T(4,128)} %strength_ref.1) | copy-start | bytes 196
  2.4 2.5 %collective-permute-start.4 = (bf16[768,512]{1,0:T(8,128)(2,1)S(1)}, bf16[768,512]{1,0:T(8,128)(2,1)S(1)}, u32[]{:S(2)}, u32[]{:S(2)}) collective-permute-start(bf16[768,512]{1,0:T(8,128)(2,1)S(1)} %get-tuple-element.38.refs_0_), channel_id=1, source_target_pairs={{0,1},{1,0},{2,3},{3,2},{4,5},{5,4},{6,7},{7,6},{8,9},{9,8},{10,11... | collective-permute-start | bytes 2359304 | tf_op jit(solution)/shard_map/ppermute | solution.py:21
  5.8 12.3 %collective-permute-start.6 = (bf16[384,512]{1,0:T(8,128)(2,1)S(1)}, bf16[384,512]{1,0:T(8,128)(2,1)S(1)}, u32[]{:S(2)}, u32[]{:S(2)}) collective-permute-start(bf16[384,512]{1,0:T(8,128)(2,1)S(1)} %get-tuple-element.43), channel_id=1, source_target_pairs={{0,2},{1,3},{2,0},{3,1},{4,6},{5,7},{6,4},{7,5},{8,10},{9,11},{10,... | collective-permute-start | bytes 1179656 | tf_op jit(solution)/shard_map/ppermute | solution.py:21
  18.1 14.4 %collective-permute-start.7 = (bf16[384,512]{1,0:T(8,128)(2,1)S(1)}, bf16[384,512]{1,0:T(8,128)(2,1)S(1)}, u32[]{:S(2)}, u32[]{:S(2)}) collective-permute-start(bf16[384,512]{1,0:T(8,128)(2,1)S(1)} %collective-permute-done.6.refs_1_.near_ref), channel_id=1, source_target_pairs={{0,1},{1,0},{2,3},{3,2},{4,5},{5,4},{6,7},{7,6},{8,9},{9,8},{10,11... | collective-permute-start | bytes 1179656 | tf_op jit(solution)/shard_map/ppermute | solution.py:21
  18.1 6.6 %collective-permute-start = (bf16[256,128]{1,0:T(8,128)(2,1)S(1)}, bf16[256,128]{1,0:T(8,128)(2,1)S(1)}, u32[]{:S(2)}, u32[]{:S(2)}) collective-permute-start(bf16[256,128]{1,0:T(8,128)(2,1)S(1)} %get-tuple-element.34), channel_id=1, source_target_pairs={{0,8},{8,0},{16,24},{24,16},{1,9},{9,1},{17,25},{25,17},{2,10},{10... | collective-permute-start | bytes 196616 | tf_op jit(solution)/shard_map/ppermute | solution.py:21
  20.0 7.0 %collective-permute-start.1 = (bf16[256,128]{1,0:T(8,128)(2,1)S(1)}, bf16[256,128]{1,0:T(8,128)(2,1)S(1)}, u32[]{:S(2)}, u32[]{:S(2)}) collective-permute-start(bf16[256,128]{1,0:T(8,128)(2,1)S(1)} %get-tuple-element.35), channel_id=1, source_target_pairs={{0,16},{8,24},{16,0},{24,8},{1,17},{9,25},{17,1},{25,9},{2,18},{10... | collective-permute-start | bytes 196616 | tf_op jit(solution)/shard_map/ppermute | solution.py:21
  22.5 6.1 %collective-permute-start.2 = (bf16[256,128]{1,0:T(8,128)(2,1)S(1)}, bf16[256,128]{1,0:T(8,128)(2,1)S(1)}, u32[]{:S(2)}, u32[]{:S(2)}) collective-permute-start(bf16[256,128]{1,0:T(8,128)(2,1)S(1)} %get-tuple-element.36), channel_id=1, source_target_pairs={{0,24},{8,16},{16,8},{24,0},{1,25},{9,17},{17,9},{25,1},{2,26},{10... | collective-permute-start | bytes 196616 | tf_op jit(solution)/shard_map/ppermute | solution.py:21
  30.3 1.6 %collective-permute-start.3 = (f32[512,128]{1,0:T(8,128)S(1)}, f32[512,128]{1,0:T(8,128)S(1)}, u32[]{:S(2)}, u32[]{:S(2)}) collective-permute-start(f32[512,128]{1,0:T(8,128)S(1)} %get-tuple-element.37.refs_0_.sent_ref), channel_id=1, source_target_pairs={{0,1},{1,0},{2,3},{3,2},{4,5},{5,4},{6,7},{7,6},{8,9},{9,8},{10,11... | collective-permute-start | bytes 786440 | tf_op jit(solution)/shard_map/ppermute | solution.py:21
  32.7 5.9 %collective-permute-start.9 = (bf16[128,512]{1,0:T(8,128)(2,1)S(1)}, bf16[128,512]{1,0:T(8,128)(2,1)S(1)}, u32[]{:S(2)}, u32[]{:S(2)}) collective-permute-start(bf16[128,512]{1,0:T(8,128)(2,1)S(1)} %get-tuple-element.49.hint_ref), channel_id=1, source_target_pairs={{0,4},{1,5},{2,6},{3,7},{4,0},{5,1},{6,2},{7,3},{8,12},{9,13},{10,... | collective-permute-start | bytes 393224 | tf_op jit(solution)/shard_map/ppermute | solution.py:21
  34.9 5.3 %collective-permute-start.5 = (bf16[512,128]{1,0:T(8,128)(2,1)S(1)}, bf16[512,128]{1,0:T(8,128)(2,1)S(1)}, u32[]{:S(2)}, u32[]{:S(2)}) collective-permute-start(bf16[512,128]{1,0:T(8,128)(2,1)S(1)} %get-tuple-element.41), channel_id=1, source_target_pairs={{0,2},{1,3},{2,0},{3,1},{4,6},{5,7},{6,4},{7,5},{8,10},{9,11},{10,... | collective-permute-start | bytes 393224 | tf_op jit(solution)/shard_map/ppermute | solution.py:21
  38.7 6.8 %collective-permute-start.10 = (bf16[128,512]{1,0:T(8,128)(2,1)S(1)}, bf16[128,512]{1,0:T(8,128)(2,1)S(1)}, u32[]{:S(2)}, u32[]{:S(2)}) collective-permute-start(bf16[128,512]{1,0:T(8,128)(2,1)S(1)} %collective-permute-done.9.near_ref), channel_id=1, source_target_pairs={{0,1},{1,0},{2,3},{3,2},{4,5},{5,4},{6,7},{7,6},{8,9},{9,8},{10,11... | collective-permute-start | bytes 393224 | tf_op jit(solution)/shard_map/ppermute | solution.py:21
  41.1 4.3 %copy-start.1 = (bf16[1,256,256]{2,1,0:T(8,128)(2,1)S(1)}, bf16[1,256,256]{2,1,0:T(8,128)(2,1)}, u32[]{:S(2)}) copy-start(bf16[1,256,256]{2,1,0:T(8,128)(2,1)} %param.10) | copy-start | bytes 393220
  41.1 4.3 %collective-permute-start.8 = (bf16[256,128]{1,0:T(8,128)(2,1)S(1)}, bf16[256,128]{1,0:T(8,128)(2,1)S(1)}, u32[]{:S(2)}, u32[]{:S(2)}) collective-permute-start(bf16[256,128]{1,0:T(8,128)(2,1)S(1)} %get-tuple-element.47), channel_id=1, source_target_pairs={{0,4},{1,5},{2,6},{3,7},{4,0},{5,1},{6,2},{7,3},{8,12},{9,13},{10,... | collective-permute-start | bytes 196616 | tf_op jit(solution)/shard_map/ppermute | solution.py:21

commit v8 on v7

--- a/solution.py
+++ b/solution.py
@@ -278,36 +278,8 @@
         if not closing:
             totals, members = grown[0], member
 
-    def last_ends(mine, near_ref, far_ref, old, bounce_ref, hint_ref, out_ref):
-        after, first = place(final - 1), place(0)
-
-        @pl.when(place(final))
-        def _():
-            its_a = jnp.where(first, far_ref[:layer], near_ref[:layer])
-            a_left = jnp.where(after, its_a, mine[rows_of[0]])
-            out_ref[rows_of[0]] = member_before(after, old[rows_of[0]], a_left)
-            out_ref[rows_of[1]] = member_turned(
-                after, old[rows_of[1]], old[rows_of[2]], a_left, bounce_ref[...]
-            )
-
-        @pl.when(~place(final))
-        def _():
-            a, b = near_ref[...], far_ref[...]
-            theirs = jnp.concatenate([jnp.where(first, b, a), jnp.where(first, a, b)], axis=0)
-            b_right = jnp.where(after, mine[rows_of[1]], theirs[rows_of[1]])
-            out_ref[rows_of[0]] = jnp.zeros(one_map, bf16)
-            out_ref[rows_of[1]] = member_behind(after, old[rows_of[1]], b_right)
-
     e_near = swapped(send, "slab", 1 << final)
     e_far = swapped(e_near, "slab", 1)
-
-    (ends_last,) = call(
-        last_ends,
-        [((2 * layer, 2 * layer), bf16)],
-        (totals, near, far, members, member, send),
-        64 * layer**3,
-        {5: pl.ANY},
-    )
 
     ways = (slice(0, layer), slice(layer, 2 * layer))
     pair = (2 * layer, width)
@@ -453,39 +425,96 @@
         4 * (low - layer) * norb * width,
     )
 
-    def finish(
-        other_ref, c_ref, near_ref, far_ref, member, reach_ref, ends_ref, mid_ref, coup_ref,
-        sent_ref, low_ref, direct_ref, out_ref, kept, sem,
+    def weights(
+        mine, near_ref, far_ref, old, bounce_ref, reach_ref, ends_ref, mid_ref, coup_ref,
+        sent_ref, low_ref, direct_ref, base_ref, wide_ref,
     ):
-        after, first = place(final), place(0)
+        after, first, right = place(final - 1), place(0), place(final)
+        c = coup_ref[...]
+        incoming = reach_ref[ways[0]].astype(bf16)
+        spun_z = turned(incoming.astype(f32)).astype(bf16)
+        outgoing = fine(c, reach_ref[ways[1]]).astype(bf16)
+        spun_u = turned(outgoing.astype(f32)).astype(bf16)
+        tail = slice(low, norb)
+
+        def held_rows(i):
+            if i == 0:
+                return [ends_ref.at[k, 0] for k in range(2)]
+            if i > blocks:
+                return [ends_ref.at[k, 1] for k in range(2)]
+            return [mid_ref.at[k, i - 1] for k in range(2)]
+
+        def twice(wide):
+            return wide, turned(wide.astype(f32)).astype(bf16)
+
+        @pl.when(right)
+        def _():
+            its_a = jnp.where(first, far_ref[:layer], near_ref[:layer])
+            a_left = jnp.where(after, its_a, mine[rows_of[0]])
+            p, spun_p = twice(member_before(after, old[rows_of[0]], a_left))
+            r = member_turned(after, old[rows_of[1]], old[rows_of[2]], a_left, bounce_ref[...])
+            s, spun_s = twice(dot(c, r).astype(bf16))
+            for i in range(blocks + 2):
+                real, imag = held_rows(i)
+                wide_ref[i * layer : (i + 1) * layer] = (
+                    dot(real[:, :layer], p)
+                    + dot(imag[:, :layer], spun_p)
+                    + dot(real[:, tail], s)
+                    + dot(imag[:, tail], spun_s)
+                ).astype(bf16)
+
+        @pl.when(~right)
+        def _():
+            a, b = near_ref[...], far_ref[...]
+            theirs = jnp.concatenate([jnp.where(first, b, a), jnp.where(first, a, b)], axis=0)
+            b_right = jnp.where(after, mine[rows_of[1]], theirs[rows_of[1]])
+            q = member_behind(after, old[rows_of[1]], b_right)
+            s, spun_s = twice(dot(c, q).astype(bf16))
+            for i in range(blocks + 2):
+                real, imag = held_rows(i)
+                wide_ref[i * layer : (i + 1) * layer] = (
+                    dot(real[:, tail], s) + dot(imag[:, tail], spun_s)
+                ).astype(bf16)
+
+        for i in range(blocks + 2):
+            real, imag = held_rows(i)
+            if i == 0:
+                direct = sent_ref[ways[1]]
+            elif i > blocks:
+                direct = low_ref[...]
+            else:
+                direct = direct_ref[i - 1]
+            base_ref[i * layer : (i + 1) * layer] = (
+                direct
+                + dot(real[:, :layer], incoming)
+                + dot(imag[:, :layer], spun_z)
+                + dot(real[:, tail], outgoing)
+                + dot(imag[:, tail], spun_u)
+            )
+
+    base, last_map = call(
+        weights,
+        [((norb, width), f32), ((norb, 2 * layer), bf16)],
+        (
+            totals, near, far, members, member, reach, ends, mid, coup,
+            sent, direct_low, direct_mid,
+        ),
+        16 * norb * layer * (width + 2 * layer),
+    )
+
+    def finish(other_ref, c_ref, near_ref, far_ref, base_ref, wide_ref, out_ref, kept, sem):
+        first = place(0)
         other = other_ref[...].astype(f32)
         c_left = c_ref[...]
         a, b = mapped(near_ref[...], c_left), mapped(far_ref[...], c_left)
         bounce = jnp.concatenate([jnp.where(first, b, a), jnp.where(first, a, b)], axis=0)
-        back = other + jnp.where(after, jnp.zeros_like(bounce), bounce)
-        more = mapped(member[ways[0]], other)
-        z = reach_ref[ways[0]] + jnp.where(after, more, jnp.zeros_like(more))
-        incoming = z.astype(bf16)
-        spun_z = turned(incoming.astype(f32)).astype(bf16)
-        u = reach_ref[ways[1]] + mapped(member[ways[1]], back)
-        outgoing = fine(coup_ref[...], u).astype(bf16)
-        spun_u = turned(outgoing.astype(f32)).astype(bf16)
+        last = other + jnp.where(place(final), jnp.zeros_like(bounce), bounce)
         copies = []
-        tail = slice(low, norb)
-        for i in range(blocks + 2):
-            if i == 0:
-                direct, held = sent_ref[ways[1]], [ends_ref.at[k, 0] for k in range(2)]
-            elif i > blocks:
-                direct, held = low_ref[...], [ends_ref.at[k, 1] for k in range(2)]
-            else:
-                direct, held = direct_ref[i - 1], [mid_ref.at[k, i - 1] for k in range(2)]
+        v, spun = last.astype(bf16), turned(last).astype(bf16)
+        for i in range(norb // layer):
             part = pl.ds(i * layer, layer)
             kept[part] = (
-                direct
-                + dot(held[0][:, :layer], incoming)
-                + dot(held[1][:, :layer], spun_z)
-                + dot(held[0][:, tail], outgoing)
-                + dot(held[1][:, tail], spun_u)
+                base_ref[part] + dot(wide_ref[part, :layer], v) + dot(wide_ref[part, layer:], spun)
             ).astype(bf16)
             copy = pltpu.make_async_copy(kept.at[part], out_ref.at[part], sem.at[i])
             copy.start()
@@ -496,11 +525,8 @@
     (out,) = call(
         finish,
         [((norb, width), bf16)],
-        (
-            arrived, c_total, e_near, e_far, ends_last, reach, ends, mid, coup,
-            sent, direct_low, direct_mid,
-        ),
-        16 * norb * layer * width,
+        (arrived, c_total, e_near, e_far, base, last_map),
+        8 * norb * layer * width,
         scratch=[pltpu.VMEM((norb, width), bf16), pltpu.SemaphoreType.DMA((norb // layer,))],
         out_space=pltpu.HBM,
     )

time: 47.8 us -> 45.6 us (0.954)
  waiting for transfers between devices: 21.7 us -> 17.9 us
  Pallas kernels: 13.6 us -> 14.7 us
  starting transfers between devices: 12.1 us -> 12.6 us
    ppermute x11, waiting for transfers between devices: 21.7 us -> 17.9 us  [swapped(): return lax.ppermute(block, axis, [(i, i ^ mask) for i in range(count)])]
    pallas_call x11, Pallas kernels: 13.6 us -> 14.7 us  [call(): pl.pallas_call(kernel, out_shape=shapes, in_specs=specs, out_specs=[pl.Bl...]
    ppermute x11, starting transfers between devices: 12.1 us -> 12.6 us  [swapped(): return lax.ppermute(block, axis, [(i, i ^ mask) for i in range(count)])]
  transfers between devices with their start and end apart: 11 -> 11, of which waited for: 7 -> 6; matrix products, arithmetic and copies ran while one was open for 0% -> 0% of each run, Pallas kernels for 17% -> 22%
where the time goes in v8:
time: 45.6 us; the launch traced here: 45.4 us
  waiting for transfers between devices  17.9 us (39%)
  Pallas kernels  14.7 us (32%)
  starting transfers between devices  12.6 us (28%)
    ppermute x11, waiting for transfers between devices, swapped(): return lax.ppermute(block, axis, [(i, i ^ mask) for i in range(count)])  17.9 us
    pallas_call x11, Pallas kernels, call(): pl.pallas_call(kernel, out_shape=shapes, in_specs=specs, out_specs=[pl.Bl...  14.7 us
    ppermute x11, starting transfers between devices, swapped(): return lax.ppermute(block, axis, [(i, i ^ mask) for i in range(count)])  12.6 us
  transfers between devices with their start and end apart: 11, of which 6 were waited for; matrix products, arithmetic and copies ran while one was open for 0% of the time, Pallas kernels for 22%

profile of v8, /device:TPU:0, one launch (start us, length us, event | category | flops | bytes accessed | tf_op | source)
XLA Modules:
  0.0 45.4 jit_solution(771214466544882883)
XLA Ops:
  0.0 2.3 %shard_map.74 = (bf16[768,512]{1,0:T(8,128)(2,1)S(1)}, bf16[256,256]{1,0:T(8,128)(2,1)S(1)}, bf16[256,128]{1,0:T(8,128)(2,1)S(1)}, bf16[256,128]{1,0:T(8,128)(2,1)S(1)}, bf16[256,128]{1,0:T(8,128)(2,1)S(1)}) custom-call(bf16[2,1024,1024]{2,1,0:T(8,128)(2,1)} %bitcast.10, bf16[256,256]{1,0:T(8,128)(2,1)} %bitcast.8, s32[4,4]{1,0:T(4,128)} %start_ref.5, ...), custom_call_target="tpu_custom_call" | custom-call | flops 134217728 | bytes 4587584 | tf_op jit(solution)/shard_map/pallas_call | solution.py:77
  2.4 0.6 %collective-permute-start.4 = (bf16[768,512]{1,0:T(8,128)(2,1)S(1)}, bf16[768,512]{1,0:T(8,128)(2,1)S(1)}, u32[]{:S(2)}, u32[]{:S(2)}) collective-permute-start(bf16[768,512]{1,0:T(8,128)(2,1)S(1)} %get-tuple-element.40.refs_0_), channel_id=1, source_target_pairs={{0,1},{1,0},{2,3},{3,2},{4,5},{5,4},{6,7},{7,6},{8,9},{9,8},{10,11... | collective-permute-start | bytes 2359304 | tf_op jit(solution)/shard_map/ppermute | solution.py:21
  2.9 1.9 %collective-permute-done.4.refs_1_ = bf16[768,512]{1,0:T(8,128)(2,1)S(1)} collective-permute-done((bf16[768,512]{1,0:T(8,128)(2,1)S(1)}, bf16[768,512]{1,0:T(8,128)(2,1)S(1)}, u32[]{:S(2)}, u32[]{:S(2)}) %collective-permute-start.4) | collective-permute-done | bytes 786464 | tf_op jit(solution)/shard_map/ppermute | solution.py:21
  4.8 0.9 %shard_map.76 = (bf16[768,512]{1,0:T(8,128)(2,1)S(1)}, bf16[768,512]{1,0:T(8,128)(2,1)S(1)}, bf16[768,512]{1,0:T(8,128)(2,1)S(1)}, bf16[384,512]{1,0:T(8,128)(2,1)S(1)}) custom-call(bf16[768,512]{1,0:T(8,128)(2,1)S(1)} %get-tuple-element.40.refs_0_, bf16[768,512]{1,0:T(8,128)(2,1)S(1)} %collective-permute-done.4.refs_1_), custom_call_target="tpu_custom_call" | custom-call | flops 1073741824 | bytes 1572864 | tf_op jit(solution)/shard_map/pallas_call | solution.py:77
  5.8 2.9 %collective-permute-start.6 = (bf16[384,512]{1,0:T(8,128)(2,1)S(1)}, bf16[384,512]{1,0:T(8,128)(2,1)S(1)}, u32[]{:S(2)}, u32[]{:S(2)}) collective-permute-start(bf16[384,512]{1,0:T(8,128)(2,1)S(1)} %get-tuple-element.45), channel_id=1, source_target_pairs={{0,2},{1,3},{2,0},{3,1},{4,6},{5,7},{6,4},{7,5},{8,10},{9,11},{10,... | collective-permute-start | bytes 1179656 | tf_op jit(solution)/shard_map/ppermute | solution.py:21
  8.7 9.4 %collective-permute-done.6.refs_1_.near_ref = bf16[384,512]{1,0:T(8,128)(2,1)S(1)} collective-permute-done((bf16[384,512]{1,0:T(8,128)(2,1)S(1)}, bf16[384,512]{1,0:T(8,128)(2,1)S(1)}, u32[]{:S(2)}, u32[]{:S(2)}) %collective-permute-start.6) | collective-permute-done | bytes 393248 | tf_op jit(solution)/shard_map/ppermute | solution.py:21
  18.1 1.8 %collective-permute-start = (bf16[256,128]{1,0:T(8,128)(2,1)S(1)}, bf16[256,128]{1,0:T(8,128)(2,1)S(1)}, u32[]{:S(2)}, u32[]{:S(2)}) collective-permute-start(bf16[256,128]{1,0:T(8,128)(2,1)S(1)} %get-tuple-element.36), channel_id=1, source_target_pairs={{0,8},{8,0},{16,24},{24,16},{1,9},{9,1},{17,25},{25,17},{2,10},{10... | collective-permute-start | bytes 196616 | tf_op jit(solution)/shard_map/ppermute | solution.py:21
  20.0 2.6 %collective-permute-start.1 = (bf16[256,128]{1,0:T(8,128)(2,1)S(1)}, bf16[256,128]{1,0:T(8,128)(2,1)S(1)}, u32[]{:S(2)}, u32[]{:S(2)}) collective-permute-start(bf16[256,128]{1,0:T(8,128)(2,1)S(1)} %get-tuple-element.37), channel_id=1, source_target_pairs={{0,16},{8,24},{16,0},{24,8},{1,17},{9,25},{17,1},{25,9},{2,18},{10... | collective-permute-start | bytes 196616 | tf_op jit(solution)/shard_map/ppermute | solution.py:21
  22.6 2.2 %shard_map.73 = (bf16[2,2,256,1024]{3,2,1,0:T(8,128)(2,1)S(1)}, f32[1024,128]{1,0:T(8,128)S(1)}, f32[3,256,128]{2,1,0:T(8,128)S(1)}) custom-call(bf16[2,1024,1024]{2,1,0:T(8,128)(2,1)} %bitcast.11, bf16[1024,128]{1,0:T(8,128)(2,1)S(1)} %bitcast.7, bf16[1024,128]{1,0:T(8,128)(2,1)S(1)} %bitcast.6, s32[4,4]{1,0:T(4,128)S(1)} %copy-done.3, ...), custom_call_target="tpu_custom_call" | custom-call | bytes 4718784 | tf_op jit(solution)/shard_map/pallas_call | solution.py:77
  24.8 2.2 %collective-permute-done.1.refs_1_ = bf16[256,128]{1,0:T(8,128)(2,1)S(1)} collective-permute-done((bf16[256,128]{1,0:T(8,128)(2,1)S(1)}, bf16[256,128]{1,0:T(8,128)(2,1)S(1)}, u32[]{:S(2)}, u32[]{:S(2)}) %collective-permute-start.1) | collective-permute-done | bytes 65568 | tf_op jit(solution)/shard_map/ppermute | solution.py:21
  27.0 1.6 %collective-permute-done.2.refs_2_ = bf16[256,128]{1,0:T(8,128)(2,1)S(1)} collective-permute-done((bf16[256,128]{1,0:T(8,128)(2,1)S(1)}, bf16[256,128]{1,0:T(8,128)(2,1)S(1)}, u32[]{:S(2)}, u32[]{:S(2)}) %collective-permute-start.2) | collective-permute-done | bytes 65568 | tf_op jit(solution)/shard_map/ppermute | solution.py:21
  28.6 1.6 %shard_map.75 = (bf16[1024,128]{1,0:T(8,128)(2,1)S(1)}, bf16[1024,128]{1,0:T(8,128)(2,1)S(1)}, f32[256,128]{1,0:T(8,128)S(1)}, f32[512,128]{1,0:T(8,128)S(1)}) custom-call(s32[4,4]{1,0:T(4,128)S(1)} %copy-done.3, f32[1024,128]{1,0:T(8,128)S(1)} %get-tuple-element.32.acc_ref, f32[3,256,128]{2,1,0:T(8,128)S(1)} %get-tuple-element.33.weight_ref, ...), custom_call_target="tpu_custom_call" | custom-call | flops 268435456 | bytes 3342400 | tf_op jit(solution)/shard_map/pallas_call | solution.py:77
  30.3 1.5 %collective-permute-done.3.refs_1_ = f32[512,128]{1,0:T(8,128)S(1)} collective-permute-done((f32[512,128]{1,0:T(8,128)S(1)}, f32[512,128]{1,0:T(8,128)S(1)}, u32[]{:S(2)}, u32[]{:S(2)}) %collective-permute-start.3) | collective-permute-done | bytes 262176 | tf_op jit(solution)/shard_map/ppermute | solution.py:21
  31.9 0.6 %shard_map.77 = (f32[512,128]{1,0:T(8,128)S(1)}, bf16[512,128]{1,0:T(8,128)(2,1)S(1)}, f32[512,128]{1,0:T(8,128)S(1)}) custom-call(f32[512,128]{1,0:T(8,128)S(1)} %get-tuple-element.39.refs_0_.sent_ref, f32[512,128]{1,0:T(8,128)S(1)} %collective-permute-done.3.refs_1_, bf16[768,512]{1,0:T(8,128)(2,1)S(1)} %get-tuple-element.41.refs_2_), custom_call_target="tpu_custom_call" | custom-call | flops 335544320 | bytes 1310720 | tf_op jit(solution)/shard_map/pallas_call | solution.py:77
  32.5 1.6 %collective-permute-start.5 = (bf16[512,128]{1,0:T(8,128)(2,1)S(1)}, bf16[512,128]{1,0:T(8,128)(2,1)S(1)}, u32[]{:S(2)}, u32[]{:S(2)}) collective-permute-start(bf16[512,128]{1,0:T(8,128)(2,1)S(1)} %get-tuple-element.43), channel_id=1, source_target_pairs={{0,2},{1,3},{2,0},{3,1},{4,6},{5,7},{6,4},{7,5},{8,10},{9,11},{10,... | collective-permute-start | bytes 393224 | tf_op jit(solution)/shard_map/ppermute | solution.py:21
  34.1 0.2 shard_map.78
  34.3 2.1 %collective-permute-start.9 = (bf16[128,512]{1,0:T(8,128)(2,1)S(1)}, bf16[128,512]{1,0:T(8,128)(2,1)S(1)}, u32[]{:S(2)}, u32[]{:S(2)}) collective-permute-start(bf16[128,512]{1,0:T(8,128)(2,1)S(1)} %get-tuple-element.51), channel_id=1, source_target_pairs={{0,4},{1,5},{2,6},{3,7},{4,0},{5,1},{6,2},{7,3},{8,12},{9,13},{10,... | collective-permute-start | bytes 393224 | tf_op jit(solution)/shard_map/ppermute | solution.py:21
  36.4 1.5 %shard_map.80.mid_ref = bf16[2,2,256,1024]{3,2,1,0:T(8,128)(2,1)S(1)} custom-call(bf16[2,1024,1024]{2,1,0:T(8,128)(2,1)} %bitcast.12, f32[256,128]{1,0:T(8,128)S(1)} %get-tuple-element.54.hint_ref.low_ref), custom_call_target="tpu_custom_call" | custom-call | bytes 4325376 | tf_op jit(solution)/shard_map/pallas_call | solution.py:77
  38.0 0.7 %shard_map.81.direct_ref = f32[2,256,128]{2,1,0:T(8,128)S(1)} custom-call(bf16[2,2,256,1024]{3,2,1,0:T(8,128)(2,1)S(1)} %shard_map.80.mid_ref, bf16[1024,128]{1,0:T(8,128)(2,1)S(1)} %get-tuple-element.55.source_ref, bf16[1024,128]{1,0:T(8,128)(2,1)S(1)} %get-tuple-element.56.spun_ref), custom_call_target="tpu_custom_call" | custom-call | flops 268435456 | bytes 2621440 | tf_op jit(solution)/shard_map/pallas_call | solution.py:77
  38.7 1.0 %shard_map.79 = (f32[256,128]{1,0:T(8,128)S(1)}, bf16[256,128]{1,0:T(8,128)(2,1)S(1)}, f32[512,128]{1,0:T(8,128)S(1)}) custom-call(f32[512,128]{1,0:T(8,128)S(1)} %get-tuple-element.42.refs_0_, bf16[512,128]{1,0:T(8,128)(2,1)S(1)} %collective-permute-done.5.refs_1_, bf16[1280,512]{1,0:T(8,128)(2,1)S(1)} %get-tuple-element.47.refs_2_, ...), custom_call_target="tpu_custom_call" | custom-call | flops 335544320 | bytes 1966080 | tf_op jit(solution)/shard_map/pallas_call | solution.py:77
  39.7 1.0 %collective-permute-start.8 = (bf16[256,128]{1,0:T(8,128)(2,1)S(1)}, bf16[256,128]{1,0:T(8,128)(2,1)S(1)}, u32[]{:S(2)}, u32[]{:S(2)}) collective-permute-start(bf16[256,128]{1,0:T(8,128)(2,1)S(1)} %get-tuple-element.49), channel_id=1, source_target_pairs={{0,4},{1,5},{2,6},{3,7},{4,0},{5,1},{6,2},{7,3},{8,12},{9,13},{10,... | collective-permute-start | bytes 196616 | tf_op jit(solution)/shard_map/ppermute | solution.py:21
  40.7 2.2 %shard_map.82 = (f32[1024,128]{1,0:T(8,128)S(1)}, bf16[1024,512]{1,0:T(8,128)(2,1)S(1)}) custom-call(bf16[768,512]{1,0:T(8,128)(2,1)S(1)} %get-tuple-element.44.refs_0_.mine, bf16[384,512]{1,0:T(8,128)(2,1)S(1)} %collective-permute-done.6.refs_1_.near_ref, bf16[384,512]{1,0:T(8,128)(2,1)S(1)} %collective-permute-done.7.refs_2_.far_ref, ...), custom_call_target="tpu_custom_call" | custom-call | flops 2684354560 | bytes 7864320 | tf_op jit(solution)/shard_map/pallas_call | solution.py:77
  42.9 1.2 %collective-permute-done.8.other_ref = bf16[256,128]{1,0:T(8,128)(2,1)S(1)} collective-permute-done((bf16[256,128]{1,0:T(8,128)(2,1)S(1)}, bf16[256,128]{1,0:T(8,128)(2,1)S(1)}, u32[]{:S(2)}, u32[]{:S(2)}) %collective-permute-start.8) | collective-permute-done | bytes 65568 | tf_op jit(solution)/shard_map/ppermute | solution.py:21
  44.0 1.4 %shard_map.83 = bf16[1024,128]{1,0:T(8,128)(2,1)} custom-call(bf16[256,128]{1,0:T(8,128)(2,1)S(1)} %collective-permute-done.8.other_ref, f32[256,128]{1,0:T(8,128)S(1)} %get-tuple-element.50.c_ref, bf16[128,512]{1,0:T(8,128)(2,1)S(1)} %collective-permute-done.9.near_ref, bf16[128,512]{1,0:T(8,128)(2,1)S(1)} %collective-permute-done.10.far_ref, ...), custom_call_target="tpu_custom_call" | custom-call | flops 268435456 | bytes 2031616 | tf_op jit(solution)/shard_map/pallas_call | solution.py:77
  (21 shorter events, 0.1 us)
Async XLA Ops:
  2.3 20.2 %copy-start = (bf16[1,1,1024,128]{3,2,1,0:T(8,128)(2,1)S(1)}, bf16[1,1,1024,128]{3,2,1,0:T(8,128)(2,1)}, u32[]{:S(2)}) copy-start(bf16[1,1,1024,128]{3,2,1,0:T(8,128)(2,1)} %param.9) | copy-start | bytes 786436
  2.3 20.2 %copy-start.1 = (bf16[1,1,1024,128]{3,2,1,0:T(8,128)(2,1)S(1)}, bf16[1,1,1024,128]{3,2,1,0:T(8,128)(2,1)}, u32[]{:S(2)}) copy-start(bf16[1,1,1024,128]{3,2,1,0:T(8,128)(2,1)} %param.8) | copy-start | bytes 786436
  2.3 20.2 %copy-start.3 = (s32[4,4]{1,0:T(4,128)S(1)}, s32[4,4]{1,0:T(4,128)}, u32[]{:S(2)}) copy-start(s32[4,4]{1,0:T(4,128)} %start_ref.5) | copy-start | bytes 196
  2.4 20.2 %copy-start.4 = (s32[4,4]{1,0:T(4,128)S(1)}, s32[4,4]{1,0:T(4,128)}, u32[]{:S(2)}) copy-start(s32[4,4]{1,0:T(4,128)} %count_ref.1) | copy-start | bytes 196
  2.4 20.2 %copy-start.5 = (f32[4,4]{1,0:T(4,128)S(1)}, f32[4,4]{1,0:T(4,128)}, u32[]{:S(2)}) copy-start(f32[4,4]{1,0:T(4,128)} %strength_ref.1) | copy-start | bytes 196
  2.4 2.5 %collective-permute-start.4 = (bf16[768,512]{1,0:T(8,128)(2,1)S(1)}, bf16[768,512]{1,0:T(8,128)(2,1)S(1)}, u32[]{:S(2)}, u32[]{:S(2)}) collective-permute-start(bf16[768,512]{1,0:T(8,128)(2,1)S(1)} %get-tuple-element.40.refs_0_), channel_id=1, source_target_pairs={{0,1},{1,0},{2,3},{3,2},{4,5},{5,4},{6,7},{7,6},{8,9},{9,8},{10,11... | collective-permute-start | bytes 2359304 | tf_op jit(solution)/shard_map/ppermute | solution.py:21
  5.8 12.3 %collective-permute-start.6 = (bf16[384,512]{1,0:T(8,128)(2,1)S(1)}, bf16[384,512]{1,0:T(8,128)(2,1)S(1)}, u32[]{:S(2)}, u32[]{:S(2)}) collective-permute-start(bf16[384,512]{1,0:T(8,128)(2,1)S(1)} %get-tuple-element.45), channel_id=1, source_target_pairs={{0,2},{1,3},{2,0},{3,1},{4,6},{5,7},{6,4},{7,5},{8,10},{9,11},{10,... | collective-permute-start | bytes 1179656 | tf_op jit(solution)/shard_map/ppermute | solution.py:21
  18.1 15.9 %collective-permute-start.7 = (bf16[384,512]{1,0:T(8,128)(2,1)S(1)}, bf16[384,512]{1,0:T(8,128)(2,1)S(1)}, u32[]{:S(2)}, u32[]{:S(2)}) collective-permute-start(bf16[384,512]{1,0:T(8,128)(2,1)S(1)} %collective-permute-done.6.refs_1_.near_ref), channel_id=1, source_target_pairs={{0,1},{1,0},{2,3},{3,2},{4,5},{5,4},{6,7},{7,6},{8,9},{9,8},{10,11... | collective-permute-start | bytes 1179656 | tf_op jit(solution)/shard_map/ppermute | solution.py:21
  18.1 6.6 %collective-permute-start = (bf16[256,128]{1,0:T(8,128)(2,1)S(1)}, bf16[256,128]{1,0:T(8,128)(2,1)S(1)}, u32[]{:S(2)}, u32[]{:S(2)}) collective-permute-start(bf16[256,128]{1,0:T(8,128)(2,1)S(1)} %get-tuple-element.36), channel_id=1, source_target_pairs={{0,8},{8,0},{16,24},{24,16},{1,9},{9,1},{17,25},{25,17},{2,10},{10... | collective-permute-start | bytes 196616 | tf_op jit(solution)/shard_map/ppermute | solution.py:21
  20.0 7.0 %collective-permute-start.1 = (bf16[256,128]{1,0:T(8,128)(2,1)S(1)}, bf16[256,128]{1,0:T(8,128)(2,1)S(1)}, u32[]{:S(2)}, u32[]{:S(2)}) collective-permute-start(bf16[256,128]{1,0:T(8,128)(2,1)S(1)} %get-tuple-element.37), channel_id=1, source_target_pairs={{0,16},{8,24},{16,0},{24,8},{1,17},{9,25},{17,1},{25,9},{2,18},{10... | collective-permute-start | bytes 196616 | tf_op jit(solution)/shard_map/ppermute | solution.py:21
  22.5 6.1 %collective-permute-start.2 = (bf16[256,128]{1,0:T(8,128)(2,1)S(1)}, bf16[256,128]{1,0:T(8,128)(2,1)S(1)}, u32[]{:S(2)}, u32[]{:S(2)}) collective-permute-start(bf16[256,128]{1,0:T(8,128)(2,1)S(1)} %get-tuple-element.38), channel_id=1, source_target_pairs={{0,24},{8,16},{16,8},{24,0},{1,25},{9,17},{17,9},{25,1},{2,26},{10... | collective-permute-start | bytes 196616 | tf_op jit(solution)/shard_map/ppermute | solution.py:21
  30.3 1.6 %collective-permute-start.3 = (f32[512,128]{1,0:T(8,128)S(1)}, f32[512,128]{1,0:T(8,128)S(1)}, u32[]{:S(2)}, u32[]{:S(2)}) collective-permute-start(f32[512,128]{1,0:T(8,128)S(1)} %get-tuple-element.39.refs_0_.sent_ref), channel_id=1, source_target_pairs={{0,1},{1,0},{2,3},{3,2},{4,5},{5,4},{6,7},{7,6},{8,9},{9,8},{10,11... | collective-permute-start | bytes 786440 | tf_op jit(solution)/shard_map/ppermute | solution.py:21
  32.5 6.2 %collective-permute-start.5 = (bf16[512,128]{1,0:T(8,128)(2,1)S(1)}, bf16[512,128]{1,0:T(8,128)(2,1)S(1)}, u32[]{:S(2)}, u32[]{:S(2)}) collective-permute-start(bf16[512,128]{1,0:T(8,128)(2,1)S(1)} %get-tuple-element.43), channel_id=1, source_target_pairs={{0,2},{1,3},{2,0},{3,1},{4,6},{5,7},{6,4},{7,5},{8,10},{9,11},{10,... | collective-permute-start | bytes 393224 | tf_op jit(solution)/shard_map/ppermute | solution.py:21
  34.3 6.4 %collective-permute-start.9 = (bf16[128,512]{1,0:T(8,128)(2,1)S(1)}, bf16[128,512]{1,0:T(8,128)(2,1)S(1)}, u32[]{:S(2)}, u32[]{:S(2)}) collective-permute-start(bf16[128,512]{1,0:T(8,128)(2,1)S(1)} %get-tuple-element.51), channel_id=1, source_target_pairs={{0,4},{1,5},{2,6},{3,7},{4,0},{5,1},{6,2},{7,3},{8,12},{9,13},{10,... | collective-permute-start | bytes 393224 | tf_op jit(solution)/shard_map/ppermute | solution.py:21
  38.0 2.7 %copy-start.2 = (bf16[1,256,256]{2,1,0:T(8,128)(2,1)S(1)}, bf16[1,256,256]{2,1,0:T(8,128)(2,1)}, u32[]{:S(2)}) copy-start(bf16[1,256,256]{2,1,0:T(8,128)(2,1)} %param.10) | copy-start | bytes 393220
  39.7 4.3 %collective-permute-start.8 = (bf16[256,128]{1,0:T(8,128)(2,1)S(1)}, bf16[256,128]{1,0:T(8,128)(2,1)S(1)}, u32[]{:S(2)}, u32[]{:S(2)}) collective-permute-start(bf16[256,128]{1,0:T(8,128)(2,1)S(1)} %get-tuple-element.49), channel_id=1, source_target_pairs={{0,4},{1,5},{2,6},{3,7},{4,0},{5,1},{6,2},{7,3},{8,12},{9,13},{10,... | collective-permute-start | bytes 196616 | tf_op jit(solution)/shard_map/ppermute | solution.py:21
  40.7 3.4 %collective-permute-start.10 = (bf16[128,512]{1,0:T(8,128)(2,1)S(1)}, bf16[128,512]{1,0:T(8,128)(2,1)S(1)}, u32[]{:S(2)}, u32[]{:S(2)}) collective-permute-start(bf16[128,512]{1,0:T(8,128)(2,1)S(1)} %collective-permute-done.9.near_ref), channel_id=1, source_target_pairs={{0,1},{1,0},{2,3},{3,2},{4,5},{5,4},{6,7},{7,6},{8,9},{9,8},{10,11... | collective-permute-start | bytes 393224 | tf_op jit(solution)/shard_map/ppermute | solution.py:21

commit v9 on v8

--- a/solution.py
+++ b/solution.py
@@ -175,109 +175,171 @@
 
     half = 3 * layer // 2
     final = levels - 1
-    plans, members, totals = [], None, maps
-    for level in range(final):
-        near = swapped(totals if level == 0 else send, "slab", 1 << level)
-        far = None if level == 0 else swapped(near, "slab", 1)
-        closing = level == final - 1
-
-        def group(*refs, level=level, closing=closing):
-            refs = list(refs)
-            mine, near_ref = refs[:2]
-            plan, member, send_ref = refs[-3:]
-            total = None if closing else refs[-4]
+    plans = []
+
+    def sides(mine, theirs, after):
+        own = [mine[rows_of[k]] for k in range(3)]
+        its = [theirs[rows_of[k]] for k in range(3)]
+        left = [jnp.where(after, b, a) for a, b in zip(own, its)]
+        right = [jnp.where(after, a, b) for a, b in zip(own, its)]
+        return left, right
+
+    def joined(near_ref, far_ref):
+        first, a, b = place(0), near_ref[...], far_ref[...]
+        return jnp.concatenate([jnp.where(first, b, a), jnp.where(first, a, b)], axis=0)
+
+    def reflected(left, right):
+        bounce = mapped(right[2], left[0]).astype(bf16)
+        return bounce, (left[2].astype(f32) + mapped(left[1], bounce)).astype(bf16)
+
+    cut = layer // 2
+    parts = [((2 * cut, 2 * layer), bf16), ((cut, 2 * layer), bf16)]
+    direct_close = final == 2
+
+    def pack(grown, x_ref, y_ref):
+        later = place(final - 1)
+        x_ref[:cut] = grown[0]
+        x_ref[cut:] = jnp.where(later, grown[2], grown[1])
+        y_ref[...] = jnp.where(later, grown[1], grown[2])
+
+    def halved(block):
+        return jnp.where(place(0), block[cut:], block[:cut])
+
+    def group0(mine, near_ref, plan, *sends):
+        def fill(left, right, begin):
+            rows_in = [slice(k * layer + begin, k * layer + begin + cut) for k in range(3)]
+            plan[rows_of[0]], plan[rows_of[1]] = right[rows_of[0]], right[rows_of[2]]
+            plan[rows_of[2]] = left[rows_of[1]]
+            bounce = mapped(right[rows_of[2]], left[rows_of[0]]).astype(bf16)
+            if direct_close:
+                b_rows = left[rows_in[1]]
+                grown = (
+                    mapped(right[rows_in[0]], left[rows_of[0]]).astype(bf16),
+                    mapped(b_rows, right[rows_of[1]]).astype(bf16),
+                    (left[rows_in[2]].astype(f32) + mapped(b_rows, bounce)).astype(bf16),
+                )
+                pack(grown, *sends)
+                return
+            whole = jnp.concatenate(
+                [
+                    mapped(right[rows_of[0]], left[rows_of[0]]).astype(bf16),
+                    mapped(left[rows_of[1]], right[rows_of[1]]).astype(bf16),
+                    (
+                        left[rows_of[2]].astype(f32) + mapped(left[rows_of[1]], bounce)
+                    ).astype(bf16),
+                ],
+                axis=0,
+            )
+            sends[0][...] = whole[half:] if begin else whole[:half]
+
+        pl.when(place(0))(lambda: fill(near_ref, mine, cut))
+        pl.when(~place(0))(lambda: fill(mine, near_ref, 0))
+
+    def grow0(mine, near_ref, total, member):
+        after = place(0)
+        left, right = sides(mine, near_ref, after)
+        bounce, e_total = reflected(left, right)
+        total[rows_of[0]] = mapped(right[0], left[0]).astype(bf16)
+        total[rows_of[1]] = mapped(left[1], right[1]).astype(bf16)
+        total[rows_of[2]] = e_total
+        row = lax.broadcasted_iota(jnp.int32, one_map, 0)
+        col = lax.broadcasted_iota(jnp.int32, one_map, 1)
+        unit = (row == col).astype(f32).astype(bf16)
+        member[rows_of[0]] = jnp.where(after, left[0], unit)
+        member[rows_of[1]] = jnp.where(after, unit, right[1])
+        member[rows_of[2]] = jnp.where(after, jnp.zeros_like(bounce), bounce)
+
+    near = swapped(maps, "slab", 1)
+    sent_half = [((half, 2 * layer), bf16)]
+    plan, *sends = call(
+        group0, [(triple, bf16)] + (parts if direct_close else sent_half), (maps, near),
+        32 * layer**3,
+    )
+    totals, members = call(grow0, [(triple, bf16)] * 2, (maps, near), 64 * layer**3)
+    plans.append(plan)
+
+    for level in range(1, final - 1):
+        near = swapped(sends[0], "slab", 1 << level)
+        far = swapped(near, "slab", 1)
+        to_close = level == final - 2
+
+        def group(
+            mine, near_ref, far_ref, old, total, plan, member, *refs, level=level, to_close=to_close
+        ):
             after = place(level)
-            if level == 0:
-                theirs = near_ref[...]
+            left, right = sides(mine, joined(near_ref, far_ref), after)
+            p, q, r = (old[rows_of[k]] for k in range(3))
+            plan_rows = (right[0], right[2], p, left[1], jnp.where(after, r, q))
+            for k, part in enumerate(plan_rows):
+                plan[rows_of[k]] = part
+            bounce, e_total = reflected(left, right)
+            member[rows_of[0]] = member_before(after, p, left[0])
+            member[rows_of[1]] = member_behind(after, q, right[1])
+            member[rows_of[2]] = member_turned(after, q, r, left[0], bounce)
+            grown = (
+                mapped(right[0], left[0]).astype(bf16),
+                mapped(left[1], right[1]).astype(bf16),
+                e_total,
+            )
+            whole = jnp.concatenate(grown, axis=0)
+            total[...] = whole
+            if to_close:
+                pack([halved(g) for g in grown], *refs)
             else:
-                first = place(0)
-                a, b = near_ref[...], refs[2][...]
-                theirs = jnp.concatenate(
-                    [jnp.where(first, b, a), jnp.where(first, a, b)], axis=0
-                )
-                old = refs[3]
-            own_a, own_b, own_e = (mine[rows_of[k]] for k in range(3))
-            its_a, its_b, its_e = (theirs[rows_of[k]] for k in range(3))
-            a_left = jnp.where(after, its_a, own_a)
-            a_right = jnp.where(after, own_a, its_a)
-            b_left = jnp.where(after, its_b, own_b)
-            b_right = jnp.where(after, own_b, its_b)
-            e_left = jnp.where(after, its_e, own_e)
-            e_right = jnp.where(after, own_e, its_e)
-            plan[rows_of[0]] = a_right
-            plan[rows_of[1]] = e_right
-            if level:
-                plan[rows_of[2]] = old[rows_of[0]]
-                plan[rows_of[3]] = b_left
-                plan[rows_of[4]] = jnp.where(after, old[rows_of[2]], old[rows_of[1]])
-            else:
-                plan[rows_of[2]] = b_left
-
-            def reflected():
-                bounce = mapped(e_right, a_left).astype(bf16)
-                return bounce, (e_left.astype(f32) + mapped(b_left, bounce)).astype(bf16)
-
-            if level == 0:
-                bounce, e_total = reflected()
-                row = lax.broadcasted_iota(jnp.int32, one_map, 0)
-                col = lax.broadcasted_iota(jnp.int32, one_map, 1)
-                unit = (row == col).astype(f32).astype(bf16)
-                ends = (
-                    jnp.where(after, a_left, unit),
-                    jnp.where(after, unit, b_right),
-                    jnp.where(after, jnp.zeros_like(bounce), bounce),
-                )
-            elif not closing:
-                bounce, e_total = reflected()
-                q, r = old[rows_of[1]], old[rows_of[2]]
-                ends = (
-                    member_before(after, old[rows_of[0]], a_left),
-                    member_behind(after, q, b_right),
-                    member_turned(after, q, r, a_left, bounce),
-                )
-            if not closing:
-                grown = (
-                    mapped(a_right, a_left).astype(bf16),
-                    mapped(b_left, b_right).astype(bf16),
-                    e_total,
-                )
-                for k in range(3):
-                    total[rows_of[k]] = grown[k]
-                whole = jnp.concatenate(grown, axis=0)
-                send_ref[...] = jnp.where(place(0), whole[half:], whole[:half])
-                for k, end in enumerate(ends):
-                    member[rows_of[k]] = end
-                return
-
-            @pl.when(place(final))
-            def _():
-                bounce, e_total = reflected()
-                member[...] = bounce
-                cut = layer // 2
-                send_ref[...] = jnp.where(place(0), e_total[cut:], e_total[:cut])
-
-            @pl.when(~place(final))
-            def _():
-                member[...] = jnp.zeros(one_map, bf16)
-                send_ref[...] = jnp.zeros((layer // 2, 2 * layer), bf16)
-
-        plan_size = (5 * layer if level else 3 * layer, 2 * layer)
-        args = (totals, near) if level == 0 else (totals, near, far, members)
-        *grown, plan, member, send = call(
+                refs[0][...] = jnp.where(place(0), whole[half:], whole[:half])
+
+        totals, plan, members, *sends = call(
             group,
-            [(triple, bf16)] * (not closing)
-            + [
-                (plan_size, bf16),
-                (one_map if closing else triple, bf16),
-                ((layer // 2 if closing else half, 2 * layer), bf16),
-            ],
-            args,
+            [
+                (triple, bf16),
+                ((5 * layer, 2 * layer), bf16),
+                (triple, bf16),
+            ]
+            + (parts if to_close else sent_half),
+            (totals, near, far, members),
             64 * layer**3,
         )
         plans.append(plan)
-        if not closing:
-            totals, members = grown[0], member
-
+
+    near_x = swapped(sends[0], "slab", 1 << (final - 1))
+    near_y = swapped(sends[1], "slab", 1 << (final - 1))
+    far_x = swapped(near_x, "slab", 1)
+    far_y = swapped(near_y, "slab", 1)
+
+    def theirs(near_ref, far_ref, begin):
+        first, a, b = place(0), near_ref[begin : begin + cut], far_ref[begin : begin + cut]
+        return jnp.concatenate([jnp.where(first, b, a), jnp.where(first, a, b)], axis=0)
+
+    def reflect(mine, near_ref, far_ref, ny_ref, bounce_ref, send_ref):
+        after, right = place(final - 1), place(final)
+
+        @pl.when(right & after)
+        def _():
+            bounce = mapped(mine[rows_of[2]], theirs(near_ref, far_ref, 0)).astype(bf16)
+            bounce_ref[...] = bounce
+            send_ref[...] = (
+                ny_ref[...].astype(f32) + mapped(near_ref[cut:], bounce)
+            ).astype(bf16)
+
+        @pl.when(right & ~after)
+        def _():
+            bounce = mapped(theirs(near_ref, far_ref, cut), mine[rows_of[0]]).astype(bf16)
+            bounce_ref[...] = bounce
+            send_ref[...] = (
+                halved(mine[rows_of[2]]).astype(f32) + mapped(halved(mine[rows_of[1]]), bounce)
+            ).astype(bf16)
+
+        @pl.when(~right)
+        def _():
+            bounce_ref[...] = jnp.zeros(bounce_ref.shape, bf16)
+            send_ref[...] = jnp.zeros(send_ref.shape, bf16)
+
+    bounced, send = call(
+        reflect,
+        [(one_map, bf16), ((cut, 2 * layer), bf16)],
+        (totals, near_x, far_x, near_y),
+        24 * layer**3,
+    )
     e_near = swapped(send, "slab", 1 << final)
     e_far = swapped(e_near, "slab", 1)
 
@@ -290,20 +352,63 @@
             other = swapped(sent, "slab", 1 << level)
             closing = level == final - 1
 
-            def step(*refs, level=level, closing=closing):
-                mine, other_ref, plan = refs[:3]
+            def step(mine, other_ref, *refs, level=level, closing=closing):
                 total_ref, sent_ref, reach_ref = refs[-3:]
                 after = place(level)
                 own = [mine[w] for w in ways]
                 its = [other_ref[w].astype(f32) for w in ways]
                 c_left, c_right = jnp.where(after, its[0], own[0]), jnp.where(after, own[0], its[0])
                 f_left, f_right = jnp.where(after, its[1], own[1]), jnp.where(after, own[1], its[1])
+                if closing:
+                    mine_ref, near_ref, far_ref, old, so_far = refs[:5]
+                    right = place(final)
+
+                    @pl.when(~after)
+                    def _():
+                        e_right = theirs(near_ref, far_ref, cut)
+                        back = f_right + mapped(e_right, c_left)
+                        reach_ref[ways[0]] = so_far[ways[0]]
+                        reach_ref[ways[1]] = so_far[ways[1]] + mapped(old[rows_of[1]], back)
+
+                        @pl.when(right)
+                        def _():
+                            f_new = f_left + mapped(mine_ref[rows_of[1]], back)
+                            total_ref[...] = f_new
+                            sent_ref[...] = f_new.astype(bf16)
+
+                        @pl.when(~right)
+                        def _():
+                            c_new = c_right + mapped(theirs(near_ref, far_ref, 0), c_left)
+                            total_ref[...] = c_new
+                            sent_ref[...] = c_new.astype(bf16)
+
+                    @pl.when(after)
+                    def _():
+                        reach_ref[ways[0]] = so_far[ways[0]] + mapped(old[rows_of[0]], c_left)
+                        reach_ref[ways[1]] = so_far[ways[1]] + mapped(old[rows_of[2]], c_left)
+
+                        @pl.when(right)
+                        def _():
+                            back = f_right + mapped(mine_ref[rows_of[2]], c_left)
+                            b_left = theirs(near_ref, far_ref, cut)
+                            f_new = f_left + mapped(b_left, back)
+                            total_ref[...] = f_new
+                            sent_ref[...] = f_new.astype(bf16)
+
+                        @pl.when(~right)
+                        def _():
+                            c_new = c_right + mapped(mine_ref[rows_of[0]], c_left)
+                            total_ref[...] = c_new
+                            sent_ref[...] = c_new.astype(bf16)
+
+                    return
+                plan = refs[0]
                 spread = mapped(plan[: (3 if level else 2) * layer], c_left)
                 back = f_right + spread[ways[1]]
                 c_new = c_right + spread[ways[0]]
                 f_new = f_left + mapped(plan[rows_of[3 if level else 2]], back)
                 if level:
-                    so_far = refs[3]
+                    so_far = refs[1]
                     more = mapped(plan[rows_of[4]], jnp.where(after, c_left, back))
                     z = so_far[ways[0]] + jnp.where(after, spread[rows_of[2]], 0.0)
                     u = so_far[ways[1]] + more
@@ -312,21 +417,22 @@
                     u = jnp.where(after, jnp.zeros_like(back), back)
                 reach_ref[ways[0]] = z
                 reach_ref[ways[1]] = u
-                if closing:
-                    total_ref[...] = c_new
-                    sent_ref[...] = jnp.where(place(final), f_new, c_new).astype(bf16)
-                else:
-                    total_ref[ways[0]] = c_new
-                    total_ref[ways[1]] = f_new
-                    sent_ref[ways[0]] = c_new.astype(bf16)
-                    sent_ref[ways[1]] = f_new.astype(bf16)
+                total_ref[ways[0]] = c_new
+                total_ref[ways[1]] = f_new
+                sent_ref[ways[0]] = c_new.astype(bf16)
+                sent_ref[ways[1]] = f_new.astype(bf16)
 
             size = (layer, width) if closing else pair
-            args = (total, other, plans[level]) + ((reach,) if level else ())
+            if closing:
+                args = (total, other, totals, near_x, far_x, members, reach)
+            else:
+                args = (total, other, plans[level]) + ((reach,) if level else ())
             total, sent, reach = call(
                 step, [(size, f32), (size, bf16), (pair, f32)], args, 40 * layer * layer * width
             )
         return total, swapped(sent, "slab", 1 << final), reach
+
+    blocks = (low - layer) // layer
 
     def fetch(green_ref, held_ref, sem, spots):
         copies = [
@@ -340,9 +446,11 @@
 
     def prepare(
         green_ref, inj_ref, panel_ref, start_ref, count_ref, strength_ref,
-        ends_ref, acc_ref, weight_ref, sem,
+        ends_ref, mid_ref, acc_ref, weight_ref, sem, sem_mid,
     ):
         copies = fetch(green_ref, ends_ref, sem, (pl.ds(0, layer), pl.ds(low, layer)))
+        spots = [pl.ds((i + 1) * layer, layer) for i in range(blocks)]
+        copies += fetch(green_ref, mid_ref, sem_mid, spots)
         me = lax.axis_index("energy")
         row = lax.broadcasted_iota(jnp.int32, (span, width), 0)
         acc_ref[...] = inj_ref[...].astype(f32)
@@ -358,17 +466,18 @@
         for copy in copies:
             copy.wait()
 
-    ends, acc, weights = call(
+    ends, mid, acc, weights = call(
         prepare,
         [
             ((2, 2, layer, norb), bf16),
+            ((2, blocks, layer, norb), bf16),
             ((norb, width), f32),
             ((energies - 1, span, width), f32),
         ],
         (far_green, injection[0, 0], panel, block_start, block_count, strength),
         0,
         {0: pltpu.HBM, 3: SMEM, 4: SMEM, 5: SMEM},
-        [pltpu.SemaphoreType.DMA((2, 2))],
+        [pltpu.SemaphoreType.DMA((2, 2)), pltpu.SemaphoreType.DMA((blocks, 2))],
     )
 
     def load(start_ref, acc_ref, weight_ref, ends_ref, turn_ref, *refs):
@@ -398,22 +507,6 @@
     )
     c_total, arrived, reach = scan(sent)
 
-    blocks = (low - layer) // layer
-
-    def fetch_mid(green_ref, hint_ref, mid_ref, sem):
-        spots = [pl.ds((i + 1) * layer, layer) for i in range(blocks)]
-        for copy in fetch(green_ref, mid_ref, sem, spots):
-            copy.wait()
-
-    (mid,) = call(
-        fetch_mid,
-        [((2, blocks, layer, norb), bf16)],
-        (far_green, direct_low),
-        0,
-        {0: pltpu.HBM, 1: pl.ANY},
-        [pltpu.SemaphoreType.DMA((blocks, 2))],
-    )
-
     def direct_step(mid_ref, source_ref, spun_ref, out_ref):
         for i in range(blocks):
             out_ref[i] = dot(mid_ref[0, i], source_ref[...]) + dot(mid_ref[1, i], spun_ref[...])
@@ -426,15 +519,11 @@
     )
 
     def weights(
-        mine, near_ref, far_ref, old, bounce_ref, reach_ref, ends_ref, mid_ref, coup_ref,
-        sent_ref, low_ref, direct_ref, base_ref, wide_ref,
+        mine, near_ref, far_ref, ny_ref, fy_ref, old, bounce_ref, hint_ref, ends_ref, mid_ref,
+        coup_ref, wide_ref,
     ):
-        after, first, right = place(final - 1), place(0), place(final)
+        after, right = place(final - 1), place(final)
         c = coup_ref[...]
-        incoming = reach_ref[ways[0]].astype(bf16)
-        spun_z = turned(incoming.astype(f32)).astype(bf16)
-        outgoing = fine(c, reach_ref[ways[1]]).astype(bf16)
-        spun_u = turned(outgoing.astype(f32)).astype(bf16)
         tail = slice(low, norb)
 
         def held_rows(i):
@@ -449,8 +538,7 @@
 
         @pl.when(right)
         def _():
-            its_a = jnp.where(first, far_ref[:layer], near_ref[:layer])
-            a_left = jnp.where(after, its_a, mine[rows_of[0]])
+            a_left = jnp.where(after, theirs(near_ref, far_ref, 0), mine[rows_of[0]])
             p, spun_p = twice(member_before(after, old[rows_of[0]], a_left))
             r = member_turned(after, old[rows_of[1]], old[rows_of[2]], a_left, bounce_ref[...])
             s, spun_s = twice(dot(c, r).astype(bf16))
@@ -465,9 +553,7 @@
 
         @pl.when(~right)
         def _():
-            a, b = near_ref[...], far_ref[...]
-            theirs = jnp.concatenate([jnp.where(first, b, a), jnp.where(first, a, b)], axis=0)
-            b_right = jnp.where(after, mine[rows_of[1]], theirs[rows_of[1]])
+            b_right = jnp.where(after, mine[rows_of[1]], theirs(ny_ref, fy_ref, 0))
             q = member_behind(after, old[rows_of[1]], b_right)
             s, spun_s = twice(dot(c, q).astype(bf16))
             for i in range(blocks + 2):
@@ -476,30 +562,39 @@
                     dot(real[:, tail], s) + dot(imag[:, tail], spun_s)
                 ).astype(bf16)
 
+    (last_map,) = call(
+        weights,
+        [((norb, 2 * layer), bf16)],
+        (totals, near_x, far_x, near_y, far_y, members, bounced, reach, ends, mid, coup),
+        32 * norb * layer * layer,
+    )
+
+    def based(reach_ref, ends_ref, mid_ref, coup_ref, sent_ref, low_ref, direct_ref, base_ref):
+        incoming = reach_ref[ways[0]].astype(bf16)
+        spun_z = turned(incoming.astype(f32)).astype(bf16)
+        outgoing = fine(coup_ref[...], reach_ref[ways[1]]).astype(bf16)
+        spun_u = turned(outgoing.astype(f32)).astype(bf16)
+        tail = slice(low, norb)
         for i in range(blocks + 2):
-            real, imag = held_rows(i)
             if i == 0:
-                direct = sent_ref[ways[1]]
+                direct, held = sent_ref[ways[1]], [ends_ref.at[k, 0] for k in range(2)]
             elif i > blocks:
-                direct = low_ref[...]
+                direct, held = low_ref[...], [ends_ref.at[k, 1] for k in range(2)]
             else:
-                direct = direct_ref[i - 1]
+                direct, held = direct_ref[i - 1], [mid_ref.at[k, i - 1] for k in range(2)]
             base_ref[i * layer : (i + 1) * layer] = (
                 direct
-                + dot(real[:, :layer], incoming)
-                + dot(imag[:, :layer], spun_z)
-                + dot(real[:, tail], outgoing)
-                + dot(imag[:, tail], spun_u)
+                + dot(held[0][:, :layer], incoming)
+                + dot(held[1][:, :layer], spun_z)
+                + dot(held[0][:, tail], outgoing)
+                + dot(held[1][:, tail], spun_u)
             )
 
-    base, last_map = call(
-        weights,
-        [((norb, width), f32), ((norb, 2 * layer), bf16)],
-        (
-            totals, near, far, members, member, reach, ends, mid, coup,
-            sent, direct_low, direct_mid,
-        ),
-        16 * norb * layer * (width + 2 * layer),
+    (base,) = call(
+        based,
+        [((norb, width), f32)],
+        (reach, ends, mid, coup, sent, direct_low, direct_mid),
+        16 * norb * layer * width,
     )
 
     def finish(other_ref, c_ref, near_ref, far_ref, base_ref, wide_ref, out_ref, kept, sem):

time: 45.6 us -> 37 us (0.81)
  waiting for transfers between devices: 17.9 us -> 9.94 us
  Pallas kernels: 14.7 us -> 14 us
    ppermute x11 -> x13, waiting for transfers between devices: 17.9 us -> 9.94 us  [swapped(): return lax.ppermute(block, axis, [(i, i ^ mask) for i in range(count)])]
    pallas_call x11 -> x12, Pallas kernels: 14.7 us -> 14 us  [call(): pl.pallas_call(kernel, out_shape=shapes, in_specs=specs, out_specs=[pl.Bl...]
    ppermute x11 -> x13, starting transfers between devices: 12.6 us -> 12.8 us  [swapped(): return lax.ppermute(block, axis, [(i, i ^ mask) for i in range(count)])]
  transfers between devices with their start and end apart: 11 -> 13, of which waited for: 6 -> 7; matrix products, arithmetic and copies ran while one was open for 0% -> 0% of each run, Pallas kernels for 22% -> 26%
where the time goes in v9:
time: 37 us; the launch traced here: 36.9 us
  Pallas kernels  14 us (38%)
  starting transfers between devices  12.8 us (35%)
  waiting for transfers between devices  9.94 us (27%)
    pallas_call x12, Pallas kernels, call(): pl.pallas_call(kernel, out_shape=shapes, in_specs=specs, out_specs=[pl.Bl...  14 us
    ppermute x13, starting transfers between devices, swapped(): return lax.ppermute(block, axis, [(i, i ^ mask) for i in range(count)])  12.8 us
    ppermute x13, waiting for transfers between devices, swapped(): return lax.ppermute(block, axis, [(i, i ^ mask) for i in range(count)])  9.94 us
  transfers between devices with their start and end apart: 13, of which 7 were waited for; matrix products, arithmetic and copies ran while one was open for 0% of the time, Pallas kernels for 26%

profile of v9, /device:TPU:0, one launch (start us, length us, event | category | flops | bytes accessed | tf_op | source)
XLA Modules:
  0.0 36.9 jit_solution(5433178017550715449)
XLA Ops:
  0.0 2.3 %shard_map.74 = (bf16[768,512]{1,0:T(8,128)(2,1)S(1)}, bf16[256,256]{1,0:T(8,128)(2,1)S(1)}, bf16[256,128]{1,0:T(8,128)(2,1)S(1)}, bf16[256,128]{1,0:T(8,128)(2,1)S(1)}, bf16[256,128]{1,0:T(8,128)(2,1)S(1)}) custom-call(bf16[2,1024,1024]{2,1,0:T(8,128)(2,1)} %bitcast.11, bf16[256,256]{1,0:T(8,128)(2,1)} %bitcast.5, s32[4,4]{1,0:T(4,128)} %start_ref.5, ...), custom_call_target="tpu_custom_call" | custom-call | flops 134217728 | bytes 4587584 | tf_op jit(solution)/shard_map/pallas_call | solution.py:77
  2.4 0.6 %collective-permute-start.4 = (bf16[768,512]{1,0:T(8,128)(2,1)S(1)}, bf16[768,512]{1,0:T(8,128)(2,1)S(1)}, u32[]{:S(2)}, u32[]{:S(2)}) collective-permute-start(bf16[768,512]{1,0:T(8,128)(2,1)S(1)} %get-tuple-element.39.mine), channel_id=1, source_target_pairs={{0,1},{1,0},{2,3},{3,2},{4,5},{5,4},{6,7},{7,6},{8,9},{9,8},{10,11... | collective-permute-start | bytes 2359304 | tf_op jit(solution)/shard_map/ppermute | solution.py:21
  2.9 1.9 %collective-permute-done.4.near_ref = bf16[768,512]{1,0:T(8,128)(2,1)S(1)} collective-permute-done((bf16[768,512]{1,0:T(8,128)(2,1)S(1)}, bf16[768,512]{1,0:T(8,128)(2,1)S(1)}, u32[]{:S(2)}, u32[]{:S(2)}) %collective-permute-start.4) | collective-permute-done | bytes 786464 | tf_op jit(solution)/shard_map/ppermute | solution.py:21
  4.9 0.6 %shard_map.76 = (bf16[768,512]{1,0:T(8,128)(2,1)S(1)}, bf16[256,512]{1,0:T(8,128)(2,1)S(1)}, bf16[128,512]{1,0:T(8,128)(2,1)S(1)}) custom-call(bf16[768,512]{1,0:T(8,128)(2,1)S(1)} %get-tuple-element.39.mine, bf16[768,512]{1,0:T(8,128)(2,1)S(1)} %collective-permute-done.4.near_ref), custom_call_target="tpu_custom_call" | custom-call | flops 536870912 | bytes 1572864 | tf_op jit(solution)/shard_map/pallas_call | solution.py:77
  5.4 2.9 %collective-permute-start.6 = (bf16[256,512]{1,0:T(8,128)(2,1)S(1)}, bf16[256,512]{1,0:T(8,128)(2,1)S(1)}, u32[]{:S(2)}, u32[]{:S(2)}) collective-permute-start(bf16[256,512]{1,0:T(8,128)(2,1)S(1)} %get-tuple-element.44), channel_id=1, source_target_pairs={{0,2},{1,3},{2,0},{3,1},{4,6},{5,7},{6,4},{7,5},{8,10},{9,11},{10,... | collective-permute-start | bytes 786440 | tf_op jit(solution)/shard_map/ppermute | solution.py:21
  8.3 1.6 %collective-permute-start = (bf16[256,128]{1,0:T(8,128)(2,1)S(1)}, bf16[256,128]{1,0:T(8,128)(2,1)S(1)}, u32[]{:S(2)}, u32[]{:S(2)}) collective-permute-start(bf16[256,128]{1,0:T(8,128)(2,1)S(1)} %get-tuple-element.35), channel_id=1, source_target_pairs={{0,8},{8,0},{16,24},{24,16},{1,9},{9,1},{17,25},{25,17},{2,10},{10... | collective-permute-start | bytes 196616 | tf_op jit(solution)/shard_map/ppermute | solution.py:21
  9.9 2.6 %collective-permute-start.1 = (bf16[256,128]{1,0:T(8,128)(2,1)S(1)}, bf16[256,128]{1,0:T(8,128)(2,1)S(1)}, u32[]{:S(2)}, u32[]{:S(2)}) collective-permute-start(bf16[256,128]{1,0:T(8,128)(2,1)S(1)} %get-tuple-element.36), channel_id=1, source_target_pairs={{0,16},{8,24},{16,0},{24,8},{1,17},{9,25},{17,1},{25,9},{2,18},{10... | collective-permute-start | bytes 196616 | tf_op jit(solution)/shard_map/ppermute | solution.py:21
  12.8 2.8 %shard_map.73 = (bf16[2,2,256,1024]{3,2,1,0:T(8,128)(2,1)S(1)}, bf16[2,2,256,1024]{3,2,1,0:T(8,128)(2,1)S(1)}, f32[1024,128]{1,0:T(8,128)S(1)}, f32[3,256,128]{2,1,0:T(8,128)S(1)}) custom-call(bf16[2,1024,1024]{2,1,0:T(8,128)(2,1)} %bitcast.12, bf16[1024,128]{1,0:T(8,128)(2,1)S(1)} %bitcast.10, bf16[1024,128]{1,0:T(8,128)(2,1)S(1)} %bitcast.9, ...), custom_call_target="tpu_custom_call" | custom-call | bytes 4718784 | tf_op jit(solution)/shard_map/pallas_call | solution.py:77
  15.6 1.6 %collective-permute-done.1.refs_1_ = bf16[256,128]{1,0:T(8,128)(2,1)S(1)} collective-permute-done((bf16[256,128]{1,0:T(8,128)(2,1)S(1)}, bf16[256,128]{1,0:T(8,128)(2,1)S(1)}, u32[]{:S(2)}, u32[]{:S(2)}) %collective-permute-start.1) | collective-permute-done | bytes 65568 | tf_op jit(solution)/shard_map/ppermute | solution.py:21
  17.2 1.4 %collective-permute-done.2.refs_2_ = bf16[256,128]{1,0:T(8,128)(2,1)S(1)} collective-permute-done((bf16[256,128]{1,0:T(8,128)(2,1)S(1)}, bf16[256,128]{1,0:T(8,128)(2,1)S(1)}, u32[]{:S(2)}, u32[]{:S(2)}) %collective-permute-start.2) | collective-permute-done | bytes 65568 | tf_op jit(solution)/shard_map/ppermute | solution.py:21
  18.6 1.7 %shard_map.75 = (bf16[1024,128]{1,0:T(8,128)(2,1)S(1)}, bf16[1024,128]{1,0:T(8,128)(2,1)S(1)}, f32[256,128]{1,0:T(8,128)S(1)}, f32[512,128]{1,0:T(8,128)S(1)}) custom-call(s32[4,4]{1,0:T(4,128)S(1)} %copy-done.3, f32[1024,128]{1,0:T(8,128)S(1)} %get-tuple-element.31.acc_ref, f32[3,256,128]{2,1,0:T(8,128)S(1)} %get-tuple-element.32.weight_ref, ...), custom_call_target="tpu_custom_call" | custom-call | flops 268435456 | bytes 3342400 | tf_op jit(solution)/shard_map/pallas_call | solution.py:77
  21.9 0.6 %shard_map.77 = (f32[512,128]{1,0:T(8,128)S(1)}, bf16[512,128]{1,0:T(8,128)(2,1)S(1)}, f32[512,128]{1,0:T(8,128)S(1)}) custom-call(f32[512,128]{1,0:T(8,128)S(1)} %get-tuple-element.38.mine.sent_ref, f32[512,128]{1,0:T(8,128)S(1)} %collective-permute-done.3.other_ref, bf16[768,512]{1,0:T(8,128)(2,1)S(1)} %get-tuple-element.40.refs_0_), custom_call_target="tpu_custom_call" | custom-call | flops 335544320 | bytes 1310720 | tf_op jit(solution)/shard_map/pallas_call | solution.py:77
  22.5 1.1 %collective-permute-start.5 = (bf16[512,128]{1,0:T(8,128)(2,1)S(1)}, bf16[512,128]{1,0:T(8,128)(2,1)S(1)}, u32[]{:S(2)}, u32[]{:S(2)}) collective-permute-start(bf16[512,128]{1,0:T(8,128)(2,1)S(1)} %get-tuple-element.42), channel_id=1, source_target_pairs={{0,2},{1,3},{2,0},{3,1},{4,6},{5,7},{6,4},{7,5},{8,10},{9,11},{10,... | collective-permute-start | bytes 393224 | tf_op jit(solution)/shard_map/ppermute | solution.py:21
  23.6 0.9 %shard_map.78 = (bf16[768,512]{1,0:T(8,128)(2,1)S(1)}, bf16[768,512]{1,0:T(8,128)(2,1)S(1)}) custom-call(bf16[768,512]{1,0:T(8,128)(2,1)S(1)} %get-tuple-element.39.mine, bf16[768,512]{1,0:T(8,128)(2,1)S(1)} %collective-permute-done.4.near_ref), custom_call_target="tpu_custom_call" | custom-call | flops 1073741824 | bytes 1572864 | tf_op jit(solution)/shard_map/pallas_call | solution.py:77
  24.5 2.7 %collective-permute-done.9.ny_ref = bf16[128,512]{1,0:T(8,128)(2,1)S(1)} collective-permute-done((bf16[128,512]{1,0:T(8,128)(2,1)S(1)}, bf16[128,512]{1,0:T(8,128)(2,1)S(1)}, u32[]{:S(2)}, u32[]{:S(2)}) %collective-permute-start.9) | collective-permute-done | bytes 131104 | tf_op jit(solution)/shard_map/ppermute | solution.py:21
  27.3 2.1 %collective-permute-start.10 = (bf16[128,512]{1,0:T(8,128)(2,1)S(1)}, bf16[128,512]{1,0:T(8,128)(2,1)S(1)}, u32[]{:S(2)}, u32[]{:S(2)}) collective-permute-start(bf16[128,512]{1,0:T(8,128)(2,1)S(1)} %get-tuple-element.50), channel_id=1, source_target_pairs={{0,4},{1,5},{2,6},{3,7},{4,0},{5,1},{6,2},{7,3},{8,12},{9,13},{10,... | collective-permute-start | bytes 393224 | tf_op jit(solution)/shard_map/ppermute | solution.py:21
  29.3 0.7 %shard_map.81.direct_ref = f32[2,256,128]{2,1,0:T(8,128)S(1)} custom-call(bf16[2,2,256,1024]{3,2,1,0:T(8,128)(2,1)S(1)} %get-tuple-element.52.mid_ref, bf16[1024,128]{1,0:T(8,128)(2,1)S(1)} %get-tuple-element.54.source_ref, bf16[1024,128]{1,0:T(8,128)(2,1)S(1)} %get-tuple-element.55.spun_ref), custom_call_target="tpu_custom_call" | custom-call | flops 268435456 | bytes 2621440 | tf_op jit(solution)/shard_map/pallas_call | solution.py:77
  30.1 0.8 %shard_map.79 = (f32[256,128]{1,0:T(8,128)S(1)}, bf16[256,128]{1,0:T(8,128)(2,1)S(1)}, f32[512,128]{1,0:T(8,128)S(1)}) custom-call(f32[512,128]{1,0:T(8,128)S(1)} %get-tuple-element.41.mine, bf16[512,128]{1,0:T(8,128)(2,1)S(1)} %collective-permute-done.5.other_ref, bf16[768,512]{1,0:T(8,128)(2,1)S(1)} %get-tuple-element.43.refs_0_.mine, ...), custom_call_target="tpu_custom_call" | custom-call | flops 335544320 | bytes 2752512 | tf_op jit(solution)/shard_map/pallas_call | solution.py:77
  30.9 0.6 %collective-permute-start.8 = (bf16[256,128]{1,0:T(8,128)(2,1)S(1)}, bf16[256,128]{1,0:T(8,128)(2,1)S(1)}, u32[]{:S(2)}, u32[]{:S(2)}) collective-permute-start(bf16[256,128]{1,0:T(8,128)(2,1)S(1)} %get-tuple-element.47), channel_id=1, source_target_pairs={{0,4},{1,5},{2,6},{3,7},{4,0},{5,1},{6,2},{7,3},{8,12},{9,13},{10,... | collective-permute-start | bytes 196616 | tf_op jit(solution)/shard_map/ppermute | solution.py:21
  31.6 0.7 %collective-permute-done.10.near_ref = bf16[128,512]{1,0:T(8,128)(2,1)S(1)} collective-permute-done((bf16[128,512]{1,0:T(8,128)(2,1)S(1)}, bf16[128,512]{1,0:T(8,128)(2,1)S(1)}, u32[]{:S(2)}, u32[]{:S(2)}) %collective-permute-start.10) | collective-permute-done | bytes 131104 | tf_op jit(solution)/shard_map/ppermute | solution.py:21
  32.3 1.2 %shard_map.83.wide_ref = bf16[1024,512]{1,0:T(8,128)(2,1)S(1)} custom-call(bf16[768,512]{1,0:T(8,128)(2,1)S(1)} %get-tuple-element.43.refs_0_.mine, bf16[256,512]{1,0:T(8,128)(2,1)S(1)} %collective-permute-done.6.refs_1_.near_ref, bf16[256,512]{1,0:T(8,128)(2,1)S(1)} %collective-permute-done.7.refs_2_.far_ref, ...), custom_call_target="tpu_custom_call" | custom-call | flops 2147483648 | bytes 7208960 | tf_op jit(solution)/shard_map/pallas_call | solution.py:77
  33.5 0.9 %shard_map.82.base_ref = f32[1024,128]{1,0:T(8,128)S(1)} custom-call(f32[512,128]{1,0:T(8,128)S(1)} %get-tuple-element.51.reach_ref.hint_ref, bf16[2,2,256,1024]{3,2,1,0:T(8,128)(2,1)S(1)} %get-tuple-element.33.ends_ref, bf16[2,2,256,1024]{3,2,1,0:T(8,128)(2,1)S(1)} %get-tuple-element.52.mid_ref, bf16[256,256]{1,0:T(8,128)(2,1)S(1)} %bitcast.7, ...), custom_call_target="tpu_custom_call" | custom-call | flops 536870912 | bytes 5242880 | tf_op jit(solution)/shard_map/pallas_call | solution.py:77
  34.4 1.0 %collective-permute-done.8.other_ref = bf16[256,128]{1,0:T(8,128)(2,1)S(1)} collective-permute-done((bf16[256,128]{1,0:T(8,128)(2,1)S(1)}, bf16[256,128]{1,0:T(8,128)(2,1)S(1)}, u32[]{:S(2)}, u32[]{:S(2)}) %collective-permute-start.8) | collective-permute-done | bytes 65568 | tf_op jit(solution)/shard_map/ppermute | solution.py:21
  35.5 1.4 %shard_map.84 = bf16[1024,128]{1,0:T(8,128)(2,1)} custom-call(bf16[256,128]{1,0:T(8,128)(2,1)S(1)} %collective-permute-done.8.other_ref, f32[256,128]{1,0:T(8,128)S(1)} %get-tuple-element.48.c_ref, bf16[128,512]{1,0:T(8,128)(2,1)S(1)} %collective-permute-done.10.near_ref, bf16[128,512]{1,0:T(8,128)(2,1)S(1)} %collective-permute-done.11.far_ref, ...), custom_call_target="tpu_custom_call" | custom-call | flops 268435456 | bytes 2031616 | tf_op jit(solution)/shard_map/pallas_call | solution.py:77
  (26 shorter events, 1.9 us)
Async XLA Ops:
  0.0 12.7 %copy-start.3 = (s32[4,4]{1,0:T(4,128)S(1)}, s32[4,4]{1,0:T(4,128)}, u32[]{:S(2)}) copy-start(s32[4,4]{1,0:T(4,128)} %start_ref.5) | copy-start | bytes 196
  0.0 12.7 %copy-start.4 = (s32[4,4]{1,0:T(4,128)S(1)}, s32[4,4]{1,0:T(4,128)}, u32[]{:S(2)}) copy-start(s32[4,4]{1,0:T(4,128)} %count_ref.1) | copy-start | bytes 196
  0.0 12.7 %copy-start.5 = (f32[4,4]{1,0:T(4,128)S(1)}, f32[4,4]{1,0:T(4,128)}, u32[]{:S(2)}) copy-start(f32[4,4]{1,0:T(4,128)} %strength_ref.1) | copy-start | bytes 196
  2.4 10.4 %copy-start.1 = (bf16[1,1,1024,128]{3,2,1,0:T(8,128)(2,1)S(1)}, bf16[1,1,1024,128]{3,2,1,0:T(8,128)(2,1)}, u32[]{:S(2)}) copy-start(bf16[1,1,1024,128]{3,2,1,0:T(8,128)(2,1)} %param.9) | copy-start | bytes 786436
  2.4 10.4 %copy-start.2 = (bf16[1,1,1024,128]{3,2,1,0:T(8,128)(2,1)S(1)}, bf16[1,1,1024,128]{3,2,1,0:T(8,128)(2,1)}, u32[]{:S(2)}) copy-start(bf16[1,1,1024,128]{3,2,1,0:T(8,128)(2,1)} %param.8) | copy-start | bytes 786436
  2.4 2.5 %collective-permute-start.4 = (bf16[768,512]{1,0:T(8,128)(2,1)S(1)}, bf16[768,512]{1,0:T(8,128)(2,1)S(1)}, u32[]{:S(2)}, u32[]{:S(2)}) collective-permute-start(bf16[768,512]{1,0:T(8,128)(2,1)S(1)} %get-tuple-element.39.mine), channel_id=1, source_target_pairs={{0,1},{1,0},{2,3},{3,2},{4,5},{5,4},{6,7},{7,6},{8,9},{9,8},{10,11... | collective-permute-start | bytes 2359304 | tf_op jit(solution)/shard_map/ppermute | solution.py:21
  5.4 14.9 %collective-permute-start.6 = (bf16[256,512]{1,0:T(8,128)(2,1)S(1)}, bf16[256,512]{1,0:T(8,128)(2,1)S(1)}, u32[]{:S(2)}, u32[]{:S(2)}) collective-permute-start(bf16[256,512]{1,0:T(8,128)(2,1)S(1)} %get-tuple-element.44), channel_id=1, source_target_pairs={{0,2},{1,3},{2,0},{3,1},{4,6},{5,7},{6,4},{7,5},{8,10},{9,11},{10,... | collective-permute-start | bytes 786440 | tf_op jit(solution)/shard_map/ppermute | solution.py:21
  8.3 7.3 %collective-permute-start = (bf16[256,128]{1,0:T(8,128)(2,1)S(1)}, bf16[256,128]{1,0:T(8,128)(2,1)S(1)}, u32[]{:S(2)}, u32[]{:S(2)}) collective-permute-start(bf16[256,128]{1,0:T(8,128)(2,1)S(1)} %get-tuple-element.35), channel_id=1, source_target_pairs={{0,8},{8,0},{16,24},{24,16},{1,9},{9,1},{17,25},{25,17},{2,10},{10... | collective-permute-start | bytes 196616 | tf_op jit(solution)/shard_map/ppermute | solution.py:21
  9.9 7.3 %collective-permute-start.1 = (bf16[256,128]{1,0:T(8,128)(2,1)S(1)}, bf16[256,128]{1,0:T(8,128)(2,1)S(1)}, u32[]{:S(2)}, u32[]{:S(2)}) collective-permute-start(bf16[256,128]{1,0:T(8,128)(2,1)S(1)} %get-tuple-element.36), channel_id=1, source_target_pairs={{0,16},{8,24},{16,0},{24,8},{1,17},{9,25},{17,1},{25,9},{2,18},{10... | collective-permute-start | bytes 196616 | tf_op jit(solution)/shard_map/ppermute | solution.py:21
  12.5 6.1 %collective-permute-start.2 = (bf16[256,128]{1,0:T(8,128)(2,1)S(1)}, bf16[256,128]{1,0:T(8,128)(2,1)S(1)}, u32[]{:S(2)}, u32[]{:S(2)}) collective-permute-start(bf16[256,128]{1,0:T(8,128)(2,1)S(1)} %get-tuple-element.37), channel_id=1, source_target_pairs={{0,24},{8,16},{16,8},{24,0},{1,25},{9,17},{17,9},{25,1},{2,26},{10... | collective-permute-start | bytes 196616 | tf_op jit(solution)/shard_map/ppermute | solution.py:21
  20.3 1.6 %collective-permute-start.3 = (f32[512,128]{1,0:T(8,128)S(1)}, f32[512,128]{1,0:T(8,128)S(1)}, u32[]{:S(2)}, u32[]{:S(2)}) collective-permute-start(f32[512,128]{1,0:T(8,128)S(1)} %get-tuple-element.38.mine.sent_ref), channel_id=1, source_target_pairs={{0,1},{1,0},{2,3},{3,2},{4,5},{5,4},{6,7},{7,6},{8,9},{9,8},{10,11... | collective-permute-start | bytes 786440 | tf_op jit(solution)/shard_map/ppermute | solution.py:21
  20.4 6.9 %collective-permute-start.7 = (bf16[256,512]{1,0:T(8,128)(2,1)S(1)}, bf16[256,512]{1,0:T(8,128)(2,1)S(1)}, u32[]{:S(2)}, u32[]{:S(2)}) collective-permute-start(bf16[256,512]{1,0:T(8,128)(2,1)S(1)} %collective-permute-done.6.refs_1_.near_ref), channel_id=1, source_target_pairs={{0,1},{1,0},{2,3},{3,2},{4,5},{5,4},{6,7},{7,6},{8,9},{9,8},{10,11... | collective-permute-start | bytes 786440 | tf_op jit(solution)/shard_map/ppermute | solution.py:21
  20.9 6.4 %collective-permute-start.9 = (bf16[128,512]{1,0:T(8,128)(2,1)S(1)}, bf16[128,512]{1,0:T(8,128)(2,1)S(1)}, u32[]{:S(2)}, u32[]{:S(2)}) collective-permute-start(bf16[128,512]{1,0:T(8,128)(2,1)S(1)} %get-tuple-element.49), channel_id=1, source_target_pairs={{0,2},{1,3},{2,0},{3,1},{4,6},{5,7},{6,4},{7,5},{8,10},{9,11},{10,... | collective-permute-start | bytes 393224 | tf_op jit(solution)/shard_map/ppermute | solution.py:21
  22.5 7.6 %collective-permute-start.5 = (bf16[512,128]{1,0:T(8,128)(2,1)S(1)}, bf16[512,128]{1,0:T(8,128)(2,1)S(1)}, u32[]{:S(2)}, u32[]{:S(2)}) collective-permute-start(bf16[512,128]{1,0:T(8,128)(2,1)S(1)} %get-tuple-element.42), channel_id=1, source_target_pairs={{0,2},{1,3},{2,0},{3,1},{4,6},{5,7},{6,4},{7,5},{8,10},{9,11},{10,... | collective-permute-start | bytes 393224 | tf_op jit(solution)/shard_map/ppermute | solution.py:21
  27.3 5.0 %collective-permute-start.10 = (bf16[128,512]{1,0:T(8,128)(2,1)S(1)}, bf16[128,512]{1,0:T(8,128)(2,1)S(1)}, u32[]{:S(2)}, u32[]{:S(2)}) collective-permute-start(bf16[128,512]{1,0:T(8,128)(2,1)S(1)} %get-tuple-element.50), channel_id=1, source_target_pairs={{0,4},{1,5},{2,6},{3,7},{4,0},{5,1},{6,2},{7,3},{8,12},{9,13},{10,... | collective-permute-start | bytes 393224 | tf_op jit(solution)/shard_map/ppermute | solution.py:21
  29.3 3.0 %collective-permute-start.12 = (bf16[128,512]{1,0:T(8,128)(2,1)S(1)}, bf16[128,512]{1,0:T(8,128)(2,1)S(1)}, u32[]{:S(2)}, u32[]{:S(2)}) collective-permute-start(bf16[128,512]{1,0:T(8,128)(2,1)S(1)} %collective-permute-done.9.ny_ref), channel_id=1, source_target_pairs={{0,1},{1,0},{2,3},{3,2},{4,5},{5,4},{6,7},{7,6},{8,9},{9,8},{10,11... | collective-permute-start | bytes 393224 | tf_op jit(solution)/shard_map/ppermute | solution.py:21
  30.1 2.2 %copy-start = (bf16[1,256,256]{2,1,0:T(8,128)(2,1)S(1)}, bf16[1,256,256]{2,1,0:T(8,128)(2,1)}, u32[]{:S(2)}) copy-start(bf16[1,256,256]{2,1,0:T(8,128)(2,1)} %param.10) | copy-start | bytes 393220
  30.9 4.6 %collective-permute-start.8 = (bf16[256,128]{1,0:T(8,128)(2,1)S(1)}, bf16[256,128]{1,0:T(8,128)(2,1)S(1)}, u32[]{:S(2)}, u32[]{:S(2)}) collective-permute-start(bf16[256,128]{1,0:T(8,128)(2,1)S(1)} %get-tuple-element.47), channel_id=1, source_target_pairs={{0,4},{1,5},{2,6},{3,7},{4,0},{5,1},{6,2},{7,3},{8,12},{9,13},{10,... | collective-permute-start | bytes 196616 | tf_op jit(solution)/shard_map/ppermute | solution.py:21
  32.3 3.2 %collective-permute-start.11 = (bf16[128,512]{1,0:T(8,128)(2,1)S(1)}, bf16[128,512]{1,0:T(8,128)(2,1)S(1)}, u32[]{:S(2)}, u32[]{:S(2)}) collective-permute-start(bf16[128,512]{1,0:T(8,128)(2,1)S(1)} %collective-permute-done.10.near_ref), channel_id=1, source_target_pairs={{0,1},{1,0},{2,3},{3,2},{4,5},{5,4},{6,7},{7,6},{8,9},{9,8},{10,11... | collective-permute-start | bytes 393224 | tf_op jit(solution)/shard_map/ppermute | solution.py:21

commit v10 on v9

--- a/solution.py
+++ b/solution.py
@@ -112,19 +112,20 @@
     triple, one_map = (3 * layer, 2 * layer), (layer, 2 * layer)
 
     def own_maps(green_ref, coup_ref, start_ref, panel_ref, *refs):
-        maps_ref, turn_ref = refs[:2]
-        pieces = refs[2 : energies + 1]
-        corner, near, whole, table, sem, sem_c, sem_t, sem_p = refs[energies + 1 :]
+        maps_ref, turn_ref, ends_ref = refs[:3]
+        pieces = refs[3 : energies + 2]
+        near, whole, table, sem, sem_c, sem_t, sem_p = refs[energies + 2 :]
         ask = pltpu.make_async_copy(start_ref, table, sem_t)
         panel_copy = pltpu.make_async_copy(panel_ref, whole, sem_p)
         first = pltpu.make_async_copy(coup_ref, near, sem_c)
-        top, end = pl.ds(0, layer), pl.ds(low, layer)
         copies = [
             [
-                pltpu.make_async_copy(green_ref.at[k, r, c], corner.at[i, k], sem.at[i, k])
+                pltpu.make_async_copy(
+                    green_ref.at[k, pl.ds(i * low, layer)], ends_ref.at[k, i], sem.at[i, k]
+                )
                 for k in range(2)
             ]
-            for i, (r, c) in enumerate(((end, top), (top, end), (top, top)))
+            for i in range(2)
         ]
         ask.start()
         first.start()
@@ -135,35 +136,33 @@
         me = lax.axis_index("energy")
         first.wait()
         c = near[...]
-        ct = c.astype(f32).T.astype(bf16)
-        turn_ref[...] = ct
         panel_copy.wait()
         ask.wait()
         for k in range(energies - 1):
             begin = pl.multiple_of(table[me ^ (k + 1), me] * rows, rows)
             pieces[k][...] = whole[pl.ds(begin, span)]
-        for i in range(3):
-            for k in range(2):
-                copies[i][k].wait()
-                held = corner[i, k]
-                if i == 0:
-                    held = dot(ct, held).astype(bf16)
-                elif i == 1:
-                    held = dot(held, c).astype(bf16)
-                maps_ref[rows_of[i], rows_of[k]] = held
-
-    maps, coup_t, *pieces = call(
+        ct = c.astype(f32).T.astype(bf16)
+        turn_ref[...] = ct
+        for pair in copies:
+            for copy in pair:
+                copy.wait()
+        for k in range(2):
+            maps_ref[rows_of[1], rows_of[k]] = dot(ends_ref[k, 0, :, low:], c).astype(bf16)
+            maps_ref[rows_of[0], rows_of[k]] = dot(ct, ends_ref[k, 1, :, :layer]).astype(bf16)
+            maps_ref[rows_of[2], rows_of[k]] = ends_ref[k, 0, :, :layer]
+
+    maps, coup_t, ends, *pieces = call(
         own_maps,
-        [(triple, bf16), ((layer, layer), bf16)] + [((span, width), bf16)] * (energies - 1),
+        [(triple, bf16), ((layer, layer), bf16), ((2, 2, layer, norb), bf16)]
+        + [((span, width), bf16)] * (energies - 1),
         (far_green, far_coup, in_hbm(block_start), in_hbm(panel)),
         8 * layer**3,
         {k: pltpu.HBM for k in range(4)},
         [
-            pltpu.VMEM((3, 2, layer, layer), bf16),
             pltpu.VMEM((layer, layer), bf16),
             pltpu.VMEM(panel.shape, bf16),
             pltpu.SMEM(block_start.shape, block_start.dtype),
-            pltpu.SemaphoreType.DMA((3, 2)),
+            pltpu.SemaphoreType.DMA((2, 2)),
             pltpu.SemaphoreType.DMA,
             pltpu.SemaphoreType.DMA,
             pltpu.SemaphoreType.DMA,
@@ -446,11 +445,10 @@
 
     def prepare(
         green_ref, inj_ref, panel_ref, start_ref, count_ref, strength_ref,
-        ends_ref, mid_ref, acc_ref, weight_ref, sem, sem_mid,
+        mid_ref, acc_ref, weight_ref, sem,
     ):
-        copies = fetch(green_ref, ends_ref, sem, (pl.ds(0, layer), pl.ds(low, layer)))
         spots = [pl.ds((i + 1) * layer, layer) for i in range(blocks)]
-        copies += fetch(green_ref, mid_ref, sem_mid, spots)
+        copies = fetch(green_ref, mid_ref, sem, spots)
         me = lax.axis_index("energy")
         row = lax.broadcasted_iota(jnp.int32, (span, width), 0)
         acc_ref[...] = inj_ref[...].astype(f32)
@@ -466,10 +464,9 @@
         for copy in copies:
             copy.wait()
 
-    ends, mid, acc, weights = call(
+    mid, acc, weights = call(
         prepare,
         [
-            ((2, 2, layer, norb), bf16),
             ((2, blocks, layer, norb), bf16),
             ((norb, width), f32),
             ((energies - 1, span, width), f32),
@@ -477,7 +474,7 @@
         (far_green, injection[0, 0], panel, block_start, block_count, strength),
         0,
         {0: pltpu.HBM, 3: SMEM, 4: SMEM, 5: SMEM},
-        [pltpu.SemaphoreType.DMA((2, 2)), pltpu.SemaphoreType.DMA((blocks, 2))],
+        [pltpu.SemaphoreType.DMA((blocks, 2))],
     )
 
     def load(start_ref, acc_ref, weight_ref, ends_ref, turn_ref, *refs):
@@ -494,8 +491,8 @@
         spun_ref[...] = spun
         direct = dot(ends_ref[0, 1], source) + dot(ends_ref[1, 1], spun)
         low_ref[...] = direct
+        sent_ref[ways[1]] = dot(ends_ref[0, 0], source) + dot(ends_ref[1, 0], spun)
         sent_ref[ways[0]] = fine(turn_ref[...], direct)
-        sent_ref[ways[1]] = dot(ends_ref[0, 0], source) + dot(ends_ref[1, 0], spun)
 
     source, spun, direct_low, sent = call(
         load,
@@ -597,13 +594,21 @@
         16 * norb * layer * width,
     )
 
-    def finish(other_ref, c_ref, near_ref, far_ref, base_ref, wide_ref, out_ref, kept, sem):
-        first = place(0)
-        other = other_ref[...].astype(f32)
-        c_left = c_ref[...]
-        a, b = mapped(near_ref[...], c_left), mapped(far_ref[...], c_left)
-        bounce = jnp.concatenate([jnp.where(first, b, a), jnp.where(first, a, b)], axis=0)
-        last = other + jnp.where(place(final), jnp.zeros_like(bounce), bounce)
+    def rebound(c_ref, near_ref, far_ref, out_ref):
+        @pl.when(place(final))
+        def _():
+            out_ref[...] = jnp.zeros(out_ref.shape, f32)
+
+        @pl.when(~place(final))
+        def _():
+            out_ref[...] = mapped(theirs(near_ref, far_ref, 0), c_ref[...])
+
+    (bounce,) = call(
+        rebound, [((layer, width), f32)], (c_total, e_near, e_far), 8 * layer * layer * width
+    )
+
+    def finish(other_ref, bounce_ref, base_ref, wide_ref, out_ref, kept, sem):
+        last = other_ref[...].astype(f32) + bounce_ref[...]
         copies = []
         v, spun = last.astype(bf16), turned(last).astype(bf16)
         for i in range(norb // layer):
@@ -620,7 +625,7 @@
     (out,) = call(
         finish,
         [((norb, width), bf16)],
-        (arrived, c_total, e_near, e_far, base, last_map),
+        (arrived, bounce, base, last_map),
         8 * norb * layer * width,
         scratch=[pltpu.VMEM((norb, width), bf16), pltpu.SemaphoreType.DMA((norb // layer,))],
         out_space=pltpu.HBM,

time: 37 us -> 36.4 us (0.984)
  Pallas kernels: 14 us -> 13 us
    pallas_call x12 -> x13, Pallas kernels: 14 us -> 13 us  [call(): pl.pallas_call(kernel, out_shape=shapes, in_specs=specs, out_specs=[pl.Bl...]
  transfers between devices with their start and end apart: 13 -> 13, of which waited for: 7 -> 7; matrix products, arithmetic and copies ran while one was open for 0% -> 0% of each run, Pallas kernels for 26% -> 25%
where the time goes in v10:
time: 36.4 us; the launch traced here: 36.2 us
  Pallas kernels  13 us (36%)
  starting transfers between devices  12.8 us (35%)
  waiting for transfers between devices  10.3 us (28%)
    pallas_call x13, Pallas kernels, call(): pl.pallas_call(kernel, out_shape=shapes, in_specs=specs, out_specs=[pl.Bl...  13 us
    ppermute x13, starting transfers between devices, swapped(): return lax.ppermute(block, axis, [(i, i ^ mask) for i in range(count)])  12.8 us
    ppermute x13, waiting for transfers between devices, swapped(): return lax.ppermute(block, axis, [(i, i ^ mask) for i in range(count)])  10.3 us
  transfers between devices with their start and end apart: 13, of which 7 were waited for; matrix products, arithmetic and copies ran while one was open for 0% of the time, Pallas kernels for 25%

profile of v10, /device:TPU:0, one launch (start us, length us, event | category | flops | bytes accessed | tf_op | source)
XLA Modules:
  0.0 36.2 jit_solution(10913166402642225162)
XLA Ops:
  0.0 2.1 %shard_map.74 = (bf16[768,512]{1,0:T(8,128)(2,1)S(1)}, bf16[256,256]{1,0:T(8,128)(2,1)S(1)}, bf16[2,2,256,1024]{3,2,1,0:T(8,128)(2,1)S(1)}, bf16[256,128]{1,0:T(...) custom-call(bf16[2,1024,1024]{2,1,0:T(8,128)(2,1)} %bitcast.11, bf16[256,256]{1,0:T(8,128)(2,1)} %bitcast.5, ...), custom_call_target="tpu_custom_call" | custom-call | flops 134217728 | bytes 4587584 | tf_op jit(solution)/shard_map/pallas_call | solution.py:77
  2.1 0.6 %collective-permute-start.4 = (bf16[768,512]{1,0:T(8,128)(2,1)S(1)}, bf16[768,512]{1,0:T(8,128)(2,1)S(1)}, u32[]{:S(2)}, u32[]{:S(2)}) collective-permute-start(bf16[768,512]{1,0:T(8,128)(2,1)S(1)} %get-tuple-element.39.mine), channel_id=1, source_target_pairs={{0,1},{1,0},{2,3},{3,2},{4,5},{5,4},{6,7},{7,6},{8,9},{9,8},{10,11... | collective-permute-start | bytes 2359304 | tf_op jit(solution)/shard_map/ppermute | solution.py:21
  2.7 1.9 %collective-permute-done.4.near_ref = bf16[768,512]{1,0:T(8,128)(2,1)S(1)} collective-permute-done((bf16[768,512]{1,0:T(8,128)(2,1)S(1)}, bf16[768,512]{1,0:T(8,128)(2,1)S(1)}, u32[]{:S(2)}, u32[]{:S(2)}) %collective-permute-start.4) | collective-permute-done | bytes 786464 | tf_op jit(solution)/shard_map/ppermute | solution.py:21
  4.6 0.6 %shard_map.76 = (bf16[768,512]{1,0:T(8,128)(2,1)S(1)}, bf16[256,512]{1,0:T(8,128)(2,1)S(1)}, bf16[128,512]{1,0:T(8,128)(2,1)S(1)}) custom-call(bf16[768,512]{1,0:T(8,128)(2,1)S(1)} %get-tuple-element.39.mine, bf16[768,512]{1,0:T(8,128)(2,1)S(1)} %collective-permute-done.4.near_ref), custom_call_target="tpu_custom_call" | custom-call | flops 536870912 | bytes 1572864 | tf_op jit(solution)/shard_map/pallas_call | solution.py:77
  5.1 2.9 %collective-permute-start.6 = (bf16[256,512]{1,0:T(8,128)(2,1)S(1)}, bf16[256,512]{1,0:T(8,128)(2,1)S(1)}, u32[]{:S(2)}, u32[]{:S(2)}) collective-permute-start(bf16[256,512]{1,0:T(8,128)(2,1)S(1)} %get-tuple-element.44), channel_id=1, source_target_pairs={{0,2},{1,3},{2,0},{3,1},{4,6},{5,7},{6,4},{7,5},{8,10},{9,11},{10,... | collective-permute-start | bytes 786440 | tf_op jit(solution)/shard_map/ppermute | solution.py:21
  8.1 1.6 %collective-permute-start = (bf16[256,128]{1,0:T(8,128)(2,1)S(1)}, bf16[256,128]{1,0:T(8,128)(2,1)S(1)}, u32[]{:S(2)}, u32[]{:S(2)}) collective-permute-start(bf16[256,128]{1,0:T(8,128)(2,1)S(1)} %get-tuple-element.35), channel_id=1, source_target_pairs={{0,8},{8,0},{16,24},{24,16},{1,9},{9,1},{17,25},{25,17},{2,10},{10... | collective-permute-start | bytes 196616 | tf_op jit(solution)/shard_map/ppermute | solution.py:21
  9.6 2.6 %collective-permute-start.1 = (bf16[256,128]{1,0:T(8,128)(2,1)S(1)}, bf16[256,128]{1,0:T(8,128)(2,1)S(1)}, u32[]{:S(2)}, u32[]{:S(2)}) collective-permute-start(bf16[256,128]{1,0:T(8,128)(2,1)S(1)} %get-tuple-element.36), channel_id=1, source_target_pairs={{0,16},{8,24},{16,0},{24,8},{1,17},{9,25},{17,1},{25,9},{2,18},{10... | collective-permute-start | bytes 196616 | tf_op jit(solution)/shard_map/ppermute | solution.py:21
  12.5 2.2 %shard_map.73 = (bf16[2,2,256,1024]{3,2,1,0:T(8,128)(2,1)S(1)}, f32[1024,128]{1,0:T(8,128)S(1)}, f32[3,256,128]{2,1,0:T(8,128)S(1)}) custom-call(bf16[2,1024,1024]{2,1,0:T(8,128)(2,1)} %bitcast.12, bf16[1024,128]{1,0:T(8,128)(2,1)S(1)} %bitcast.10, bf16[1024,128]{1,0:T(8,128)(2,1)S(1)} %bitcast.9, s32[4,4]{1,0:T(4,128)S(1)} %copy-done.3, ...), custom_call_target="tpu_custom_call" | custom-call | bytes 4718784 | tf_op jit(solution)/shard_map/pallas_call | solution.py:77
  14.7 2.3 %collective-permute-done.1.refs_1_ = bf16[256,128]{1,0:T(8,128)(2,1)S(1)} collective-permute-done((bf16[256,128]{1,0:T(8,128)(2,1)S(1)}, bf16[256,128]{1,0:T(8,128)(2,1)S(1)}, u32[]{:S(2)}, u32[]{:S(2)}) %collective-permute-start.1) | collective-permute-done | bytes 65568 | tf_op jit(solution)/shard_map/ppermute | solution.py:21
  16.9 1.4 %collective-permute-done.2.refs_2_ = bf16[256,128]{1,0:T(8,128)(2,1)S(1)} collective-permute-done((bf16[256,128]{1,0:T(8,128)(2,1)S(1)}, bf16[256,128]{1,0:T(8,128)(2,1)S(1)}, u32[]{:S(2)}, u32[]{:S(2)}) %collective-permute-start.2) | collective-permute-done | bytes 65568 | tf_op jit(solution)/shard_map/ppermute | solution.py:21
  18.3 1.5 %shard_map.75 = (bf16[1024,128]{1,0:T(8,128)(2,1)S(1)}, bf16[1024,128]{1,0:T(8,128)(2,1)S(1)}, f32[256,128]{1,0:T(8,128)S(1)}, f32[512,128]{1,0:T(8,128)S(1)}) custom-call(s32[4,4]{1,0:T(4,128)S(1)} %copy-done.3, f32[1024,128]{1,0:T(8,128)S(1)} %get-tuple-element.31.acc_ref, f32[3,256,128]{2,1,0:T(8,128)S(1)} %get-tuple-element.32.weight_ref, ...), custom_call_target="tpu_custom_call" | custom-call | flops 268435456 | bytes 3342400 | tf_op jit(solution)/shard_map/pallas_call | solution.py:77
  21.5 0.6 %shard_map.77 = (f32[512,128]{1,0:T(8,128)S(1)}, bf16[512,128]{1,0:T(8,128)(2,1)S(1)}, f32[512,128]{1,0:T(8,128)S(1)}) custom-call(f32[512,128]{1,0:T(8,128)S(1)} %get-tuple-element.38.mine.sent_ref, f32[512,128]{1,0:T(8,128)S(1)} %collective-permute-done.3.other_ref, bf16[768,512]{1,0:T(8,128)(2,1)S(1)} %get-tuple-element.40.refs_0_), custom_call_target="tpu_custom_call" | custom-call | flops 335544320 | bytes 1310720 | tf_op jit(solution)/shard_map/pallas_call | solution.py:77
  22.1 1.1 %collective-permute-start.5 = (bf16[512,128]{1,0:T(8,128)(2,1)S(1)}, bf16[512,128]{1,0:T(8,128)(2,1)S(1)}, u32[]{:S(2)}, u32[]{:S(2)}) collective-permute-start(bf16[512,128]{1,0:T(8,128)(2,1)S(1)} %get-tuple-element.42), channel_id=1, source_target_pairs={{0,2},{1,3},{2,0},{3,1},{4,6},{5,7},{6,4},{7,5},{8,10},{9,11},{10,... | collective-permute-start | bytes 393224 | tf_op jit(solution)/shard_map/ppermute | solution.py:21
  23.2 0.9 %shard_map.78 = (bf16[768,512]{1,0:T(8,128)(2,1)S(1)}, bf16[768,512]{1,0:T(8,128)(2,1)S(1)}) custom-call(bf16[768,512]{1,0:T(8,128)(2,1)S(1)} %get-tuple-element.39.mine, bf16[768,512]{1,0:T(8,128)(2,1)S(1)} %collective-permute-done.4.near_ref), custom_call_target="tpu_custom_call" | custom-call | flops 1073741824 | bytes 1572864 | tf_op jit(solution)/shard_map/pallas_call | solution.py:77
  24.1 2.7 %collective-permute-done.9.ny_ref = bf16[128,512]{1,0:T(8,128)(2,1)S(1)} collective-permute-done((bf16[128,512]{1,0:T(8,128)(2,1)S(1)}, bf16[128,512]{1,0:T(8,128)(2,1)S(1)}, u32[]{:S(2)}, u32[]{:S(2)}) %collective-permute-start.9) | collective-permute-done | bytes 131104 | tf_op jit(solution)/shard_map/ppermute | solution.py:21
  26.8 2.1 %collective-permute-start.10 = (bf16[128,512]{1,0:T(8,128)(2,1)S(1)}, bf16[128,512]{1,0:T(8,128)(2,1)S(1)}, u32[]{:S(2)}, u32[]{:S(2)}) collective-permute-start(bf16[128,512]{1,0:T(8,128)(2,1)S(1)} %get-tuple-element.50), channel_id=1, source_target_pairs={{0,4},{1,5},{2,6},{3,7},{4,0},{5,1},{6,2},{7,3},{8,12},{9,13},{10,... | collective-permute-start | bytes 393224 | tf_op jit(solution)/shard_map/ppermute | solution.py:21
  28.9 0.7 %shard_map.82.direct_ref = f32[2,256,128]{2,1,0:T(8,128)S(1)} custom-call(bf16[2,2,256,1024]{3,2,1,0:T(8,128)(2,1)S(1)} %get-tuple-element.52.mid_ref, bf16[1024,128]{1,0:T(8,128)(2,1)S(1)} %get-tuple-element.54.source_ref, bf16[1024,128]{1,0:T(8,128)(2,1)S(1)} %get-tuple-element.55.spun_ref), custom_call_target="tpu_custom_call" | custom-call | flops 268435456 | bytes 2621440 | tf_op jit(solution)/shard_map/pallas_call | solution.py:77
  29.7 0.8 %shard_map.79 = (f32[256,128]{1,0:T(8,128)S(1)}, bf16[256,128]{1,0:T(8,128)(2,1)S(1)}, f32[512,128]{1,0:T(8,128)S(1)}) custom-call(f32[512,128]{1,0:T(8,128)S(1)} %get-tuple-element.41.mine, bf16[512,128]{1,0:T(8,128)(2,1)S(1)} %collective-permute-done.5.other_ref, bf16[768,512]{1,0:T(8,128)(2,1)S(1)} %get-tuple-element.43.refs_0_.mine, ...), custom_call_target="tpu_custom_call" | custom-call | flops 335544320 | bytes 2752512 | tf_op jit(solution)/shard_map/pallas_call | solution.py:77
  30.5 0.6 %collective-permute-start.8 = (bf16[256,128]{1,0:T(8,128)(2,1)S(1)}, bf16[256,128]{1,0:T(8,128)(2,1)S(1)}, u32[]{:S(2)}, u32[]{:S(2)}) collective-permute-start(bf16[256,128]{1,0:T(8,128)(2,1)S(1)} %get-tuple-element.47), channel_id=1, source_target_pairs={{0,4},{1,5},{2,6},{3,7},{4,0},{5,1},{6,2},{7,3},{8,12},{9,13},{10,... | collective-permute-start | bytes 196616 | tf_op jit(solution)/shard_map/ppermute | solution.py:21
  31.1 0.8 %collective-permute-done.10.near_ref = bf16[128,512]{1,0:T(8,128)(2,1)S(1)} collective-permute-done((bf16[128,512]{1,0:T(8,128)(2,1)S(1)}, bf16[128,512]{1,0:T(8,128)(2,1)S(1)}, u32[]{:S(2)}, u32[]{:S(2)}) %collective-permute-start.10) | collective-permute-done | bytes 131104 | tf_op jit(solution)/shard_map/ppermute | solution.py:21
  31.9 1.2 %shard_map.84.wide_ref = bf16[1024,512]{1,0:T(8,128)(2,1)S(1)} custom-call(bf16[768,512]{1,0:T(8,128)(2,1)S(1)} %get-tuple-element.43.refs_0_.mine, bf16[256,512]{1,0:T(8,128)(2,1)S(1)} %collective-permute-done.6.refs_1_.near_ref, bf16[256,512]{1,0:T(8,128)(2,1)S(1)} %collective-permute-done.7.refs_2_.far_ref, ...), custom_call_target="tpu_custom_call" | custom-call | flops 2147483648 | bytes 7208960 | tf_op jit(solution)/shard_map/pallas_call | solution.py:77
  33.1 0.9 %shard_map.83.base_ref = f32[1024,128]{1,0:T(8,128)S(1)} custom-call(f32[512,128]{1,0:T(8,128)S(1)} %get-tuple-element.51.reach_ref.hint_ref, bf16[2,2,256,1024]{3,2,1,0:T(8,128)(2,1)S(1)} %get-tuple-element.33.ends_ref, bf16[2,2,256,1024]{3,2,1,0:T(8,128)(2,1)S(1)} %get-tuple-element.52.mid_ref, bf16[256,256]{1,0:T(8,128)(2,1)S(1)} %bitcast.7, ...), custom_call_target="tpu_custom_call" | custom-call | flops 536870912 | bytes 5242880 | tf_op jit(solution)/shard_map/pallas_call | solution.py:77
  34.3 0.7 %collective-permute-done.8.other_ref = bf16[256,128]{1,0:T(8,128)(2,1)S(1)} collective-permute-done((bf16[256,128]{1,0:T(8,128)(2,1)S(1)}, bf16[256,128]{1,0:T(8,128)(2,1)S(1)}, u32[]{:S(2)}, u32[]{:S(2)}) %collective-permute-start.8) | collective-permute-done | bytes 65568 | tf_op jit(solution)/shard_map/ppermute | solution.py:21
  35.0 1.2 %shard_map.85 = bf16[1024,128]{1,0:T(8,128)(2,1)} custom-call(bf16[256,128]{1,0:T(8,128)(2,1)S(1)} %collective-permute-done.8.other_ref, f32[256,128]{1,0:T(8,128)S(1)} %shard_map.81.bounce_ref, f32[1024,128]{1,0:T(8,128)S(1)} %shard_map.83.base_ref, bf16[1024,512]{1,0:T(8,128)(2,1)S(1)} %shard_map.84.wide_ref), custom_call_target="tpu_custom_call" | custom-call | flops 268435456 | bytes 1769472 | tf_op jit(solution)/shard_map/pallas_call | solution.py:77
  (27 shorter events, 2.2 us)
Async XLA Ops:
  0.0 12.4 %copy-start.3 = (s32[4,4]{1,0:T(4,128)S(1)}, s32[4,4]{1,0:T(4,128)}, u32[]{:S(2)}) copy-start(s32[4,4]{1,0:T(4,128)} %start_ref.5) | copy-start | bytes 196
  0.0 12.4 %copy-start.4 = (s32[4,4]{1,0:T(4,128)S(1)}, s32[4,4]{1,0:T(4,128)}, u32[]{:S(2)}) copy-start(s32[4,4]{1,0:T(4,128)} %count_ref.1) | copy-start | bytes 196
  0.0 12.4 %copy-start.5 = (f32[4,4]{1,0:T(4,128)S(1)}, f32[4,4]{1,0:T(4,128)}, u32[]{:S(2)}) copy-start(f32[4,4]{1,0:T(4,128)} %strength_ref.1) | copy-start | bytes 196
  2.1 10.4 %copy-start.1 = (bf16[1,1,1024,128]{3,2,1,0:T(8,128)(2,1)S(1)}, bf16[1,1,1024,128]{3,2,1,0:T(8,128)(2,1)}, u32[]{:S(2)}) copy-start(bf16[1,1,1024,128]{3,2,1,0:T(8,128)(2,1)} %param.9) | copy-start | bytes 786436
  2.1 10.4 %copy-start.2 = (bf16[1,1,1024,128]{3,2,1,0:T(8,128)(2,1)S(1)}, bf16[1,1,1024,128]{3,2,1,0:T(8,128)(2,1)}, u32[]{:S(2)}) copy-start(bf16[1,1,1024,128]{3,2,1,0:T(8,128)(2,1)} %param.8) | copy-start | bytes 786436
  2.1 2.5 %collective-permute-start.4 = (bf16[768,512]{1,0:T(8,128)(2,1)S(1)}, bf16[768,512]{1,0:T(8,128)(2,1)S(1)}, u32[]{:S(2)}, u32[]{:S(2)}) collective-permute-start(bf16[768,512]{1,0:T(8,128)(2,1)S(1)} %get-tuple-element.39.mine), channel_id=1, source_target_pairs={{0,1},{1,0},{2,3},{3,2},{4,5},{5,4},{6,7},{7,6},{8,9},{9,8},{10,11... | collective-permute-start | bytes 2359304 | tf_op jit(solution)/shard_map/ppermute | solution.py:21
  5.1 14.8 %collective-permute-start.6 = (bf16[256,512]{1,0:T(8,128)(2,1)S(1)}, bf16[256,512]{1,0:T(8,128)(2,1)S(1)}, u32[]{:S(2)}, u32[]{:S(2)}) collective-permute-start(bf16[256,512]{1,0:T(8,128)(2,1)S(1)} %get-tuple-element.44), channel_id=1, source_target_pairs={{0,2},{1,3},{2,0},{3,1},{4,6},{5,7},{6,4},{7,5},{8,10},{9,11},{10,... | collective-permute-start | bytes 786440 | tf_op jit(solution)/shard_map/ppermute | solution.py:21
  8.1 6.6 %collective-permute-start = (bf16[256,128]{1,0:T(8,128)(2,1)S(1)}, bf16[256,128]{1,0:T(8,128)(2,1)S(1)}, u32[]{:S(2)}, u32[]{:S(2)}) collective-permute-start(bf16[256,128]{1,0:T(8,128)(2,1)S(1)} %get-tuple-element.35), channel_id=1, source_target_pairs={{0,8},{8,0},{16,24},{24,16},{1,9},{9,1},{17,25},{25,17},{2,10},{10... | collective-permute-start | bytes 196616 | tf_op jit(solution)/shard_map/ppermute | solution.py:21
  9.6 7.3 %collective-permute-start.1 = (bf16[256,128]{1,0:T(8,128)(2,1)S(1)}, bf16[256,128]{1,0:T(8,128)(2,1)S(1)}, u32[]{:S(2)}, u32[]{:S(2)}) collective-permute-start(bf16[256,128]{1,0:T(8,128)(2,1)S(1)} %get-tuple-element.36), channel_id=1, source_target_pairs={{0,16},{8,24},{16,0},{24,8},{1,17},{9,25},{17,1},{25,9},{2,18},{10... | collective-permute-start | bytes 196616 | tf_op jit(solution)/shard_map/ppermute | solution.py:21
  12.2 6.1 %collective-permute-start.2 = (bf16[256,128]{1,0:T(8,128)(2,1)S(1)}, bf16[256,128]{1,0:T(8,128)(2,1)S(1)}, u32[]{:S(2)}, u32[]{:S(2)}) collective-permute-start(bf16[256,128]{1,0:T(8,128)(2,1)S(1)} %get-tuple-element.37), channel_id=1, source_target_pairs={{0,24},{8,16},{16,8},{24,0},{1,25},{9,17},{17,9},{25,1},{2,26},{10... | collective-permute-start | bytes 196616 | tf_op jit(solution)/shard_map/ppermute | solution.py:21
  19.9 1.6 %collective-permute-start.3 = (f32[512,128]{1,0:T(8,128)S(1)}, f32[512,128]{1,0:T(8,128)S(1)}, u32[]{:S(2)}, u32[]{:S(2)}) collective-permute-start(f32[512,128]{1,0:T(8,128)S(1)} %get-tuple-element.38.mine.sent_ref), channel_id=1, source_target_pairs={{0,1},{1,0},{2,3},{3,2},{4,5},{5,4},{6,7},{7,6},{8,9},{9,8},{10,11... | collective-permute-start | bytes 786440 | tf_op jit(solution)/shard_map/ppermute | solution.py:21
  19.9 6.9 %collective-permute-start.7 = (bf16[256,512]{1,0:T(8,128)(2,1)S(1)}, bf16[256,512]{1,0:T(8,128)(2,1)S(1)}, u32[]{:S(2)}, u32[]{:S(2)}) collective-permute-start(bf16[256,512]{1,0:T(8,128)(2,1)S(1)} %collective-permute-done.6.refs_1_.near_ref), channel_id=1, source_target_pairs={{0,1},{1,0},{2,3},{3,2},{4,5},{5,4},{6,7},{7,6},{8,9},{9,8},{10,11... | collective-permute-start | bytes 786440 | tf_op jit(solution)/shard_map/ppermute | solution.py:21
  20.4 6.4 %collective-permute-start.9 = (bf16[128,512]{1,0:T(8,128)(2,1)S(1)}, bf16[128,512]{1,0:T(8,128)(2,1)S(1)}, u32[]{:S(2)}, u32[]{:S(2)}) collective-permute-start(bf16[128,512]{1,0:T(8,128)(2,1)S(1)} %get-tuple-element.49), channel_id=1, source_target_pairs={{0,2},{1,3},{2,0},{3,1},{4,6},{5,7},{6,4},{7,5},{8,10},{9,11},{10,... | collective-permute-start | bytes 393224 | tf_op jit(solution)/shard_map/ppermute | solution.py:21
  22.1 7.6 %collective-permute-start.5 = (bf16[512,128]{1,0:T(8,128)(2,1)S(1)}, bf16[512,128]{1,0:T(8,128)(2,1)S(1)}, u32[]{:S(2)}, u32[]{:S(2)}) collective-permute-start(bf16[512,128]{1,0:T(8,128)(2,1)S(1)} %get-tuple-element.42), channel_id=1, source_target_pairs={{0,2},{1,3},{2,0},{3,1},{4,6},{5,7},{6,4},{7,5},{8,10},{9,11},{10,... | collective-permute-start | bytes 393224 | tf_op jit(solution)/shard_map/ppermute | solution.py:21
  26.8 5.0 %collective-permute-start.10 = (bf16[128,512]{1,0:T(8,128)(2,1)S(1)}, bf16[128,512]{1,0:T(8,128)(2,1)S(1)}, u32[]{:S(2)}, u32[]{:S(2)}) collective-permute-start(bf16[128,512]{1,0:T(8,128)(2,1)S(1)} %get-tuple-element.50), channel_id=1, source_target_pairs={{0,4},{1,5},{2,6},{3,7},{4,0},{5,1},{6,2},{7,3},{8,12},{9,13},{10,... | collective-permute-start | bytes 393224 | tf_op jit(solution)/shard_map/ppermute | solution.py:21
  28.9 3.0 %collective-permute-start.12 = (bf16[128,512]{1,0:T(8,128)(2,1)S(1)}, bf16[128,512]{1,0:T(8,128)(2,1)S(1)}, u32[]{:S(2)}, u32[]{:S(2)}) collective-permute-start(bf16[128,512]{1,0:T(8,128)(2,1)S(1)} %collective-permute-done.9.ny_ref), channel_id=1, source_target_pairs={{0,1},{1,0},{2,3},{3,2},{4,5},{5,4},{6,7},{7,6},{8,9},{9,8},{10,11... | collective-permute-start | bytes 393224 | tf_op jit(solution)/shard_map/ppermute | solution.py:21
  29.6 2.3 %copy-start = (bf16[1,256,256]{2,1,0:T(8,128)(2,1)S(1)}, bf16[1,256,256]{2,1,0:T(8,128)(2,1)}, u32[]{:S(2)}) copy-start(bf16[1,256,256]{2,1,0:T(8,128)(2,1)} %param.10) | copy-start | bytes 393220
  30.5 4.6 %collective-permute-start.8 = (bf16[256,128]{1,0:T(8,128)(2,1)S(1)}, bf16[256,128]{1,0:T(8,128)(2,1)S(1)}, u32[]{:S(2)}, u32[]{:S(2)}) collective-permute-start(bf16[256,128]{1,0:T(8,128)(2,1)S(1)} %get-tuple-element.47), channel_id=1, source_target_pairs={{0,4},{1,5},{2,6},{3,7},{4,0},{5,1},{6,2},{7,3},{8,12},{9,13},{10,... | collective-permute-start | bytes 196616 | tf_op jit(solution)/shard_map/ppermute | solution.py:21
  31.9 2.1 %collective-permute-start.11 = (bf16[128,512]{1,0:T(8,128)(2,1)S(1)}, bf16[128,512]{1,0:T(8,128)(2,1)S(1)}, u32[]{:S(2)}, u32[]{:S(2)}) collective-permute-start(bf16[128,512]{1,0:T(8,128)(2,1)S(1)} %collective-permute-done.10.near_ref), channel_id=1, source_target_pairs={{0,1},{1,0},{2,3},{3,2},{4,5},{5,4},{6,7},{7,6},{8,9},{9,8},{10,11... | collective-permute-start | bytes 393224 | tf_op jit(solution)/shard_map/ppermute | solution.py:21

commit v11 on v10

--- a/solution.py
+++ b/solution.py
@@ -611,8 +611,8 @@
         last = other_ref[...].astype(f32) + bounce_ref[...]
         copies = []
         v, spun = last.astype(bf16), turned(last).astype(bf16)
-        for i in range(norb // layer):
-            part = pl.ds(i * layer, layer)
+        for i in range(norb // cut):
+            part = pl.ds(i * cut, cut)
             kept[part] = (
                 base_ref[part] + dot(wide_ref[part, :layer], v) + dot(wide_ref[part, layer:], spun)
             ).astype(bf16)
@@ -627,7 +627,7 @@
         [((norb, width), bf16)],
         (arrived, bounce, base, last_map),
         8 * norb * layer * width,
-        scratch=[pltpu.VMEM((norb, width), bf16), pltpu.SemaphoreType.DMA((norb // layer,))],
+        scratch=[pltpu.VMEM((norb, width), bf16), pltpu.SemaphoreType.DMA((norb // cut,))],
         out_space=pltpu.HBM,
     )
     return out[None, None]

time: 36.4 us -> 36.4 us (level)
  no operation moved by 1% of the time
where the time goes in v11:
time: 36.4 us; the launch traced here: 36.2 us
  Pallas kernels  13 us (36%)
  starting transfers between devices  12.8 us (35%)
  waiting for transfers between devices  10.3 us (28%)
    pallas_call x13, Pallas kernels, call(): pl.pallas_call(kernel, out_shape=shapes, in_specs=specs, out_specs=[pl.Bl...  13 us
    ppermute x13, starting transfers between devices, swapped(): return lax.ppermute(block, axis, [(i, i ^ mask) for i in range(count)])  12.8 us
    ppermute x13, waiting for transfers between devices, swapped(): return lax.ppermute(block, axis, [(i, i ^ mask) for i in range(count)])  10.3 us
  transfers between devices with their start and end apart: 13, of which 7 were waited for; matrix products, arithmetic and copies ran while one was open for 0% of the time, Pallas kernels for 25%

profile of v11, /device:TPU:0, one launch (start us, length us, event | category | flops | bytes accessed | tf_op | source)
XLA Modules:
  0.0 36.2 jit_solution(16775908249469214125)
XLA Ops:
  0.0 2.1 %shard_map.74 = (bf16[768,512]{1,0:T(8,128)(2,1)S(1)}, bf16[256,256]{1,0:T(8,128)(2,1)S(1)}, bf16[2,2,256,1024]{3,2,1,0:T(8,128)(2,1)S(1)}, bf16[256,128]{1,0:T(...) custom-call(bf16[2,1024,1024]{2,1,0:T(8,128)(2,1)} %bitcast.11, bf16[256,256]{1,0:T(8,128)(2,1)} %bitcast.5, ...), custom_call_target="tpu_custom_call" | custom-call | flops 134217728 | bytes 4587584 | tf_op jit(solution)/shard_map/pallas_call | solution.py:77
  2.1 0.6 %collective-permute-start.4 = (bf16[768,512]{1,0:T(8,128)(2,1)S(1)}, bf16[768,512]{1,0:T(8,128)(2,1)S(1)}, u32[]{:S(2)}, u32[]{:S(2)}) collective-permute-start(bf16[768,512]{1,0:T(8,128)(2,1)S(1)} %get-tuple-element.39.mine), channel_id=1, source_target_pairs={{0,1},{1,0},{2,3},{3,2},{4,5},{5,4},{6,7},{7,6},{8,9},{9,8},{10,11... | collective-permute-start | bytes 2359304 | tf_op jit(solution)/shard_map/ppermute | solution.py:21
  2.7 1.9 %collective-permute-done.4.near_ref = bf16[768,512]{1,0:T(8,128)(2,1)S(1)} collective-permute-done((bf16[768,512]{1,0:T(8,128)(2,1)S(1)}, bf16[768,512]{1,0:T(8,128)(2,1)S(1)}, u32[]{:S(2)}, u32[]{:S(2)}) %collective-permute-start.4) | collective-permute-done | bytes 786464 | tf_op jit(solution)/shard_map/ppermute | solution.py:21
  4.6 0.6 %shard_map.76 = (bf16[768,512]{1,0:T(8,128)(2,1)S(1)}, bf16[256,512]{1,0:T(8,128)(2,1)S(1)}, bf16[128,512]{1,0:T(8,128)(2,1)S(1)}) custom-call(bf16[768,512]{1,0:T(8,128)(2,1)S(1)} %get-tuple-element.39.mine, bf16[768,512]{1,0:T(8,128)(2,1)S(1)} %collective-permute-done.4.near_ref), custom_call_target="tpu_custom_call" | custom-call | flops 536870912 | bytes 1572864 | tf_op jit(solution)/shard_map/pallas_call | solution.py:77
  5.1 2.9 %collective-permute-start.6 = (bf16[256,512]{1,0:T(8,128)(2,1)S(1)}, bf16[256,512]{1,0:T(8,128)(2,1)S(1)}, u32[]{:S(2)}, u32[]{:S(2)}) collective-permute-start(bf16[256,512]{1,0:T(8,128)(2,1)S(1)} %get-tuple-element.44), channel_id=1, source_target_pairs={{0,2},{1,3},{2,0},{3,1},{4,6},{5,7},{6,4},{7,5},{8,10},{9,11},{10,... | collective-permute-start | bytes 786440 | tf_op jit(solution)/shard_map/ppermute | solution.py:21
  8.1 1.6 %collective-permute-start = (bf16[256,128]{1,0:T(8,128)(2,1)S(1)}, bf16[256,128]{1,0:T(8,128)(2,1)S(1)}, u32[]{:S(2)}, u32[]{:S(2)}) collective-permute-start(bf16[256,128]{1,0:T(8,128)(2,1)S(1)} %get-tuple-element.35), channel_id=1, source_target_pairs={{0,8},{8,0},{16,24},{24,16},{1,9},{9,1},{17,25},{25,17},{2,10},{10... | collective-permute-start | bytes 196616 | tf_op jit(solution)/shard_map/ppermute | solution.py:21
  9.6 2.6 %collective-permute-start.1 = (bf16[256,128]{1,0:T(8,128)(2,1)S(1)}, bf16[256,128]{1,0:T(8,128)(2,1)S(1)}, u32[]{:S(2)}, u32[]{:S(2)}) collective-permute-start(bf16[256,128]{1,0:T(8,128)(2,1)S(1)} %get-tuple-element.36), channel_id=1, source_target_pairs={{0,16},{8,24},{16,0},{24,8},{1,17},{9,25},{17,1},{25,9},{2,18},{10... | collective-permute-start | bytes 196616 | tf_op jit(solution)/shard_map/ppermute | solution.py:21
  12.5 2.2 %shard_map.73 = (bf16[2,2,256,1024]{3,2,1,0:T(8,128)(2,1)S(1)}, f32[1024,128]{1,0:T(8,128)S(1)}, f32[3,256,128]{2,1,0:T(8,128)S(1)}) custom-call(bf16[2,1024,1024]{2,1,0:T(8,128)(2,1)} %bitcast.12, bf16[1024,128]{1,0:T(8,128)(2,1)S(1)} %bitcast.10, bf16[1024,128]{1,0:T(8,128)(2,1)S(1)} %bitcast.9, s32[4,4]{1,0:T(4,128)S(1)} %copy-done.3, ...), custom_call_target="tpu_custom_call" | custom-call | bytes 4718784 | tf_op jit(solution)/shard_map/pallas_call | solution.py:77
  14.7 2.3 %collective-permute-done.1.refs_1_ = bf16[256,128]{1,0:T(8,128)(2,1)S(1)} collective-permute-done((bf16[256,128]{1,0:T(8,128)(2,1)S(1)}, bf16[256,128]{1,0:T(8,128)(2,1)S(1)}, u32[]{:S(2)}, u32[]{:S(2)}) %collective-permute-start.1) | collective-permute-done | bytes 65568 | tf_op jit(solution)/shard_map/ppermute | solution.py:21
  16.9 1.4 %collective-permute-done.2.refs_2_ = bf16[256,128]{1,0:T(8,128)(2,1)S(1)} collective-permute-done((bf16[256,128]{1,0:T(8,128)(2,1)S(1)}, bf16[256,128]{1,0:T(8,128)(2,1)S(1)}, u32[]{:S(2)}, u32[]{:S(2)}) %collective-permute-start.2) | collective-permute-done | bytes 65568 | tf_op jit(solution)/shard_map/ppermute | solution.py:21
  18.3 1.5 %shard_map.75 = (bf16[1024,128]{1,0:T(8,128)(2,1)S(1)}, bf16[1024,128]{1,0:T(8,128)(2,1)S(1)}, f32[256,128]{1,0:T(8,128)S(1)}, f32[512,128]{1,0:T(8,128)S(1)}) custom-call(s32[4,4]{1,0:T(4,128)S(1)} %copy-done.3, f32[1024,128]{1,0:T(8,128)S(1)} %get-tuple-element.31.acc_ref, f32[3,256,128]{2,1,0:T(8,128)S(1)} %get-tuple-element.32.weight_ref, ...), custom_call_target="tpu_custom_call" | custom-call | flops 268435456 | bytes 3342400 | tf_op jit(solution)/shard_map/pallas_call | solution.py:77
  21.5 0.6 %shard_map.77 = (f32[512,128]{1,0:T(8,128)S(1)}, bf16[512,128]{1,0:T(8,128)(2,1)S(1)}, f32[512,128]{1,0:T(8,128)S(1)}) custom-call(f32[512,128]{1,0:T(8,128)S(1)} %get-tuple-element.38.mine.sent_ref, f32[512,128]{1,0:T(8,128)S(1)} %collective-permute-done.3.other_ref, bf16[768,512]{1,0:T(8,128)(2,1)S(1)} %get-tuple-element.40.refs_0_), custom_call_target="tpu_custom_call" | custom-call | flops 335544320 | bytes 1310720 | tf_op jit(solution)/shard_map/pallas_call | solution.py:77
  22.1 1.1 %collective-permute-start.5 = (bf16[512,128]{1,0:T(8,128)(2,1)S(1)}, bf16[512,128]{1,0:T(8,128)(2,1)S(1)}, u32[]{:S(2)}, u32[]{:S(2)}) collective-permute-start(bf16[512,128]{1,0:T(8,128)(2,1)S(1)} %get-tuple-element.42), channel_id=1, source_target_pairs={{0,2},{1,3},{2,0},{3,1},{4,6},{5,7},{6,4},{7,5},{8,10},{9,11},{10,... | collective-permute-start | bytes 393224 | tf_op jit(solution)/shard_map/ppermute | solution.py:21
  23.2 0.9 %shard_map.78 = (bf16[768,512]{1,0:T(8,128)(2,1)S(1)}, bf16[768,512]{1,0:T(8,128)(2,1)S(1)}) custom-call(bf16[768,512]{1,0:T(8,128)(2,1)S(1)} %get-tuple-element.39.mine, bf16[768,512]{1,0:T(8,128)(2,1)S(1)} %collective-permute-done.4.near_ref), custom_call_target="tpu_custom_call" | custom-call | flops 1073741824 | bytes 1572864 | tf_op jit(solution)/shard_map/pallas_call | solution.py:77
  24.1 2.7 %collective-permute-done.9.ny_ref = bf16[128,512]{1,0:T(8,128)(2,1)S(1)} collective-permute-done((bf16[128,512]{1,0:T(8,128)(2,1)S(1)}, bf16[128,512]{1,0:T(8,128)(2,1)S(1)}, u32[]{:S(2)}, u32[]{:S(2)}) %collective-permute-start.9) | collective-permute-done | bytes 131104 | tf_op jit(solution)/shard_map/ppermute | solution.py:21
  26.8 2.1 %collective-permute-start.10 = (bf16[128,512]{1,0:T(8,128)(2,1)S(1)}, bf16[128,512]{1,0:T(8,128)(2,1)S(1)}, u32[]{:S(2)}, u32[]{:S(2)}) collective-permute-start(bf16[128,512]{1,0:T(8,128)(2,1)S(1)} %get-tuple-element.50), channel_id=1, source_target_pairs={{0,4},{1,5},{2,6},{3,7},{4,0},{5,1},{6,2},{7,3},{8,12},{9,13},{10,... | collective-permute-start | bytes 393224 | tf_op jit(solution)/shard_map/ppermute | solution.py:21
  28.9 0.7 %shard_map.82.direct_ref = f32[2,256,128]{2,1,0:T(8,128)S(1)} custom-call(bf16[2,2,256,1024]{3,2,1,0:T(8,128)(2,1)S(1)} %get-tuple-element.52.mid_ref, bf16[1024,128]{1,0:T(8,128)(2,1)S(1)} %get-tuple-element.54.source_ref, bf16[1024,128]{1,0:T(8,128)(2,1)S(1)} %get-tuple-element.55.spun_ref), custom_call_target="tpu_custom_call" | custom-call | flops 268435456 | bytes 2621440 | tf_op jit(solution)/shard_map/pallas_call | solution.py:77
  29.7 0.8 %shard_map.79 = (f32[256,128]{1,0:T(8,128)S(1)}, bf16[256,128]{1,0:T(8,128)(2,1)S(1)}, f32[512,128]{1,0:T(8,128)S(1)}) custom-call(f32[512,128]{1,0:T(8,128)S(1)} %get-tuple-element.41.mine, bf16[512,128]{1,0:T(8,128)(2,1)S(1)} %collective-permute-done.5.other_ref, bf16[768,512]{1,0:T(8,128)(2,1)S(1)} %get-tuple-element.43.refs_0_.mine, ...), custom_call_target="tpu_custom_call" | custom-call | flops 335544320 | bytes 2752512 | tf_op jit(solution)/shard_map/pallas_call | solution.py:77
  30.5 0.6 %collective-permute-start.8 = (bf16[256,128]{1,0:T(8,128)(2,1)S(1)}, bf16[256,128]{1,0:T(8,128)(2,1)S(1)}, u32[]{:S(2)}, u32[]{:S(2)}) collective-permute-start(bf16[256,128]{1,0:T(8,128)(2,1)S(1)} %get-tuple-element.47), channel_id=1, source_target_pairs={{0,4},{1,5},{2,6},{3,7},{4,0},{5,1},{6,2},{7,3},{8,12},{9,13},{10,... | collective-permute-start | bytes 196616 | tf_op jit(solution)/shard_map/ppermute | solution.py:21
  31.1 0.8 %collective-permute-done.10.near_ref = bf16[128,512]{1,0:T(8,128)(2,1)S(1)} collective-permute-done((bf16[128,512]{1,0:T(8,128)(2,1)S(1)}, bf16[128,512]{1,0:T(8,128)(2,1)S(1)}, u32[]{:S(2)}, u32[]{:S(2)}) %collective-permute-start.10) | collective-permute-done | bytes 131104 | tf_op jit(solution)/shard_map/ppermute | solution.py:21
  31.9 1.2 %shard_map.84.wide_ref = bf16[1024,512]{1,0:T(8,128)(2,1)S(1)} custom-call(bf16[768,512]{1,0:T(8,128)(2,1)S(1)} %get-tuple-element.43.refs_0_.mine, bf16[256,512]{1,0:T(8,128)(2,1)S(1)} %collective-permute-done.6.refs_1_.near_ref, bf16[256,512]{1,0:T(8,128)(2,1)S(1)} %collective-permute-done.7.refs_2_.far_ref, ...), custom_call_target="tpu_custom_call" | custom-call | flops 2147483648 | bytes 7208960 | tf_op jit(solution)/shard_map/pallas_call | solution.py:77
  33.1 0.9 %shard_map.83.base_ref = f32[1024,128]{1,0:T(8,128)S(1)} custom-call(f32[512,128]{1,0:T(8,128)S(1)} %get-tuple-element.51.reach_ref.hint_ref, bf16[2,2,256,1024]{3,2,1,0:T(8,128)(2,1)S(1)} %get-tuple-element.33.ends_ref, bf16[2,2,256,1024]{3,2,1,0:T(8,128)(2,1)S(1)} %get-tuple-element.52.mid_ref, bf16[256,256]{1,0:T(8,128)(2,1)S(1)} %bitcast.7, ...), custom_call_target="tpu_custom_call" | custom-call | flops 536870912 | bytes 5242880 | tf_op jit(solution)/shard_map/pallas_call | solution.py:77
  34.3 0.7 %collective-permute-done.8.other_ref = bf16[256,128]{1,0:T(8,128)(2,1)S(1)} collective-permute-done((bf16[256,128]{1,0:T(8,128)(2,1)S(1)}, bf16[256,128]{1,0:T(8,128)(2,1)S(1)}, u32[]{:S(2)}, u32[]{:S(2)}) %collective-permute-start.8) | collective-permute-done | bytes 65568 | tf_op jit(solution)/shard_map/ppermute | solution.py:21
  35.0 1.2 %shard_map.85 = bf16[1024,128]{1,0:T(8,128)(2,1)} custom-call(bf16[256,128]{1,0:T(8,128)(2,1)S(1)} %collective-permute-done.8.other_ref, f32[256,128]{1,0:T(8,128)S(1)} %shard_map.81.bounce_ref, f32[1024,128]{1,0:T(8,128)S(1)} %shard_map.83.base_ref, bf16[1024,512]{1,0:T(8,128)(2,1)S(1)} %shard_map.84.wide_ref), custom_call_target="tpu_custom_call" | custom-call | flops 268435456 | bytes 1769472 | tf_op jit(solution)/shard_map/pallas_call | solution.py:77
  (27 shorter events, 2.2 us)
Async XLA Ops:
  0.0 12.4 %copy-start.3 = (s32[4,4]{1,0:T(4,128)S(1)}, s32[4,4]{1,0:T(4,128)}, u32[]{:S(2)}) copy-start(s32[4,4]{1,0:T(4,128)} %start_ref.5) | copy-start | bytes 196
  0.0 12.4 %copy-start.4 = (s32[4,4]{1,0:T(4,128)S(1)}, s32[4,4]{1,0:T(4,128)}, u32[]{:S(2)}) copy-start(s32[4,4]{1,0:T(4,128)} %count_ref.1) | copy-start | bytes 196
  0.0 12.4 %copy-start.5 = (f32[4,4]{1,0:T(4,128)S(1)}, f32[4,4]{1,0:T(4,128)}, u32[]{:S(2)}) copy-start(f32[4,4]{1,0:T(4,128)} %strength_ref.1) | copy-start | bytes 196
  2.1 10.4 %copy-start.1 = (bf16[1,1,1024,128]{3,2,1,0:T(8,128)(2,1)S(1)}, bf16[1,1,1024,128]{3,2,1,0:T(8,128)(2,1)}, u32[]{:S(2)}) copy-start(bf16[1,1,1024,128]{3,2,1,0:T(8,128)(2,1)} %param.9) | copy-start | bytes 786436
  2.1 10.4 %copy-start.2 = (bf16[1,1,1024,128]{3,2,1,0:T(8,128)(2,1)S(1)}, bf16[1,1,1024,128]{3,2,1,0:T(8,128)(2,1)}, u32[]{:S(2)}) copy-start(bf16[1,1,1024,128]{3,2,1,0:T(8,128)(2,1)} %param.8) | copy-start | bytes 786436
  2.1 2.5 %collective-permute-start.4 = (bf16[768,512]{1,0:T(8,128)(2,1)S(1)}, bf16[768,512]{1,0:T(8,128)(2,1)S(1)}, u32[]{:S(2)}, u32[]{:S(2)}) collective-permute-start(bf16[768,512]{1,0:T(8,128)(2,1)S(1)} %get-tuple-element.39.mine), channel_id=1, source_target_pairs={{0,1},{1,0},{2,3},{3,2},{4,5},{5,4},{6,7},{7,6},{8,9},{9,8},{10,11... | collective-permute-start | bytes 2359304 | tf_op jit(solution)/shard_map/ppermute | solution.py:21
  5.1 14.8 %collective-permute-start.6 = (bf16[256,512]{1,0:T(8,128)(2,1)S(1)}, bf16[256,512]{1,0:T(8,128)(2,1)S(1)}, u32[]{:S(2)}, u32[]{:S(2)}) collective-permute-start(bf16[256,512]{1,0:T(8,128)(2,1)S(1)} %get-tuple-element.44), channel_id=1, source_target_pairs={{0,2},{1,3},{2,0},{3,1},{4,6},{5,7},{6,4},{7,5},{8,10},{9,11},{10,... | collective-permute-start | bytes 786440 | tf_op jit(solution)/shard_map/ppermute | solution.py:21
  8.1 6.6 %collective-permute-start = (bf16[256,128]{1,0:T(8,128)(2,1)S(1)}, bf16[256,128]{1,0:T(8,128)(2,1)S(1)}, u32[]{:S(2)}, u32[]{:S(2)}) collective-permute-start(bf16[256,128]{1,0:T(8,128)(2,1)S(1)} %get-tuple-element.35), channel_id=1, source_target_pairs={{0,8},{8,0},{16,24},{24,16},{1,9},{9,1},{17,25},{25,17},{2,10},{10... | collective-permute-start | bytes 196616 | tf_op jit(solution)/shard_map/ppermute | solution.py:21
  9.6 7.3 %collective-permute-start.1 = (bf16[256,128]{1,0:T(8,128)(2,1)S(1)}, bf16[256,128]{1,0:T(8,128)(2,1)S(1)}, u32[]{:S(2)}, u32[]{:S(2)}) collective-permute-start(bf16[256,128]{1,0:T(8,128)(2,1)S(1)} %get-tuple-element.36), channel_id=1, source_target_pairs={{0,16},{8,24},{16,0},{24,8},{1,17},{9,25},{17,1},{25,9},{2,18},{10... | collective-permute-start | bytes 196616 | tf_op jit(solution)/shard_map/ppermute | solution.py:21
  12.2 6.1 %collective-permute-start.2 = (bf16[256,128]{1,0:T(8,128)(2,1)S(1)}, bf16[256,128]{1,0:T(8,128)(2,1)S(1)}, u32[]{:S(2)}, u32[]{:S(2)}) collective-permute-start(bf16[256,128]{1,0:T(8,128)(2,1)S(1)} %get-tuple-element.37), channel_id=1, source_target_pairs={{0,24},{8,16},{16,8},{24,0},{1,25},{9,17},{17,9},{25,1},{2,26},{10... | collective-permute-start | bytes 196616 | tf_op jit(solution)/shard_map/ppermute | solution.py:21
  19.9 1.6 %collective-permute-start.3 = (f32[512,128]{1,0:T(8,128)S(1)}, f32[512,128]{1,0:T(8,128)S(1)}, u32[]{:S(2)}, u32[]{:S(2)}) collective-permute-start(f32[512,128]{1,0:T(8,128)S(1)} %get-tuple-element.38.mine.sent_ref), channel_id=1, source_target_pairs={{0,1},{1,0},{2,3},{3,2},{4,5},{5,4},{6,7},{7,6},{8,9},{9,8},{10,11... | collective-permute-start | bytes 786440 | tf_op jit(solution)/shard_map/ppermute | solution.py:21
  19.9 6.9 %collective-permute-start.7 = (bf16[256,512]{1,0:T(8,128)(2,1)S(1)}, bf16[256,512]{1,0:T(8,128)(2,1)S(1)}, u32[]{:S(2)}, u32[]{:S(2)}) collective-permute-start(bf16[256,512]{1,0:T(8,128)(2,1)S(1)} %collective-permute-done.6.refs_1_.near_ref), channel_id=1, source_target_pairs={{0,1},{1,0},{2,3},{3,2},{4,5},{5,4},{6,7},{7,6},{8,9},{9,8},{10,11... | collective-permute-start | bytes 786440 | tf_op jit(solution)/shard_map/ppermute | solution.py:21
  20.4 6.4 %collective-permute-start.9 = (bf16[128,512]{1,0:T(8,128)(2,1)S(1)}, bf16[128,512]{1,0:T(8,128)(2,1)S(1)}, u32[]{:S(2)}, u32[]{:S(2)}) collective-permute-start(bf16[128,512]{1,0:T(8,128)(2,1)S(1)} %get-tuple-element.49), channel_id=1, source_target_pairs={{0,2},{1,3},{2,0},{3,1},{4,6},{5,7},{6,4},{7,5},{8,10},{9,11},{10,... | collective-permute-start | bytes 393224 | tf_op jit(solution)/shard_map/ppermute | solution.py:21
  22.1 7.6 %collective-permute-start.5 = (bf16[512,128]{1,0:T(8,128)(2,1)S(1)}, bf16[512,128]{1,0:T(8,128)(2,1)S(1)}, u32[]{:S(2)}, u32[]{:S(2)}) collective-permute-start(bf16[512,128]{1,0:T(8,128)(2,1)S(1)} %get-tuple-element.42), channel_id=1, source_target_pairs={{0,2},{1,3},{2,0},{3,1},{4,6},{5,7},{6,4},{7,5},{8,10},{9,11},{10,... | collective-permute-start | bytes 393224 | tf_op jit(solution)/shard_map/ppermute | solution.py:21
  26.8 5.0 %collective-permute-start.10 = (bf16[128,512]{1,0:T(8,128)(2,1)S(1)}, bf16[128,512]{1,0:T(8,128)(2,1)S(1)}, u32[]{:S(2)}, u32[]{:S(2)}) collective-permute-start(bf16[128,512]{1,0:T(8,128)(2,1)S(1)} %get-tuple-element.50), channel_id=1, source_target_pairs={{0,4},{1,5},{2,6},{3,7},{4,0},{5,1},{6,2},{7,3},{8,12},{9,13},{10,... | collective-permute-start | bytes 393224 | tf_op jit(solution)/shard_map/ppermute | solution.py:21
  28.9 3.0 %collective-permute-start.12 = (bf16[128,512]{1,0:T(8,128)(2,1)S(1)}, bf16[128,512]{1,0:T(8,128)(2,1)S(1)}, u32[]{:S(2)}, u32[]{:S(2)}) collective-permute-start(bf16[128,512]{1,0:T(8,128)(2,1)S(1)} %collective-permute-done.9.ny_ref), channel_id=1, source_target_pairs={{0,1},{1,0},{2,3},{3,2},{4,5},{5,4},{6,7},{7,6},{8,9},{9,8},{10,11... | collective-permute-start | bytes 393224 | tf_op jit(solution)/shard_map/ppermute | solution.py:21
  29.6 2.3 %copy-start = (bf16[1,256,256]{2,1,0:T(8,128)(2,1)S(1)}, bf16[1,256,256]{2,1,0:T(8,128)(2,1)}, u32[]{:S(2)}) copy-start(bf16[1,256,256]{2,1,0:T(8,128)(2,1)} %param.10) | copy-start | bytes 393220
  30.5 4.6 %collective-permute-start.8 = (bf16[256,128]{1,0:T(8,128)(2,1)S(1)}, bf16[256,128]{1,0:T(8,128)(2,1)S(1)}, u32[]{:S(2)}, u32[]{:S(2)}) collective-permute-start(bf16[256,128]{1,0:T(8,128)(2,1)S(1)} %get-tuple-element.47), channel_id=1, source_target_pairs={{0,4},{1,5},{2,6},{3,7},{4,0},{5,1},{6,2},{7,3},{8,12},{9,13},{10,... | collective-permute-start | bytes 196616 | tf_op jit(solution)/shard_map/ppermute | solution.py:21
  31.9 2.1 %collective-permute-start.11 = (bf16[128,512]{1,0:T(8,128)(2,1)S(1)}, bf16[128,512]{1,0:T(8,128)(2,1)S(1)}, u32[]{:S(2)}, u32[]{:S(2)}) collective-permute-start(bf16[128,512]{1,0:T(8,128)(2,1)S(1)} %collective-permute-done.10.near_ref), channel_id=1, source_target_pairs={{0,1},{1,0},{2,3},{3,2},{4,5},{5,4},{6,7},{7,6},{8,9},{9,8},{10,11... | collective-permute-start | bytes 393224 | tf_op jit(solution)/shard_map/ppermute | solution.py:21
